TPU v7x, 32 devices: a whole 2x2x4 slice. The times are simulated.
32 devices in a mesh: dp: 8 (over z, core), tensor: 4 (over y, x).
Axes of the slice: x: 2, y: 2, z: 4, core: 2. Of those that a mesh axis runs over, the one named last changes fastest.
Arguments:
- block_input: bfloat16 [8192, 2048], P('dp'), may hold values from -6 to 6
- block_owner: int32 [64], P('dp'), may hold values from 0 to 63, as said below
- token_mask: int32 [8192], P('dp'), may hold values from 0 to 1, as said below
- attention_gain: float32 [2048], replicated, may hold values from 0.5 to 1.5
- query_weight: bfloat16 [2048, 2048], P(None, 'tensor')
- key_weight: bfloat16 [2048, 2048], P(None, 'tensor')
- value_weight: bfloat16 [2048, 2048], P(None, 'tensor'), may hold values from -0.125 to 0.125
- output_weight: bfloat16 [2048, 2048], P('tensor'), may hold values from -0.5 to 0.5
- feedforward_gain: float32 [2048], replicated, may hold values from 0.5 to 1.5
- gate_weight: bfloat16 [2048, 8192], P(None, 'tensor'), may hold values from -0.125 to 0.125
- up_weight: bfloat16 [2048, 8192], P(None, 'tensor'), may hold values from -0.125 to 0.125
- down_weight: bfloat16 [8192, 2048], P('tensor'), may hold values from -0.0625 to 0.0625
- cotangent: bfloat16 [8192, 2048], P('dp'), may hold values from -6 to 6
Outputs:
- block_output: bfloat16 [8192, 2048], P('dp')
- input_gradient: float32 [8192, 2048], P('dp')
- attention_gain_gradient: float32 [2048], P('dp')
- query_gradient: float32 [2048, 2048], P('dp', 'tensor')
- key_gradient: float32 [2048, 2048], P('dp', 'tensor')
- value_gradient: float32 [2048, 2048], P('dp', 'tensor')
- output_gradient: float32 [2048, 2048], P('tensor', 'dp')
- feedforward_gain_gradient: float32 [2048], P('dp')
- gate_gradient: float32 [2048, 8192], P('dp', 'tensor')
- up_gradient: float32 [2048, 8192], P('dp', 'tensor')
- down_gradient: float32 [8192, 2048], P('tensor', 'dp')
Inputs may be any that keep to these rules, and one draw needn't show every extreme that they name: `block_owner`: each sequence takes one to 4 consecutive blocks of a single index of dp; a block's entry is the index of its sequence's first block in the whole array. The first 4 blocks of every index of dp form one sequence. `token_mask`: in each sequence the real tokens come first and there is at least one unless the sequence is a single block of padding; the first sequence of every index of dp is all real (512 tokens). Blocks after the last real token of an index of dp are padding, each its own sequence.
All inputs are finite; a program needn't handle non-finite values.
Results may differ from a plain program's by a relative error of at most 0.014.
Values sent between devices are 32-bit elements; how exact they have to be, the bound alone decides.
No kernel may reach another device: no remote copies, remote signals or barrier semaphores. Data moves between devices by JAX's collectives and lax.ppermute only.
A program may use at most 384 MiB of HBM per device.

v0:
```python
import jax
import jax.numpy as jnp
from jax import lax
from jax.sharding import PartitionSpec as P

HD = 64
BLK = 128
GROUP = 512
WINDOW = 896


NORM_EPS = 1e-05
ROPE_BASE = 130000.0
MASKED = -1e30


def rms_forward(values, norm_gain):
    inverse = lax.rsqrt(jnp.mean(values * values, axis=-1, keepdims=True) + NORM_EPS)
    return (values * inverse * norm_gain, inverse)


def rms_backward(values, inverse, norm_gain, upstream):
    unit_rows = values * inverse
    gain_part = jnp.sum(upstream * unit_rows, axis=0)
    scaled = upstream * norm_gain
    back = inverse * (scaled - unit_rows * jnp.mean(scaled * unit_rows, axis=-1, keepdims=True))
    return (back, gain_part)


def rope_tables(positions, width):
    half_width = width // 2
    frequency = ROPE_BASE ** (-(jnp.arange(half_width, dtype=jnp.float32) * 2.0 / width))
    angles = positions.astype(jnp.float32)[:, None] * frequency[None, :]
    return (jnp.cos(angles)[:, None, :], jnp.sin(angles)[:, None, :])


def rotate(values, cosine, sine):
    half_width = values.shape[-1] // 2
    first_half = values[..., :half_width]
    second_half = values[..., half_width:]
    return jnp.concatenate(
        [first_half * cosine - second_half * sine, second_half * cosine + first_half * sine],
        axis=-1,
    )


def allowed_keys(query_owner, query_pos, key_owner, key_pos, key_valid):
    same = query_owner[:, None] == key_owner[None, :]
    causal = key_pos[None, :] <= query_pos[:, None]
    usable = (key_valid[None, :] > 0) | (key_pos[None, :] == 0)
    return same & causal & usable


def masked_scores(query_block, key_block, allowed, scale):
    scores = (
        jnp.einsum("qhd,khd->hqk", query_block, key_block, preferred_element_type=jnp.float32)
        * scale
    )
    return jnp.where(allowed[None], scores, MASKED)


def on_device(
    block_input,
    block_owner,
    token_mask,
    attention_gain,
    query_weight,
    key_weight,
    value_weight,
    output_weight,
    feedforward_gain,
    gate_weight,
    up_weight,
    down_weight,
    cotangent,
):
    row_count = block_input.shape[0]
    head_count = query_weight.shape[1] // HD
    scale = HD ** (-0.5)
    front = WINDOW - GROUP
    group_count = row_count // GROUP
    first_block = lax.axis_index("dp") * (row_count // BLK)
    owners = jnp.repeat(block_owner, BLK, total_repeat_length=row_count)
    row_index = jnp.arange(row_count, dtype=jnp.int32)
    positions = (row_index // BLK + first_block - owners) * BLK + row_index % BLK
    cosine, sine = rope_tables(positions, HD)
    key_owner = jnp.concatenate([jnp.full((front,), -1, jnp.int32), owners])
    key_pos = jnp.concatenate([jnp.zeros((front,), jnp.int32), positions])
    key_valid = jnp.concatenate([jnp.zeros((front,), jnp.int32), token_mask])
    group_masks = []
    for group in range(group_count):
        start = group * GROUP
        group_masks.append(
            allowed_keys(
                owners[start : start + GROUP],
                positions[start : start + GROUP],
                key_owner[start : start + WINDOW],
                key_pos[start : start + WINDOW],
                key_valid[start : start + WINDOW],
            )
        )
    inputs_f = block_input.astype(jnp.float32)
    normed_one, inverse_one = rms_forward(inputs_f, attention_gain)
    act_one = normed_one.astype(jnp.bfloat16)

    def project(weight):
        return jnp.dot(act_one, weight, preferred_element_type=jnp.float32).reshape(
            row_count, head_count, HD
        )

    queries = rotate(project(query_weight), cosine, sine).astype(jnp.bfloat16)
    keys_rot = rotate(project(key_weight), cosine, sine).astype(jnp.bfloat16)
    values_b = project(value_weight).astype(jnp.bfloat16)
    pad_block = jnp.zeros((front, head_count, HD), jnp.bfloat16)
    key_pad = jnp.concatenate([pad_block, keys_rot], axis=0)
    value_pad = jnp.concatenate([pad_block, values_b], axis=0)
    attn_list = []
    logsum_list = []
    for group in range(group_count):
        start = group * GROUP
        scores = masked_scores(
            queries[start : start + GROUP],
            key_pad[start : start + WINDOW],
            group_masks[group],
            scale,
        )
        peak = jnp.max(scores, axis=-1, keepdims=True)
        logsum = peak + jnp.log(jnp.sum(jnp.exp(scores - peak), axis=-1, keepdims=True))
        probs = jnp.exp(scores - logsum).astype(jnp.bfloat16)
        result = jnp.einsum(
            "hqk,khd->qhd",
            probs,
            value_pad[start : start + WINDOW],
            preferred_element_type=jnp.float32,
        )
        attn_list.append(result.astype(jnp.bfloat16))
        logsum_list.append(logsum)
    attn_heads = jnp.concatenate(attn_list, axis=0)
    attn_flat = attn_heads.reshape(row_count, head_count * HD)
    attn_part = jnp.dot(attn_flat, output_weight, preferred_element_type=jnp.float32)
    attn_total = lax.psum(attn_part, "tensor")
    hidden_sum = inputs_f + attn_total
    normed_two, inverse_two = rms_forward(hidden_sum, feedforward_gain)
    act_two = normed_two.astype(jnp.bfloat16)
    gate_pre = jnp.dot(act_two, gate_weight, preferred_element_type=jnp.float32)
    up_pre = jnp.dot(act_two, up_weight, preferred_element_type=jnp.float32)
    sigmoid_gate = jax.nn.sigmoid(gate_pre)
    inner = (gate_pre * sigmoid_gate * up_pre).astype(jnp.bfloat16)
    mlp_part = jnp.dot(inner, down_weight, preferred_element_type=jnp.float32)
    mlp_total = lax.psum(mlp_part, "tensor")
    block_output = (hidden_sum + mlp_total).astype(jnp.bfloat16)
    grad_rows = jnp.where(token_mask[:, None] > 0, cotangent, jnp.zeros_like(cotangent))
    down_grad = jnp.dot(inner.T, grad_rows, preferred_element_type=jnp.float32)
    inner_grad = jnp.dot(grad_rows, down_weight.T, preferred_element_type=jnp.float32)
    gate_back = (
        inner_grad * up_pre * sigmoid_gate * (1.0 + gate_pre * (1.0 - sigmoid_gate))
    ).astype(jnp.bfloat16)
    up_back = (inner_grad * gate_pre * sigmoid_gate).astype(jnp.bfloat16)
    gate_grad = jnp.dot(act_two.T, gate_back, preferred_element_type=jnp.float32)
    up_grad = jnp.dot(act_two.T, up_back, preferred_element_type=jnp.float32)
    act_two_part = jnp.dot(gate_back, gate_weight.T, preferred_element_type=jnp.float32) + jnp.dot(
        up_back, up_weight.T, preferred_element_type=jnp.float32
    )
    act_two_grad = lax.psum(act_two_part, "tensor")
    hidden_norm_back, second_gain_grad = rms_backward(
        hidden_sum, inverse_two, feedforward_gain, act_two_grad
    )
    hidden_grad = grad_rows.astype(jnp.float32) + hidden_norm_back
    mlp_summed = (
        lax.psum_scatter(gate_grad, "dp", scatter_dimension=0, tiled=True),
        lax.psum_scatter(up_grad, "dp", scatter_dimension=0, tiled=True),
        lax.psum_scatter(down_grad, "dp", scatter_dimension=1, tiled=True),
        lax.psum_scatter(second_gain_grad, "dp", scatter_dimension=0, tiled=True),
    )
    hidden_back = hidden_grad.astype(jnp.bfloat16)
    out_grad = jnp.dot(attn_flat.T, hidden_back, preferred_element_type=jnp.float32)
    attention_grad = (
        jnp.dot(hidden_back, output_weight.T, preferred_element_type=jnp.float32)
        .astype(jnp.bfloat16)
        .reshape(row_count, head_count, HD)
    )
    key_acc = jnp.zeros((front + row_count, head_count, HD), jnp.float32)
    value_acc = jnp.zeros((front + row_count, head_count, HD), jnp.float32)
    query_parts = []
    for group in range(group_count):
        start = group * GROUP
        query_block = queries[start : start + GROUP]
        key_block = key_pad[start : start + WINDOW]
        value_block = value_pad[start : start + WINDOW]
        grad_block = attention_grad[start : start + GROUP]
        scores = masked_scores(query_block, key_block, group_masks[group], scale)
        probs_f = jnp.exp(scores - logsum_list[group])
        probs_b = probs_f.astype(jnp.bfloat16)
        value_acc = value_acc.at[start : start + WINDOW].add(
            jnp.einsum("hqk,qhd->khd", probs_b, grad_block, preferred_element_type=jnp.float32)
        )
        prob_grad = jnp.einsum(
            "qhd,khd->hqk", grad_block, value_block, preferred_element_type=jnp.float32
        )
        delta = jnp.sum(
            grad_block.astype(jnp.float32) * attn_heads[start : start + GROUP].astype(jnp.float32),
            axis=-1,
        ).T[:, :, None]
        score_grad = (probs_f * (prob_grad - delta) * scale).astype(jnp.bfloat16)
        query_parts.append(
            jnp.einsum("hqk,khd->qhd", score_grad, key_block, preferred_element_type=jnp.float32)
        )
        key_acc = key_acc.at[start : start + WINDOW].add(
            jnp.einsum("hqk,qhd->khd", score_grad, query_block, preferred_element_type=jnp.float32)
        )
    query_back = (
        rotate(jnp.concatenate(query_parts, axis=0), cosine, -sine)
        .astype(jnp.bfloat16)
        .reshape(row_count, head_count * HD)
    )
    key_back = (
        rotate(key_acc[front:], cosine, -sine)
        .astype(jnp.bfloat16)
        .reshape(row_count, head_count * HD)
    )
    value_back = value_acc[front:].astype(jnp.bfloat16).reshape(row_count, head_count * HD)
    query_grad = jnp.dot(act_one.T, query_back, preferred_element_type=jnp.float32)
    key_grad = jnp.dot(act_one.T, key_back, preferred_element_type=jnp.float32)
    value_grad = jnp.dot(act_one.T, value_back, preferred_element_type=jnp.float32)
    act_one_part = (
        jnp.dot(query_back, query_weight.T, preferred_element_type=jnp.float32)
        + jnp.dot(key_back, key_weight.T, preferred_element_type=jnp.float32)
        + jnp.dot(value_back, value_weight.T, preferred_element_type=jnp.float32)
    )
    act_one_grad = lax.psum(act_one_part, "tensor")
    input_norm_back, first_gain_grad = rms_backward(
        inputs_f, inverse_one, attention_gain, act_one_grad
    )
    input_gradient = hidden_grad + input_norm_back
    first_summed = (
        lax.psum_scatter(first_gain_grad, "dp", scatter_dimension=0, tiled=True),
        lax.psum_scatter(query_grad, "dp", scatter_dimension=0, tiled=True),
        lax.psum_scatter(key_grad, "dp", scatter_dimension=0, tiled=True),
        lax.psum_scatter(value_grad, "dp", scatter_dimension=0, tiled=True),
        lax.psum_scatter(out_grad, "dp", scatter_dimension=1, tiled=True),
    )
    gate_sum, up_sum, down_sum, second_gain_sum = mlp_summed
    first_gain_sum, query_sum, key_sum, value_sum, out_sum = first_summed
    return (
        block_output,
        input_gradient,
        first_gain_sum,
        query_sum,
        key_sum,
        value_sum,
        out_sum,
        second_gain_sum,
        gate_sum,
        up_sum,
        down_sum,
    )


def solution(mesh):
    return jax.shard_map(
        on_device,
        mesh=mesh,
        in_specs=(
            P("dp", None),
            P("dp"),
            P("dp"),
            P(),
            P(None, "tensor"),
            P(None, "tensor"),
            P(None, "tensor"),
            P("tensor", None),
            P(),
            P(None, "tensor"),
            P(None, "tensor"),
            P("tensor", None),
            P("dp", None),
        ),
        out_specs=(
            P("dp", None),
            P("dp", None),
            P("dp"),
            P("dp", "tensor"),
            P("dp", "tensor"),
            P("dp", "tensor"),
            P("tensor", "dp"),
            P("dp"),
            P("dp", "tensor"),
            P("dp", "tensor"),
            P("tensor", "dp"),
        ),
        check_vma=False,
    )
```

profile of v0, /device:TPU:0, one launch (start us, length us, event | category | flops | bytes accessed | tf_op | source)
XLA Modules:
  0.0 1624.1 jit_solution(13321575594222905438)
XLA Ops:
  7.3 1.6 fusion.80
  8.9 4.5 compare_select_fusion.1
  13.4 0.7 fusion.75
  14.1 3.1 fusion.14
  17.2 5.5 fusion.72
  22.8 2.6 fusion.70
  25.4 1.2 fusion.31
  26.6 0.7 add_convert_fusion.3
  28.0 2.8 fusion.6
  30.8 4.1 exponential_reduce_fusion.1
  34.9 2.6 convolution_convert_fusion
  38.1 6.8 fusion.7
  44.9 7.3 exponential_reduce_fusion
  52.3 4.1 fusion.24
  56.5 18.0 %fusion.25 = bf16[512,8,64]{0,2,1:T(8,128)(2,1)S(1)} fusion(bf16[896,8,64]{0,2,1:T(8,128)(2,1)S(1)} %bitcast.110, f32[8,512,896]{2,1,0:T(8,128)} %get-tuple-element.125, f32[8,512]{1,0:T(8,128)S(1)} %log_add_fusion, pred[512,896]{1,0:T(8,128)(4,1)S(1)} %and_and_fusion), kind=kOutput, calls=%fused_computation.63 | convolution fusion | flops 484704256 | bytes 16596992 | tf_op jit(solution)/shard_map/hqk,khd->qhd/dot_general | solution.py:130
  74.7 0.7 copy-done.25
  75.4 1.0 copy-done.31
  76.3 5.8 fusion.81
  82.2 174.8 %all-reduce.15.cloned.1.call-done = f32[1024,2048]{1,0:T(8,128)} async-done(((f32[1024,2048]{1,0:T(8,128)}), f32[1024,2048]{1,0:T(8,128)}) %all-reduce.15.cloned.1.call-update) | async-done | bytes 8388624 | tf_op jit(solution)/shard_map/psum | solution.py:141
  257.1 5.7 multiply_reduce_fusion.2
  262.8 0.7 multiply_convert_fusion.5
  263.6 16.6 %fusion.82 = f32[1024,2048]{1,0:T(8,128)} fusion(bf16[1024,2048]{1,0:T(8,128)(2,1)S(1)} %multiply_convert_fusion.5, bf16[2048,2048]{1,0:T(8,128)(2,1)} %param.32), kind=kOutput, calls=%fused_computation.154 | convolution fusion | flops 8589934592 | bytes 20971520 | tf_op jit(solution)/shard_map/dot_general | solution.py:145
  280.2 13.3 fusion.83
  293.5 21.9 %multiply_convert_fusion.2 = (bf16[1024,2048]{1,0:T(8,128)(2,1)}, bf16[1024,2048]{1,0:T(8,128)(2,1)}, bf16[1024,2048]{1,0:T(8,128)(2,1)}) fusion(f32[1024,2048]{1,0:T(8,128)} %fusion.82, f32[1024,2048]{1,0:T(8,128)} %fusion.83, bf16[2048,2048]{1,0:T(8,128)(2,1)} %param.34, bf16[1024,2048]{1,0:T(8,128)(2,1)} %param.35, ...), kind=kOutput, calls=%fused_computation.30 | convolution fusion | flops 8625586176 | bytes 41944064 | tf_op jit(solution)/shard_map/dot_general | solution.py:154
  315.4 12.9 fusion.85
  328.3 13.6 convolution_add_fusion
  342.0 14.9 fusion.84
  356.9 157.9 %all-reduce.17.cloned.1.call-done = f32[1024,2048]{1,0:T(8,128)} async-done(((f32[1024,2048]{1,0:T(8,128)}), f32[1024,2048]{1,0:T(8,128)}) %all-reduce.17.cloned.1.call-update) | async-done | bytes 8388624 | tf_op jit(solution)/shard_map/psum | solution.py:164
  514.8 7.6 multiply_reduce_fusion
  522.5 9.5 multiply_add_fusion
  532.0 6.6 fusion.21
  539.2 4.0 convolution_bitcast_fusion
  543.2 7.5 multiply_convert_fusion.1
  550.8 5.6 convolution_bitcast_fusion.3
  556.4 1.4 convolution_bitcast_fusion.1
  558.1 7.4 fusion.19
  565.7 9.0 multiply_convert_fusion
  574.7 2.3 convolution_bitcast_fusion.2
  577.3 1.5 fusion.20
  579.6 1.0 copy-done.35
  580.6 2.4 fusion.87
  583.1 1.0 copy-done.33
  584.0 2.4 fusion.86
  586.5 5.8 add_add_fusion
  593.0 7.2 fusion.64
  600.3 7.8 fusion.15
  608.1 7.0 fusion.66
  615.2 7.3 fusion.68
  622.8 15.6 fusion.88
  638.4 15.5 fusion.89
  654.2 15.6 fusion.62
  671.7 228.8 %all-reduce.19.cloned.1.call-done = (f32[1024,2048]{1,0:T(8,128)}, f32[1024,2048]{1,0:T(8,128)}) async-done(((f32[1024,2048]{1,0:T(8,128)}, f32[1024,2048]{1,0:T(8,128)}), (f32[1024,2048]{1,0:T(8,128)}, f32[1024,2048]{1,0:T(8,128)})) %all-reduce.19.cloned.1.call-update) | async-done | bytes 16777232 | tf_op jit(solution)/shard_map/psum | solution.py:150
  900.5 5.9 fusion.13
  906.4 29.6 %all-reduce.9 = (f32[2048]{0:T(1024)S(1)}, f32[2048]{0:T(1024)S(1)}) all-reduce(f32[2048]{0:T(1024)S(1)} %get-tuple-element.73, f32[2048]{0:T(1024)S(1)} %copy-done.47), channel_id=2, replica_groups=mesh['dp'=8,'tensor'=4] {'dp'}, use_global_device_ids=true, to_apply=%region_15.16.clone | all-reduce | flops 4096 | bytes 32768
  936.0 0.6 dynamic-slice.41
  936.6 0.6 dynamic-slice.43
  937.3 9.6 add_convert_fusion
  946.9 9.8 fusion.12
  956.7 49.2 %reduce-scatter.14.cloned.1.call-done = f32[512,256]{1,0:T(8,128)} async-done(((f32[512,2048]{1,0:T(8,128)}), f32[512,256]{1,0:T(8,128)}) %reduce-scatter.14.cloned.1.call-update) | async-done | bytes 524304 | tf_op jit(solution)/shard_map/reduce_scatter | solution.py:240
  1005.9 51.1 %reduce-scatter.10.cloned.1.call-done = f32[256,512]{1,0:T(8,128)} async-done(((f32[2048,512]{1,0:T(8,128)}), f32[256,512]{1,0:T(8,128)}) %reduce-scatter.10.cloned.1.call-update) | async-done | bytes 524304 | tf_op jit(solution)/shard_map/reduce_scatter | solution.py:238
  1057.1 51.3 %reduce-scatter.8.cloned.1.call-done = f32[256,512]{1,0:T(8,128)} async-done(((f32[2048,512]{1,0:T(8,128)}), f32[256,512]{1,0:T(8,128)}) %reduce-scatter.8.cloned.1.call-update) | async-done | bytes 524304 | tf_op jit(solution)/shard_map/reduce_scatter | solution.py:237
  1108.4 169.6 %reduce-scatter.16.cloned.1.call-done = f32[256,2048]{1,0:T(8,128)} async-done(((f32[2048,2048]{1,0:T(8,128)}), f32[256,2048]{1,0:T(8,128)}) %reduce-scatter.16.cloned.1.call-update) | async-done | bytes 2097168 | tf_op jit(solution)/shard_map/reduce_scatter | solution.py:170
  1278.0 169.6 %reduce-scatter.18.cloned.1.call-done = f32[256,2048]{1,0:T(8,128)} async-done(((f32[2048,2048]{1,0:T(8,128)}), f32[256,2048]{1,0:T(8,128)}) %reduce-scatter.18.cloned.1.call-update) | async-done | bytes 2097168 | tf_op jit(solution)/shard_map/reduce_scatter | solution.py:171
  1447.6 169.4 %reduce-scatter.20.cloned.1.call-done = f32[2048,256]{1,0:T(8,128)} async-done(((f32[2048,2048]{1,0:T(8,128)}), f32[2048,256]{1,0:T(8,128)}) %reduce-scatter.20.cloned.1.call-update) | async-done | bytes 2097168 | tf_op jit(solution)/shard_map/reduce_scatter | solution.py:172
  (172 shorter events, 6.2 us)
Async XLA Ops:
  7.2 69.2 %copy-start = (bf16[512,2048]{1,0:T(8,128)(2,1)S(1)}, bf16[512,2048]{1,0:T(8,128)(2,1)}, u32[]{:S(2)}) copy-start(bf16[512,2048]{1,0:T(8,128)(2,1)} %param.30) | copy-start | bytes 6291460
  7.2 249.9 %all-reduce.15.cloned.1.call-start = ((), (), s32[]{:S(2)}) async-start(), calls=%async_computation.7 | async-start | bytes 16777216 | tf_op jit(solution)/shard_map/psum | solution.py:141
  17.2 17.7 %copy-start.44 = (f32[1024]{0:T(1024)}, f32[1024]{0:T(1024)S(1)}, u32[]{:S(2)}) copy-start(f32[1024]{0:T(1024)S(1)} %add_rsqrt_fusion.1) | copy-start | bytes 12292
  17.2 5.5 copy-start.3
  17.2 5.5 copy-start.48
  17.2 5.5 copy-start.54
  22.8 2.6 copy-start.46
  27.3 10.7 copy-start.9
  27.4 10.7 copy-start.11
  27.4 10.7 copy-start.13
  27.4 10.7 copy-start.15
  27.5 3.3 copy-start.7
  28.0 24.3 %copy-start.19 = (pred[512,896]{1,0:T(8,128)(4,1)}, pred[512,896]{1,0:T(8,128)(4,1)S(1)}, u32[]{:S(2)}) copy-start(pred[512,896]{1,0:T(8,128)(4,1)S(1)} %and_and_fusion.1) | copy-start | bytes 1376260
  30.8 21.5 %copy-start.5 = (f32[8,512,896]{2,1,0:T(8,128)}, f32[8,512,896]{2,1,0:T(8,128)S(1)}, u32[]{:S(2)}) copy-start(f32[8,512,896]{2,1,0:T(8,128)S(1)} %get-tuple-element.127) | copy-start | bytes 44040196
  30.8 4.1 copy-start.21
  34.9 17.4 %copy-start.52 = (f32[8,512]{1,0:T(8,128)}, f32[8,512]{1,0:T(8,128)S(1)}, u32[]{:S(2)}) copy-start(f32[8,512]{1,0:T(8,128)S(1)} %log_add_fusion.1) | copy-start | bytes 49156
  37.6 14.8 copy-start.39
  38.1 18.4 %copy-start.27 = (pred[512,896]{1,0:T(8,128)(4,1)}, pred[512,896]{1,0:T(8,128)(4,1)S(1)}, u32[]{:S(2)}) copy-start(pred[512,896]{1,0:T(8,128)(4,1)S(1)} %and_and_fusion) | copy-start | bytes 1376260
  52.2 4.3 copy-start.50
  52.3 4.2 copy-start.37
  56.5 18.1 %copy-start.23 = (bf16[512,8,64]{0,2,1:T(8,128)(2,1)}, bf16[512,8,64]{0,2,1:T(8,128)(2,1)S(1)}, u32[]{:S(2)}) copy-start(bf16[512,8,64]{0,2,1:T(8,128)(2,1)S(1)} %fusion.24) | copy-start | bytes 1572868
  82.2 432.7 %all-reduce.17.cloned.1.call-start = ((), (), s32[]{:S(2)}) async-start(), calls=%async_computation.8 | async-start | bytes 16777216 | tf_op jit(solution)/shard_map/psum | solution.py:164
  82.2 180.6 %copy-start.43 = (f32[2048]{0:T(1024)S(1)}, f32[2048]{0:T(1024)}, u32[]{:S(2)}) copy-start(f32[2048]{0:T(1024)} %param.31) | copy-start | bytes 24580
  262.8 17.4 %copy-start.2 = (f32[1024,2048]{1,0:T(8,128)}, f32[1024,2048]{1,0:T(8,128)S(1)}, u32[]{:S(2)}) copy-start(f32[1024,2048]{1,0:T(8,128)S(1)} %get-tuple-element.82) | copy-start | bytes 25165828
  263.6 16.6 %copy-start.17 = (bf16[1024,2048]{1,0:T(8,128)(2,1)}, bf16[1024,2048]{1,0:T(8,128)(2,1)S(1)}, u32[]{:S(2)}) copy-start(bf16[1024,2048]{1,0:T(8,128)(2,1)S(1)} %multiply_convert_fusion.5) | copy-start | bytes 12582916
  315.4 12.9 copy-start.58
  341.9 558.6 %all-reduce.19.cloned.1.call-start = ((), (), s32[]{:S(2)}) async-start(), calls=%async_computation.16 | async-start | bytes 33554432 | tf_op jit(solution)/shard_map/psum | solution.py:150
  514.8 7.6 copy-start.18
  522.5 16.7 %slice-start = ((s8[14680064]{0:T(1024)(128)(4,1)}), s8[4194304]{0:T(1024)(128)(4,1)S(1)}, s32[]{:S(2)}) async-start(s8[14680064]{0:T(1024)(128)(4,1)} %bitcast.98), calls=%async_computation.17 | async-start | bytes 8388608
  522.5 16.7 %slice-start.1 = ((s8[14680064]{0:T(1024)(128)(4,1)}), s8[4194304]{0:T(1024)(128)(4,1)S(1)}, s32[]{:S(2)}) async-start(s8[14680064]{0:T(1024)(128)(4,1)} %bitcast.98), calls=%async_computation.18 | async-start | bytes 8388608
  522.5 16.7 %slice-start.2 = ((s8[14680064]{0:T(1024)(128)(4,1)}), s8[4194304]{0:T(1024)(128)(4,1)S(1)}, s32[]{:S(2)}) async-start(s8[14680064]{0:T(1024)(128)(4,1)} %bitcast.98), calls=%async_computation.19 | async-start | bytes 8388608
  532.0 6.7 copy-start.24
  532.0 6.7 copy-start.26
  532.0 7.1 slice-start.3
  532.0 7.1 copy-start.20
  532.0 7.1 copy-start.53
  538.8 19.3 %copy-start.42 = (bf16[512,512]{0,1:T(8,128)(2,1)}, bf16[512,512]{0,1:T(8,128)(2,1)S(1)}, u32[]{:S(2)}) copy-start(bf16[512,512]{0,1:T(8,128)(2,1)S(1)} %get-tuple-element.98) | copy-start | bytes 1572868
  539.2 4.0 copy-start.40
  543.2 7.6 copy-start.8
  550.8 5.6 copy-start.6
  550.8 5.6 copy-start.10
  550.8 5.6 copy-start.12
  556.4 1.7 copy-start.28
  556.4 1.7 copy-start.51
  558.1 7.6 copy-start.38
  565.7 9.0 copy-start.14
  565.7 9.0 copy-start.16
  577.3 1.5 copy-start.30
  578.8 1.7 copy-start.55
  579.5 4.5 copy-start.56
  583.0 3.5 copy-start.22
  592.3 7.9 copy-start.32
  592.3 364.4 %reduce-scatter.12.cloned.1.call-start = ((), (), s32[]{:S(2)}) async-start(), calls=%async_computation.11 | async-start | bytes 4718592 | tf_op jit(solution)/shard_map/reduce_scatter | solution.py:239
  600.2 7.9 copy-start.36
  600.2 405.7 %reduce-scatter.14.cloned.1.call-start = ((), (), s32[]{:S(2)}) async-start(), calls=%async_computation.12 | async-start | bytes 4718592 | tf_op jit(solution)/shard_map/reduce_scatter | solution.py:240
  608.1 7.2 copy-start.34
  608.1 449.0 %reduce-scatter.10.cloned.1.call-start = ((), (), s32[]{:S(2)}) async-start(), calls=%async_computation.10 | async-start | bytes 4718592 | tf_op jit(solution)/shard_map/reduce_scatter | solution.py:238
  615.2 493.2 %reduce-scatter.8.cloned.1.call-start = ((), (), s32[]{:S(2)}) async-start(), calls=%async_computation.9 | async-start | bytes 4718592 | tf_op jit(solution)/shard_map/reduce_scatter | solution.py:237
  622.5 655.4 %reduce-scatter.16.cloned.1.call-start = ((), (), s32[]{:S(2)}) async-start(), calls=%async_computation.13 | async-start | bytes 18874368 | tf_op jit(solution)/shard_map/reduce_scatter | solution.py:170
  638.4 809.2 %reduce-scatter.18.cloned.1.call-start = ((), (), s32[]{:S(2)}) async-start(), calls=%async_computation.14 | async-start | bytes 18874368 | tf_op jit(solution)/shard_map/reduce_scatter | solution.py:171
  654.0 963.0 %reduce-scatter.20.cloned.1.call-start = ((), (), s32[]{:S(2)}) async-start(), calls=%async_computation.15 | async-start | bytes 18874368 | tf_op jit(solution)/shard_map/reduce_scatter | solution.py:172
  669.8 236.5 %copy-start.47 = (f32[2048]{0:T(1024)S(1)}, f32[2048]{0:T(1024)}, u32[]{:S(2)}) copy-start(f32[2048]{0:T(1024)} %get-tuple-element.71) | copy-start | bytes 24580
  937.3 9.6 copy-start.4
  937.3 679.7 %copy-start.1 = (bf16[512,2048]{1,0:T(8,128)(2,1)S(1)}, bf16[512,2048]{1,0:T(8,128)(2,1)}, u32[]{:S(2)}) copy-start(bf16[512,2048]{1,0:T(8,128)(2,1)} %param.30) | copy-start | bytes 6291460
  (9 other events, 8.7 us)
Sparse Core Ops, SparseCore 0:
  82.3 174.7 all-reduce.14
  342.0 172.7 all-reduce.16
  592.4 308.0 all-reduce.18
  903.2 51.4 reduce-scatter.11
  957.5 48.4 reduce-scatter.13
  1008.7 48.3 reduce-scatter.9
  1060.0 48.3 reduce-scatter.7
  1111.3 166.6 reduce-scatter.15
  1280.9 166.6 reduce-scatter.17
  1450.3 166.6 reduce-scatter.19
where the time goes:
time: 1630 us; the launch traced here: 1620 us
  waiting for transfers between devices  1220 us (75%)
  matrix products  273 us (17%)
  other arithmetic  72.9 us (4%)
  blocking collectives  29.6 us (2%)
    psum x1, waiting for transfers between devices, on_device(): mlp_total = lax.psum(mlp_part, 'tensor')  229 us
    psum x1, waiting for transfers between devices, on_device(): attn_total = lax.psum(attn_part, 'tensor')  175 us
    reduce_scatter x1, waiting for transfers between devices, on_device(): lax.psum_scatter(up_grad, 'dp', scatter_dimension=0, tiled=True)  170 us
    reduce_scatter x1, waiting for transfers between devices, on_device(): lax.psum_scatter(gate_grad, 'dp', scatter_dimension=0, tiled=True)  170 us
    reduce_scatter x1, waiting for transfers between devices, on_device(): lax.psum_scatter(down_grad, 'dp', scatter_dimension=1, tiled=True)  169 us
    psum x1, waiting for transfers between devices, on_device(): act_two_grad = lax.psum(act_two_part, 'tensor')  158 us
    reduce_scatter x1, waiting for transfers between devices, on_device(): lax.psum_scatter(query_grad, 'dp', scatter_dimension=0, tiled=True)  51.3 us
    reduce_scatter x1, waiting for transfers between devices, on_device(): lax.psum_scatter(key_grad, 'dp', scatter_dimension=0, tiled=True)  51.1 us
  transfers between devices with their start and end apart: 10, of which 9 were waited for; matrix products, arithmetic and copies ran while one was open for 7% of the time, Pallas kernels for 0%

commit v1 on v0

v1 whole, which is shorter than its diff:
```python
import functools

import jax
import jax.numpy as jnp
from jax import lax
from jax.experimental import pallas as pl
from jax.experimental.pallas import tpu as pltpu
from jax.sharding import PartitionSpec as P


HD = 64
BLK = 128
SEQ_BLOCKS = 4
FIRST = BLK * SEQ_BLOCKS

NORM_EPS = 1e-05
ROPE_BASE = 130000.0
MASKED = -1e30


F32 = jnp.float32
BF16 = jnp.bfloat16


def mm(a, b):
    return jnp.dot(a, b, preferred_element_type=F32)


def mm_nt(a, b):
    return lax.dot_general(a, b, (((1,), (1,)), ((), ())), preferred_element_type=F32)


def mm_tn(a, b):
    return lax.dot_general(a, b, (((0,), (0,)), ((), ())), preferred_element_type=F32)


def rope_tables(positions, width, lanes):
    half_width = width // 2
    frequency = ROPE_BASE ** (-(jnp.arange(half_width, dtype=F32) * 2.0 / width))
    angles = positions.astype(F32)[:, None] * frequency[None, :]
    cosine, sine = jnp.cos(angles), jnp.sin(angles)
    copies = lanes // width
    return (
        jnp.concatenate([cosine, cosine] * copies, axis=1),
        jnp.concatenate([-sine, sine] * copies, axis=1),
    )


def turn(values, cosine, signed_sine):
    lanes = values.shape[1]
    half = HD // 2
    lane = lax.broadcasted_iota(jnp.int32, values.shape, 1)
    other = jnp.where(
        lane % HD < half,
        pltpu.roll(values, lanes - half, 1),
        pltpu.roll(values, half, 1),
    )
    return values * cosine + other * signed_sine


def head_probs(q, k, mask):
    scores = mm_nt(q, k) * HD ** (-0.5)
    scores = jnp.where(mask > 0, scores, MASKED)
    peak = jnp.max(scores, axis=-1, keepdims=True)
    raised = jnp.exp(scores - peak)
    return raised * (1.0 / jnp.sum(raised, axis=-1, keepdims=True))


def attend_body(act, wq, wk, wv, cos, sin, mask, q_out, k_out, v_out, attn_out):
    rows = act[...]
    q = turn(mm(rows, wq[...]), cos[...], sin[...]).astype(BF16)
    k = turn(mm(rows, wk[...]), cos[...], sin[...]).astype(BF16)
    v = mm(rows, wv[...]).astype(BF16)
    q_out[...] = q
    k_out[...] = k
    v_out[...] = v
    allowed = mask[...]
    outs = []
    for h in range(q.shape[1] // HD):
        at = slice(h * HD, (h + 1) * HD)
        probs = head_probs(q[:, at], k[:, at], allowed)
        outs.append(mm(probs.astype(BF16), v[:, at]))
    attn_out[...] = jnp.concatenate(outs, axis=1).astype(BF16)


def attend(act, wq, wk, wv, cos, sin, mask):
    rows, width = act.shape
    cols = wq.shape[1]
    step = min(256, cols)
    column = pl.BlockSpec((rows, step), lambda i: (0, i))
    whole = lambda shape: pl.BlockSpec(shape, lambda i: (0, 0))
    weight = pl.BlockSpec((width, step), lambda i: (0, i))
    return pl.pallas_call(
        attend_body,
        grid=(cols // step,),
        in_specs=[whole((rows, width)), weight, weight, weight]
        + [whole((rows, step)), whole((rows, step)), whole((rows, rows))],
        out_specs=[column] * 4,
        out_shape=[jax.ShapeDtypeStruct((rows, cols), BF16)] * 4,
        cost_estimate=pl.CostEstimate(
            flops=6 * rows * width * cols + 16 * rows * rows * cols,
            bytes_accessed=2 * rows * width + 6 * width * cols + 8 * rows * cols,
            transcendentals=rows * rows * cols // HD,
        ),
        name="attend",
    )(act, wq, wk, wv, cos, sin, mask)


def attend_back_body(hidden, wo, q_in, k_in, v_in, attn_in, cos, sin, mask, *rest):
    out = rest[-1]
    grad = mm_nt(hidden[...], wo[...]).astype(BF16)
    allowed = mask[...]
    scale = HD ** (-0.5)
    q_all, k_all, v_all, attn = q_in[...], k_in[...], v_in[...], attn_in[...]
    q_list, k_list, v_list = [], [], []
    for h in range(grad.shape[1] // HD):
        at = slice(h * HD, (h + 1) * HD)
        q, k, v, g = q_all[:, at], k_all[:, at], v_all[:, at], grad[:, at]
        probs = head_probs(q, k, allowed)
        v_list.append(mm_tn(probs.astype(BF16), g))
        delta = jnp.sum(g.astype(F32) * attn[:, at].astype(F32), axis=-1, keepdims=True)
        score_grad = (probs * (mm_nt(g, v) - delta) * scale).astype(BF16)
        q_list.append(mm(score_grad, k))
        k_list.append(mm_tn(score_grad, q))
    cosine, back_sine = cos[...], -sin[...]
    out[0] = turn(jnp.concatenate(q_list, axis=1), cosine, back_sine).astype(BF16)
    out[1] = turn(jnp.concatenate(k_list, axis=1), cosine, back_sine).astype(BF16)
    out[2] = jnp.concatenate(v_list, axis=1).astype(BF16)


def attend_back(hidden, wo, q, k, v, attn, cos, sin, mask, after):
    rows, width = hidden.shape
    cols = wo.shape[0]
    step = min(256, cols)
    column = pl.BlockSpec((rows, step), lambda i: (0, i))
    whole = lambda shape: pl.BlockSpec(shape, lambda i: (0, 0))
    return pl.pallas_call(
        attend_back_body,
        grid=(cols // step,),
        in_specs=[whole((rows, width)), pl.BlockSpec((step, width), lambda i: (i, 0))]
        + [column] * 4
        + [whole((rows, step)), whole((rows, step)), whole((rows, rows))]
        + [pl.BlockSpec(memory_space=pl.ANY)] * len(after),
        out_specs=pl.BlockSpec((3, rows, step), lambda i: (0, 0, i)),
        out_shape=jax.ShapeDtypeStruct((3, rows, cols), BF16),
        cost_estimate=pl.CostEstimate(
            flops=2 * rows * width * cols + 40 * rows * rows * cols,
            bytes_accessed=2 * rows * width + 2 * width * cols + 14 * rows * cols,
            transcendentals=rows * rows * cols // HD,
        ),
        name="attend_back",
    )(hidden, wo, q, k, v, attn, cos, sin, mask, *after)


def outer_body(count, has_add, which, *refs):
    total = None
    for c in range(count):
        part = mm_tn(refs[c][...], refs[count + c][...])
        total = part if total is None else total + part
    if has_add:
        total = total + refs[2 * count][...]
    refs[-1][...] = total


def outer(lefts, rights, which, pieces, add=None):
    count = len(lefts)
    piece = lefts[0].shape[1] // pieces
    stacked = rights[0].ndim == 3
    cols = rights[0].shape[-1]
    if stacked:
        step, blocks = cols, rights[0].shape[0]
        right_spec = lambda r: pl.BlockSpec((None, r, step), lambda n, j, w: (n, 0, 0))
    else:
        step = min(1024, cols)
        blocks = cols // step
        right_spec = lambda r: pl.BlockSpec((r, step), lambda n, j, w: (0, n))
    out_spec = pl.BlockSpec((piece, step), lambda n, j, w: (j, n))
    rows = [v.shape[0] for v in lefts]
    out_rows, out_cols = pieces // 2 * piece, blocks * step
    specs = [
        pl.BlockSpec((r, piece), lambda n, j, w: (0, 2 * j + w[0])) for r in rows
    ] + [right_spec(r) for r in rows]
    args = list(lefts) + list(rights)
    if add is not None:
        specs.append(out_spec)
        args.append(add)
    return pl.pallas_call(
        functools.partial(outer_body, count, add is not None),
        grid_spec=pltpu.PrefetchScalarGridSpec(
            num_scalar_prefetch=1,
            grid=(blocks, pieces // 2),
            in_specs=specs,
            out_specs=out_spec,
        ),
        out_shape=jax.ShapeDtypeStruct((out_rows, out_cols), F32),
        cost_estimate=pl.CostEstimate(
            flops=2 * sum(rows) * out_rows * out_cols,
            bytes_accessed=2 * sum(rows) * (out_rows + out_cols) + 4 * out_rows * out_cols,
            transcendentals=0,
        ),
    )(which.reshape(1).astype(jnp.int32), *args)


class Cube:
    def __init__(self, axis, size):
        self.axis = axis
        self.size = size
        self.bits = [1 << i for i in range(size.bit_length() - 1)]
        self.me = lax.axis_index(axis)

    def swap(self, value, bit):
        return lax.ppermute(value, self.axis, [(i, i ^ bit) for i in range(self.size)])

    def bit_of(self, bit):
        return (self.me // bit) % 2

    def own_start(self, rows, bits):
        start = 0
        for bit in bits:
            rows = rows // 2
            start = start + self.bit_of(bit) * rows
        return start

    def scatter(self, make, rows, bits):
        first = True
        value = None
        for bit in bits:
            half = rows // 2
            mine = self.bit_of(bit)
            if first:
                away = make((1 - mine) * half, half)
                got = self.swap(away, bit)
                value = make(mine * half, half) + got
                first = False
            else:
                away = lax.dynamic_slice_in_dim(value, (1 - mine) * half, half, 0)
                got = self.swap(away, bit)
                value = lax.dynamic_slice_in_dim(value, mine * half, half, 0) + got
            rows = half
        return value

    def gather(self, value, bits):
        for bit in reversed(bits):
            got = self.swap(value, bit)
            mine = self.bit_of(bit)
            value = jnp.where(
                mine == 0,
                jnp.concatenate([value, got], axis=0),
                jnp.concatenate([got, value], axis=0),
            )
        return value

    def total(self, value):
        for bit in self.bits:
            value = value + self.swap(value, bit)
        return value


def on_device(sizes):
    dp_size, tensor_size = sizes

    def run(
        block_input,
        block_owner,
        token_mask,
        attention_gain,
        query_weight,
        key_weight,
        value_weight,
        output_weight,
        feedforward_gain,
        gate_weight,
        up_weight,
        down_weight,
        cotangent,
    ):
        row_count, width = block_input.shape
        head_count = query_weight.shape[1] // HD
        head_cols = head_count * HD
        tensor = Cube("tensor", tensor_size)
        data = Cube("dp", dp_size)
        core = data.bit_of(1)
        pair_lists = [[i for i in range(dp_size) if i % 2 == c] for c in range(2)]

        bounds = [(0, FIRST), (FIRST, row_count)]
        orders = (tensor.bits, tensor.bits[::-1])

        def halves(size):
            return [(0, size // 2, orders[0]), (size // 2, size // 2, orders[1])]

        def own_rows(value):
            size = value.shape[0]
            return jnp.concatenate(
                [
                    lax.dynamic_slice_in_dim(
                        value, base + tensor.own_start(rows, bits), rows // tensor_size, 0
                    )
                    for base, rows, bits in halves(size)
                ],
                axis=0,
            )

        def scatter_rows(make, size):
            return jnp.concatenate(
                [
                    tensor.scatter(lambda s, n, base=base: make(base + s, n), rows, bits)
                    for base, rows, bits in halves(size)
                ],
                axis=0,
            )

        def gather_rows(value, size):
            quarter = size // 2 // tensor_size
            return jnp.concatenate(
                [
                    tensor.gather(value[i * quarter : (i + 1) * quarter], bits)
                    for i, (_, _, bits) in enumerate(halves(size))
                ],
                axis=0,
            )

        def rows_of(value, start, size):
            return lax.dynamic_slice_in_dim(value, start, size, 0)

        def core_sum(lefts, rights):
            away = outer(lefts, rights, 1 - core, dp_size)
            got = data.swap(away, 1)
            return outer(lefts, rights, core, dp_size, add=got)

        def z_scatter(value):
            return lax.psum_scatter(
                value, "dp", scatter_dimension=0, tiled=True, axis_index_groups=pair_lists
            )

        first_block = lax.axis_index("dp") * (row_count // BLK)
        owners = jnp.broadcast_to(block_owner[:, None], (row_count // BLK, BLK)).reshape(-1)
        row_index = jnp.arange(row_count, dtype=jnp.int32)
        positions = (row_index // BLK + first_block - owners) * BLK + row_index % BLK
        cosine, sine = rope_tables(positions, HD, min(256, head_cols))

        saved = []
        for lo, hi in bounds:
            size = hi - lo
            x_f = block_input[lo:hi].astype(F32)
            inv_f = lax.rsqrt(jnp.mean(x_f * x_f, axis=-1, keepdims=True) + NORM_EPS)
            act = (x_f * inv_f * attention_gain).astype(BF16)
            rows = jnp.where(
                token_mask[lo:hi, None] > 0, cotangent[lo:hi], jnp.zeros_like(cotangent[lo:hi])
            )
            cos_g, sin_g = cosine[lo:hi], sine[lo:hi]
            own_g, pos_g, mask_g = owners[lo:hi], positions[lo:hi], token_mask[lo:hi]
            allowed = (
                (own_g[:, None] == own_g[None, :])
                & (pos_g[None, :] <= pos_g[:, None])
                & ((mask_g[None, :] > 0) | (pos_g[None, :] == 0))
            ).astype(F32)
            q, k, v, flat = attend(
                act, query_weight, key_weight, value_weight, cos_g, sin_g, allowed
            )
            added = scatter_rows(
                lambda s, n, flat=flat: mm(rows_of(flat, s, n), output_weight), size
            )
            x_own = own_rows(block_input[lo:hi]).astype(F32)
            hid = x_own + added
            inv_two = lax.rsqrt(jnp.mean(hid * hid, axis=-1, keepdims=True) + NORM_EPS)
            unit = gather_rows(hid * inv_two, size)
            act_two = (unit * feedforward_gain).astype(BF16)
            saved.append(
                dict(q=q, k=k, v=v, allowed=allowed, flat=flat, act=act, rows=rows, x_f=x_f,
                     cos=cos_g, sin=sin_g, x_own=x_own, hid=hid, added=added, inv_two=inv_two,
                     act_two=act_two)
            )

        def chunks(key):
            return [s[key] for s in saved]

        for (lo, hi), s in zip(bounds, saved):
            s["gate_pre"] = mm(s["act_two"], gate_weight)
            s["up_pre"] = mm(s["act_two"], up_weight)
            s["sig"] = jax.nn.sigmoid(s["gate_pre"])
            s["inner"] = (s["gate_pre"] * s["sig"] * s["up_pre"]).astype(BF16)
        down_part = core_sum(chunks("rows"), chunks("inner"))
        down_sum = z_scatter(down_part).T

        gain_parts = jnp.zeros((width,), F32)
        for (lo, hi), s in zip(bounds, saved):
            size = hi - lo
            rows = s["rows"]
            inner_grad = mm_nt(rows, down_weight)
            gate_pre, up_pre, sig = s["gate_pre"], s["up_pre"], s["sig"]
            gate_pre, up_pre, _ = lax.optimization_barrier((gate_pre, up_pre, down_part))
            gate_back = (inner_grad * up_pre * sig * (1.0 + gate_pre * (1.0 - sig))).astype(BF16)
            up_back = (inner_grad * gate_pre * sig).astype(BF16)
            s["gate_back"], s["up_back"] = gate_back, up_back
            part = scatter_rows(
                lambda st, n, a=gate_back, b=up_back: mm_nt(rows_of(a, st, n), gate_weight)
                + mm_nt(rows_of(b, st, n), up_weight),
                size,
            )
            s["part"] = part
            unit = s["hid"] * s["inv_two"]
            gain_parts = gain_parts + jnp.sum(part * unit, axis=0)
            scaled = part * feedforward_gain
            back = s["inv_two"] * (
                scaled - unit * jnp.mean(scaled * unit, axis=-1, keepdims=True)
            )
            s["hidden_grad"] = own_rows(rows).astype(F32) + back
            s["hidden_back"] = (rows.astype(F32) + gather_rows(back, size)).astype(BF16)

        gate_part = core_sum(chunks("act_two"), chunks("gate_back"))
        gate_sum = z_scatter(gate_part)
        up_part = core_sum(chunks("act_two"), chunks("up_back"))
        up_sum = z_scatter(up_part)

        outs = []
        for (lo, hi), s in zip(bounds, saved):
            size = hi - lo
            late_inner, _ = lax.optimization_barrier((s["inner"], saved[-1]["part"]))
            mlp = scatter_rows(
                lambda st, n, a=late_inner: mm(rows_of(a, st, n), down_weight), size
            )
            full = gather_rows(s["added"] + mlp, size)
            outs.append((s["x_f"] + full).astype(BF16))
        block_output = jnp.concatenate(outs, axis=0)

        first_parts = jnp.zeros((width,), F32)
        input_grads = []
        for (lo, hi), s in zip(bounds, saved):
            size = hi - lo
            back3 = attend_back(
                s["hidden_back"], output_weight, s["q"], s["k"], s["v"], s["flat"],
                s["cos"], s["sin"], s["allowed"], (down_part, gate_part, up_part),
            )
            s["qkv_back"] = back3
            q_back, k_back, v_back = back3[0], back3[1], back3[2]
            part = scatter_rows(
                lambda st, n, a=q_back, b=k_back, c=v_back: mm_nt(rows_of(a, st, n), query_weight)
                + mm_nt(rows_of(b, st, n), key_weight)
                + mm_nt(rows_of(c, st, n), value_weight),
                size,
            )
            x_own = s["x_own"]
            inv_one = lax.rsqrt(jnp.mean(x_own * x_own, axis=-1, keepdims=True) + NORM_EPS)
            unit = x_own * inv_one
            first_parts = first_parts + jnp.sum(part * unit, axis=0)
            scaled = part * attention_gain
            back = inv_one * (scaled - unit * jnp.mean(scaled * unit, axis=-1, keepdims=True))
            input_grads.append(gather_rows(s["hidden_grad"] + back, size))
        input_gradient = jnp.concatenate(input_grads, axis=0)

        out_sum = z_scatter(core_sum(chunks("hidden_back"), chunks("flat"))).T
        qkv_sum = z_scatter(core_sum(chunks("act"), chunks("qkv_back")))
        query_sum = qkv_sum[:, :head_cols]
        key_sum = qkv_sum[:, head_cols : 2 * head_cols]
        value_sum = qkv_sum[:, 2 * head_cols :]

        gains = data.total(tensor.total(jnp.stack([first_parts, gain_parts])))
        gain_piece = width // dp_size
        gains = lax.dynamic_slice_in_dim(gains, lax.axis_index("dp") * gain_piece, gain_piece, 1)
        return (
            block_output,
            input_gradient,
            gains[0],
            query_sum,
            key_sum,
            value_sum,
            out_sum,
            gains[1],
            gate_sum,
            up_sum,
            down_sum,
        )

    return run


def solution(mesh):
    sizes = (mesh.shape["dp"], mesh.shape["tensor"])
    body = on_device(sizes)

    return jax.shard_map(
        body,
        mesh=mesh,
        in_specs=(
            P("dp", None),
            P("dp"),
            P("dp"),
            P(),
            P(None, "tensor"),
            P(None, "tensor"),
            P(None, "tensor"),
            P("tensor", None),
            P(),
            P(None, "tensor"),
            P(None, "tensor"),
            P("tensor", None),
            P("dp", None),
        ),
        out_specs=(
            P("dp", None),
            P("dp", None),
            P("dp"),
            P("dp", "tensor"),
            P("dp", "tensor"),
            P("dp", "tensor"),
            P("tensor", "dp"),
            P("dp"),
            P("dp", "tensor"),
            P("dp", "tensor"),
            P("tensor", "dp"),
        ),
        check_vma=False,
    )
```

time: 1630 us -> 1090 us (0.67)
  waiting for transfers between devices: 1220 us -> 538 us
  Pallas kernels: 0 us -> 175 us
  matrix products: 273 us -> 166 us
  starting transfers between devices: 1.2 us -> 86.1 us
  blocking collectives: 29.6 us -> 0 us
  local copies, waits for them, and re-layouts: 8.87 us -> 35.1 us
    psum x3 -> x0, waiting for transfers between devices: 562 us -> none  [the longest x1 229 us: on_device(): mlp_total = lax.psum(mlp_part, 'tensor')]
    reduce_scatter x7 -> x5, waiting for transfers between devices: 660 us -> 153 us  [z_scatter(): lax.psum_scatter(value, 'dp', scatter_dimension=0, tiled=True, axis_index...]
    ppermute x0 -> x74, waiting for transfers between devices: none -> 384 us  [swap(): lax.ppermute(value, self.axis, [(i, i ^ bit) for i in range(self.size)])]
    pallas_call x0 -> x14, Pallas kernels: none -> 175 us  [the longest x10 114 us: outer(): pl.pallas_call(functools.partial(outer_body, count, add is not None), gri...]
    dot_general x33 -> x62, matrix products: 273 us -> 166 us  [the longest x42 112 us: mm_nt(): lax.dot_general(a, b, (((1,), (1,)), ((), ())), preferred_element_type=F32)]
    ppermute x0 -> x74, starting transfers between devices: none -> 85.7 us  [swap(): lax.ppermute(value, self.axis, [(i, i ^ bit) for i in range(self.size)])]
    unnamed x1 -> x0, blocking collectives: 29.6 us -> none
    select_n x0 -> x33, other arithmetic: none -> 28.5 us  [the longest x32 26.3 us: gather(): jnp.where(mine == 0, jnp.concatenate([value, got], axis=0), jnp.concatena...]
  transfers between devices with their start and end apart: 10 -> 79, of which waited for: 9 -> 45; matrix products, arithmetic and copies ran while one was open for 7% -> 15% of each run, Pallas kernels for 0% -> 12%
where the time goes in v1:
time: 1090 us
  waiting for transfers between devices  538 us (49%)
  Pallas kernels  175 us (16%)
  matrix products  166 us (15%)
  starting transfers between devices  86.1 us (8%)
  other arithmetic  72.3 us (7%)
  local copies, waits for them, and re-layouts  35.1 us (3%)
  between operations  16.1 us (1%)
    ppermute x74, waiting for transfers between devices, swap(): lax.ppermute(value, self.axis, [(i, i ^ bit) for i in range(self.size)])  384 us
    reduce_scatter x5, waiting for transfers between devices, z_scatter(): lax.psum_scatter(value, 'dp', scatter_dimension=0, tiled=True, axis_index...  153 us
    pallas_call x10, Pallas kernels, outer(): pl.pallas_call(functools.partial(outer_body, count, add is not None), gri...  114 us
    dot_general x42, matrix products, mm_nt(): lax.dot_general(a, b, (((1,), (1,)), ((), ())), preferred_element_type=F32)  112 us
    ppermute x74, starting transfers between devices, swap(): lax.ppermute(value, self.axis, [(i, i ^ bit) for i in range(self.size)])  85.7 us
    dot_general x20, matrix products, mm(): return jnp.dot(a, b, preferred_element_type=F32)  54.6 us
    pallas_call x2, Pallas kernels, attend_back(): pl.pallas_call(attend_back_body, grid=(cols // step,), in_specs=[whole((r...  34 us
    pallas_call x2, Pallas kernels, attend(): pl.pallas_call(attend_body, grid=(cols // step,), in_specs=[whole((rows,...  26.9 us
  transfers between devices with their start and end apart: 79, of which 45 were waited for; matrix products, arithmetic and copies ran while one was open for 15% of the time, Pallas kernels for 12%

profile of v1, /device:TPU:0, one launch (start us, length us, event | category | flops | bytes accessed | tf_op | source)
XLA Modules:
  0.0 1088.4 jit_solution(9482009361574901838)
XLA Ops:
  29.0 13.4 %attend.2 = (bf16[512,512]{1,0:T(8,128)(2,1)}, bf16[512,512]{1,0:T(8,128)(2,1)}, bf16[512,512]{1,0:T(8,128)(2,1)}, bf16[512,512]{1,0:T(8,128)(2,1)}) custom-call(bf16[512,2048]{1,0:T(8,128)(2,1)} %get-tuple-element.85.act.refs_0_, bf16[2048,512]{1,0:T(8,128)(2,1)} %wq.3, bf16[2048,512]{1,0:T(8,128)(2,1)} %wk.3, bf16[2048,512]{1,0:T(8,128)(2,1)} %wv.3, ...), custom_call_target="tpu_custom_call" | custom-call | flops 5368709120 | bytes 10485760 | tf_op jit(solution)/shard_map/attend/pallas_call | solution.py:93
  50.7 13.5 %attend.3 = (bf16[512,512]{1,0:T(8,128)(2,1)}, bf16[512,512]{1,0:T(8,128)(2,1)}, bf16[512,512]{1,0:T(8,128)(2,1)}, bf16[512,512]{1,0:T(8,128)(2,1)}) custom-call(bf16[512,2048]{1,0:T(8,128)(2,1)} %get-tuple-element.86.act.refs_1_, bf16[2048,512]{1,0:T(8,128)(2,1)} %wq.3, bf16[2048,512]{1,0:T(8,128)(2,1)} %wk.3, bf16[2048,512]{1,0:T(8,128)(2,1)} %wv.3, ...), custom_call_target="tpu_custom_call" | custom-call | flops 5368709120 | bytes 10485760 | tf_op jit(solution)/shard_map/attend/pallas_call | solution.py:93
  81.0 13.6 %collective-permute-done.10 = f32[128,2048]{1,0:T(8,128)} collective-permute-done((f32[128,2048]{1,0:T(8,128)}, f32[128,2048]{1,0:T(8,128)}, u32[]{:S(2)}, u32[]{:S(2)}) %collective-permute-start.10) | collective-permute-done | bytes 1048608 | tf_op jit(solution)/shard_map/ppermute | solution.py:212
  101.7 7.5 collective-permute-done.3
  112.5 7.9 collective-permute-done.11
  125.6 6.2 collective-permute-done.6
  136.9 6.1 collective-permute-done.14
  152.2 10.4 collective-permute-done.7
  167.3 16.3 %collective-permute-done.15 = f32[128,2048]{1,0:T(8,128)} collective-permute-done((f32[128,2048]{1,0:T(8,128)}, f32[128,2048]{1,0:T(8,128)}, u32[]{:S(2)}, u32[]{:S(2)}) %collective-permute-start.15) | collective-permute-done | bytes 1048608 | tf_op jit(solution)/shard_map/ppermute | solution.py:212
  191.6 4.5 fusion.233
  196.1 4.5 fusion.235
  200.6 6.5 multiply_convert_fusion.5
  207.2 6.6 multiply_convert_fusion.4
  213.7 11.9 %shard_map.212 = f32[1024,2048]{1,0:T(8,128)} custom-call(s32[1]{0:T(128)} %bitcast.4.which, bf16[512,2048]{1,0:T(8,128)(2,1)} %get-tuple-element.92.refs_0_, bf16[512,2048]{1,0:T(8,128)(2,1)} %get-tuple-element.91.refs_1_, bf16[512,2048]{1,0:T(8,128)(2,1)} %get-tuple-element.29.refs_2_, bf16[512,2048]{1,0:T(8,128)(2,1)} %get-tuple-element.30.refs_3_), custom_call_target="tpu_custom_call" | custom-call | flops 4294967296 | bytes 14680064 | tf_op jit(solution)/shard_map/pallas_call | solution.py:187
  225.7 10.6 fusion.234
  236.4 9.5 fusion.236
  245.9 13.4 %shard_map.213.rest_0_ = f32[1024,2048]{1,0:T(8,128)} custom-call(s32[1]{0:T(128)} %bitcast.3.which, bf16[512,2048]{1,0:T(8,128)(2,1)} %get-tuple-element.92.refs_0_, bf16[512,2048]{1,0:T(8,128)(2,1)} %get-tuple-element.91.refs_1_, bf16[512,2048]{1,0:T(8,128)(2,1)} %get-tuple-element.29.refs_2_, bf16[512,2048]{1,0:T(8,128)(2,1)} %get-tuple-element.30.refs_3_, ...), custom_call_target="tpu_custom_call" | custom-call | flops 4294967296 | bytes 14680064 | tf_op jit(solution)/shard_map/pallas_call | solution.py:187
  259.3 6.1 multiply_convert_fusion.2
  265.5 8.8 fusion.65
  274.3 7.4 fusion.68
  288.6 5.3 multiply_convert_fusion
  303.6 5.1 convolution_add_fusion.28
  310.1 5.1 convolution_add_fusion.30
  316.6 5.2 convolution_add_fusion.20
  329.8 5.2 collective-permute-done.19
  340.7 16.2 %collective-permute-done.39 = f32[128,2048]{1,0:T(8,128)} collective-permute-done((f32[128,2048]{1,0:T(8,128)}, f32[128,2048]{1,0:T(8,128)}, u32[]{:S(2)}, u32[]{:S(2)}) %collective-permute-start.39) | collective-permute-done | bytes 1048608 | tf_op jit(solution)/shard_map/ppermute | solution.py:212
  367.4 4.3 fusion.16
  373.3 12.1 %collective-permute-done.40 = f32[64,2048]{1,0:T(8,128)S(1)} collective-permute-done((f32[64,2048]{1,0:T(8,128)S(1)}, f32[64,2048]{1,0:T(8,128)S(1)}, u32[]{:S(2)}, u32[]{:S(2)}) %collective-permute-start.40) | collective-permute-done | bytes 524320 | tf_op jit(solution)/shard_map/ppermute | solution.py:212
  386.0 4.3 collective-permute-done.18
  394.5 11.6 %collective-permute-done.57 = f32[64,2048]{1,0:T(8,128)S(1)} collective-permute-done((f32[64,2048]{1,0:T(8,128)S(1)}, f32[64,2048]{1,0:T(8,128)S(1)}, u32[]{:S(2)}, u32[]{:S(2)}) %collective-permute-start.57) | collective-permute-done | bytes 524320 | tf_op jit(solution)/shard_map/ppermute | solution.py:212
  409.9 7.4 collective-permute-done.43
  418.5 25.0 %collective-permute-done.41 = f32[64,2048]{1,0:T(8,128)S(1)} collective-permute-done((f32[64,2048]{1,0:T(8,128)S(1)}, f32[64,2048]{1,0:T(8,128)S(1)}, u32[]{:S(2)}, u32[]{:S(2)}) %collective-permute-start.41) | collective-permute-done | bytes 524320 | tf_op jit(solution)/shard_map/ppermute | solution.py:212
  445.6 14.3 %collective-permute-done.44 = f32[128,2048]{1,0:T(8,128)S(1)} collective-permute-done((f32[128,2048]{1,0:T(8,128)S(1)}, f32[128,2048]{1,0:T(8,128)S(1)}, u32[]{:S(2)}, u32[]{:S(2)}) %collective-permute-start.44) | collective-permute-done | bytes 1048608 | tf_op jit(solution)/shard_map/ppermute | solution.py:212
  465.9 5.0 shard_map.220
  470.9 4.5 collective-permute-done.73.refs_4_
  475.4 5.5 shard_map.221
  480.9 12.0 %shard_map.214 = f32[1024,2048]{1,0:T(8,128)} custom-call(s32[1]{0:T(128)} %bitcast.4.which, bf16[512,2048]{1,0:T(8,128)(2,1)} %copy-done.6, bf16[512,2048]{1,0:T(8,128)(2,1)} %copy-done.7, bf16[512,2048]{1,0:T(8,128)(2,1)} %copy-done.14, bf16[512,2048]{1,0:T(8,128)(2,1)} %copy-done.13), custom_call_target="tpu_custom_call" | custom-call | flops 4294967296 | bytes 14680064 | tf_op jit(solution)/shard_map/pallas_call | solution.py:187
  493.0 11.8 %shard_map.216 = f32[1024,2048]{1,0:T(8,128)} custom-call(s32[1]{0:T(128)} %bitcast.4.which, bf16[512,2048]{1,0:T(8,128)(2,1)} %copy-done.6, bf16[512,2048]{1,0:T(8,128)(2,1)} %copy-done.7, bf16[512,2048]{1,0:T(8,128)(2,1)} %copy-done.12, bf16[512,2048]{1,0:T(8,128)(2,1)} %copy-done.11), custom_call_target="tpu_custom_call" | custom-call | flops 4294967296 | bytes 14680064 | tf_op jit(solution)/shard_map/pallas_call | solution.py:187
  506.4 13.8 %shard_map.215.rest_1_ = f32[1024,2048]{1,0:T(8,128)} custom-call(s32[1]{0:T(128)} %bitcast.3.which, bf16[512,2048]{1,0:T(8,128)(2,1)} %copy-done.6, bf16[512,2048]{1,0:T(8,128)(2,1)} %copy-done.7, bf16[512,2048]{1,0:T(8,128)(2,1)} %copy-done.14, bf16[512,2048]{1,0:T(8,128)(2,1)} %copy-done.13, f32[1024,2048]{1,0:T(8,128)} %collective-permute-done.45.refs_4_), custom_call_target="tpu_custom_call" | custom-call | flops 4294967296 | bytes 14680064 | tf_op jit(solution)/shard_map/pallas_call | solution.py:187
  520.2 13.4 %shard_map.217.rest_2_ = f32[1024,2048]{1,0:T(8,128)} custom-call(s32[1]{0:T(128)} %bitcast.3.which, bf16[512,2048]{1,0:T(8,128)(2,1)} %copy-done.6, bf16[512,2048]{1,0:T(8,128)(2,1)} %copy-done.7, bf16[512,2048]{1,0:T(8,128)(2,1)} %copy-done.12, bf16[512,2048]{1,0:T(8,128)(2,1)} %copy-done.11, f32[1024,2048]{1,0:T(8,128)} %collective-permute-done.46.refs_4_), custom_call_target="tpu_custom_call" | custom-call | flops 4294967296 | bytes 14680064 | tf_op jit(solution)/shard_map/pallas_call | solution.py:187
  533.6 16.8 %attend_back.3.refs_3_ = bf16[3,512,512]{2,1,0:T(8,128)(2,1)} custom-call(bf16[512,2048]{1,0:T(8,128)(2,1)} %fusion.11.hidden.refs_1_, bf16[512,2048]{1,0:T(8,128)(2,1)} %wo.3, bf16[512,512]{1,0:T(8,128)(2,1)} %get-tuple-element.36.q_in, bf16[512,512]{1,0:T(8,128)(2,1)} %get-tuple-element.37.k_in, bf16[512,512]{1,0:T(8,128)(2,1)} %get-tuple-element.38.v_in, ...), custom_call_target="tpu_custom_call" | custom-call | flops 6442450944 | bytes 7864320 | tf_op jit(solution)/shard_map/attend_back/pallas_call | solution.py:137
  550.4 17.3 %attend_back.2.refs_2_ = bf16[3,512,512]{2,1,0:T(8,128)(2,1)} custom-call(bf16[512,2048]{1,0:T(8,128)(2,1)} %fusion.10.hidden.refs_0_, bf16[512,2048]{1,0:T(8,128)(2,1)} %wo.3, bf16[512,512]{1,0:T(8,128)(2,1)} %get-tuple-element.33.q_in, bf16[512,512]{1,0:T(8,128)(2,1)} %get-tuple-element.34.k_in, bf16[512,512]{1,0:T(8,128)(2,1)} %get-tuple-element.35.v_in, ...), custom_call_target="tpu_custom_call" | custom-call | flops 6442450944 | bytes 7864320 | tf_op jit(solution)/shard_map/attend_back/pallas_call | solution.py:137
  567.7 12.8 %shard_map.218 = f32[1024,1536]{1,0:T(8,128)} custom-call(s32[1]{0:T(128)} %bitcast.4.which, bf16[512,2048]{1,0:T(8,128)(2,1)} %get-tuple-element.85.act.refs_0_, bf16[512,2048]{1,0:T(8,128)(2,1)} %get-tuple-element.86.act.refs_1_, bf16[3,512,512]{2,1,0:T(8,128)(2,1)} %attend_back.2.refs_2_, bf16[3,512,512]{2,1,0:T(8,128)(2,1)} %attend_back.3.refs_3_), custom_call_target="tpu_custom_call" | custom-call | flops 3221225472 | bytes 11534336 | tf_op jit(solution)/shard_map/pallas_call | solution.py:187
  580.8 10.1 collective-permute-done.72.refs_4_
  590.9 14.4 %shard_map.219 = f32[1024,1536]{1,0:T(8,128)} custom-call(s32[1]{0:T(128)} %bitcast.3.which, bf16[512,2048]{1,0:T(8,128)(2,1)} %get-tuple-element.85.act.refs_0_, bf16[512,2048]{1,0:T(8,128)(2,1)} %get-tuple-element.86.act.refs_1_, bf16[3,512,512]{2,1,0:T(8,128)(2,1)} %attend_back.2.refs_2_, bf16[3,512,512]{2,1,0:T(8,128)(2,1)} %attend_back.3.refs_3_, ...), custom_call_target="tpu_custom_call" | custom-call | flops 3221225472 | bytes 11534336 | tf_op jit(solution)/shard_map/pallas_call | solution.py:187
  608.0 5.0 fusion.58
  613.5 4.9 fusion.61
  624.7 14.4 %collective-permute-done.23 = f32[128,2048]{1,0:T(8,128)S(1)} collective-permute-done((f32[128,2048]{1,0:T(8,128)S(1)}, f32[128,2048]{1,0:T(8,128)S(1)}, u32[]{:S(2)}, u32[]{:S(2)}) %collective-permute-start.23) | collective-permute-done | bytes 1048608 | tf_op jit(solution)/shard_map/ppermute | solution.py:212
  647.5 14.1 %collective-permute-done.31 = f32[128,2048]{1,0:T(8,128)S(1)} collective-permute-done((f32[128,2048]{1,0:T(8,128)S(1)}, f32[128,2048]{1,0:T(8,128)S(1)}, u32[]{:S(2)}, u32[]{:S(2)}) %collective-permute-start.31) | collective-permute-done | bytes 1048608 | tf_op jit(solution)/shard_map/ppermute | solution.py:212
  670.0 8.3 collective-permute-done.24
  680.8 8.7 collective-permute-done.32
  693.7 7.1 collective-permute-done.27
  705.7 6.3 collective-permute-done.35
  716.6 14.0 %collective-permute-done.28 = f32[128,2048]{1,0:T(8,128)S(1)} collective-permute-done((f32[128,2048]{1,0:T(8,128)S(1)}, f32[128,2048]{1,0:T(8,128)S(1)}, u32[]{:S(2)}, u32[]{:S(2)}) %collective-permute-start.28) | collective-permute-done | bytes 1048608 | tf_op jit(solution)/shard_map/ppermute | solution.py:212
  734.6 16.7 %collective-permute-done.36 = f32[128,2048]{1,0:T(8,128)S(1)} collective-permute-done((f32[128,2048]{1,0:T(8,128)S(1)}, f32[128,2048]{1,0:T(8,128)S(1)}, u32[]{:S(2)}, u32[]{:S(2)}) %collective-permute-start.36) | collective-permute-done | bytes 1048608 | tf_op jit(solution)/shard_map/ppermute | solution.py:212
  751.4 4.8 collective-permute-done.34
  784.7 8.4 collective-permute-done.61
  795.7 18.5 %collective-permute-done.49 = f32[128,2048]{1,0:T(8,128)S(1)} collective-permute-done((f32[128,2048]{1,0:T(8,128)S(1)}, f32[128,2048]{1,0:T(8,128)S(1)}, u32[]{:S(2)}, u32[]{:S(2)}) %collective-permute-start.49) | collective-permute-done | bytes 1048608 | tf_op jit(solution)/shard_map/ppermute | solution.py:212
  822.6 16.8 %collective-permute-done.50 = f32[64,2048]{1,0:T(8,128)S(1)} collective-permute-done((f32[64,2048]{1,0:T(8,128)S(1)}, f32[64,2048]{1,0:T(8,128)S(1)}, u32[]{:S(2)}, u32[]{:S(2)}) %collective-permute-start.50) | collective-permute-done | bytes 524320 | tf_op jit(solution)/shard_map/ppermute | solution.py:212
  866.0 7.9 collective-permute-done.53
  879.2 17.8 %collective-permute-done.66 = f32[128,2048]{1,0:T(8,128)S(1)} collective-permute-done((f32[128,2048]{1,0:T(8,128)S(1)}, f32[128,2048]{1,0:T(8,128)S(1)}, u32[]{:S(2)}, u32[]{:S(2)}) %collective-permute-start.66) | collective-permute-done | bytes 1048608 | tf_op jit(solution)/shard_map/ppermute | solution.py:212
  897.4 21.0 %collective-permute-done.54 = f32[128,2048]{1,0:T(8,128)S(1)} collective-permute-done((f32[128,2048]{1,0:T(8,128)S(1)}, f32[128,2048]{1,0:T(8,128)S(1)}, u32[]{:S(2)}, u32[]{:S(2)}) %collective-permute-start.54) | collective-permute-done | bytes 1048608 | tf_op jit(solution)/shard_map/ppermute | solution.py:212
  928.3 5.3 reduce-scatter.10.cloned.1.call-done
  933.6 148.0 %reduce-scatter.12.cloned.1.call-done = f32[256,2048]{1,0:T(8,128)} async-done(((f32[1024,2048]{1,0:T(8,128)}), f32[256,2048]{1,0:T(8,128)}) %reduce-scatter.12.cloned.1.call-update) | async-done | bytes 2097168 | tf_op jit(solution)/shard_map/reduce_scatter | solution.py:331
  (469 shorter events, 281.2 us)
Async XLA Ops:
  7.2 850.5 %reduce-scatter.8.cloned.1.call-start = ((), (), s32[]{:S(2)}) async-start(), calls=%async_computation.6 | async-start | bytes 2621440 | tf_op jit(solution)/shard_map/reduce_scatter | solution.py:331
  44.8 28.9 %collective-permute-start.2 = (f32[128,2048]{1,0:T(8,128)}, f32[128,2048]{1,0:T(8,128)}, u32[]{:S(2)}, u32[]{:S(2)}) collective-permute-start(f32[128,2048]{1,0:T(8,128)} %fusion.139), channel_id=1, source_target_pairs={{0,2},{1,3},{2,0},{3,1},{4,6},{5,7},{6,4},{7,5},{8,10},{9,11},{10,... | collective-permute-start | bytes 3145736 | tf_op jit(solution)/shard_map/ppermute | solution.py:212
  49.2 28.5 %collective-permute-start = (f32[128,2048]{1,0:T(8,128)}, f32[128,2048]{1,0:T(8,128)}, u32[]{:S(2)}, u32[]{:S(2)}) collective-permute-start(f32[128,2048]{1,0:T(8,128)} %fusion.142), channel_id=1, source_target_pairs={{0,1},{1,0},{2,3},{3,2},{4,5},{5,4},{6,7},{7,6},{8,9},{9,8},{10,11... | collective-permute-start | bytes 3145736 | tf_op jit(solution)/shard_map/ppermute | solution.py:212
  66.7 27.9 %collective-permute-start.10 = (f32[128,2048]{1,0:T(8,128)}, f32[128,2048]{1,0:T(8,128)}, u32[]{:S(2)}, u32[]{:S(2)}) collective-permute-start(f32[128,2048]{1,0:T(8,128)} %fusion.133), channel_id=1, source_target_pairs={{0,2},{1,3},{2,0},{3,1},{4,6},{5,7},{6,4},{7,5},{8,10},{9,11},{10,... | collective-permute-start | bytes 3145736 | tf_op jit(solution)/shard_map/ppermute | solution.py:212
  68.8 29.6 %collective-permute-start.8 = (f32[128,2048]{1,0:T(8,128)}, f32[128,2048]{1,0:T(8,128)}, u32[]{:S(2)}, u32[]{:S(2)}) collective-permute-start(f32[128,2048]{1,0:T(8,128)} %fusion.136), channel_id=1, source_target_pairs={{0,1},{1,0},{2,3},{3,2},{4,5},{5,4},{6,7},{7,6},{8,9},{9,8},{10,11... | collective-permute-start | bytes 3145736 | tf_op jit(solution)/shard_map/ppermute | solution.py:212
  75.6 33.5 %collective-permute-start.3 = (f32[64,2048]{1,0:T(8,128)S(1)}, f32[64,2048]{1,0:T(8,128)S(1)}, u32[]{:S(2)}, u32[]{:S(2)}) collective-permute-start(f32[64,2048]{1,0:T(8,128)S(1)} %constant_dynamic-slice_fusion.24), channel_id=1, source_target_pairs={{0,1},{1,0},{2,3},{3,2},{4,5},{5,4},{6,7},{7,6},{8,9},{9,8},{10,11... | collective-permute-start | bytes 1572872 | tf_op jit(solution)/shard_map/ppermute | solution.py:212
  79.4 29.8 %collective-permute-start.1 = (f32[64,2048]{1,0:T(8,128)S(1)}, f32[64,2048]{1,0:T(8,128)S(1)}, u32[]{:S(2)}, u32[]{:S(2)}) collective-permute-start(f32[64,2048]{1,0:T(8,128)S(1)} %constant_dynamic-slice_fusion.25), channel_id=1, source_target_pairs={{0,2},{1,3},{2,0},{3,1},{4,6},{5,7},{6,4},{7,5},{8,10},{9,11},{10,... | collective-permute-start | bytes 1572872 | tf_op jit(solution)/shard_map/ppermute | solution.py:212
  96.3 24.1 %collective-permute-start.11 = (f32[64,2048]{1,0:T(8,128)S(1)}, f32[64,2048]{1,0:T(8,128)S(1)}, u32[]{:S(2)}, u32[]{:S(2)}) collective-permute-start(f32[64,2048]{1,0:T(8,128)S(1)} %constant_dynamic-slice_fusion.18), channel_id=1, source_target_pairs={{0,1},{1,0},{2,3},{3,2},{4,5},{5,4},{6,7},{7,6},{8,9},{9,8},{10,11... | collective-permute-start | bytes 1572872 | tf_op jit(solution)/shard_map/ppermute | solution.py:212
  100.1 20.4 %collective-permute-start.9 = (f32[64,2048]{1,0:T(8,128)S(1)}, f32[64,2048]{1,0:T(8,128)S(1)}, u32[]{:S(2)}, u32[]{:S(2)}) collective-permute-start(f32[64,2048]{1,0:T(8,128)S(1)} %constant_dynamic-slice_fusion.19), channel_id=1, source_target_pairs={{0,2},{1,3},{2,0},{3,1},{4,6},{5,7},{6,4},{7,5},{8,10},{9,11},{10,... | collective-permute-start | bytes 1572872 | tf_op jit(solution)/shard_map/ppermute | solution.py:212
  110.4 21.3 %collective-permute-start.6 = (f32[64,2048]{1,0:T(8,128)S(1)}, f32[64,2048]{1,0:T(8,128)}, u32[]{:S(2)}, u32[]{:S(2)}) collective-permute-start(f32[64,2048]{1,0:T(8,128)S(1)} %get-tuple-element.123), channel_id=1, source_target_pairs={{0,1},{1,0},{2,3},{3,2},{4,5},{5,4},{6,7},{7,6},{8,9},{9,8},{10,11... | collective-permute-start | bytes 1572872 | tf_op jit(solution)/shard_map/ppermute | solution.py:212
  112.0 21.1 %collective-permute-start.4 = (f32[64,2048]{1,0:T(8,128)S(1)}, f32[64,2048]{1,0:T(8,128)}, u32[]{:S(2)}, u32[]{:S(2)}) collective-permute-start(f32[64,2048]{1,0:T(8,128)S(1)} %get-tuple-element.122), channel_id=1, source_target_pairs={{0,2},{1,3},{2,0},{3,1},{4,6},{5,7},{6,4},{7,5},{8,10},{9,11},{10,... | collective-permute-start | bytes 1572872 | tf_op jit(solution)/shard_map/ppermute | solution.py:212
  123.6 19.4 %collective-permute-start.14 = (f32[64,2048]{1,0:T(8,128)}, f32[64,2048]{1,0:T(8,128)}, u32[]{:S(2)}, u32[]{:S(2)}) collective-permute-start(f32[64,2048]{1,0:T(8,128)} %get-tuple-element.129), channel_id=1, source_target_pairs={{0,1},{1,0},{2,3},{3,2},{4,5},{5,4},{6,7},{7,6},{8,9},{9,8},{10,11... | collective-permute-start | bytes 1572872 | tf_op jit(solution)/shard_map/ppermute | solution.py:212
  125.1 20.6 %collective-permute-start.12 = (f32[64,2048]{1,0:T(8,128)}, f32[64,2048]{1,0:T(8,128)S(1)}, u32[]{:S(2)}, u32[]{:S(2)}) collective-permute-start(f32[64,2048]{1,0:T(8,128)} %get-tuple-element.128), channel_id=1, source_target_pairs={{0,2},{1,3},{2,0},{3,1},{4,6},{5,7},{6,4},{7,5},{8,10},{9,11},{10,... | collective-permute-start | bytes 1572872 | tf_op jit(solution)/shard_map/ppermute | solution.py:212
  133.0 29.6 %collective-permute-start.7 = (f32[128,2048]{1,0:T(8,128)S(1)}, f32[128,2048]{1,0:T(8,128)}, u32[]{:S(2)}, u32[]{:S(2)}) collective-permute-start(f32[128,2048]{1,0:T(8,128)S(1)} %maximum_select_fusion.17), channel_id=1, source_target_pairs={{0,2},{1,3},{2,0},{3,1},{4,6},{5,7},{6,4},{7,5},{8,10},{9,11},{10,... | collective-permute-start | bytes 3145736 | tf_op jit(solution)/shard_map/ppermute | solution.py:212
  134.8 30.6 %collective-permute-start.5 = (f32[128,2048]{1,0:T(8,128)S(1)}, f32[128,2048]{1,0:T(8,128)}, u32[]{:S(2)}, u32[]{:S(2)}) collective-permute-start(f32[128,2048]{1,0:T(8,128)S(1)} %maximum_select_fusion.16), channel_id=1, source_target_pairs={{0,1},{1,0},{2,3},{3,2},{4,5},{5,4},{6,7},{7,6},{8,9},{9,8},{10,11... | collective-permute-start | bytes 3145736 | tf_op jit(solution)/shard_map/ppermute | solution.py:212
  145.7 37.9 %collective-permute-start.15 = (f32[128,2048]{1,0:T(8,128)}, f32[128,2048]{1,0:T(8,128)}, u32[]{:S(2)}, u32[]{:S(2)}) collective-permute-start(f32[128,2048]{1,0:T(8,128)} %maximum_select_fusion.19), channel_id=1, source_target_pairs={{0,2},{1,3},{2,0},{3,1},{4,6},{5,7},{6,4},{7,5},{8,10},{9,11},{10,... | collective-permute-start | bytes 3145736 | tf_op jit(solution)/shard_map/ppermute | solution.py:212
  148.0 38.5 %collective-permute-start.13 = (f32[128,2048]{1,0:T(8,128)}, f32[128,2048]{1,0:T(8,128)}, u32[]{:S(2)}, u32[]{:S(2)}) collective-permute-start(f32[128,2048]{1,0:T(8,128)} %maximum_select_fusion.18), channel_id=1, source_target_pairs={{0,1},{1,0},{2,3},{3,2},{4,5},{5,4},{6,7},{7,6},{8,9},{9,8},{10,11... | collective-permute-start | bytes 3145736 | tf_op jit(solution)/shard_map/ppermute | solution.py:212
  225.7 20.2 %collective-permute-start.16 = (f32[1024,2048]{1,0:T(8,128)}, f32[1024,2048]{1,0:T(8,128)}, u32[]{:S(2)}, u32[]{:S(2)}) collective-permute-start(f32[1024,2048]{1,0:T(8,128)} %shard_map.212), channel_id=1, source_target_pairs={{0,4},{4,0},{8,12},{12,8},{16,20},{20,16},{24,28},{28,24},{1,5},{5... | collective-permute-start | bytes 25165832 | tf_op jit(solution)/shard_map/ppermute | solution.py:212
  308.6 26.3 %collective-permute-start.19 = (f32[128,2048]{1,0:T(8,128)}, f32[128,2048]{1,0:T(8,128)}, u32[]{:S(2)}, u32[]{:S(2)}) collective-permute-start(f32[128,2048]{1,0:T(8,128)} %convolution_add_fusion.28), channel_id=1, source_target_pairs={{0,2},{1,3},{2,0},{3,1},{4,6},{5,7},{6,4},{7,5},{8,10},{9,11},{10,... | collective-permute-start | bytes 3145736 | tf_op jit(solution)/shard_map/ppermute | solution.py:212
  315.2 52.3 %collective-permute-start.17 = (f32[128,2048]{1,0:T(8,128)}, f32[128,2048]{1,0:T(8,128)}, u32[]{:S(2)}, u32[]{:S(2)}) collective-permute-start(f32[128,2048]{1,0:T(8,128)} %convolution_add_fusion.30), channel_id=1, source_target_pairs={{0,1},{1,0},{2,3},{3,2},{4,5},{5,4},{6,7},{7,6},{8,9},{9,8},{10,11... | collective-permute-start | bytes 3145736 | tf_op jit(solution)/shard_map/ppermute | solution.py:212
  321.9 34.9 %collective-permute-start.39 = (f32[128,2048]{1,0:T(8,128)}, f32[128,2048]{1,0:T(8,128)}, u32[]{:S(2)}, u32[]{:S(2)}) collective-permute-start(f32[128,2048]{1,0:T(8,128)} %convolution_add_fusion.20), channel_id=1, source_target_pairs={{0,2},{1,3},{2,0},{3,1},{4,6},{5,7},{6,4},{7,5},{8,10},{9,11},{10,... | collective-permute-start | bytes 3145736 | tf_op jit(solution)/shard_map/ppermute | solution.py:212
  329.2 34.7 %collective-permute-start.37 = (f32[128,2048]{1,0:T(8,128)S(1)}, f32[128,2048]{1,0:T(8,128)S(1)}, u32[]{:S(2)}, u32[]{:S(2)}) collective-permute-start(f32[128,2048]{1,0:T(8,128)S(1)} %convolution_add_fusion.22), channel_id=1, source_target_pairs={{0,1},{1,0},{2,3},{3,2},{4,5},{5,4},{6,7},{7,6},{8,9},{9,8},{10,11... | collective-permute-start | bytes 3145736 | tf_op jit(solution)/shard_map/ppermute | solution.py:212
  339.1 46.8 %collective-permute-start.20 = (f32[64,2048]{1,0:T(8,128)S(1)}, f32[64,2048]{1,0:T(8,128)S(1)}, u32[]{:S(2)}, u32[]{:S(2)}) collective-permute-start(f32[64,2048]{1,0:T(8,128)S(1)} %constant_dynamic-slice_fusion.16), channel_id=1, source_target_pairs={{0,1},{1,0},{2,3},{3,2},{4,5},{5,4},{6,7},{7,6},{8,9},{9,8},{10,11... | collective-permute-start | bytes 1572872 | tf_op jit(solution)/shard_map/ppermute | solution.py:212
  361.0 24.5 %collective-permute-start.40 = (f32[64,2048]{1,0:T(8,128)S(1)}, f32[64,2048]{1,0:T(8,128)S(1)}, u32[]{:S(2)}, u32[]{:S(2)}) collective-permute-start(f32[64,2048]{1,0:T(8,128)S(1)} %constant_dynamic-slice_fusion.8), channel_id=1, source_target_pairs={{0,1},{1,0},{2,3},{3,2},{4,5},{5,4},{6,7},{7,6},{8,9},{9,8},{10,11... | collective-permute-start | bytes 1572872 | tf_op jit(solution)/shard_map/ppermute | solution.py:212
  366.8 18.7 %collective-permute-start.38 = (f32[64,2048]{1,0:T(8,128)S(1)}, f32[64,2048]{1,0:T(8,128)S(1)}, u32[]{:S(2)}, u32[]{:S(2)}) collective-permute-start(f32[64,2048]{1,0:T(8,128)S(1)} %constant_dynamic-slice_fusion.9), channel_id=1, source_target_pairs={{0,2},{1,3},{2,0},{3,1},{4,6},{5,7},{6,4},{7,5},{8,10},{9,11},{10,... | collective-permute-start | bytes 1572872 | tf_op jit(solution)/shard_map/ppermute | solution.py:212
  393.4 23.9 %collective-permute-start.43 = (f32[64,2048]{1,0:T(8,128)S(1)}, f32[64,2048]{1,0:T(8,128)S(1)}, u32[]{:S(2)}, u32[]{:S(2)}) collective-permute-start(f32[64,2048]{1,0:T(8,128)S(1)} %get-tuple-element.113), channel_id=1, source_target_pairs={{0,1},{1,0},{2,3},{3,2},{4,5},{5,4},{6,7},{7,6},{8,9},{9,8},{10,11... | collective-permute-start | bytes 1572872 | tf_op jit(solution)/shard_map/ppermute | solution.py:212
  406.2 39.0 %collective-permute-start.58 = (f32[128,2048]{1,0:T(8,128)S(1)}, f32[128,2048]{1,0:T(8,128)S(1)}, u32[]{:S(2)}, u32[]{:S(2)}) collective-permute-start(f32[128,2048]{1,0:T(8,128)S(1)} %maximum_select_fusion.29), channel_id=1, source_target_pairs={{0,2},{1,3},{2,0},{3,1},{4,6},{5,7},{6,4},{7,5},{8,10},{9,11},{10,... | collective-permute-start | bytes 3145736 | tf_op jit(solution)/shard_map/ppermute | solution.py:212
  407.3 36.2 %collective-permute-start.41 = (f32[64,2048]{1,0:T(8,128)S(1)}, f32[64,2048]{1,0:T(8,128)S(1)}, u32[]{:S(2)}, u32[]{:S(2)}) collective-permute-start(f32[64,2048]{1,0:T(8,128)S(1)} %get-tuple-element.112), channel_id=1, source_target_pairs={{0,2},{1,3},{2,0},{3,1},{4,6},{5,7},{6,4},{7,5},{8,10},{9,11},{10,... | collective-permute-start | bytes 1572872 | tf_op jit(solution)/shard_map/ppermute | solution.py:212
  408.4 37.0 %collective-permute-start.56 = (f32[128,2048]{1,0:T(8,128)S(1)}, f32[128,2048]{1,0:T(8,128)S(1)}, u32[]{:S(2)}, u32[]{:S(2)}) collective-permute-start(f32[128,2048]{1,0:T(8,128)S(1)} %maximum_select_fusion.28), channel_id=1, source_target_pairs={{0,1},{1,0},{2,3},{3,2},{4,5},{5,4},{6,7},{7,6},{8,9},{9,8},{10,11... | collective-permute-start | bytes 3145736 | tf_op jit(solution)/shard_map/ppermute | solution.py:212
  417.4 42.6 %collective-permute-start.44 = (f32[128,2048]{1,0:T(8,128)S(1)}, f32[128,2048]{1,0:T(8,128)S(1)}, u32[]{:S(2)}, u32[]{:S(2)}) collective-permute-start(f32[128,2048]{1,0:T(8,128)S(1)} %maximum_select_fusion.25), channel_id=1, source_target_pairs={{0,2},{1,3},{2,0},{3,1},{4,6},{5,7},{6,4},{7,5},{8,10},{9,11},{10,... | collective-permute-start | bytes 3145736 | tf_op jit(solution)/shard_map/ppermute | solution.py:212
  443.6 18.6 %collective-permute-start.42 = (f32[128,2048]{1,0:T(8,128)S(1)}, f32[128,2048]{1,0:T(8,128)S(1)}, u32[]{:S(2)}, u32[]{:S(2)}) collective-permute-start(f32[128,2048]{1,0:T(8,128)S(1)} %maximum_select_fusion.24), channel_id=1, source_target_pairs={{0,1},{1,0},{2,3},{3,2},{4,5},{5,4},{6,7},{7,6},{8,9},{9,8},{10,11... | collective-permute-start | bytes 3145736 | tf_op jit(solution)/shard_map/ppermute | solution.py:212
  480.9 442.0 %reduce-scatter.14.cloned.1.call-start = ((), (), s32[]{:S(2)}) async-start(), calls=%async_computation.9 | async-start | bytes 10485760 | tf_op jit(solution)/shard_map/reduce_scatter | solution.py:331
  505.2 420.5 %reduce-scatter.6.cloned.1.call-start = ((), (), s32[]{:S(2)}) async-start(), calls=%async_computation.5 | async-start | bytes 7864320 | tf_op jit(solution)/shard_map/reduce_scatter | solution.py:331
  605.4 328.2 %reduce-scatter.10.cloned.1.call-start = ((), (), s32[]{:S(2)}) async-start(), calls=%async_computation.7 | async-start | bytes 10485760 | tf_op jit(solution)/shard_map/reduce_scatter | solution.py:331
  606.0 475.7 %reduce-scatter.12.cloned.1.call-start = ((), (), s32[]{:S(2)}) async-start(), calls=%async_computation.8 | async-start | bytes 10485760 | tf_op jit(solution)/shard_map/reduce_scatter | solution.py:331
  613.0 26.1 %collective-permute-start.23 = (f32[128,2048]{1,0:T(8,128)S(1)}, f32[128,2048]{1,0:T(8,128)S(1)}, u32[]{:S(2)}, u32[]{:S(2)}) collective-permute-start(f32[128,2048]{1,0:T(8,128)S(1)} %fusion.58), channel_id=1, source_target_pairs={{0,2},{1,3},{2,0},{3,1},{4,6},{5,7},{6,4},{7,5},{8,10},{9,11},{10,... | collective-permute-start | bytes 3145736 | tf_op jit(solution)/shard_map/ppermute | solution.py:212
  618.4 26.1 %collective-permute-start.21 = (f32[128,2048]{1,0:T(8,128)S(1)}, f32[128,2048]{1,0:T(8,128)S(1)}, u32[]{:S(2)}, u32[]{:S(2)}) collective-permute-start(f32[128,2048]{1,0:T(8,128)S(1)} %fusion.61), channel_id=1, source_target_pairs={{0,1},{1,0},{2,3},{3,2},{4,5},{5,4},{6,7},{7,6},{8,9},{9,8},{10,11... | collective-permute-start | bytes 3145736 | tf_op jit(solution)/shard_map/ppermute | solution.py:212
  622.6 39.0 %collective-permute-start.31 = (f32[128,2048]{1,0:T(8,128)S(1)}, f32[128,2048]{1,0:T(8,128)S(1)}, u32[]{:S(2)}, u32[]{:S(2)}) collective-permute-start(f32[128,2048]{1,0:T(8,128)S(1)} %fusion.52), channel_id=1, source_target_pairs={{0,2},{1,3},{2,0},{3,1},{4,6},{5,7},{6,4},{7,5},{8,10},{9,11},{10,... | collective-permute-start | bytes 3145736 | tf_op jit(solution)/shard_map/ppermute | solution.py:212
  623.2 43.8 %collective-permute-start.29 = (f32[128,2048]{1,0:T(8,128)S(1)}, f32[128,2048]{1,0:T(8,128)S(1)}, u32[]{:S(2)}, u32[]{:S(2)}) collective-permute-start(f32[128,2048]{1,0:T(8,128)S(1)} %fusion.55), channel_id=1, source_target_pairs={{0,1},{1,0},{2,3},{3,2},{4,5},{5,4},{6,7},{7,6},{8,9},{9,8},{10,11... | collective-permute-start | bytes 3145736 | tf_op jit(solution)/shard_map/ppermute | solution.py:212
  640.5 37.7 %collective-permute-start.24 = (f32[64,2048]{1,0:T(8,128)S(1)}, f32[64,2048]{1,0:T(8,128)S(1)}, u32[]{:S(2)}, u32[]{:S(2)}) collective-permute-start(f32[64,2048]{1,0:T(8,128)S(1)} %constant_dynamic-slice_fusion.14), channel_id=1, source_target_pairs={{0,1},{1,0},{2,3},{3,2},{4,5},{5,4},{6,7},{7,6},{8,9},{9,8},{10,11... | collective-permute-start | bytes 1572872 | tf_op jit(solution)/shard_map/ppermute | solution.py:212
  645.9 32.4 %collective-permute-start.22 = (f32[64,2048]{1,0:T(8,128)S(1)}, f32[64,2048]{1,0:T(8,128)S(1)}, u32[]{:S(2)}, u32[]{:S(2)}) collective-permute-start(f32[64,2048]{1,0:T(8,128)S(1)} %constant_dynamic-slice_fusion.15), channel_id=1, source_target_pairs={{0,2},{1,3},{2,0},{3,1},{4,6},{5,7},{6,4},{7,5},{8,10},{9,11},{10,... | collective-permute-start | bytes 1572872 | tf_op jit(solution)/shard_map/ppermute | solution.py:212
  663.0 26.5 %collective-permute-start.32 = (f32[64,2048]{1,0:T(8,128)S(1)}, f32[64,2048]{1,0:T(8,128)S(1)}, u32[]{:S(2)}, u32[]{:S(2)}) collective-permute-start(f32[64,2048]{1,0:T(8,128)S(1)} %constant_dynamic-slice_fusion.12), channel_id=1, source_target_pairs={{0,1},{1,0},{2,3},{3,2},{4,5},{5,4},{6,7},{7,6},{8,9},{9,8},{10,11... | collective-permute-start | bytes 1572872 | tf_op jit(solution)/shard_map/ppermute | solution.py:212
  668.4 21.1 %collective-permute-start.30 = (f32[64,2048]{1,0:T(8,128)S(1)}, f32[64,2048]{1,0:T(8,128)S(1)}, u32[]{:S(2)}, u32[]{:S(2)}) collective-permute-start(f32[64,2048]{1,0:T(8,128)S(1)} %constant_dynamic-slice_fusion.13), channel_id=1, source_target_pairs={{0,2},{1,3},{2,0},{3,1},{4,6},{5,7},{6,4},{7,5},{8,10},{9,11},{10,... | collective-permute-start | bytes 1572872 | tf_op jit(solution)/shard_map/ppermute | solution.py:212
  678.7 22.1 %collective-permute-start.27 = (f32[64,2048]{1,0:T(8,128)S(1)}, f32[64,2048]{1,0:T(8,128)}, u32[]{:S(2)}, u32[]{:S(2)}) collective-permute-start(f32[64,2048]{1,0:T(8,128)S(1)} %get-tuple-element.119), channel_id=1, source_target_pairs={{0,1},{1,0},{2,3},{3,2},{4,5},{5,4},{6,7},{7,6},{8,9},{9,8},{10,11... | collective-permute-start | bytes 1572872 | tf_op jit(solution)/shard_map/ppermute | solution.py:212
  680.3 23.5 %collective-permute-start.25 = (f32[64,2048]{1,0:T(8,128)S(1)}, f32[64,2048]{1,0:T(8,128)}, u32[]{:S(2)}, u32[]{:S(2)}) collective-permute-start(f32[64,2048]{1,0:T(8,128)S(1)} %get-tuple-element.118), channel_id=1, source_target_pairs={{0,2},{1,3},{2,0},{3,1},{4,6},{5,7},{6,4},{7,5},{8,10},{9,11},{10,... | collective-permute-start | bytes 1572872 | tf_op jit(solution)/shard_map/ppermute | solution.py:212
  690.8 21.2 %collective-permute-start.35 = (f32[64,2048]{1,0:T(8,128)}, f32[64,2048]{1,0:T(8,128)}, u32[]{:S(2)}, u32[]{:S(2)}) collective-permute-start(f32[64,2048]{1,0:T(8,128)} %get-tuple-element.121), channel_id=1, source_target_pairs={{0,1},{1,0},{2,3},{3,2},{4,5},{5,4},{6,7},{7,6},{8,9},{9,8},{10,11... | collective-permute-start | bytes 1572872 | tf_op jit(solution)/shard_map/ppermute | solution.py:212
  693.1 22.7 %collective-permute-start.33 = (f32[64,2048]{1,0:T(8,128)}, f32[64,2048]{1,0:T(8,128)S(1)}, u32[]{:S(2)}, u32[]{:S(2)}) collective-permute-start(f32[64,2048]{1,0:T(8,128)} %get-tuple-element.120), channel_id=1, source_target_pairs={{0,2},{1,3},{2,0},{3,1},{4,6},{5,7},{6,4},{7,5},{8,10},{9,11},{10,... | collective-permute-start | bytes 1572872 | tf_op jit(solution)/shard_map/ppermute | solution.py:212
  702.2 28.4 %collective-permute-start.28 = (f32[128,2048]{1,0:T(8,128)S(1)}, f32[128,2048]{1,0:T(8,128)S(1)}, u32[]{:S(2)}, u32[]{:S(2)}) collective-permute-start(f32[128,2048]{1,0:T(8,128)S(1)} %maximum_select_fusion.21), channel_id=1, source_target_pairs={{0,2},{1,3},{2,0},{3,1},{4,6},{5,7},{6,4},{7,5},{8,10},{9,11},{10,... | collective-permute-start | bytes 3145736 | tf_op jit(solution)/shard_map/ppermute | solution.py:212
  705.1 29.3 %collective-permute-start.26 = (f32[128,2048]{1,0:T(8,128)S(1)}, f32[128,2048]{1,0:T(8,128)S(1)}, u32[]{:S(2)}, u32[]{:S(2)}) collective-permute-start(f32[128,2048]{1,0:T(8,128)S(1)} %maximum_select_fusion.20), channel_id=1, source_target_pairs={{0,1},{1,0},{2,3},{3,2},{4,5},{5,4},{6,7},{7,6},{8,9},{9,8},{10,11... | collective-permute-start | bytes 3145736 | tf_op jit(solution)/shard_map/ppermute | solution.py:212
  714.1 37.2 %collective-permute-start.36 = (f32[128,2048]{1,0:T(8,128)S(1)}, f32[128,2048]{1,0:T(8,128)S(1)}, u32[]{:S(2)}, u32[]{:S(2)}) collective-permute-start(f32[128,2048]{1,0:T(8,128)S(1)} %maximum_select_fusion.23), channel_id=1, source_target_pairs={{0,2},{1,3},{2,0},{3,1},{4,6},{5,7},{6,4},{7,5},{8,10},{9,11},{10,... | collective-permute-start | bytes 3145736 | tf_op jit(solution)/shard_map/ppermute | solution.py:212
  716.0 40.3 %collective-permute-start.34 = (f32[128,2048]{1,0:T(8,128)S(1)}, f32[128,2048]{1,0:T(8,128)S(1)}, u32[]{:S(2)}, u32[]{:S(2)}) collective-permute-start(f32[128,2048]{1,0:T(8,128)S(1)} %maximum_select_fusion.22), channel_id=1, source_target_pairs={{0,1},{1,0},{2,3},{3,2},{4,5},{5,4},{6,7},{7,6},{8,9},{9,8},{10,11... | collective-permute-start | bytes 3145736 | tf_op jit(solution)/shard_map/ppermute | solution.py:212
  767.0 26.1 %collective-permute-start.61 = (f32[128,2048]{1,0:T(8,128)S(1)}, f32[128,2048]{1,0:T(8,128)S(1)}, u32[]{:S(2)}, u32[]{:S(2)}) collective-permute-start(f32[128,2048]{1,0:T(8,128)S(1)} %convolution_add_fusion), channel_id=1, source_target_pairs={{0,2},{1,3},{2,0},{3,1},{4,6},{5,7},{6,4},{7,5},{8,10},{9,11},{10,... | collective-permute-start | bytes 3145736 | tf_op jit(solution)/shard_map/ppermute | solution.py:212
  770.0 50.3 %collective-permute-start.59 = (f32[128,2048]{1,0:T(8,128)S(1)}, f32[128,2048]{1,0:T(8,128)S(1)}, u32[]{:S(2)}, u32[]{:S(2)}) collective-permute-start(f32[128,2048]{1,0:T(8,128)S(1)} %convolution_add_fusion.4), channel_id=1, source_target_pairs={{0,1},{1,0},{2,3},{3,2},{4,5},{5,4},{6,7},{7,6},{8,9},{9,8},{10,11... | collective-permute-start | bytes 3145736 | tf_op jit(solution)/shard_map/ppermute | solution.py:212
  773.8 40.4 %collective-permute-start.49 = (f32[128,2048]{1,0:T(8,128)S(1)}, f32[128,2048]{1,0:T(8,128)S(1)}, u32[]{:S(2)}, u32[]{:S(2)}) collective-permute-start(f32[128,2048]{1,0:T(8,128)S(1)} %convolution_add_fusion.8), channel_id=1, source_target_pairs={{0,2},{1,3},{2,0},{3,1},{4,6},{5,7},{6,4},{7,5},{8,10},{9,11},{10,... | collective-permute-start | bytes 3145736 | tf_op jit(solution)/shard_map/ppermute | solution.py:212
  783.3 35.3 %collective-permute-start.47 = (f32[128,2048]{1,0:T(8,128)S(1)}, f32[128,2048]{1,0:T(8,128)S(1)}, u32[]{:S(2)}, u32[]{:S(2)}) collective-permute-start(f32[128,2048]{1,0:T(8,128)S(1)} %convolution_add_fusion.12), channel_id=1, source_target_pairs={{0,1},{1,0},{2,3},{3,2},{4,5},{5,4},{6,7},{7,6},{8,9},{9,8},{10,11... | collective-permute-start | bytes 3145736 | tf_op jit(solution)/shard_map/ppermute | solution.py:212
  793.9 46.0 %collective-permute-start.62 = (f32[64,2048]{1,0:T(8,128)S(1)}, f32[64,2048]{1,0:T(8,128)S(1)}, u32[]{:S(2)}, u32[]{:S(2)}) collective-permute-start(f32[64,2048]{1,0:T(8,128)S(1)} %constant_dynamic-slice_fusion.2), channel_id=1, source_target_pairs={{0,1},{1,0},{2,3},{3,2},{4,5},{5,4},{6,7},{7,6},{8,9},{9,8},{10,11... | collective-permute-start | bytes 1572872 | tf_op jit(solution)/shard_map/ppermute | solution.py:212
  815.1 24.3 %collective-permute-start.50 = (f32[64,2048]{1,0:T(8,128)S(1)}, f32[64,2048]{1,0:T(8,128)S(1)}, u32[]{:S(2)}, u32[]{:S(2)}) collective-permute-start(f32[64,2048]{1,0:T(8,128)S(1)} %constant_dynamic-slice_fusion.6), channel_id=1, source_target_pairs={{0,1},{1,0},{2,3},{3,2},{4,5},{5,4},{6,7},{7,6},{8,9},{9,8},{10,11... | collective-permute-start | bytes 1572872 | tf_op jit(solution)/shard_map/ppermute | solution.py:212
  819.5 19.9 %collective-permute-start.48 = (f32[64,2048]{1,0:T(8,128)S(1)}, f32[64,2048]{1,0:T(8,128)S(1)}, u32[]{:S(2)}, u32[]{:S(2)}) collective-permute-start(f32[64,2048]{1,0:T(8,128)S(1)} %constant_dynamic-slice_fusion.7), channel_id=1, source_target_pairs={{0,2},{1,3},{2,0},{3,1},{4,6},{5,7},{6,4},{7,5},{8,10},{9,11},{10,... | collective-permute-start | bytes 1572872 | tf_op jit(solution)/shard_map/ppermute | solution.py:212
  821.3 20.5 %collective-permute-start.60 = (f32[64,2048]{1,0:T(8,128)S(1)}, f32[64,2048]{1,0:T(8,128)S(1)}, u32[]{:S(2)}, u32[]{:S(2)}) collective-permute-start(f32[64,2048]{1,0:T(8,128)S(1)} %constant_dynamic-slice_fusion.3), channel_id=1, source_target_pairs={{0,2},{1,3},{2,0},{3,1},{4,6},{5,7},{6,4},{7,5},{8,10},{9,11},{10,... | collective-permute-start | bytes 1572872 | tf_op jit(solution)/shard_map/ppermute | solution.py:212
  851.1 22.8 %collective-permute-start.53 = (f32[64,2048]{1,0:T(8,128)S(1)}, f32[64,2048]{1,0:T(8,128)}, u32[]{:S(2)}, u32[]{:S(2)}) collective-permute-start(f32[64,2048]{1,0:T(8,128)S(1)} %get-tuple-element.111), channel_id=1, source_target_pairs={{0,1},{1,0},{2,3},{3,2},{4,5},{5,4},{6,7},{7,6},{8,9},{9,8},{10,11... | collective-permute-start | bytes 1572872 | tf_op jit(solution)/shard_map/ppermute | solution.py:212
  862.6 34.4 %collective-permute-start.66 = (f32[128,2048]{1,0:T(8,128)S(1)}, f32[128,2048]{1,0:T(8,128)S(1)}, u32[]{:S(2)}, u32[]{:S(2)}) collective-permute-start(f32[128,2048]{1,0:T(8,128)S(1)} %maximum_select_fusion.31), channel_id=1, source_target_pairs={{0,2},{1,3},{2,0},{3,1},{4,6},{5,7},{6,4},{7,5},{8,10},{9,11},{10,... | collective-permute-start | bytes 3145736 | tf_op jit(solution)/shard_map/ppermute | solution.py:212
  864.0 33.2 %collective-permute-start.64 = (f32[128,2048]{1,0:T(8,128)S(1)}, f32[128,2048]{1,0:T(8,128)S(1)}, u32[]{:S(2)}, u32[]{:S(2)}) collective-permute-start(f32[128,2048]{1,0:T(8,128)S(1)} %maximum_select_fusion.30), channel_id=1, source_target_pairs={{0,1},{1,0},{2,3},{3,2},{4,5},{5,4},{6,7},{7,6},{8,9},{9,8},{10,11... | collective-permute-start | bytes 3145736 | tf_op jit(solution)/shard_map/ppermute | solution.py:212
  875.3 43.2 %collective-permute-start.54 = (f32[128,2048]{1,0:T(8,128)S(1)}, f32[128,2048]{1,0:T(8,128)S(1)}, u32[]{:S(2)}, u32[]{:S(2)}) collective-permute-start(f32[128,2048]{1,0:T(8,128)S(1)} %maximum_select_fusion.27), channel_id=1, source_target_pairs={{0,2},{1,3},{2,0},{3,1},{4,6},{5,7},{6,4},{7,5},{8,10},{9,11},{10,... | collective-permute-start | bytes 3145736 | tf_op jit(solution)/shard_map/ppermute | solution.py:212
  876.6 42.0 %collective-permute-start.52 = (f32[128,2048]{1,0:T(8,128)S(1)}, f32[128,2048]{1,0:T(8,128)S(1)}, u32[]{:S(2)}, u32[]{:S(2)}) collective-permute-start(f32[128,2048]{1,0:T(8,128)S(1)} %maximum_select_fusion.26), channel_id=1, source_target_pairs={{0,1},{1,0},{2,3},{3,2},{4,5},{5,4},{6,7},{7,6},{8,9},{9,8},{10,11... | collective-permute-start | bytes 3145736 | tf_op jit(solution)/shard_map/ppermute | solution.py:212
  (92 other events, 1022.1 us)
Sparse Core Ops, SparseCore 0:
  481.0 43.9 reduce-scatter.7
  527.4 143.7 reduce-scatter.13
  673.5 111.4 reduce-scatter.5
  787.8 145.7 reduce-scatter.9
  936.4 145.2 reduce-scatter.11

commit v2 on v1

--- a/solution.py
+++ b/solution.py
@@ -34,16 +34,17 @@
     return lax.dot_general(a, b, (((0,), (0,)), ((), ())), preferred_element_type=F32)
 
 
-def rope_tables(positions, width, lanes):
-    half_width = width // 2
-    frequency = ROPE_BASE ** (-(jnp.arange(half_width, dtype=F32) * 2.0 / width))
+def rope_tables(positions, lanes):
+    half_width = HD // 2
+    lane = jnp.arange(lanes, dtype=jnp.int32)
+    frequency = ROPE_BASE ** (-((lane % half_width).astype(F32) * 2.0 / HD))
+    sign = jnp.where(lane % HD < half_width, -1.0, 1.0).astype(F32)
     angles = positions.astype(F32)[:, None] * frequency[None, :]
-    cosine, sine = jnp.cos(angles), jnp.sin(angles)
-    copies = lanes // width
-    return (
-        jnp.concatenate([cosine, cosine] * copies, axis=1),
-        jnp.concatenate([-sine, sine] * copies, axis=1),
-    )
+    return jnp.cos(angles), jnp.sin(angles) * sign[None, :]
+
+
+def widen(table, lanes):
+    return jnp.concatenate([table] * (lanes // table.shape[1]), axis=1)
 
 
 def turn(values, cosine, signed_sine):
@@ -68,8 +69,10 @@
 
 def attend_body(act, wq, wk, wv, cos, sin, mask, q_out, k_out, v_out, attn_out):
     rows = act[...]
-    q = turn(mm(rows, wq[...]), cos[...], sin[...]).astype(BF16)
-    k = turn(mm(rows, wk[...]), cos[...], sin[...]).astype(BF16)
+    cosine = widen(cos[...], wq.shape[1])
+    sine = widen(sin[...], wq.shape[1])
+    q = turn(mm(rows, wq[...]), cosine, sine).astype(BF16)
+    k = turn(mm(rows, wk[...]), cosine, sine).astype(BF16)
     v = mm(rows, wv[...]).astype(BF16)
     q_out[...] = q
     k_out[...] = k
@@ -94,7 +97,7 @@
         attend_body,
         grid=(cols // step,),
         in_specs=[whole((rows, width)), weight, weight, weight]
-        + [whole((rows, step)), whole((rows, step)), whole((rows, rows))],
+        + [whole(cos.shape), whole(cos.shape), whole((rows, rows))],
         out_specs=[column] * 4,
         out_shape=[jax.ShapeDtypeStruct((rows, cols), BF16)] * 4,
         cost_estimate=pl.CostEstimate(
@@ -122,7 +125,7 @@
         score_grad = (probs * (mm_nt(g, v) - delta) * scale).astype(BF16)
         q_list.append(mm(score_grad, k))
         k_list.append(mm_tn(score_grad, q))
-    cosine, back_sine = cos[...], -sin[...]
+    cosine, back_sine = widen(cos[...], wo.shape[0]), -widen(sin[...], wo.shape[0])
     out[0] = turn(jnp.concatenate(q_list, axis=1), cosine, back_sine).astype(BF16)
     out[1] = turn(jnp.concatenate(k_list, axis=1), cosine, back_sine).astype(BF16)
     out[2] = jnp.concatenate(v_list, axis=1).astype(BF16)
@@ -139,7 +142,7 @@
         grid=(cols // step,),
         in_specs=[whole((rows, width)), pl.BlockSpec((step, width), lambda i: (i, 0))]
         + [column] * 4
-        + [whole((rows, step)), whole((rows, step)), whole((rows, rows))]
+        + [whole(cos.shape), whole(cos.shape), whole((rows, rows))]
         + [pl.BlockSpec(memory_space=pl.ANY)] * len(after),
         out_specs=pl.BlockSpec((3, rows, step), lambda i: (0, 0, i)),
         out_shape=jax.ShapeDtypeStruct((3, rows, cols), BF16),
@@ -153,33 +156,41 @@
 
 
 def outer_body(count, has_add, which, *refs):
-    total = None
-    for c in range(count):
-        part = mm_tn(refs[c][...], refs[count + c][...])
-        total = part if total is None else total + part
-    if has_add:
-        total = total + refs[2 * count][...]
-    refs[-1][...] = total
-
-
-def outer(lefts, rights, which, pieces, add=None):
+    lefts = [refs[c][...].T for c in range(count)]
+    rights, out = refs[count : 2 * count], refs[-1]
+    width = rights[0].shape[-1]
+    planes = rights[0].shape[0] if len(rights[0].shape) == 3 else 1
+    tile = min(512, width)
+    for plane in range(planes):
+        for start in range(0, width, tile):
+            total = None
+            for left, right in zip(lefts, rights):
+                at = pl.ds(start, tile)
+                block = right[plane, :, at] if len(right.shape) == 3 else right[:, at]
+                part = mm(left, block)
+                total = part if total is None else total + part
+            at = pl.ds(plane * width + start, tile)
+            if has_add:
+                total = total + refs[2 * count][:, at]
+            out[:, at] = total
+
+
+def outer(lefts, rights, which, pieces, add=None, part=(0, 1)):
     count = len(lefts)
     piece = lefts[0].shape[1] // pieces
-    stacked = rights[0].ndim == 3
-    cols = rights[0].shape[-1]
-    if stacked:
-        step, blocks = cols, rights[0].shape[0]
-        right_spec = lambda r: pl.BlockSpec((None, r, step), lambda n, j, w: (n, 0, 0))
+    index, parts = part
+    rows = [v.shape[0] for v in lefts]
+    if rights[0].ndim == 3:
+        planes, _, cols = rights[0].shape
+        out_cols = planes * cols
+        right_specs = [pl.BlockSpec((planes, r, cols), lambda j, w: (0, 0, 0)) for r in rows]
     else:
-        step = min(1024, cols)
-        blocks = cols // step
-        right_spec = lambda r: pl.BlockSpec((r, step), lambda n, j, w: (0, n))
-    out_spec = pl.BlockSpec((piece, step), lambda n, j, w: (j, n))
-    rows = [v.shape[0] for v in lefts]
-    out_rows, out_cols = pieces // 2 * piece, blocks * step
-    specs = [
-        pl.BlockSpec((r, piece), lambda n, j, w: (0, 2 * j + w[0])) for r in rows
-    ] + [right_spec(r) for r in rows]
+        out_cols = rights[0].shape[1] // parts
+        right_specs = [pl.BlockSpec((r, out_cols), lambda j, w: (0, index)) for r in rows]
+    out_spec = pl.BlockSpec((piece, out_cols), lambda j, w: (j, 0))
+    out_rows = pieces // 2 * piece
+    specs = [pl.BlockSpec((r, piece), lambda j, w: (0, 2 * j + w[0])) for r in rows]
+    specs += right_specs
     args = list(lefts) + list(rights)
     if add is not None:
         specs.append(out_spec)
@@ -188,7 +199,7 @@
         functools.partial(outer_body, count, add is not None),
         grid_spec=pltpu.PrefetchScalarGridSpec(
             num_scalar_prefetch=1,
-            grid=(blocks, pieces // 2),
+            grid=(pieces // 2,),
             in_specs=specs,
             out_specs=out_spec,
         ),
@@ -212,7 +223,7 @@
         return lax.ppermute(value, self.axis, [(i, i ^ bit) for i in range(self.size)])
 
     def bit_of(self, bit):
-        return (self.me // bit) % 2
+        return (self.me >> (bit.bit_length() - 1)) & 1
 
     def own_start(self, rows, bits):
         start = 0
@@ -221,27 +232,22 @@
             start = start + self.bit_of(bit) * rows
         return start
 
-    def scatter(self, make, rows, bits):
-        first = True
-        value = None
+    def scatter(self, value, rows, bits):
         for bit in bits:
             half = rows // 2
             mine = self.bit_of(bit)
-            if first:
-                away = make((1 - mine) * half, half)
-                got = self.swap(away, bit)
-                value = make(mine * half, half) + got
-                first = False
-            else:
-                away = lax.dynamic_slice_in_dim(value, (1 - mine) * half, half, 0)
-                got = self.swap(away, bit)
-                value = lax.dynamic_slice_in_dim(value, mine * half, half, 0) + got
+            away = lax.dynamic_slice_in_dim(value, (1 - mine) * half, half, 0)
+            got = self.swap(away, bit)
+            value = lax.dynamic_slice_in_dim(value, mine * half, half, 0) + got
             rows = half
         return value
 
-    def gather(self, value, bits):
-        for bit in reversed(bits):
+    def gather(self, value, bits, after):
+        for step, bit in enumerate(reversed(bits)):
+            last = step == len(bits) - 1
             got = self.swap(value, bit)
+            if last and after is not None:
+                value, got, _ = lax.optimization_barrier((value, got, after))
             mine = self.bit_of(bit)
             value = jnp.where(
                 mine == 0,
@@ -301,31 +307,49 @@
             )
 
         def scatter_rows(make, size):
+            parts = halves(size)
+            half = parts[0][1] // 2
+
+            def piece(flip):
+                starts = []
+                for base, _, bits in parts:
+                    mine = tensor.bit_of(bits[0])
+                    starts.append(base + (1 - mine if flip else mine) * half)
+                return make(starts, half)
+
+            away = piece(True)
+            got = [
+                tensor.swap(away[i * half : (i + 1) * half], bits[0])
+                for i, (_, _, bits) in enumerate(parts)
+            ]
+            keep = piece(False)
             return jnp.concatenate(
                 [
-                    tensor.scatter(lambda s, n, base=base: make(base + s, n), rows, bits)
-                    for base, rows, bits in halves(size)
+                    tensor.scatter(keep[i * half : (i + 1) * half] + got[i], half, bits[1:])
+                    for i, (_, _, bits) in enumerate(parts)
                 ],
                 axis=0,
             )
 
-        def gather_rows(value, size):
+        def gather_rows(value, size, after=None):
             quarter = size // 2 // tensor_size
             return jnp.concatenate(
                 [
-                    tensor.gather(value[i * quarter : (i + 1) * quarter], bits)
+                    tensor.gather(value[i * quarter : (i + 1) * quarter], bits, after)
                     for i, (_, _, bits) in enumerate(halves(size))
                 ],
                 axis=0,
             )
 
-        def rows_of(value, start, size):
-            return lax.dynamic_slice_in_dim(value, start, size, 0)
-
-        def core_sum(lefts, rights):
-            away = outer(lefts, rights, 1 - core, dp_size)
+        def rows_of(value, starts, size):
+            return jnp.concatenate(
+                [lax.dynamic_slice_in_dim(value, start, size, 0) for start in starts], axis=0
+            )
+
+        def core_sum(lefts, rights, part=(0, 1)):
+            away = outer(lefts, rights, 1 - core, dp_size, part=part)
             got = data.swap(away, 1)
-            return outer(lefts, rights, core, dp_size, add=got)
+            return outer(lefts, rights, core, dp_size, add=got, part=part)
 
         def z_scatter(value):
             return lax.psum_scatter(
@@ -336,7 +360,7 @@
         owners = jnp.broadcast_to(block_owner[:, None], (row_count // BLK, BLK)).reshape(-1)
         row_index = jnp.arange(row_count, dtype=jnp.int32)
         positions = (row_index // BLK + first_block - owners) * BLK + row_index % BLK
-        cosine, sine = rope_tables(positions, HD, min(256, head_cols))
+        cosine, sine = rope_tables(positions, min(128, head_cols))
 
         saved = []
         for lo, hi in bounds:
@@ -363,7 +387,8 @@
             x_own = own_rows(block_input[lo:hi]).astype(F32)
             hid = x_own + added
             inv_two = lax.rsqrt(jnp.mean(hid * hid, axis=-1, keepdims=True) + NORM_EPS)
-            unit = gather_rows(hid * inv_two, size)
+            after = saved[-1]["act_two"] if saved else None
+            unit = gather_rows(hid * inv_two, size, after)
             act_two = (unit * feedforward_gain).astype(BF16)
             saved.append(
                 dict(q=q, k=k, v=v, allowed=allowed, flat=flat, act=act, rows=rows, x_f=x_f,
@@ -374,21 +399,22 @@
         def chunks(key):
             return [s[key] for s in saved]
 
-        for (lo, hi), s in zip(bounds, saved):
+        for s in saved:
+            s["inner_grad"] = mm_nt(s["rows"], down_weight)
             s["gate_pre"] = mm(s["act_two"], gate_weight)
             s["up_pre"] = mm(s["act_two"], up_weight)
             s["sig"] = jax.nn.sigmoid(s["gate_pre"])
             s["inner"] = (s["gate_pre"] * s["sig"] * s["up_pre"]).astype(BF16)
-        down_part = core_sum(chunks("rows"), chunks("inner"))
-        down_sum = z_scatter(down_part).T
+        down_parts = [core_sum(chunks("rows"), chunks("inner"), (i, 2)) for i in range(2)]
+        down_sums = [z_scatter(v) for v in down_parts]
 
         gain_parts = jnp.zeros((width,), F32)
-        for (lo, hi), s in zip(bounds, saved):
+        for index, ((lo, hi), s) in enumerate(zip(bounds, saved)):
             size = hi - lo
             rows = s["rows"]
-            inner_grad = mm_nt(rows, down_weight)
+            inner_grad = s["inner_grad"]
             gate_pre, up_pre, sig = s["gate_pre"], s["up_pre"], s["sig"]
-            gate_pre, up_pre, _ = lax.optimization_barrier((gate_pre, up_pre, down_part))
+            gate_pre, up_pre, _ = lax.optimization_barrier((gate_pre, up_pre, down_parts))
             gate_back = (inner_grad * up_pre * sig * (1.0 + gate_pre * (1.0 - sig))).astype(BF16)
             up_back = (inner_grad * gate_pre * sig).astype(BF16)
             s["gate_back"], s["up_back"] = gate_back, up_back
@@ -405,7 +431,9 @@
                 scaled - unit * jnp.mean(scaled * unit, axis=-1, keepdims=True)
             )
             s["hidden_grad"] = own_rows(rows).astype(F32) + back
-            s["hidden_back"] = (rows.astype(F32) + gather_rows(back, size)).astype(BF16)
+            after = saved[index - 1]["hidden_back"] if index else None
+            full = gather_rows(back, size, after)
+            s["hidden_back"] = (rows.astype(F32) + full).astype(BF16)
 
         gate_part = core_sum(chunks("act_two"), chunks("gate_back"))
         gate_sum = z_scatter(gate_part)
@@ -415,7 +443,7 @@
         outs = []
         for (lo, hi), s in zip(bounds, saved):
             size = hi - lo
-            late_inner, _ = lax.optimization_barrier((s["inner"], saved[-1]["part"]))
+            late_inner, _ = lax.optimization_barrier((s["inner"], saved[-1]["hidden_back"]))
             mlp = scatter_rows(
                 lambda st, n, a=late_inner: mm(rows_of(a, st, n), down_weight), size
             )
@@ -429,7 +457,7 @@
             size = hi - lo
             back3 = attend_back(
                 s["hidden_back"], output_weight, s["q"], s["k"], s["v"], s["flat"],
-                s["cos"], s["sin"], s["allowed"], (down_part, gate_part, up_part),
+                s["cos"], s["sin"], s["allowed"], (gate_part, up_part),
             )
             s["qkv_back"] = back3
             q_back, k_back, v_back = back3[0], back3[1], back3[2]
@@ -449,7 +477,10 @@
         input_gradient = jnp.concatenate(input_grads, axis=0)
 
         out_sum = z_scatter(core_sum(chunks("hidden_back"), chunks("flat"))).T
-        qkv_sum = z_scatter(core_sum(chunks("act"), chunks("qkv_back")))
+        qkv_part = core_sum(chunks("act"), chunks("qkv_back"))
+        qkv_sum = z_scatter(qkv_part)
+        down_sums, _ = lax.optimization_barrier((down_sums, qkv_part))
+        down_sum = jnp.concatenate([v.T for v in down_sums], axis=0)
         query_sum = qkv_sum[:, :head_cols]
         key_sum = qkv_sum[:, head_cols : 2 * head_cols]
         value_sum = qkv_sum[:, 2 * head_cols :]

time: 1090 us -> 1060 us (0.972)
  matrix products: 166 us -> 122 us
  waiting for transfers between devices: 538 us -> 571 us
  Pallas kernels: 175 us -> 157 us
  local copies, waits for them, and re-layouts: 35.1 us -> 46.9 us
    dot_general x42 -> x22, matrix products: 112 us -> 74.3 us  [mm_nt(): lax.dot_general(a, b, (((1,), (1,)), ((), ())), preferred_element_type=F32)]
    reduce_scatter x5 -> x6, waiting for transfers between devices: 153 us -> 179 us  [z_scatter(): lax.psum_scatter(value, 'dp', scatter_dimension=0, tiled=True, axis_index...]
    pallas_call x10 -> x12, Pallas kernels: 114 us -> 96.9 us  [outer(): pl.pallas_call(functools.partial(outer_body, count, add is not None), gri...]
    ppermute x74 -> x75, starting transfers between devices: 85.7 us -> 76 us  [swap(): lax.ppermute(value, self.axis, [(i, i ^ bit) for i in range(self.size)])]
    dot_general x20 -> x12, matrix products: 54.6 us -> 47.2 us  [mm(): return jnp.dot(a, b, preferred_element_type=F32)]
    ppermute x74 -> x75, waiting for transfers between devices: 384 us -> 391 us  [swap(): lax.ppermute(value, self.axis, [(i, i ^ bit) for i in range(self.size)])]
  transfers between devices with their start and end apart: 79 -> 81, of which waited for: 45 -> 50; matrix products, arithmetic and copies ran while one was open for 15% -> 15% of each run, Pallas kernels for 12% -> 11%
where the time goes in v2:
time: 1060 us
  waiting for transfers between devices  571 us (54%)
  Pallas kernels  157 us (15%)
  matrix products  122 us (12%)
  starting transfers between devices  76.4 us (7%)
  other arithmetic  69.2 us (7%)
  local copies, waits for them, and re-layouts  46.9 us (4%)
  between operations  16.3 us (2%)
    ppermute x75, waiting for transfers between devices, swap(): lax.ppermute(value, self.axis, [(i, i ^ bit) for i in range(self.size)])  391 us
    reduce_scatter x6, waiting for transfers between devices, z_scatter(): lax.psum_scatter(value, 'dp', scatter_dimension=0, tiled=True, axis_index...  179 us
    pallas_call x12, Pallas kernels, outer(): pl.pallas_call(functools.partial(outer_body, count, add is not None), gri...  96.9 us
    ppermute x75, starting transfers between devices, swap(): lax.ppermute(value, self.axis, [(i, i ^ bit) for i in range(self.size)])  76 us
    dot_general x22, matrix products, mm_nt(): lax.dot_general(a, b, (((1,), (1,)), ((), ())), preferred_element_type=F32)  74.3 us
    dot_general x12, matrix products, mm(): return jnp.dot(a, b, preferred_element_type=F32)  47.2 us
    pallas_call x2, Pallas kernels, attend_back(): pl.pallas_call(attend_back_body, grid=(cols // step,), in_specs=[whole((r...  33.6 us
    pallas_call x2, Pallas kernels, attend(): pl.pallas_call(attend_body, grid=(cols // step,), in_specs=[whole((rows,...  26.8 us
  transfers between devices with their start and end apart: 81, of which 50 were waited for; matrix products, arithmetic and copies ran while one was open for 15% of the time, Pallas kernels for 11%

profile of v2, /device:TPU:0, one launch (start us, length us, event | category | flops | bytes accessed | tf_op | source)
XLA Modules:
  0.0 1058.3 jit_solution(17858674198291335400)
XLA Ops:
  21.1 13.3 %attend.2 = (bf16[512,512]{1,0:T(8,128)(2,1)}, bf16[512,512]{1,0:T(8,128)(2,1)}, bf16[512,512]{1,0:T(8,128)(2,1)}, bf16[512,512]{1,0:T(8,128)(2,1)}) custom-call(bf16[512,2048]{1,0:T(8,128)(2,1)} %get-tuple-element.94.act.refs_0_, bf16[2048,512]{1,0:T(8,128)(2,1)} %wq.3, bf16[2048,512]{1,0:T(8,128)(2,1)} %wk.3, bf16[2048,512]{1,0:T(8,128)(2,1)} %wv.3, ...), custom_call_target="tpu_custom_call" | custom-call | flops 5368709120 | bytes 10485760 | tf_op jit(solution)/shard_map/attend/pallas_call | solution.py:96
  42.1 13.5 %attend.3 = (bf16[512,512]{1,0:T(8,128)(2,1)}, bf16[512,512]{1,0:T(8,128)(2,1)}, bf16[512,512]{1,0:T(8,128)(2,1)}, bf16[512,512]{1,0:T(8,128)(2,1)}) custom-call(bf16[512,2048]{1,0:T(8,128)(2,1)} %get-tuple-element.95.act.refs_1_, bf16[2048,512]{1,0:T(8,128)(2,1)} %wq.3, bf16[2048,512]{1,0:T(8,128)(2,1)} %wk.3, bf16[2048,512]{1,0:T(8,128)(2,1)} %wv.3, ...), custom_call_target="tpu_custom_call" | custom-call | flops 5368709120 | bytes 10485760 | tf_op jit(solution)/shard_map/attend/pallas_call | solution.py:96
  60.2 4.8 fusion.180
  74.4 12.9 %collective-permute-done.8 = f32[128,2048]{1,0:T(8,128)} collective-permute-done((f32[128,2048]{1,0:T(8,128)}, f32[128,2048]{1,0:T(8,128)}, u32[]{:S(2)}, u32[]{:S(2)}) %collective-permute-start.8) | collective-permute-done | bytes 1048608 | tf_op jit(solution)/shard_map/ppermute | solution.py:223
  93.5 5.0 collective-permute-done.3
  101.4 7.5 collective-permute-done.11
  117.3 9.0 collective-permute-done.6
  131.1 6.6 collective-permute-done.14
  143.4 17.4 %collective-permute-done.7 = f32[128,2048]{1,0:T(8,128)} collective-permute-done((f32[128,2048]{1,0:T(8,128)S(1)}, f32[128,2048]{1,0:T(8,128)}, u32[]{:S(2)}, u32[]{:S(2)}) %collective-permute-start.7) | collective-permute-done | bytes 1048608 | tf_op jit(solution)/shard_map/ppermute | solution.py:223
  165.1 15.9 %collective-permute-done.15 = f32[128,2048]{1,0:T(8,128)S(1)} collective-permute-done((f32[128,2048]{1,0:T(8,128)S(1)}, f32[128,2048]{1,0:T(8,128)S(1)}, u32[]{:S(2)}, u32[]{:S(2)}) %collective-permute-start.15) | collective-permute-done | bytes 1048608 | tf_op jit(solution)/shard_map/ppermute | solution.py:223
  180.9 4.5 fusion.205
  186.6 4.5 fusion.207
  191.2 12.0 %multiply_convert_fusion.5 = (bf16[512,2048]{1,0:T(8,128)(2,1)}, f32[512,2048]{1,0:T(8,128)}) fusion(f32[512,2048]{1,0:T(8,128)S(1)} %fusion.205, bf16[512,2048]{1,0:T(8,128)(2,1)S(1)} %fusion.8.refs_0_, bf16[2048,2048]{1,0:T(8,128)(2,1)} %param.23), kind=kOutput, calls=%fused_computation.30 | convolution fusion | flops 4301258752 | bytes 20971520 | tf_op jit(solution)/shard_map/dot_general | solution.py:26
  203.1 6.9 multiply_convert_fusion.4
  210.0 6.4 shard_map.212
  216.4 6.6 shard_map.214
  223.3 9.6 fusion.206
  233.0 9.4 fusion.208
  242.4 7.4 shard_map.213
  249.8 7.3 shard_map.215
  257.1 6.0 multiply_convert_fusion.2
  265.3 5.7 fusion.37
  271.1 5.9 convolution_add_fusion.10
  285.4 5.7 fusion.51
  291.2 5.7 convolution_add_fusion.8
  299.1 5.7 fusion.30
  304.8 5.8 convolution_add_fusion.11
  310.6 5.7 fusion.44
  316.4 6.0 convolution_add_fusion.9
  329.5 8.0 collective-permute-done.21
  338.4 9.0 collective-permute-done.27
  351.9 10.7 %collective-permute-done.30 = f32[64,2048]{1,0:T(8,128)S(1)} collective-permute-done((f32[64,2048]{1,0:T(8,128)S(1)}, f32[64,2048]{1,0:T(8,128)S(1)}, u32[]{:S(2)}, u32[]{:S(2)}) %collective-permute-start.30) | collective-permute-done | bytes 524320 | tf_op jit(solution)/shard_map/ppermute | solution.py:223
  367.1 12.0 %collective-permute-done.32 = f32[64,2048]{1,0:T(8,128)S(1)} collective-permute-done((f32[64,2048]{1,0:T(8,128)S(1)}, f32[64,2048]{1,0:T(8,128)S(1)}, u32[]{:S(2)}, u32[]{:S(2)}) %collective-permute-start.32) | collective-permute-done | bytes 524320 | tf_op jit(solution)/shard_map/ppermute | solution.py:223
  379.8 20.1 %collective-permute-done.22 = f32[64,2048]{1,0:T(8,128)S(1)} collective-permute-done((f32[64,2048]{1,0:T(8,128)S(1)}, f32[64,2048]{1,0:T(8,128)S(1)}, u32[]{:S(2)}, u32[]{:S(2)}) %collective-permute-start.22) | collective-permute-done | bytes 524320 | tf_op jit(solution)/shard_map/ppermute | solution.py:223
  404.8 14.9 %collective-permute-done.33 = f32[128,2048]{1,0:T(8,128)S(1)} collective-permute-done((f32[128,2048]{1,0:T(8,128)S(1)}, f32[128,2048]{1,0:T(8,128)S(1)}, u32[]{:S(2)}, u32[]{:S(2)}) %collective-permute-start.33) | collective-permute-done | bytes 1048608 | tf_op jit(solution)/shard_map/ppermute | solution.py:223
  424.8 5.0 shard_map.222
  434.3 5.4 shard_map.223
  439.8 9.2 shard_map.216
  449.2 9.2 shard_map.218
  462.6 11.8 %shard_map.217.rest_0_ = f32[1024,2048]{1,0:T(8,128)} custom-call(s32[1]{0:T(128)} %bitcast.3.which, bf16[512,2048]{1,0:T(8,128)(2,1)} %copy-done.7, bf16[512,2048]{1,0:T(8,128)(2,1)} %copy-done.8, bf16[512,2048]{1,0:T(8,128)(2,1)} %copy-done.15, bf16[512,2048]{1,0:T(8,128)(2,1)} %copy-done.13, f32[1024,2048]{1,0:T(8,128)} %collective-permute-done.50.refs_4_), custom_call_target="tpu_custom_call" | custom-call | flops 4294967296 | bytes 14680064 | tf_op jit(solution)/shard_map/pallas_call | solution.py:198
  474.6 11.5 %shard_map.219.rest_1_ = f32[1024,2048]{1,0:T(8,128)} custom-call(s32[1]{0:T(128)} %bitcast.3.which, bf16[512,2048]{1,0:T(8,128)(2,1)} %copy-done.7, bf16[512,2048]{1,0:T(8,128)(2,1)} %copy-done.8, bf16[512,2048]{1,0:T(8,128)(2,1)} %copy-done.14, bf16[512,2048]{1,0:T(8,128)(2,1)} %copy-done.12, f32[1024,2048]{1,0:T(8,128)} %collective-permute-done.51.refs_4_), custom_call_target="tpu_custom_call" | custom-call | flops 4294967296 | bytes 14680064 | tf_op jit(solution)/shard_map/pallas_call | solution.py:198
  486.1 16.6 %attend_back.3.refs_3_ = bf16[3,512,512]{2,1,0:T(8,128)(2,1)} custom-call(bf16[512,2048]{1,0:T(8,128)(2,1)} %fusion.11.hidden.refs_1_, bf16[512,2048]{1,0:T(8,128)(2,1)} %wo.3, bf16[512,512]{1,0:T(8,128)(2,1)} %get-tuple-element.54.q_in, bf16[512,512]{1,0:T(8,128)(2,1)} %get-tuple-element.55.k_in, bf16[512,512]{1,0:T(8,128)(2,1)} %get-tuple-element.56.v_in, ...), custom_call_target="tpu_custom_call" | custom-call | flops 6442450944 | bytes 7864320 | tf_op jit(solution)/shard_map/attend_back/pallas_call | solution.py:140
  502.7 17.0 %attend_back.2.refs_2_ = bf16[3,512,512]{2,1,0:T(8,128)(2,1)} custom-call(bf16[512,2048]{1,0:T(8,128)(2,1)} %fusion.10.hidden.refs_0_, bf16[512,2048]{1,0:T(8,128)(2,1)} %wo.3, bf16[512,512]{1,0:T(8,128)(2,1)} %get-tuple-element.51.q_in, bf16[512,512]{1,0:T(8,128)(2,1)} %get-tuple-element.52.k_in, bf16[512,512]{1,0:T(8,128)(2,1)} %get-tuple-element.53.v_in, ...), custom_call_target="tpu_custom_call" | custom-call | flops 6442450944 | bytes 7864320 | tf_op jit(solution)/shard_map/attend_back/pallas_call | solution.py:140
  519.7 7.8 shard_map.220
  527.8 10.2 collective-permute-done.73.refs_4_
  538.0 9.5 shard_map.221
  551.8 5.7 fusion.70
  559.4 6.0 fusion.62
  573.2 10.7 %collective-permute-done.42 = f32[128,2048]{1,0:T(8,128)S(1)} collective-permute-done((f32[128,2048]{1,0:T(8,128)S(1)}, f32[128,2048]{1,0:T(8,128)S(1)}, u32[]{:S(2)}, u32[]{:S(2)}) %collective-permute-start.42) | collective-permute-done | bytes 1048608 | tf_op jit(solution)/shard_map/ppermute | solution.py:223
  587.2 19.2 %collective-permute-done.34 = f32[128,2048]{1,0:T(8,128)S(1)} collective-permute-done((f32[128,2048]{1,0:T(8,128)S(1)}, f32[128,2048]{1,0:T(8,128)S(1)}, u32[]{:S(2)}, u32[]{:S(2)}) %collective-permute-start.34) | collective-permute-done | bytes 1048608 | tf_op jit(solution)/shard_map/ppermute | solution.py:223
  609.6 8.0 collective-permute-done.45
  620.7 8.1 collective-permute-done.37
  633.6 6.5 collective-permute-done.48
  644.4 7.1 collective-permute-done.40
  655.3 19.4 %collective-permute-done.49 = f32[128,2048]{1,0:T(8,128)S(1)} collective-permute-done((f32[128,2048]{1,0:T(8,128)S(1)}, f32[128,2048]{1,0:T(8,128)S(1)}, u32[]{:S(2)}, u32[]{:S(2)}) %collective-permute-start.49) | collective-permute-done | bytes 1048608 | tf_op jit(solution)/shard_map/ppermute | solution.py:223
  675.1 20.9 %collective-permute-done.41 = f32[128,2048]{1,0:T(8,128)S(1)} collective-permute-done((f32[128,2048]{1,0:T(8,128)S(1)}, f32[128,2048]{1,0:T(8,128)S(1)}, u32[]{:S(2)}, u32[]{:S(2)}) %collective-permute-start.41) | collective-permute-done | bytes 1048608 | tf_op jit(solution)/shard_map/ppermute | solution.py:223
  719.6 35.2 %collective-permute-done.52 = f32[128,2048]{1,0:T(8,128)S(1)} collective-permute-done((f32[128,2048]{1,0:T(8,128)S(1)}, f32[128,2048]{1,0:T(8,128)S(1)}, u32[]{:S(2)}, u32[]{:S(2)}) %collective-permute-start.52) | collective-permute-done | bytes 1048608 | tf_op jit(solution)/shard_map/ppermute | solution.py:223
  761.2 10.1 collective-permute-done.55
  772.5 7.2 collective-permute-done.63
  810.7 6.7 collective-permute-done.64
  818.7 21.2 %collective-permute-done.59 = f32[128,2048]{1,0:T(8,128)S(1)} collective-permute-done((f32[128,2048]{1,0:T(8,128)S(1)}, f32[128,2048]{1,0:T(8,128)S(1)}, u32[]{:S(2)}, u32[]{:S(2)}) %collective-permute-start.59) | collective-permute-done | bytes 1048608 | tf_op jit(solution)/shard_map/ppermute | solution.py:223
  840.3 21.3 %collective-permute-done.67 = f32[128,2048]{1,0:T(8,128)S(1)} collective-permute-done((f32[128,2048]{1,0:T(8,128)S(1)}, f32[128,2048]{1,0:T(8,128)S(1)}, u32[]{:S(2)}, u32[]{:S(2)}) %collective-permute-start.67) | collective-permute-done | bytes 1048608 | tf_op jit(solution)/shard_map/ppermute | solution.py:223
  872.1 31.1 %reduce-scatter.11.cloned.1.call-done = f32[256,2048]{1,0:T(8,128)} async-done(((f32[1024,2048]{1,0:T(8,128)}), f32[256,2048]{1,0:T(8,128)}) %reduce-scatter.11.cloned.1.call-update) | async-done | bytes 2097168 | tf_op jit(solution)/shard_map/reduce_scatter | solution.py:355
  903.1 148.0 %reduce-scatter.13.cloned.1.call-done = f32[256,2048]{1,0:T(8,128)} async-done(((f32[1024,2048]{1,0:T(8,128)}), f32[256,2048]{1,0:T(8,128)}) %reduce-scatter.13.cloned.1.call-update) | async-done | bytes 2097168 | tf_op jit(solution)/shard_map/reduce_scatter | solution.py:355
  (454 shorter events, 228.8 us)
Async XLA Ops:
  7.2 788.8 %reduce-scatter.9.cloned.1.call-start = ((), (), s32[]{:S(2)}) async-start(), calls=%async_computation.7 | async-start | bytes 2621440 | tf_op jit(solution)/shard_map/reduce_scatter | solution.py:355
  37.6 31.5 %collective-permute-start = (f32[128,2048]{1,0:T(8,128)}, f32[128,2048]{1,0:T(8,128)S(1)}, u32[]{:S(2)}, u32[]{:S(2)}) collective-permute-start(f32[128,2048]{1,0:T(8,128)} %get-tuple-element.158), channel_id=1, source_target_pairs={{0,1},{1,0},{2,3},{3,2},{4,5},{5,4},{6,7},{7,6},{8,9},{9,8},{10,11... | collective-permute-start | bytes 3145736 | tf_op jit(solution)/shard_map/ppermute | solution.py:223
  40.6 28.6 %collective-permute-start.2 = (f32[128,2048]{1,0:T(8,128)}, f32[128,2048]{1,0:T(8,128)}, u32[]{:S(2)}, u32[]{:S(2)}) collective-permute-start(f32[128,2048]{1,0:T(8,128)} %get-tuple-element.159), channel_id=1, source_target_pairs={{0,2},{1,3},{2,0},{3,1},{4,6},{5,7},{6,4},{7,5},{8,10},{9,11},{10,... | collective-permute-start | bytes 3145736 | tf_op jit(solution)/shard_map/ppermute | solution.py:223
  59.7 27.7 %collective-permute-start.8 = (f32[128,2048]{1,0:T(8,128)}, f32[128,2048]{1,0:T(8,128)}, u32[]{:S(2)}, u32[]{:S(2)}) collective-permute-start(f32[128,2048]{1,0:T(8,128)} %get-tuple-element.164), channel_id=1, source_target_pairs={{0,1},{1,0},{2,3},{3,2},{4,5},{5,4},{6,7},{7,6},{8,9},{9,8},{10,11... | collective-permute-start | bytes 3145736 | tf_op jit(solution)/shard_map/ppermute | solution.py:223
  60.2 29.2 %collective-permute-start.10 = (f32[128,2048]{1,0:T(8,128)}, f32[128,2048]{1,0:T(8,128)}, u32[]{:S(2)}, u32[]{:S(2)}) collective-permute-start(f32[128,2048]{1,0:T(8,128)} %get-tuple-element.165), channel_id=1, source_target_pairs={{0,2},{1,3},{2,0},{3,1},{4,6},{5,7},{6,4},{7,5},{8,10},{9,11},{10,... | collective-permute-start | bytes 3145736 | tf_op jit(solution)/shard_map/ppermute | solution.py:223
  70.8 27.7 %collective-permute-start.3 = (f32[64,2048]{1,0:T(8,128)S(1)}, f32[64,2048]{1,0:T(8,128)S(1)}, u32[]{:S(2)}, u32[]{:S(2)}) collective-permute-start(f32[64,2048]{1,0:T(8,128)S(1)} %constant_dynamic-slice_fusion.52), channel_id=1, source_target_pairs={{0,1},{1,0},{2,3},{3,2},{4,5},{5,4},{6,7},{7,6},{8,9},{9,8},{10,11... | collective-permute-start | bytes 1572872 | tf_op jit(solution)/shard_map/ppermute | solution.py:223
  72.9 27.7 %collective-permute-start.1 = (f32[64,2048]{1,0:T(8,128)S(1)}, f32[64,2048]{1,0:T(8,128)S(1)}, u32[]{:S(2)}, u32[]{:S(2)}) collective-permute-start(f32[64,2048]{1,0:T(8,128)S(1)} %constant_dynamic-slice_fusion.53), channel_id=1, source_target_pairs={{0,2},{1,3},{2,0},{3,1},{4,6},{5,7},{6,4},{7,5},{8,10},{9,11},{10,... | collective-permute-start | bytes 1572872 | tf_op jit(solution)/shard_map/ppermute | solution.py:223
  91.4 17.5 %collective-permute-start.11 = (f32[64,2048]{1,0:T(8,128)S(1)}, f32[64,2048]{1,0:T(8,128)S(1)}, u32[]{:S(2)}, u32[]{:S(2)}) collective-permute-start(f32[64,2048]{1,0:T(8,128)S(1)} %constant_dynamic-slice_fusion.42), channel_id=1, source_target_pairs={{0,1},{1,0},{2,3},{3,2},{4,5},{5,4},{6,7},{7,6},{8,9},{9,8},{10,11... | collective-permute-start | bytes 1572872 | tf_op jit(solution)/shard_map/ppermute | solution.py:223
  91.5 18.9 %collective-permute-start.9 = (f32[64,2048]{1,0:T(8,128)S(1)}, f32[64,2048]{1,0:T(8,128)S(1)}, u32[]{:S(2)}, u32[]{:S(2)}) collective-permute-start(f32[64,2048]{1,0:T(8,128)S(1)} %constant_dynamic-slice_fusion.43), channel_id=1, source_target_pairs={{0,2},{1,3},{2,0},{3,1},{4,6},{5,7},{6,4},{7,5},{8,10},{9,11},{10,... | collective-permute-start | bytes 1572872 | tf_op jit(solution)/shard_map/ppermute | solution.py:223
  112.2 15.9 %collective-permute-start.4 = (f32[64,2048]{1,0:T(8,128)S(1)}, f32[64,2048]{1,0:T(8,128)S(1)}, u32[]{:S(2)}, u32[]{:S(2)}) collective-permute-start(f32[64,2048]{1,0:T(8,128)S(1)} %get-tuple-element.189), channel_id=1, source_target_pairs={{0,2},{1,3},{2,0},{3,1},{4,6},{5,7},{6,4},{7,5},{8,10},{9,11},{10,... | collective-permute-start | bytes 1572872 | tf_op jit(solution)/shard_map/ppermute | solution.py:223
  115.0 26.1 %collective-permute-start.12 = (f32[64,2048]{1,0:T(8,128)}, f32[64,2048]{1,0:T(8,128)}, u32[]{:S(2)}, u32[]{:S(2)}) collective-permute-start(f32[64,2048]{1,0:T(8,128)} %get-tuple-element.187), channel_id=1, source_target_pairs={{0,2},{1,3},{2,0},{3,1},{4,6},{5,7},{6,4},{7,5},{8,10},{9,11},{10,... | collective-permute-start | bytes 1572872 | tf_op jit(solution)/shard_map/ppermute | solution.py:223
  115.9 21.9 %collective-permute-start.14 = (f32[64,2048]{1,0:T(8,128)}, f32[64,2048]{1,0:T(8,128)}, u32[]{:S(2)}, u32[]{:S(2)}) collective-permute-start(f32[64,2048]{1,0:T(8,128)} %get-tuple-element.188), channel_id=1, source_target_pairs={{0,1},{1,0},{2,3},{3,2},{4,5},{5,4},{6,7},{7,6},{8,9},{9,8},{10,11... | collective-permute-start | bytes 1572872 | tf_op jit(solution)/shard_map/ppermute | solution.py:223
  126.5 34.4 %collective-permute-start.7 = (f32[128,2048]{1,0:T(8,128)S(1)}, f32[128,2048]{1,0:T(8,128)}, u32[]{:S(2)}, u32[]{:S(2)}) collective-permute-start(f32[128,2048]{1,0:T(8,128)S(1)} %maximum_select_fusion.17), channel_id=1, source_target_pairs={{0,2},{1,3},{2,0},{3,1},{4,6},{5,7},{6,4},{7,5},{8,10},{9,11},{10,... | collective-permute-start | bytes 3145736 | tf_op jit(solution)/shard_map/ppermute | solution.py:223
  128.2 34.5 %collective-permute-start.5 = (f32[128,2048]{1,0:T(8,128)S(1)}, f32[128,2048]{1,0:T(8,128)}, u32[]{:S(2)}, u32[]{:S(2)}) collective-permute-start(f32[128,2048]{1,0:T(8,128)S(1)} %maximum_select_fusion.16), channel_id=1, source_target_pairs={{0,1},{1,0},{2,3},{3,2},{4,5},{5,4},{6,7},{7,6},{8,9},{9,8},{10,11... | collective-permute-start | bytes 3145736 | tf_op jit(solution)/shard_map/ppermute | solution.py:223
  139.4 41.5 %collective-permute-start.15 = (f32[128,2048]{1,0:T(8,128)S(1)}, f32[128,2048]{1,0:T(8,128)S(1)}, u32[]{:S(2)}, u32[]{:S(2)}) collective-permute-start(f32[128,2048]{1,0:T(8,128)S(1)} %maximum_select_fusion.19), channel_id=1, source_target_pairs={{0,2},{1,3},{2,0},{3,1},{4,6},{5,7},{6,4},{7,5},{8,10},{9,11},{10,... | collective-permute-start | bytes 3145736 | tf_op jit(solution)/shard_map/ppermute | solution.py:223
  142.8 38.1 %collective-permute-start.13 = (f32[128,2048]{1,0:T(8,128)S(1)}, f32[128,2048]{1,0:T(8,128)S(1)}, u32[]{:S(2)}, u32[]{:S(2)}) collective-permute-start(f32[128,2048]{1,0:T(8,128)S(1)} %maximum_select_fusion.18), channel_id=1, source_target_pairs={{0,1},{1,0},{2,3},{3,2},{4,5},{5,4},{6,7},{7,6},{8,9},{9,8},{10,11... | collective-permute-start | bytes 3145736 | tf_op jit(solution)/shard_map/ppermute | solution.py:223
  216.4 26.0 %collective-permute-start.16 = (f32[1024,1024]{1,0:T(8,128)}, f32[1024,1024]{1,0:T(8,128)}, u32[]{:S(2)}, u32[]{:S(2)}) collective-permute-start(f32[1024,1024]{1,0:T(8,128)} %shard_map.212), channel_id=1, source_target_pairs={{0,4},{4,0},{8,12},{12,8},{16,20},{20,16},{24,28},{28,24},{1,5},{5... | collective-permute-start | bytes 12582920 | tf_op jit(solution)/shard_map/ppermute | solution.py:223
  223.0 26.8 %collective-permute-start.17 = (f32[1024,1024]{1,0:T(8,128)}, f32[1024,1024]{1,0:T(8,128)}, u32[]{:S(2)}, u32[]{:S(2)}) collective-permute-start(f32[1024,1024]{1,0:T(8,128)} %shard_map.214), channel_id=1, source_target_pairs={{0,4},{4,0},{8,12},{12,8},{16,20},{20,16},{24,28},{28,24},{1,5},{5... | collective-permute-start | bytes 12582920 | tf_op jit(solution)/shard_map/ppermute | solution.py:223
  277.2 45.1 %collective-permute-start.18 = (f32[128,2048]{1,0:T(8,128)S(1)}, f32[128,2048]{1,0:T(8,128)S(1)}, u32[]{:S(2)}, u32[]{:S(2)}) collective-permute-start(f32[128,2048]{1,0:T(8,128)S(1)} %get-tuple-element.144), channel_id=1, source_target_pairs={{0,1},{1,0},{2,3},{3,2},{4,5},{5,4},{6,7},{7,6},{8,9},{9,8},{10,11... | collective-permute-start | bytes 3145736 | tf_op jit(solution)/shard_map/ppermute | solution.py:223
  278.6 43.7 %collective-permute-start.20 = (f32[128,2048]{1,0:T(8,128)S(1)}, f32[128,2048]{1,0:T(8,128)S(1)}, u32[]{:S(2)}, u32[]{:S(2)}) collective-permute-start(f32[128,2048]{1,0:T(8,128)S(1)} %get-tuple-element.145), channel_id=1, source_target_pairs={{0,2},{1,3},{2,0},{3,1},{4,6},{5,7},{6,4},{7,5},{8,10},{9,11},{10,... | collective-permute-start | bytes 3145736 | tf_op jit(solution)/shard_map/ppermute | solution.py:223
  297.2 27.9 %collective-permute-start.24 = (f32[128,2048]{1,0:T(8,128)S(1)}, f32[128,2048]{1,0:T(8,128)S(1)}, u32[]{:S(2)}, u32[]{:S(2)}) collective-permute-start(f32[128,2048]{1,0:T(8,128)S(1)} %get-tuple-element.132), channel_id=1, source_target_pairs={{0,1},{1,0},{2,3},{3,2},{4,5},{5,4},{6,7},{7,6},{8,9},{9,8},{10,11... | collective-permute-start | bytes 3145736 | tf_op jit(solution)/shard_map/ppermute | solution.py:223
  297.9 28.8 %collective-permute-start.26 = (f32[128,2048]{1,0:T(8,128)S(1)}, f32[128,2048]{1,0:T(8,128)S(1)}, u32[]{:S(2)}, u32[]{:S(2)}) collective-permute-start(f32[128,2048]{1,0:T(8,128)S(1)} %get-tuple-element.133), channel_id=1, source_target_pairs={{0,2},{1,3},{2,0},{3,1},{4,6},{5,7},{6,4},{7,5},{8,10},{9,11},{10,... | collective-permute-start | bytes 3145736 | tf_op jit(solution)/shard_map/ppermute | solution.py:223
  327.0 20.4 %collective-permute-start.27 = (f32[64,2048]{1,0:T(8,128)S(1)}, f32[64,2048]{1,0:T(8,128)S(1)}, u32[]{:S(2)}, u32[]{:S(2)}) collective-permute-start(f32[64,2048]{1,0:T(8,128)S(1)} %constant_dynamic-slice_fusion.22), channel_id=1, source_target_pairs={{0,1},{1,0},{2,3},{3,2},{4,5},{5,4},{6,7},{7,6},{8,9},{9,8},{10,11... | collective-permute-start | bytes 1572872 | tf_op jit(solution)/shard_map/ppermute | solution.py:223
  327.5 21.0 %collective-permute-start.25 = (f32[64,2048]{1,0:T(8,128)S(1)}, f32[64,2048]{1,0:T(8,128)S(1)}, u32[]{:S(2)}, u32[]{:S(2)}) collective-permute-start(f32[64,2048]{1,0:T(8,128)S(1)} %constant_dynamic-slice_fusion.23), channel_id=1, source_target_pairs={{0,2},{1,3},{2,0},{3,1},{4,6},{5,7},{6,4},{7,5},{8,10},{9,11},{10,... | collective-permute-start | bytes 1572872 | tf_op jit(solution)/shard_map/ppermute | solution.py:223
  362.7 38.2 %collective-permute-start.31 = (f32[128,2048]{1,0:T(8,128)S(1)}, f32[128,2048]{1,0:T(8,128)S(1)}, u32[]{:S(2)}, u32[]{:S(2)}) collective-permute-start(f32[128,2048]{1,0:T(8,128)S(1)} %maximum_select_fusion.22), channel_id=1, source_target_pairs={{0,2},{1,3},{2,0},{3,1},{4,6},{5,7},{6,4},{7,5},{8,10},{9,11},{10,... | collective-permute-start | bytes 3145736 | tf_op jit(solution)/shard_map/ppermute | solution.py:223
  365.0 35.0 %collective-permute-start.22 = (f32[64,2048]{1,0:T(8,128)S(1)}, f32[64,2048]{1,0:T(8,128)S(1)}, u32[]{:S(2)}, u32[]{:S(2)}) collective-permute-start(f32[64,2048]{1,0:T(8,128)S(1)} %get-tuple-element.183), channel_id=1, source_target_pairs={{0,2},{1,3},{2,0},{3,1},{4,6},{5,7},{6,4},{7,5},{8,10},{9,11},{10,... | collective-permute-start | bytes 1572872 | tf_op jit(solution)/shard_map/ppermute | solution.py:223
  365.7 35.4 %collective-permute-start.29 = (f32[128,2048]{1,0:T(8,128)S(1)}, f32[128,2048]{1,0:T(8,128)S(1)}, u32[]{:S(2)}, u32[]{:S(2)}) collective-permute-start(f32[128,2048]{1,0:T(8,128)S(1)} %maximum_select_fusion.21), channel_id=1, source_target_pairs={{0,1},{1,0},{2,3},{3,2},{4,5},{5,4},{6,7},{7,6},{8,9},{9,8},{10,11... | collective-permute-start | bytes 3145736 | tf_op jit(solution)/shard_map/ppermute | solution.py:223
  379.2 40.5 %collective-permute-start.33 = (f32[128,2048]{1,0:T(8,128)S(1)}, f32[128,2048]{1,0:T(8,128)S(1)}, u32[]{:S(2)}, u32[]{:S(2)}) collective-permute-start(f32[128,2048]{1,0:T(8,128)S(1)} %maximum_select_fusion.23), channel_id=1, source_target_pairs={{0,2},{1,3},{2,0},{3,1},{4,6},{5,7},{6,4},{7,5},{8,10},{9,11},{10,... | collective-permute-start | bytes 3145736 | tf_op jit(solution)/shard_map/ppermute | solution.py:223
  400.1 20.8 %collective-permute-start.23 = (f32[128,2048]{1,0:T(8,128)S(1)}, f32[128,2048]{1,0:T(8,128)S(1)}, u32[]{:S(2)}, u32[]{:S(2)}) collective-permute-start(f32[128,2048]{1,0:T(8,128)S(1)} %maximum_select_fusion.20), channel_id=1, source_target_pairs={{0,1},{1,0},{2,3},{3,2},{4,5},{5,4},{6,7},{7,6},{8,9},{9,8},{10,11... | collective-permute-start | bytes 3145736 | tf_op jit(solution)/shard_map/ppermute | solution.py:223
  439.7 426.3 %reduce-scatter.15.cloned.1.call-start = ((), (), s32[]{:S(2)}) async-start(), calls=%async_computation.10 | async-start | bytes 5242880 | tf_op jit(solution)/shard_map/reduce_scatter | solution.py:355
  449.0 417.1 %reduce-scatter.17.cloned.1.call-start = ((), (), s32[]{:S(2)}) async-start(), calls=%async_computation.11 | async-start | bytes 5242880 | tf_op jit(solution)/shard_map/reduce_scatter | solution.py:355
  458.4 16.2 %collective-permute-start.51 = (f32[1024,2048]{1,0:T(8,128)}, f32[1024,2048]{1,0:T(8,128)}, u32[]{:S(2)}, u32[]{:S(2)}) collective-permute-start(f32[1024,2048]{1,0:T(8,128)} %shard_map.218), channel_id=1, source_target_pairs={{0,4},{4,0},{8,12},{12,8},{16,20},{20,16},{24,28},{28,24},{1,5},{5... | collective-permute-start | bytes 25165832 | tf_op jit(solution)/shard_map/ppermute | solution.py:223
  458.8 410.8 %reduce-scatter.7.cloned.1.call-start = ((), (), s32[]{:S(2)}) async-start(), calls=%async_computation.6 | async-start | bytes 7864320 | tf_op jit(solution)/shard_map/reduce_scatter | solution.py:355
  547.5 355.6 %reduce-scatter.11.cloned.1.call-start = ((), (), s32[]{:S(2)}) async-start(), calls=%async_computation.8 | async-start | bytes 10485760 | tf_op jit(solution)/shard_map/reduce_scatter | solution.py:355
  548.1 503.0 %reduce-scatter.13.cloned.1.call-start = ((), (), s32[]{:S(2)}) async-start(), calls=%async_computation.9 | async-start | bytes 10485760 | tf_op jit(solution)/shard_map/reduce_scatter | solution.py:355
  557.8 26.1 %collective-permute-start.42 = (f32[128,2048]{1,0:T(8,128)S(1)}, f32[128,2048]{1,0:T(8,128)S(1)}, u32[]{:S(2)}, u32[]{:S(2)}) collective-permute-start(f32[128,2048]{1,0:T(8,128)S(1)} %get-tuple-element.124), channel_id=1, source_target_pairs={{0,1},{1,0},{2,3},{3,2},{4,5},{5,4},{6,7},{7,6},{8,9},{9,8},{10,11... | collective-permute-start | bytes 3145736 | tf_op jit(solution)/shard_map/ppermute | solution.py:223
  558.8 26.0 %collective-permute-start.44 = (f32[128,2048]{1,0:T(8,128)S(1)}, f32[128,2048]{1,0:T(8,128)S(1)}, u32[]{:S(2)}, u32[]{:S(2)}) collective-permute-start(f32[128,2048]{1,0:T(8,128)S(1)} %get-tuple-element.125), channel_id=1, source_target_pairs={{0,2},{1,3},{2,0},{3,1},{4,6},{5,7},{6,4},{7,5},{8,10},{9,11},{10,... | collective-permute-start | bytes 3145736 | tf_op jit(solution)/shard_map/ppermute | solution.py:223
  565.7 40.7 %collective-permute-start.34 = (f32[128,2048]{1,0:T(8,128)S(1)}, f32[128,2048]{1,0:T(8,128)S(1)}, u32[]{:S(2)}, u32[]{:S(2)}) collective-permute-start(f32[128,2048]{1,0:T(8,128)S(1)} %get-tuple-element.116), channel_id=1, source_target_pairs={{0,1},{1,0},{2,3},{3,2},{4,5},{5,4},{6,7},{7,6},{8,9},{9,8},{10,11... | collective-permute-start | bytes 3145736 | tf_op jit(solution)/shard_map/ppermute | solution.py:223
  567.1 40.2 %collective-permute-start.36 = (f32[128,2048]{1,0:T(8,128)S(1)}, f32[128,2048]{1,0:T(8,128)S(1)}, u32[]{:S(2)}, u32[]{:S(2)}) collective-permute-start(f32[128,2048]{1,0:T(8,128)S(1)} %get-tuple-element.117), channel_id=1, source_target_pairs={{0,2},{1,3},{2,0},{3,1},{4,6},{5,7},{6,4},{7,5},{8,10},{9,11},{10,... | collective-permute-start | bytes 3145736 | tf_op jit(solution)/shard_map/ppermute | solution.py:223
  585.2 32.4 %collective-permute-start.45 = (f32[64,2048]{1,0:T(8,128)S(1)}, f32[64,2048]{1,0:T(8,128)S(1)}, u32[]{:S(2)}, u32[]{:S(2)}) collective-permute-start(f32[64,2048]{1,0:T(8,128)S(1)} %constant_dynamic-slice_fusion.10), channel_id=1, source_target_pairs={{0,1},{1,0},{2,3},{3,2},{4,5},{5,4},{6,7},{7,6},{8,9},{9,8},{10,11... | collective-permute-start | bytes 1572872 | tf_op jit(solution)/shard_map/ppermute | solution.py:223
  586.4 32.1 %collective-permute-start.43 = (f32[64,2048]{1,0:T(8,128)S(1)}, f32[64,2048]{1,0:T(8,128)S(1)}, u32[]{:S(2)}, u32[]{:S(2)}) collective-permute-start(f32[64,2048]{1,0:T(8,128)S(1)} %constant_dynamic-slice_fusion.11), channel_id=1, source_target_pairs={{0,2},{1,3},{2,0},{3,1},{4,6},{5,7},{6,4},{7,5},{8,10},{9,11},{10,... | collective-permute-start | bytes 1572872 | tf_op jit(solution)/shard_map/ppermute | solution.py:223
  607.7 21.1 %collective-permute-start.37 = (f32[64,2048]{1,0:T(8,128)S(1)}, f32[64,2048]{1,0:T(8,128)S(1)}, u32[]{:S(2)}, u32[]{:S(2)}) collective-permute-start(f32[64,2048]{1,0:T(8,128)S(1)} %constant_dynamic-slice_fusion.16), channel_id=1, source_target_pairs={{0,1},{1,0},{2,3},{3,2},{4,5},{5,4},{6,7},{7,6},{8,9},{9,8},{10,11... | collective-permute-start | bytes 1572872 | tf_op jit(solution)/shard_map/ppermute | solution.py:223
  608.9 20.9 %collective-permute-start.35 = (f32[64,2048]{1,0:T(8,128)S(1)}, f32[64,2048]{1,0:T(8,128)S(1)}, u32[]{:S(2)}, u32[]{:S(2)}) collective-permute-start(f32[64,2048]{1,0:T(8,128)S(1)} %constant_dynamic-slice_fusion.17), channel_id=1, source_target_pairs={{0,2},{1,3},{2,0},{3,1},{4,6},{5,7},{6,4},{7,5},{8,10},{9,11},{10,... | collective-permute-start | bytes 1572872 | tf_op jit(solution)/shard_map/ppermute | solution.py:223
  618.8 23.5 %collective-permute-start.46 = (f32[64,2048]{1,0:T(8,128)S(1)}, f32[64,2048]{1,0:T(8,128)}, u32[]{:S(2)}, u32[]{:S(2)}) collective-permute-start(f32[64,2048]{1,0:T(8,128)S(1)} %get-tuple-element.181), channel_id=1, source_target_pairs={{0,2},{1,3},{2,0},{3,1},{4,6},{5,7},{6,4},{7,5},{8,10},{9,11},{10,... | collective-permute-start | bytes 1572872 | tf_op jit(solution)/shard_map/ppermute | solution.py:223
  619.4 20.8 %collective-permute-start.48 = (f32[64,2048]{1,0:T(8,128)S(1)}, f32[64,2048]{1,0:T(8,128)}, u32[]{:S(2)}, u32[]{:S(2)}) collective-permute-start(f32[64,2048]{1,0:T(8,128)S(1)} %get-tuple-element.182), channel_id=1, source_target_pairs={{0,1},{1,0},{2,3},{3,2},{4,5},{5,4},{6,7},{7,6},{8,9},{9,8},{10,11... | collective-permute-start | bytes 1572872 | tf_op jit(solution)/shard_map/ppermute | solution.py:223
  631.0 20.4 %collective-permute-start.40 = (f32[64,2048]{1,0:T(8,128)}, f32[64,2048]{1,0:T(8,128)}, u32[]{:S(2)}, u32[]{:S(2)}) collective-permute-start(f32[64,2048]{1,0:T(8,128)} %get-tuple-element.180), channel_id=1, source_target_pairs={{0,1},{1,0},{2,3},{3,2},{4,5},{5,4},{6,7},{7,6},{8,9},{9,8},{10,11... | collective-permute-start | bytes 1572872 | tf_op jit(solution)/shard_map/ppermute | solution.py:223
  632.9 21.2 %collective-permute-start.38 = (f32[64,2048]{1,0:T(8,128)}, f32[64,2048]{1,0:T(8,128)S(1)}, u32[]{:S(2)}, u32[]{:S(2)}) collective-permute-start(f32[64,2048]{1,0:T(8,128)} %get-tuple-element.179), channel_id=1, source_target_pairs={{0,2},{1,3},{2,0},{3,1},{4,6},{5,7},{6,4},{7,5},{8,10},{9,11},{10,... | collective-permute-start | bytes 1572872 | tf_op jit(solution)/shard_map/ppermute | solution.py:223
  641.5 33.1 %collective-permute-start.49 = (f32[128,2048]{1,0:T(8,128)S(1)}, f32[128,2048]{1,0:T(8,128)S(1)}, u32[]{:S(2)}, u32[]{:S(2)}) collective-permute-start(f32[128,2048]{1,0:T(8,128)S(1)} %maximum_select_fusion.27), channel_id=1, source_target_pairs={{0,2},{1,3},{2,0},{3,1},{4,6},{5,7},{6,4},{7,5},{8,10},{9,11},{10,... | collective-permute-start | bytes 3145736 | tf_op jit(solution)/shard_map/ppermute | solution.py:223
  643.6 31.3 %collective-permute-start.47 = (f32[128,2048]{1,0:T(8,128)S(1)}, f32[128,2048]{1,0:T(8,128)S(1)}, u32[]{:S(2)}, u32[]{:S(2)}) collective-permute-start(f32[128,2048]{1,0:T(8,128)S(1)} %maximum_select_fusion.26), channel_id=1, source_target_pairs={{0,1},{1,0},{2,3},{3,2},{4,5},{5,4},{6,7},{7,6},{8,9},{9,8},{10,11... | collective-permute-start | bytes 3145736 | tf_op jit(solution)/shard_map/ppermute | solution.py:223
  653.1 42.9 %collective-permute-start.41 = (f32[128,2048]{1,0:T(8,128)S(1)}, f32[128,2048]{1,0:T(8,128)S(1)}, u32[]{:S(2)}, u32[]{:S(2)}) collective-permute-start(f32[128,2048]{1,0:T(8,128)S(1)} %maximum_select_fusion.25), channel_id=1, source_target_pairs={{0,2},{1,3},{2,0},{3,1},{4,6},{5,7},{6,4},{7,5},{8,10},{9,11},{10,... | collective-permute-start | bytes 3145736 | tf_op jit(solution)/shard_map/ppermute | solution.py:223
  654.3 41.9 %collective-permute-start.39 = (f32[128,2048]{1,0:T(8,128)S(1)}, f32[128,2048]{1,0:T(8,128)S(1)}, u32[]{:S(2)}, u32[]{:S(2)}) collective-permute-start(f32[128,2048]{1,0:T(8,128)S(1)} %maximum_select_fusion.24), channel_id=1, source_target_pairs={{0,1},{1,0},{2,3},{3,2},{4,5},{5,4},{6,7},{7,6},{8,9},{9,8},{10,11... | collective-permute-start | bytes 3145736 | tf_op jit(solution)/shard_map/ppermute | solution.py:223
  708.2 49.7 %collective-permute-start.60 = (f32[128,2048]{1,0:T(8,128)S(1)}, f32[128,2048]{1,0:T(8,128)S(1)}, u32[]{:S(2)}, u32[]{:S(2)}) collective-permute-start(f32[128,2048]{1,0:T(8,128)S(1)} %get-tuple-element.112), channel_id=1, source_target_pairs={{0,1},{1,0},{2,3},{3,2},{4,5},{5,4},{6,7},{7,6},{8,9},{9,8},{10,11... | collective-permute-start | bytes 3145736 | tf_op jit(solution)/shard_map/ppermute | solution.py:223
  709.6 48.3 %collective-permute-start.62 = (f32[128,2048]{1,0:T(8,128)S(1)}, f32[128,2048]{1,0:T(8,128)S(1)}, u32[]{:S(2)}, u32[]{:S(2)}) collective-permute-start(f32[128,2048]{1,0:T(8,128)S(1)} %get-tuple-element.113), channel_id=1, source_target_pairs={{0,2},{1,3},{2,0},{3,1},{4,6},{5,7},{6,4},{7,5},{8,10},{9,11},{10,... | collective-permute-start | bytes 3145736 | tf_op jit(solution)/shard_map/ppermute | solution.py:223
  713.0 41.8 %collective-permute-start.52 = (f32[128,2048]{1,0:T(8,128)S(1)}, f32[128,2048]{1,0:T(8,128)S(1)}, u32[]{:S(2)}, u32[]{:S(2)}) collective-permute-start(f32[128,2048]{1,0:T(8,128)S(1)} %get-tuple-element.106), channel_id=1, source_target_pairs={{0,1},{1,0},{2,3},{3,2},{4,5},{5,4},{6,7},{7,6},{8,9},{9,8},{10,11... | collective-permute-start | bytes 3145736 | tf_op jit(solution)/shard_map/ppermute | solution.py:223
  713.7 42.3 %collective-permute-start.54 = (f32[128,2048]{1,0:T(8,128)S(1)}, f32[128,2048]{1,0:T(8,128)S(1)}, u32[]{:S(2)}, u32[]{:S(2)}) collective-permute-start(f32[128,2048]{1,0:T(8,128)S(1)} %get-tuple-element.107), channel_id=1, source_target_pairs={{0,2},{1,3},{2,0},{3,1},{4,6},{5,7},{6,4},{7,5},{8,10},{9,11},{10,... | collective-permute-start | bytes 3145736 | tf_op jit(solution)/shard_map/ppermute | solution.py:223
  758.3 21.4 %collective-permute-start.63 = (f32[64,2048]{1,0:T(8,128)S(1)}, f32[64,2048]{1,0:T(8,128)S(1)}, u32[]{:S(2)}, u32[]{:S(2)}) collective-permute-start(f32[64,2048]{1,0:T(8,128)S(1)} %constant_dynamic-slice_fusion.2), channel_id=1, source_target_pairs={{0,1},{1,0},{2,3},{3,2},{4,5},{5,4},{6,7},{7,6},{8,9},{9,8},{10,11... | collective-permute-start | bytes 1572872 | tf_op jit(solution)/shard_map/ppermute | solution.py:223
  759.7 20.4 %collective-permute-start.61 = (f32[64,2048]{1,0:T(8,128)S(1)}, f32[64,2048]{1,0:T(8,128)S(1)}, u32[]{:S(2)}, u32[]{:S(2)}) collective-permute-start(f32[64,2048]{1,0:T(8,128)S(1)} %constant_dynamic-slice_fusion.3), channel_id=1, source_target_pairs={{0,2},{1,3},{2,0},{3,1},{4,6},{5,7},{6,4},{7,5},{8,10},{9,11},{10,... | collective-permute-start | bytes 1572872 | tf_op jit(solution)/shard_map/ppermute | solution.py:223
  782.6 20.2 %collective-permute-start.58 = (f32[64,2048]{1,0:T(8,128)S(1)}, f32[64,2048]{1,0:T(8,128)}, u32[]{:S(2)}, u32[]{:S(2)}) collective-permute-start(f32[64,2048]{1,0:T(8,128)S(1)} %get-tuple-element.176), channel_id=1, source_target_pairs={{0,1},{1,0},{2,3},{3,2},{4,5},{5,4},{6,7},{7,6},{8,9},{9,8},{10,11... | collective-permute-start | bytes 1572872 | tf_op jit(solution)/shard_map/ppermute | solution.py:223
  789.9 18.3 %collective-permute-start.66 = (f32[64,2048]{1,0:T(8,128)}, f32[64,2048]{1,0:T(8,128)}, u32[]{:S(2)}, u32[]{:S(2)}) collective-permute-start(f32[64,2048]{1,0:T(8,128)} %get-tuple-element.178), channel_id=1, source_target_pairs={{0,1},{1,0},{2,3},{3,2},{4,5},{5,4},{6,7},{7,6},{8,9},{9,8},{10,11... | collective-permute-start | bytes 1572872 | tf_op jit(solution)/shard_map/ppermute | solution.py:223
  798.0 19.5 %collective-permute-start.64 = (f32[64,2048]{1,0:T(8,128)}, f32[64,2048]{1,0:T(8,128)S(1)}, u32[]{:S(2)}, u32[]{:S(2)}) collective-permute-start(f32[64,2048]{1,0:T(8,128)} %get-tuple-element.177), channel_id=1, source_target_pairs={{0,2},{1,3},{2,0},{3,1},{4,6},{5,7},{6,4},{7,5},{8,10},{9,11},{10,... | collective-permute-start | bytes 1572872 | tf_op jit(solution)/shard_map/ppermute | solution.py:223
  804.1 35.8 %collective-permute-start.59 = (f32[128,2048]{1,0:T(8,128)S(1)}, f32[128,2048]{1,0:T(8,128)S(1)}, u32[]{:S(2)}, u32[]{:S(2)}) collective-permute-start(f32[128,2048]{1,0:T(8,128)S(1)} %maximum_select_fusion.29), channel_id=1, source_target_pairs={{0,2},{1,3},{2,0},{3,1},{4,6},{5,7},{6,4},{7,5},{8,10},{9,11},{10,... | collective-permute-start | bytes 3145736 | tf_op jit(solution)/shard_map/ppermute | solution.py:223
  807.6 32.5 %collective-permute-start.57 = (f32[128,2048]{1,0:T(8,128)S(1)}, f32[128,2048]{1,0:T(8,128)S(1)}, u32[]{:S(2)}, u32[]{:S(2)}) collective-permute-start(f32[128,2048]{1,0:T(8,128)S(1)} %maximum_select_fusion.28), channel_id=1, source_target_pairs={{0,1},{1,0},{2,3},{3,2},{4,5},{5,4},{6,7},{7,6},{8,9},{9,8},{10,11... | collective-permute-start | bytes 3145736 | tf_op jit(solution)/shard_map/ppermute | solution.py:223
  809.9 51.7 %collective-permute-start.67 = (f32[128,2048]{1,0:T(8,128)S(1)}, f32[128,2048]{1,0:T(8,128)S(1)}, u32[]{:S(2)}, u32[]{:S(2)}) collective-permute-start(f32[128,2048]{1,0:T(8,128)S(1)} %maximum_select_fusion.31), channel_id=1, source_target_pairs={{0,2},{1,3},{2,0},{3,1},{4,6},{5,7},{6,4},{7,5},{8,10},{9,11},{10,... | collective-permute-start | bytes 3145736 | tf_op jit(solution)/shard_map/ppermute | solution.py:223
  817.5 44.3 %collective-permute-start.65 = (f32[128,2048]{1,0:T(8,128)S(1)}, f32[128,2048]{1,0:T(8,128)S(1)}, u32[]{:S(2)}, u32[]{:S(2)}) collective-permute-start(f32[128,2048]{1,0:T(8,128)S(1)} %maximum_select_fusion.30), channel_id=1, source_target_pairs={{0,1},{1,0},{2,3},{3,2},{4,5},{5,4},{6,7},{7,6},{8,9},{9,8},{10,11... | collective-permute-start | bytes 3145736 | tf_op jit(solution)/shard_map/ppermute | solution.py:223
  (83 other events, 900.7 us)
Sparse Core Ops, SparseCore 0:
  439.8 43.2 reduce-scatter.8
  485.4 75.9 reduce-scatter.14
  563.7 77.3 reduce-scatter.16
  643.3 111.2 reduce-scatter.6
  757.3 145.7 reduce-scatter.10
  905.9 145.1 reduce-scatter.12

commit v3 on v2

--- a/solution.py
+++ b/solution.py
@@ -67,8 +67,14 @@
     return raised * (1.0 / jnp.sum(raised, axis=-1, keepdims=True))
 
 
-def attend_body(act, wq, wk, wv, cos, sin, mask, q_out, k_out, v_out, attn_out):
-    rows = act[...]
+def attend_body(x, gain, wq, wk, wv, cos, sin, mask, act_out, q_out, k_out, v_out, attn_out):
+    @pl.when(pl.program_id(0) == 0)
+    def _():
+        values = x[...].astype(F32)
+        inverse = lax.rsqrt(jnp.mean(values * values, axis=-1, keepdims=True) + NORM_EPS)
+        act_out[...] = (values * inverse * gain[...]).astype(BF16)
+
+    rows = act_out[...]
     cosine = widen(cos[...], wq.shape[1])
     sine = widen(sin[...], wq.shape[1])
     q = turn(mm(rows, wq[...]), cosine, sine).astype(BF16)
@@ -77,17 +83,21 @@
     q_out[...] = q
     k_out[...] = k
     v_out[...] = v
-    allowed = mask[...]
-    outs = []
-    for h in range(q.shape[1] // HD):
-        at = slice(h * HD, (h + 1) * HD)
-        probs = head_probs(q[:, at], k[:, at], allowed)
-        outs.append(mm(probs.astype(BF16), v[:, at]))
-    attn_out[...] = jnp.concatenate(outs, axis=1).astype(BF16)
-
-
-def attend(act, wq, wk, wv, cos, sin, mask):
-    rows, width = act.shape
+    count = rows.shape[0]
+    tile = min(256, count)
+    for start in range(0, count, tile):
+        end = start + tile
+        allowed = mask[start:end, :end]
+        outs = []
+        for h in range(q.shape[1] // HD):
+            at = slice(h * HD, (h + 1) * HD)
+            probs = head_probs(q[start:end, at], k[:end, at], allowed)
+            outs.append(mm(probs.astype(BF16), v[:end, at]))
+        attn_out[start:end, :] = jnp.concatenate(outs, axis=1).astype(BF16)
+
+
+def attend(x, gain, wq, wk, wv, cos, sin, mask):
+    rows, width = x.shape
     cols = wq.shape[1]
     step = min(256, cols)
     column = pl.BlockSpec((rows, step), lambda i: (0, i))
@@ -96,17 +106,18 @@
     return pl.pallas_call(
         attend_body,
         grid=(cols // step,),
-        in_specs=[whole((rows, width)), weight, weight, weight]
+        in_specs=[whole((rows, width)), whole((1, width)), weight, weight, weight]
         + [whole(cos.shape), whole(cos.shape), whole((rows, rows))],
-        out_specs=[column] * 4,
-        out_shape=[jax.ShapeDtypeStruct((rows, cols), BF16)] * 4,
+        out_specs=[whole((rows, width))] + [column] * 4,
+        out_shape=[jax.ShapeDtypeStruct((rows, width), BF16)]
+        + [jax.ShapeDtypeStruct((rows, cols), BF16)] * 4,
         cost_estimate=pl.CostEstimate(
             flops=6 * rows * width * cols + 16 * rows * rows * cols,
-            bytes_accessed=2 * rows * width + 6 * width * cols + 8 * rows * cols,
+            bytes_accessed=4 * rows * width + 6 * width * cols + 8 * rows * cols,
             transcendentals=rows * rows * cols // HD,
         ),
         name="attend",
-    )(act, wq, wk, wv, cos, sin, mask)
+    )(x, gain.reshape(1, width), wq, wk, wv, cos, sin, mask)
 
 
 def attend_back_body(hidden, wo, q_in, k_in, v_in, attn_in, cos, sin, mask, *rest):
@@ -155,48 +166,57 @@
     )(hidden, wo, q, k, v, attn, cos, sin, mask, *after)
 
 
-def outer_body(count, has_add, which, *refs):
-    lefts = [refs[c][...].T for c in range(count)]
-    rights, out = refs[count : 2 * count], refs[-1]
-    width = rights[0].shape[-1]
-    planes = rights[0].shape[0] if len(rights[0].shape) == 3 else 1
-    tile = min(512, width)
-    for plane in range(planes):
-        for start in range(0, width, tile):
-            total = None
-            for left, right in zip(lefts, rights):
-                at = pl.ds(start, tile)
-                block = right[plane, :, at] if len(right.shape) == 3 else right[:, at]
-                part = mm(left, block)
-                total = part if total is None else total + part
-            at = pl.ds(plane * width + start, tile)
-            if has_add:
-                total = total + refs[2 * count][:, at]
-            out[:, at] = total
-
-
-def outer(lefts, rights, which, pieces, add=None, part=(0, 1)):
-    count = len(lefts)
-    piece = lefts[0].shape[1] // pieces
+def outer_body(shape, has_add, which, *refs):
+    out, column, at = refs[-1], 0, 0
+    adder = refs[-2] if has_add else None
+    for count in shape:
+        lefts = [refs[at + c][...].T for c in range(count)]
+        rights = refs[at + count : at + 2 * count]
+        at += 2 * count
+        planes = rights[0].shape[0] if len(rights[0].shape) == 3 else 1
+        width = rights[0].shape[-1]
+        tile = min(512, width)
+        for plane in range(planes):
+            for start in range(0, width, tile):
+                total = None
+                for left, right in zip(lefts, rights):
+                    span = pl.ds(start, tile)
+                    block = right[plane, :, span] if len(right.shape) == 3 else right[:, span]
+                    part = mm(left, block)
+                    total = part if total is None else total + part
+                span = pl.ds(column, tile)
+                if has_add:
+                    total = total + adder[:, span]
+                out[:, span] = total
+                column += tile
+
+
+def outer(groups, which, pieces, add=None, part=(0, 1)):
+    piece = groups[0][0][0].shape[1] // pieces
     index, parts = part
-    rows = [v.shape[0] for v in lefts]
-    if rights[0].ndim == 3:
-        planes, _, cols = rights[0].shape
-        out_cols = planes * cols
-        right_specs = [pl.BlockSpec((planes, r, cols), lambda j, w: (0, 0, 0)) for r in rows]
-    else:
-        out_cols = rights[0].shape[1] // parts
-        right_specs = [pl.BlockSpec((r, out_cols), lambda j, w: (0, index)) for r in rows]
+    specs, args, out_cols, work, moved = [], [], 0, 0, 0
+    for lefts, rights in groups:
+        for v in lefts:
+            specs.append(pl.BlockSpec((v.shape[0], piece), lambda j, w: (0, 2 * j + w[0])))
+            moved += v.size
+        for v in rights:
+            if v.ndim == 3:
+                cols = v.shape[0] * v.shape[2]
+                specs.append(pl.BlockSpec(v.shape, lambda j, w: (0, 0, 0)))
+            else:
+                cols = v.shape[1] // parts
+                specs.append(pl.BlockSpec((v.shape[0], cols), lambda j, w: (0, index)))
+            moved += v.size // parts * 2
+        work += sum(v.shape[0] for v in lefts) * cols
+        out_cols += cols
+        args += list(lefts) + list(rights)
+    out_rows = pieces // 2 * piece
     out_spec = pl.BlockSpec((piece, out_cols), lambda j, w: (j, 0))
-    out_rows = pieces // 2 * piece
-    specs = [pl.BlockSpec((r, piece), lambda j, w: (0, 2 * j + w[0])) for r in rows]
-    specs += right_specs
-    args = list(lefts) + list(rights)
     if add is not None:
         specs.append(out_spec)
         args.append(add)
     return pl.pallas_call(
-        functools.partial(outer_body, count, add is not None),
+        functools.partial(outer_body, [len(g[0]) for g in groups], add is not None),
         grid_spec=pltpu.PrefetchScalarGridSpec(
             num_scalar_prefetch=1,
             grid=(pieces // 2,),
@@ -205,8 +225,8 @@
         ),
         out_shape=jax.ShapeDtypeStruct((out_rows, out_cols), F32),
         cost_estimate=pl.CostEstimate(
-            flops=2 * sum(rows) * out_rows * out_cols,
-            bytes_accessed=2 * sum(rows) * (out_rows + out_cols) + 4 * out_rows * out_cols,
+            flops=2 * work * out_rows,
+            bytes_accessed=moved + 4 * out_rows * out_cols,
             transcendentals=0,
         ),
     )(which.reshape(1).astype(jnp.int32), *args)
@@ -346,10 +366,10 @@
                 [lax.dynamic_slice_in_dim(value, start, size, 0) for start in starts], axis=0
             )
 
-        def core_sum(lefts, rights, part=(0, 1)):
-            away = outer(lefts, rights, 1 - core, dp_size, part=part)
+        def core_sum(groups, part=(0, 1)):
+            away = outer(groups, 1 - core, dp_size, part=part)
             got = data.swap(away, 1)
-            return outer(lefts, rights, core, dp_size, add=got, part=part)
+            return outer(groups, core, dp_size, add=got, part=part)
 
         def z_scatter(value):
             return lax.psum_scatter(
@@ -366,8 +386,6 @@
         for lo, hi in bounds:
             size = hi - lo
             x_f = block_input[lo:hi].astype(F32)
-            inv_f = lax.rsqrt(jnp.mean(x_f * x_f, axis=-1, keepdims=True) + NORM_EPS)
-            act = (x_f * inv_f * attention_gain).astype(BF16)
             rows = jnp.where(
                 token_mask[lo:hi, None] > 0, cotangent[lo:hi], jnp.zeros_like(cotangent[lo:hi])
             )
@@ -378,8 +396,9 @@
                 & (pos_g[None, :] <= pos_g[:, None])
                 & ((mask_g[None, :] > 0) | (pos_g[None, :] == 0))
             ).astype(F32)
-            q, k, v, flat = attend(
-                act, query_weight, key_weight, value_weight, cos_g, sin_g, allowed
+            act, q, k, v, flat = attend(
+                block_input[lo:hi], attention_gain, query_weight, key_weight, value_weight,
+                cos_g, sin_g, allowed,
             )
             added = scatter_rows(
                 lambda s, n, flat=flat: mm(rows_of(flat, s, n), output_weight), size
@@ -405,7 +424,7 @@
             s["up_pre"] = mm(s["act_two"], up_weight)
             s["sig"] = jax.nn.sigmoid(s["gate_pre"])
             s["inner"] = (s["gate_pre"] * s["sig"] * s["up_pre"]).astype(BF16)
-        down_parts = [core_sum(chunks("rows"), chunks("inner"), (i, 2)) for i in range(2)]
+        down_parts = [core_sum([(chunks("rows"), chunks("inner"))], (i, 2)) for i in range(2)]
         down_sums = [z_scatter(v) for v in down_parts]
 
         gain_parts = jnp.zeros((width,), F32)
@@ -414,7 +433,8 @@
             rows = s["rows"]
             inner_grad = s["inner_grad"]
             gate_pre, up_pre, sig = s["gate_pre"], s["up_pre"], s["sig"]
-            gate_pre, up_pre, _ = lax.optimization_barrier((gate_pre, up_pre, down_parts))
+            if index:
+                gate_pre, up_pre, _ = lax.optimization_barrier((gate_pre, up_pre, down_parts))
             gate_back = (inner_grad * up_pre * sig * (1.0 + gate_pre * (1.0 - sig))).astype(BF16)
             up_back = (inner_grad * gate_pre * sig).astype(BF16)
             s["gate_back"], s["up_back"] = gate_back, up_back
@@ -435,18 +455,16 @@
             full = gather_rows(back, size, after)
             s["hidden_back"] = (rows.astype(F32) + full).astype(BF16)
 
-        gate_part = core_sum(chunks("act_two"), chunks("gate_back"))
-        gate_sum = z_scatter(gate_part)
-        up_part = core_sum(chunks("act_two"), chunks("up_back"))
-        up_sum = z_scatter(up_part)
+        both_part = core_sum(
+            [(chunks("act_two"), chunks("gate_back")), (chunks("act_two"), chunks("up_back"))],
+        )
+        both_sum = z_scatter(both_part)
 
         outs = []
-        for (lo, hi), s in zip(bounds, saved):
-            size = hi - lo
-            late_inner, _ = lax.optimization_barrier((s["inner"], saved[-1]["hidden_back"]))
-            mlp = scatter_rows(
-                lambda st, n, a=late_inner: mm(rows_of(a, st, n), down_weight), size
-            )
+        for s in saved:
+            size = s["rows"].shape[0]
+            late_inner, _ = lax.optimization_barrier((s["inner"], saved[-1]["part"]))
+            mlp = scatter_rows(lambda st, n, a=late_inner: mm(rows_of(a, st, n), down_weight), size)
             full = gather_rows(s["added"] + mlp, size)
             outs.append((s["x_f"] + full).astype(BF16))
         block_output = jnp.concatenate(outs, axis=0)
@@ -457,7 +475,7 @@
             size = hi - lo
             back3 = attend_back(
                 s["hidden_back"], output_weight, s["q"], s["k"], s["v"], s["flat"],
-                s["cos"], s["sin"], s["allowed"], (gate_part, up_part),
+                s["cos"], s["sin"], s["allowed"], (both_part,),
             )
             s["qkv_back"] = back3
             q_back, k_back, v_back = back3[0], back3[1], back3[2]
@@ -476,14 +494,18 @@
             input_grads.append(gather_rows(s["hidden_grad"] + back, size))
         input_gradient = jnp.concatenate(input_grads, axis=0)
 
-        out_sum = z_scatter(core_sum(chunks("hidden_back"), chunks("flat"))).T
-        qkv_part = core_sum(chunks("act"), chunks("qkv_back"))
-        qkv_sum = z_scatter(qkv_part)
-        down_sums, _ = lax.optimization_barrier((down_sums, qkv_part))
+        last_part = core_sum(
+            [(chunks("act"), chunks("qkv_back")), (chunks("hidden_back"), chunks("flat"))]
+        )
+        last_sum = z_scatter(last_part)
+        down_sums, both_sum, _ = lax.optimization_barrier((down_sums, both_sum, last_part))
         down_sum = jnp.concatenate([v.T for v in down_sums], axis=0)
-        query_sum = qkv_sum[:, :head_cols]
-        key_sum = qkv_sum[:, head_cols : 2 * head_cols]
-        value_sum = qkv_sum[:, 2 * head_cols :]
+        ff_cols = gate_weight.shape[1]
+        gate_sum, up_sum = both_sum[:, :ff_cols], both_sum[:, ff_cols:]
+        query_sum = last_sum[:, :head_cols]
+        key_sum = last_sum[:, head_cols : 2 * head_cols]
+        value_sum = last_sum[:, 2 * head_cols : 3 * head_cols]
+        out_sum = last_sum[:, 3 * head_cols :].T
 
         gains = data.total(tensor.total(jnp.stack([first_parts, gain_parts])))
         gain_piece = width // dp_size

time: 1060 us -> 1150 us (1.085)
  waiting for transfers between devices: 571 us -> 667 us
  other arithmetic: 69.2 us -> 56.6 us
    reduce_scatter x6 -> x4, waiting for transfers between devices: 179 us -> 267 us  [z_scatter(): lax.psum_scatter(value, 'dp', scatter_dimension=0, tiled=True, axis_index...]
    pallas_call x12 -> x8, Pallas kernels: 96.9 us -> 84.9 us  [outer(): pl.pallas_call(functools.partial(outer_body, [len(g[0]) for g in groups],...]
    ppermute x75 -> x73, starting transfers between devices: 76 us -> 83.8 us  [swap(): lax.ppermute(value, self.axis, [(i, i ^ bit) for i in range(self.size)])]
    ppermute x75 -> x73, waiting for transfers between devices: 391 us -> 399 us  [swap(): lax.ppermute(value, self.axis, [(i, i ^ bit) for i in range(self.size)])]
  transfers between devices with their start and end apart: 81 -> 77, of which waited for: 50 -> 48; matrix products, arithmetic and copies ran while one was open for 15% -> 13% of each run, Pallas kernels for 11% -> 3%
where the time goes in v3:
time: 1150 us; the launch traced here: 1140 us
  waiting for transfers between devices  667 us (58%)
  Pallas kernels  151 us (13%)
  matrix products  116 us (10%)
  starting transfers between devices  84.1 us (7%)
  other arithmetic  56.6 us (5%)
  local copies, waits for them, and re-layouts  51.7 us (4%)
  between operations  16.2 us (1%)
    ppermute x73, waiting for transfers between devices, swap(): lax.ppermute(value, self.axis, [(i, i ^ bit) for i in range(self.size)])  399 us
    reduce_scatter x4, waiting for transfers between devices, z_scatter(): lax.psum_scatter(value, 'dp', scatter_dimension=0, tiled=True, axis_index...  267 us
    pallas_call x8, Pallas kernels, outer(): pl.pallas_call(functools.partial(outer_body, [len(g[0]) for g in groups],...  84.9 us
    ppermute x73, starting transfers between devices, swap(): lax.ppermute(value, self.axis, [(i, i ^ bit) for i in range(self.size)])  83.8 us
    dot_general x22, matrix products, mm_nt(): lax.dot_general(a, b, (((1,), (1,)), ((), ())), preferred_element_type=F32)  66.3 us
    dot_general x12, matrix products, mm(): return jnp.dot(a, b, preferred_element_type=F32)  49.3 us
    pallas_call x2, Pallas kernels, attend_back(): pl.pallas_call(attend_back_body, grid=(cols // step,), in_specs=[whole((r...  33.8 us
    pallas_call x2, Pallas kernels, attend(): pl.pallas_call(attend_body, grid=(cols // step,), in_specs=[whole((rows,...  32.6 us
  transfers between devices with their start and end apart: 77, of which 48 were waited for; matrix products, arithmetic and copies ran while one was open for 13% of the time, Pallas kernels for 3%

profile of v3, /device:TPU:0, one launch (start us, length us, event | category | flops | bytes accessed | tf_op | source)
XLA Modules:
  0.0 1142.6 jit_solution(9804164674229483819)
XLA Ops:
  13.2 4.8 fusion.175
  19.9 16.3 %attend.3 = (bf16[512,2048]{1,0:T(8,128)(2,1)}, bf16[512,512]{1,0:T(8,128)(2,1)}, bf16[512,512]{1,0:T(8,128)(2,1)}, bf16[512,512]{1,0:T(8,128)(2,1)}, bf16[512,512]{1,0:T(8,128)(2,1)}) custom-call(bf16[512,2048]{1,0:T(8,128)(2,1)} %get-tuple-element.102.x, f32[1,2048]{1,0:T(1,128)} %bitcast.114, bf16[2048,512]{1,0:T(8,128)(2,1)} %wq.3, ...), custom_call_target="tpu_custom_call" | custom-call | flops 5368709120 | bytes 12582912 | tf_op jit(solution)/shard_map/attend/pallas_call | solution.py:106
  39.5 3.0 collective-permute-start.8
  44.0 16.3 %attend.2 = (bf16[512,2048]{1,0:T(8,128)(2,1)}, bf16[512,512]{1,0:T(8,128)(2,1)}, bf16[512,512]{1,0:T(8,128)(2,1)}, bf16[512,512]{1,0:T(8,128)(2,1)}, bf16[512,512]{1,0:T(8,128)(2,1)}) custom-call(bf16[512,2048]{1,0:T(8,128)(2,1)} %get-tuple-element.101.x, f32[1,2048]{1,0:T(1,128)} %bitcast.115, bf16[2048,512]{1,0:T(8,128)(2,1)} %wq.3, ...), custom_call_target="tpu_custom_call" | custom-call | flops 5368709120 | bytes 12582912 | tf_op jit(solution)/shard_map/attend/pallas_call | solution.py:106
  78.8 11.3 collective-permute-done
  95.3 5.9 collective-permute-done.11
  103.1 7.6 collective-permute-done.3
  119.0 9.9 collective-permute-done.6
  131.3 6.1 fusion.202
  137.4 2.8 collective-permute-done.14
  145.2 18.3 %collective-permute-done.7 = f32[128,2048]{1,0:T(8,128)} collective-permute-done((f32[128,2048]{1,0:T(8,128)S(1)}, f32[128,2048]{1,0:T(8,128)}, u32[]{:S(2)}, u32[]{:S(2)}) %collective-permute-start.7) | collective-permute-done | bytes 1048608 | tf_op jit(solution)/shard_map/ppermute | solution.py:243
  167.8 16.0 %collective-permute-done.15 = f32[128,2048]{1,0:T(8,128)S(1)} collective-permute-done((f32[128,2048]{1,0:T(8,128)S(1)}, f32[128,2048]{1,0:T(8,128)S(1)}, u32[]{:S(2)}, u32[]{:S(2)}) %collective-permute-start.15) | collective-permute-done | bytes 1048608 | tf_op jit(solution)/shard_map/ppermute | solution.py:243
  183.7 6.5 fusion.199
  191.2 4.6 fusion.201
  197.9 6.9 multiply_convert_fusion.4
  204.8 9.9 multiply_convert_fusion
  214.7 6.4 shard_map.212
  221.1 6.6 shard_map.214
  228.0 9.8 fusion.200
  239.6 7.1 fusion.61
  246.7 7.4 shard_map.213
  254.1 7.3 shard_map.215
  261.4 7.2 multiply_convert_fusion.2
  268.7 15.6 %shard_map.216 = f32[1024,4096]{1,0:T(8,128)} custom-call(s32[1]{0:T(128)} %bitcast.5.which, bf16[512,2048]{1,0:T(8,128)(2,1)} %copy-done.5, bf16[512,2048]{1,0:T(8,128)(2,1)} %copy-done.6, bf16[512,2048]{1,0:T(8,128)(2,1)} %get-tuple-element.93.refs_2_, bf16[512,2048]{1,0:T(8,128)(2,1)} %get-tuple-element.91.refs_3_, bf16[512,2048]{1,0:T(8,128)(2,1)} %copy-done.5, ...), custom_call_target="tpu_custom_call" | custom-call | flops 8589934592 | bytes 29360128 | tf_op jit(solution)/shard_map/pallas_call | solution.py:218
  284.3 6.3 convolution_add_fusion.8
  293.6 5.7 fusion.54
  299.3 5.9 convolution_add_fusion.9
  305.3 11.1 collective-permute-done.38
  320.1 10.8 collective-permute-done.41
  335.7 6.0 convolution_add_fusion.10
  347.0 5.8 convolution_add_fusion.11
  352.8 12.4 %collective-permute-done.18 = f32[128,2048]{1,0:T(8,128)S(1)} collective-permute-done((f32[128,2048]{1,0:T(8,128)S(1)}, f32[128,2048]{1,0:T(8,128)S(1)}, u32[]{:S(2)}, u32[]{:S(2)}) %collective-permute-start.18) | collective-permute-done | bytes 1048608 | tf_op jit(solution)/shard_map/ppermute | solution.py:243
  369.1 8.2 collective-permute-done.21
  382.2 7.4 collective-permute-done.44
  394.4 12.6 %collective-permute-done.57 = f32[64,2048]{1,0:T(8,128)S(1)} collective-permute-done((f32[64,2048]{1,0:T(8,128)S(1)}, f32[64,2048]{1,0:T(8,128)S(1)}, u32[]{:S(2)}, u32[]{:S(2)}) %collective-permute-start.57) | collective-permute-done | bytes 524320 | tf_op jit(solution)/shard_map/ppermute | solution.py:243
  407.1 20.1 %collective-permute-done.55 = f32[64,2048]{1,0:T(8,128)S(1)} collective-permute-done((f32[64,2048]{1,0:T(8,128)S(1)}, f32[64,2048]{1,0:T(8,128)S(1)}, u32[]{:S(2)}, u32[]{:S(2)}) %collective-permute-start.55) | collective-permute-done | bytes 524320 | tf_op jit(solution)/shard_map/ppermute | solution.py:243
  432.9 13.0 %collective-permute-done.58 = f32[128,2048]{1,0:T(8,128)S(1)} collective-permute-done((f32[128,2048]{1,0:T(8,128)S(1)}, f32[128,2048]{1,0:T(8,128)S(1)}, u32[]{:S(2)}, u32[]{:S(2)}) %collective-permute-start.58) | collective-permute-done | bytes 1048608 | tf_op jit(solution)/shard_map/ppermute | solution.py:243
  449.8 19.9 %shard_map.217.rest_0_ = f32[1024,4096]{1,0:T(8,128)} custom-call(s32[1]{0:T(128)} %bitcast.4.which, bf16[512,2048]{1,0:T(8,128)(2,1)} %copy-done.5, bf16[512,2048]{1,0:T(8,128)(2,1)} %copy-done.6, bf16[512,2048]{1,0:T(8,128)(2,1)} %get-tuple-element.93.refs_2_, bf16[512,2048]{1,0:T(8,128)(2,1)} %get-tuple-element.91.refs_3_, bf16[512,2048]{1,0:T(8,128)(2,1)} %copy-done.5, ...), custom_call_target="tpu_custom_call" | custom-call | flops 8589934592 | bytes 29360128 | tf_op jit(solution)/shard_map/pallas_call | solution.py:218
  469.7 17.0 %attend_back.2.refs_2_ = bf16[3,512,512]{2,1,0:T(8,128)(2,1)} custom-call(bf16[512,2048]{1,0:T(8,128)(2,1)} %fusion.4.hidden.refs_4_, bf16[512,2048]{1,0:T(8,128)(2,1)} %wo.3, bf16[512,512]{1,0:T(8,128)(2,1)} %get-tuple-element.46.q_in, bf16[512,512]{1,0:T(8,128)(2,1)} %get-tuple-element.47.k_in, bf16[512,512]{1,0:T(8,128)(2,1)} %get-tuple-element.48.v_in, ...), custom_call_target="tpu_custom_call" | custom-call | flops 6442450944 | bytes 7864320 | tf_op jit(solution)/shard_map/attend_back/pallas_call | solution.py:151
  486.7 16.7 %attend_back.3.refs_3_ = bf16[3,512,512]{2,1,0:T(8,128)(2,1)} custom-call(bf16[512,2048]{1,0:T(8,128)(2,1)} %fusion.5.hidden.refs_5_, bf16[512,2048]{1,0:T(8,128)(2,1)} %wo.3, bf16[512,512]{1,0:T(8,128)(2,1)} %get-tuple-element.53.q_in, bf16[512,512]{1,0:T(8,128)(2,1)} %get-tuple-element.54.k_in, bf16[512,512]{1,0:T(8,128)(2,1)} %get-tuple-element.55.v_in, ...), custom_call_target="tpu_custom_call" | custom-call | flops 6442450944 | bytes 7864320 | tf_op jit(solution)/shard_map/attend_back/pallas_call | solution.py:151
  503.4 9.8 shard_map.218
  513.3 13.5 %collective-permute-done.72.refs_8_ = f32[1024,2048]{1,0:T(8,128)} collective-permute-done((f32[1024,2048]{1,0:T(8,128)}, f32[1024,2048]{1,0:T(8,128)}, u32[]{:S(2)}, u32[]{:S(2)}) %collective-permute-start.72) | collective-permute-done | bytes 8388640 | tf_op jit(solution)/shard_map/ppermute | solution.py:243
  526.8 11.9 %shard_map.219 = f32[1024,2048]{1,0:T(8,128)} custom-call(s32[1]{0:T(128)} %bitcast.4.which, bf16[512,2048]{1,0:T(8,128)(2,1)} %get-tuple-element.56.refs_0_, bf16[512,2048]{1,0:T(8,128)(2,1)} %get-tuple-element.57.refs_1_, bf16[3,512,512]{2,1,0:T(8,128)(2,1)} %attend_back.2.refs_2_, bf16[3,512,512]{2,1,0:T(8,128)(2,1)} %attend_back.3.refs_3_, ...), custom_call_target="tpu_custom_call" | custom-call | flops 4294967296 | bytes 16777216 | tf_op jit(solution)/shard_map/pallas_call | solution.py:218
  544.3 6.5 fusion.50
  553.8 6.0 fusion.42
  566.5 10.7 collective-permute-done.30
  581.1 18.5 %collective-permute-done.22 = f32[128,2048]{1,0:T(8,128)S(1)} collective-permute-done((f32[128,2048]{1,0:T(8,128)S(1)}, f32[128,2048]{1,0:T(8,128)S(1)}, u32[]{:S(2)}, u32[]{:S(2)}) %collective-permute-start.22) | collective-permute-done | bytes 1048608 | tf_op jit(solution)/shard_map/ppermute | solution.py:243
  603.6 7.3 collective-permute-done.33
  615.6 6.5 collective-permute-done.25
  627.6 5.8 collective-permute-done.36
  639.4 5.3 collective-permute-done.28
  649.2 18.9 %collective-permute-done.37 = f32[128,2048]{1,0:T(8,128)S(1)} collective-permute-done((f32[128,2048]{1,0:T(8,128)S(1)}, f32[128,2048]{1,0:T(8,128)S(1)}, u32[]{:S(2)}, u32[]{:S(2)}) %collective-permute-start.37) | collective-permute-done | bytes 1048608 | tf_op jit(solution)/shard_map/ppermute | solution.py:243
  668.5 21.0 %collective-permute-done.29 = f32[128,2048]{1,0:T(8,128)S(1)} collective-permute-done((f32[128,2048]{1,0:T(8,128)S(1)}, f32[128,2048]{1,0:T(8,128)S(1)}, u32[]{:S(2)}, u32[]{:S(2)}) %collective-permute-start.29) | collective-permute-done | bytes 1048608 | tf_op jit(solution)/shard_map/ppermute | solution.py:243
  711.1 35.7 %collective-permute-done.47 = f32[128,2048]{1,0:T(8,128)S(1)} collective-permute-done((f32[128,2048]{1,0:T(8,128)S(1)}, f32[128,2048]{1,0:T(8,128)S(1)}, u32[]{:S(2)}, u32[]{:S(2)}) %collective-permute-start.47) | collective-permute-done | bytes 1048608 | tf_op jit(solution)/shard_map/ppermute | solution.py:243
  752.8 10.1 collective-permute-done.50
  764.4 7.1 collective-permute-done.62
  788.6 2.8 collective-permute-start.71
  792.9 4.1 collective-permute-done.51
  800.2 8.1 collective-permute-done.63
  810.0 20.8 %collective-permute-done.54 = f32[128,2048]{1,0:T(8,128)S(1)} collective-permute-done((f32[128,2048]{1,0:T(8,128)S(1)}, f32[128,2048]{1,0:T(8,128)S(1)}, u32[]{:S(2)}, u32[]{:S(2)}) %collective-permute-start.54) | collective-permute-done | bytes 1048608 | tf_op jit(solution)/shard_map/ppermute | solution.py:243
  831.2 21.3 %collective-permute-done.66 = f32[128,2048]{1,0:T(8,128)S(1)} collective-permute-done((f32[128,2048]{1,0:T(8,128)S(1)}, f32[128,2048]{1,0:T(8,128)S(1)}, u32[]{:S(2)}, u32[]{:S(2)}) %collective-permute-start.66) | collective-permute-done | bytes 1048608 | tf_op jit(solution)/shard_map/ppermute | solution.py:243
  852.9 4.0 pad_maximum_fusion
  860.6 266.8 %reduce-scatter.11.cloned.1.call-done = f32[256,4096]{1,0:T(8,128)} async-done(((f32[1024,4096]{1,0:T(8,128)}), f32[256,4096]{1,0:T(8,128)}) %reduce-scatter.11.cloned.1.call-update) | async-done | bytes 4194320 | tf_op jit(solution)/shard_map/reduce_scatter | solution.py:375
  1130.9 4.7 fusion.174
  (440 shorter events, 207.0 us)
Async XLA Ops:
  7.2 849.7 %reduce-scatter.5.cloned.1.call-start = ((), (), s32[]{:S(2)}) async-start(), calls=%async_computation.4 | async-start | bytes 10485760 | tf_op jit(solution)/shard_map/reduce_scatter | solution.py:375
  39.5 33.0 %collective-permute-start.8 = (f32[128,2048]{1,0:T(8,128)}, f32[128,2048]{1,0:T(8,128)}, u32[]{:S(2)}, u32[]{:S(2)}) collective-permute-start(f32[128,2048]{1,0:T(8,128)} %get-tuple-element.169), channel_id=1, source_target_pairs={{0,1},{1,0},{2,3},{3,2},{4,5},{5,4},{6,7},{7,6},{8,9},{9,8},{10,11... | collective-permute-start | bytes 3145736 | tf_op jit(solution)/shard_map/ppermute | solution.py:243
  42.4 30.0 %collective-permute-start.10 = (f32[128,2048]{1,0:T(8,128)}, f32[128,2048]{1,0:T(8,128)}, u32[]{:S(2)}, u32[]{:S(2)}) collective-permute-start(f32[128,2048]{1,0:T(8,128)} %get-tuple-element.170), channel_id=1, source_target_pairs={{0,2},{1,3},{2,0},{3,1},{4,6},{5,7},{6,4},{7,5},{8,10},{9,11},{10,... | collective-permute-start | bytes 3145736 | tf_op jit(solution)/shard_map/ppermute | solution.py:243
  63.7 26.3 %collective-permute-start = (f32[128,2048]{1,0:T(8,128)}, f32[128,2048]{1,0:T(8,128)}, u32[]{:S(2)}, u32[]{:S(2)}) collective-permute-start(f32[128,2048]{1,0:T(8,128)} %get-tuple-element.163), channel_id=1, source_target_pairs={{0,1},{1,0},{2,3},{3,2},{4,5},{5,4},{6,7},{7,6},{8,9},{9,8},{10,11... | collective-permute-start | bytes 3145736 | tf_op jit(solution)/shard_map/ppermute | solution.py:243
  64.2 26.9 %collective-permute-start.2 = (f32[128,2048]{1,0:T(8,128)}, f32[128,2048]{1,0:T(8,128)}, u32[]{:S(2)}, u32[]{:S(2)}) collective-permute-start(f32[128,2048]{1,0:T(8,128)} %get-tuple-element.164), channel_id=1, source_target_pairs={{0,2},{1,3},{2,0},{3,1},{4,6},{5,7},{6,4},{7,5},{8,10},{9,11},{10,... | collective-permute-start | bytes 3145736 | tf_op jit(solution)/shard_map/ppermute | solution.py:243
  75.1 26.1 %collective-permute-start.11 = (f32[64,2048]{1,0:T(8,128)S(1)}, f32[64,2048]{1,0:T(8,128)S(1)}, u32[]{:S(2)}, u32[]{:S(2)}) collective-permute-start(f32[64,2048]{1,0:T(8,128)S(1)} %constant_dynamic-slice_fusion.42), channel_id=1, source_target_pairs={{0,1},{1,0},{2,3},{3,2},{4,5},{5,4},{6,7},{7,6},{8,9},{9,8},{10,11... | collective-permute-start | bytes 1572872 | tf_op jit(solution)/shard_map/ppermute | solution.py:243
  77.2 25.0 %collective-permute-start.9 = (f32[64,2048]{1,0:T(8,128)S(1)}, f32[64,2048]{1,0:T(8,128)S(1)}, u32[]{:S(2)}, u32[]{:S(2)}) collective-permute-start(f32[64,2048]{1,0:T(8,128)S(1)} %constant_dynamic-slice_fusion.43), channel_id=1, source_target_pairs={{0,2},{1,3},{2,0},{3,1},{4,6},{5,7},{6,4},{7,5},{8,10},{9,11},{10,... | collective-permute-start | bytes 1572872 | tf_op jit(solution)/shard_map/ppermute | solution.py:243
  93.1 17.7 %collective-permute-start.3 = (f32[64,2048]{1,0:T(8,128)S(1)}, f32[64,2048]{1,0:T(8,128)S(1)}, u32[]{:S(2)}, u32[]{:S(2)}) collective-permute-start(f32[64,2048]{1,0:T(8,128)S(1)} %constant_dynamic-slice_fusion.52), channel_id=1, source_target_pairs={{0,1},{1,0},{2,3},{3,2},{4,5},{5,4},{6,7},{7,6},{8,9},{9,8},{10,11... | collective-permute-start | bytes 1572872 | tf_op jit(solution)/shard_map/ppermute | solution.py:243
  94.1 18.1 %collective-permute-start.1 = (f32[64,2048]{1,0:T(8,128)S(1)}, f32[64,2048]{1,0:T(8,128)S(1)}, u32[]{:S(2)}, u32[]{:S(2)}) collective-permute-start(f32[64,2048]{1,0:T(8,128)S(1)} %constant_dynamic-slice_fusion.53), channel_id=1, source_target_pairs={{0,2},{1,3},{2,0},{3,1},{4,6},{5,7},{6,4},{7,5},{8,10},{9,11},{10,... | collective-permute-start | bytes 1572872 | tf_op jit(solution)/shard_map/ppermute | solution.py:243
  114.0 14.9 %collective-permute-start.6 = (f32[64,2048]{1,0:T(8,128)S(1)}, f32[64,2048]{1,0:T(8,128)S(1)}, u32[]{:S(2)}, u32[]{:S(2)}) collective-permute-start(f32[64,2048]{1,0:T(8,128)S(1)} %get-tuple-element.192), channel_id=1, source_target_pairs={{0,1},{1,0},{2,3},{3,2},{4,5},{5,4},{6,7},{7,6},{8,9},{9,8},{10,11... | collective-permute-start | bytes 1572872 | tf_op jit(solution)/shard_map/ppermute | solution.py:243
  114.9 15.7 %collective-permute-start.4 = (f32[64,2048]{1,0:T(8,128)S(1)}, f32[64,2048]{1,0:T(8,128)S(1)}, u32[]{:S(2)}, u32[]{:S(2)}) collective-permute-start(f32[64,2048]{1,0:T(8,128)S(1)} %get-tuple-element.191), channel_id=1, source_target_pairs={{0,2},{1,3},{2,0},{3,1},{4,6},{5,7},{6,4},{7,5},{8,10},{9,11},{10,... | collective-permute-start | bytes 1572872 | tf_op jit(solution)/shard_map/ppermute | solution.py:243
  116.5 26.6 %collective-permute-start.12 = (f32[64,2048]{1,0:T(8,128)S(1)}, f32[64,2048]{1,0:T(8,128)}, u32[]{:S(2)}, u32[]{:S(2)}) collective-permute-start(f32[64,2048]{1,0:T(8,128)S(1)} %get-tuple-element.189), channel_id=1, source_target_pairs={{0,2},{1,3},{2,0},{3,1},{4,6},{5,7},{6,4},{7,5},{8,10},{9,11},{10,... | collective-permute-start | bytes 1572872 | tf_op jit(solution)/shard_map/ppermute | solution.py:243
  117.5 22.7 %collective-permute-start.14 = (f32[64,2048]{1,0:T(8,128)S(1)}, f32[64,2048]{1,0:T(8,128)}, u32[]{:S(2)}, u32[]{:S(2)}) collective-permute-start(f32[64,2048]{1,0:T(8,128)S(1)} %get-tuple-element.190), channel_id=1, source_target_pairs={{0,1},{1,0},{2,3},{3,2},{4,5},{5,4},{6,7},{7,6},{8,9},{9,8},{10,11... | collective-permute-start | bytes 1572872 | tf_op jit(solution)/shard_map/ppermute | solution.py:243
  129.0 34.5 %collective-permute-start.7 = (f32[128,2048]{1,0:T(8,128)S(1)}, f32[128,2048]{1,0:T(8,128)}, u32[]{:S(2)}, u32[]{:S(2)}) collective-permute-start(f32[128,2048]{1,0:T(8,128)S(1)} %maximum_select_fusion.17), channel_id=1, source_target_pairs={{0,2},{1,3},{2,0},{3,1},{4,6},{5,7},{6,4},{7,5},{8,10},{9,11},{10,... | collective-permute-start | bytes 3145736 | tf_op jit(solution)/shard_map/ppermute | solution.py:243
  130.6 34.6 %collective-permute-start.5 = (f32[128,2048]{1,0:T(8,128)S(1)}, f32[128,2048]{1,0:T(8,128)}, u32[]{:S(2)}, u32[]{:S(2)}) collective-permute-start(f32[128,2048]{1,0:T(8,128)S(1)} %maximum_select_fusion.16), channel_id=1, source_target_pairs={{0,1},{1,0},{2,3},{3,2},{4,5},{5,4},{6,7},{7,6},{8,9},{9,8},{10,11... | collective-permute-start | bytes 3145736 | tf_op jit(solution)/shard_map/ppermute | solution.py:243
  141.5 42.2 %collective-permute-start.15 = (f32[128,2048]{1,0:T(8,128)S(1)}, f32[128,2048]{1,0:T(8,128)S(1)}, u32[]{:S(2)}, u32[]{:S(2)}) collective-permute-start(f32[128,2048]{1,0:T(8,128)S(1)} %maximum_select_fusion.19), channel_id=1, source_target_pairs={{0,2},{1,3},{2,0},{3,1},{4,6},{5,7},{6,4},{7,5},{8,10},{9,11},{10,... | collective-permute-start | bytes 3145736 | tf_op jit(solution)/shard_map/ppermute | solution.py:243
  144.6 39.2 %collective-permute-start.13 = (f32[128,2048]{1,0:T(8,128)S(1)}, f32[128,2048]{1,0:T(8,128)S(1)}, u32[]{:S(2)}, u32[]{:S(2)}) collective-permute-start(f32[128,2048]{1,0:T(8,128)S(1)} %maximum_select_fusion.18), channel_id=1, source_target_pairs={{0,1},{1,0},{2,3},{3,2},{4,5},{5,4},{6,7},{7,6},{8,9},{9,8},{10,11... | collective-permute-start | bytes 3145736 | tf_op jit(solution)/shard_map/ppermute | solution.py:243
  221.1 25.6 %collective-permute-start.16 = (f32[1024,1024]{1,0:T(8,128)}, f32[1024,1024]{1,0:T(8,128)}, u32[]{:S(2)}, u32[]{:S(2)}) collective-permute-start(f32[1024,1024]{1,0:T(8,128)} %shard_map.212), channel_id=1, source_target_pairs={{0,4},{4,0},{8,12},{12,8},{16,20},{20,16},{24,28},{28,24},{1,5},{5... | collective-permute-start | bytes 12582920 | tf_op jit(solution)/shard_map/ppermute | solution.py:243
  227.7 26.4 %collective-permute-start.17 = (f32[1024,1024]{1,0:T(8,128)}, f32[1024,1024]{1,0:T(8,128)}, u32[]{:S(2)}, u32[]{:S(2)}) collective-permute-start(f32[1024,1024]{1,0:T(8,128)} %shard_map.214), channel_id=1, source_target_pairs={{0,4},{4,0},{8,12},{12,8},{16,20},{20,16},{24,28},{28,24},{1,5},{5... | collective-permute-start | bytes 12582920 | tf_op jit(solution)/shard_map/ppermute | solution.py:243
  284.2 165.5 %collective-permute-start.46 = (f32[1024,4096]{1,0:T(8,128)}, f32[1024,4096]{1,0:T(8,128)}, u32[]{:S(2)}, u32[]{:S(2)}) collective-permute-start(f32[1024,4096]{1,0:T(8,128)} %shard_map.216), channel_id=1, source_target_pairs={{0,4},{4,0},{8,12},{12,8},{16,20},{20,16},{24,28},{28,24},{1,5},{5... | collective-permute-start | bytes 50331656 | tf_op jit(solution)/shard_map/ppermute | solution.py:243
  290.9 25.5 %collective-permute-start.38 = (f32[128,2048]{1,0:T(8,128)S(1)}, f32[128,2048]{1,0:T(8,128)S(1)}, u32[]{:S(2)}, u32[]{:S(2)}) collective-permute-start(f32[128,2048]{1,0:T(8,128)S(1)} %get-tuple-element.121), channel_id=1, source_target_pairs={{0,1},{1,0},{2,3},{3,2},{4,5},{5,4},{6,7},{7,6},{8,9},{9,8},{10,11... | collective-permute-start | bytes 3145736 | tf_op jit(solution)/shard_map/ppermute | solution.py:243
  292.2 25.2 %collective-permute-start.40 = (f32[128,2048]{1,0:T(8,128)S(1)}, f32[128,2048]{1,0:T(8,128)S(1)}, u32[]{:S(2)}, u32[]{:S(2)}) collective-permute-start(f32[128,2048]{1,0:T(8,128)S(1)} %get-tuple-element.122), channel_id=1, source_target_pairs={{0,2},{1,3},{2,0},{3,1},{4,6},{5,7},{6,4},{7,5},{8,10},{9,11},{10,... | collective-permute-start | bytes 3145736 | tf_op jit(solution)/shard_map/ppermute | solution.py:243
  341.9 23.3 %collective-permute-start.18 = (f32[128,2048]{1,0:T(8,128)S(1)}, f32[128,2048]{1,0:T(8,128)S(1)}, u32[]{:S(2)}, u32[]{:S(2)}) collective-permute-start(f32[128,2048]{1,0:T(8,128)S(1)} %get-tuple-element.149), channel_id=1, source_target_pairs={{0,1},{1,0},{2,3},{3,2},{4,5},{5,4},{6,7},{7,6},{8,9},{9,8},{10,11... | collective-permute-start | bytes 3145736 | tf_op jit(solution)/shard_map/ppermute | solution.py:243
  343.2 22.9 %collective-permute-start.20 = (f32[128,2048]{1,0:T(8,128)S(1)}, f32[128,2048]{1,0:T(8,128)S(1)}, u32[]{:S(2)}, u32[]{:S(2)}) collective-permute-start(f32[128,2048]{1,0:T(8,128)S(1)} %get-tuple-element.150), channel_id=1, source_target_pairs={{0,2},{1,3},{2,0},{3,1},{4,6},{5,7},{6,4},{7,5},{8,10},{9,11},{10,... | collective-permute-start | bytes 3145736 | tf_op jit(solution)/shard_map/ppermute | solution.py:243
  389.6 39.3 %collective-permute-start.45 = (f32[128,2048]{1,0:T(8,128)S(1)}, f32[128,2048]{1,0:T(8,128)S(1)}, u32[]{:S(2)}, u32[]{:S(2)}) collective-permute-start(f32[128,2048]{1,0:T(8,128)S(1)} %maximum_select_fusion.25), channel_id=1, source_target_pairs={{0,2},{1,3},{2,0},{3,1},{4,6},{5,7},{6,4},{7,5},{8,10},{9,11},{10,... | collective-permute-start | bytes 3145736 | tf_op jit(solution)/shard_map/ppermute | solution.py:243
  392.1 14.9 %collective-permute-start.57 = (f32[64,2048]{1,0:T(8,128)S(1)}, f32[64,2048]{1,0:T(8,128)S(1)}, u32[]{:S(2)}, u32[]{:S(2)}) collective-permute-start(f32[64,2048]{1,0:T(8,128)S(1)} %get-tuple-element.182), channel_id=1, source_target_pairs={{0,1},{1,0},{2,3},{3,2},{4,5},{5,4},{6,7},{7,6},{8,9},{9,8},{10,11... | collective-permute-start | bytes 1572872 | tf_op jit(solution)/shard_map/ppermute | solution.py:243
  393.7 33.5 %collective-permute-start.55 = (f32[64,2048]{1,0:T(8,128)S(1)}, f32[64,2048]{1,0:T(8,128)S(1)}, u32[]{:S(2)}, u32[]{:S(2)}) collective-permute-start(f32[64,2048]{1,0:T(8,128)S(1)} %get-tuple-element.181), channel_id=1, source_target_pairs={{0,2},{1,3},{2,0},{3,1},{4,6},{5,7},{6,4},{7,5},{8,10},{9,11},{10,... | collective-permute-start | bytes 1572872 | tf_op jit(solution)/shard_map/ppermute | solution.py:243
  393.8 35.4 %collective-permute-start.43 = (f32[128,2048]{1,0:T(8,128)S(1)}, f32[128,2048]{1,0:T(8,128)S(1)}, u32[]{:S(2)}, u32[]{:S(2)}) collective-permute-start(f32[128,2048]{1,0:T(8,128)S(1)} %maximum_select_fusion.24), channel_id=1, source_target_pairs={{0,1},{1,0},{2,3},{3,2},{4,5},{5,4},{6,7},{7,6},{8,9},{9,8},{10,11... | collective-permute-start | bytes 3145736 | tf_op jit(solution)/shard_map/ppermute | solution.py:243
  407.1 38.8 %collective-permute-start.58 = (f32[128,2048]{1,0:T(8,128)S(1)}, f32[128,2048]{1,0:T(8,128)S(1)}, u32[]{:S(2)}, u32[]{:S(2)}) collective-permute-start(f32[128,2048]{1,0:T(8,128)S(1)} %maximum_select_fusion.29), channel_id=1, source_target_pairs={{0,2},{1,3},{2,0},{3,1},{4,6},{5,7},{6,4},{7,5},{8,10},{9,11},{10,... | collective-permute-start | bytes 3145736 | tf_op jit(solution)/shard_map/ppermute | solution.py:243
  427.4 18.5 %collective-permute-start.56 = (f32[128,2048]{1,0:T(8,128)S(1)}, f32[128,2048]{1,0:T(8,128)S(1)}, u32[]{:S(2)}, u32[]{:S(2)}) collective-permute-start(f32[128,2048]{1,0:T(8,128)S(1)} %maximum_select_fusion.28), channel_id=1, source_target_pairs={{0,1},{1,0},{2,3},{3,2},{4,5},{5,4},{6,7},{7,6},{8,9},{9,8},{10,11... | collective-permute-start | bytes 3145736 | tf_op jit(solution)/shard_map/ppermute | solution.py:243
  538.7 321.9 %reduce-scatter.7.cloned.1.call-start = ((), (), s32[]{:S(2)}) async-start(), calls=%async_computation.5 | async-start | bytes 5242880 | tf_op jit(solution)/shard_map/reduce_scatter | solution.py:375
  539.5 321.1 %reduce-scatter.9.cloned.1.call-start = ((), (), s32[]{:S(2)}) async-start(), calls=%async_computation.6 | async-start | bytes 5242880 | tf_op jit(solution)/shard_map/reduce_scatter | solution.py:375
  540.2 587.2 %reduce-scatter.11.cloned.1.call-start = ((), (), s32[]{:S(2)}) async-start(), calls=%async_computation.7 | async-start | bytes 20971520 | tf_op jit(solution)/shard_map/reduce_scatter | solution.py:375
  551.1 26.1 %collective-permute-start.30 = (f32[128,2048]{1,0:T(8,128)S(1)}, f32[128,2048]{1,0:T(8,128)S(1)}, u32[]{:S(2)}, u32[]{:S(2)}) collective-permute-start(f32[128,2048]{1,0:T(8,128)S(1)} %get-tuple-element.141), channel_id=1, source_target_pairs={{0,1},{1,0},{2,3},{3,2},{4,5},{5,4},{6,7},{7,6},{8,9},{9,8},{10,11... | collective-permute-start | bytes 3145736 | tf_op jit(solution)/shard_map/ppermute | solution.py:243
  552.1 26.0 %collective-permute-start.32 = (f32[128,2048]{1,0:T(8,128)S(1)}, f32[128,2048]{1,0:T(8,128)S(1)}, u32[]{:S(2)}, u32[]{:S(2)}) collective-permute-start(f32[128,2048]{1,0:T(8,128)S(1)} %get-tuple-element.142), channel_id=1, source_target_pairs={{0,2},{1,3},{2,0},{3,1},{4,6},{5,7},{6,4},{7,5},{8,10},{9,11},{10,... | collective-permute-start | bytes 3145736 | tf_op jit(solution)/shard_map/ppermute | solution.py:243
  560.0 39.6 %collective-permute-start.22 = (f32[128,2048]{1,0:T(8,128)S(1)}, f32[128,2048]{1,0:T(8,128)S(1)}, u32[]{:S(2)}, u32[]{:S(2)}) collective-permute-start(f32[128,2048]{1,0:T(8,128)S(1)} %get-tuple-element.133), channel_id=1, source_target_pairs={{0,1},{1,0},{2,3},{3,2},{4,5},{5,4},{6,7},{7,6},{8,9},{9,8},{10,11... | collective-permute-start | bytes 3145736 | tf_op jit(solution)/shard_map/ppermute | solution.py:243
  561.1 39.6 %collective-permute-start.24 = (f32[128,2048]{1,0:T(8,128)S(1)}, f32[128,2048]{1,0:T(8,128)S(1)}, u32[]{:S(2)}, u32[]{:S(2)}) collective-permute-start(f32[128,2048]{1,0:T(8,128)S(1)} %get-tuple-element.134), channel_id=1, source_target_pairs={{0,2},{1,3},{2,0},{3,1},{4,6},{5,7},{6,4},{7,5},{8,10},{9,11},{10,... | collective-permute-start | bytes 3145736 | tf_op jit(solution)/shard_map/ppermute | solution.py:243
  578.6 32.3 %collective-permute-start.33 = (f32[64,2048]{1,0:T(8,128)S(1)}, f32[64,2048]{1,0:T(8,128)S(1)}, u32[]{:S(2)}, u32[]{:S(2)}) collective-permute-start(f32[64,2048]{1,0:T(8,128)S(1)} %constant_dynamic-slice_fusion.20), channel_id=1, source_target_pairs={{0,1},{1,0},{2,3},{3,2},{4,5},{5,4},{6,7},{7,6},{8,9},{9,8},{10,11... | collective-permute-start | bytes 1572872 | tf_op jit(solution)/shard_map/ppermute | solution.py:243
  579.7 32.2 %collective-permute-start.31 = (f32[64,2048]{1,0:T(8,128)S(1)}, f32[64,2048]{1,0:T(8,128)S(1)}, u32[]{:S(2)}, u32[]{:S(2)}) collective-permute-start(f32[64,2048]{1,0:T(8,128)S(1)} %constant_dynamic-slice_fusion.21), channel_id=1, source_target_pairs={{0,2},{1,3},{2,0},{3,1},{4,6},{5,7},{6,4},{7,5},{8,10},{9,11},{10,... | collective-permute-start | bytes 1572872 | tf_op jit(solution)/shard_map/ppermute | solution.py:243
  601.1 21.0 %collective-permute-start.25 = (f32[64,2048]{1,0:T(8,128)S(1)}, f32[64,2048]{1,0:T(8,128)S(1)}, u32[]{:S(2)}, u32[]{:S(2)}) collective-permute-start(f32[64,2048]{1,0:T(8,128)S(1)} %constant_dynamic-slice_fusion.26), channel_id=1, source_target_pairs={{0,1},{1,0},{2,3},{3,2},{4,5},{5,4},{6,7},{7,6},{8,9},{9,8},{10,11... | collective-permute-start | bytes 1572872 | tf_op jit(solution)/shard_map/ppermute | solution.py:243
  602.2 20.9 %collective-permute-start.23 = (f32[64,2048]{1,0:T(8,128)S(1)}, f32[64,2048]{1,0:T(8,128)S(1)}, u32[]{:S(2)}, u32[]{:S(2)}) collective-permute-start(f32[64,2048]{1,0:T(8,128)S(1)} %constant_dynamic-slice_fusion.27), channel_id=1, source_target_pairs={{0,2},{1,3},{2,0},{3,1},{4,6},{5,7},{6,4},{7,5},{8,10},{9,11},{10,... | collective-permute-start | bytes 1572872 | tf_op jit(solution)/shard_map/ppermute | solution.py:243
  613.2 23.5 %collective-permute-start.34 = (f32[64,2048]{1,0:T(8,128)}, f32[64,2048]{1,0:T(8,128)}, u32[]{:S(2)}, u32[]{:S(2)}) collective-permute-start(f32[64,2048]{1,0:T(8,128)} %get-tuple-element.187), channel_id=1, source_target_pairs={{0,2},{1,3},{2,0},{3,1},{4,6},{5,7},{6,4},{7,5},{8,10},{9,11},{10,... | collective-permute-start | bytes 1572872 | tf_op jit(solution)/shard_map/ppermute | solution.py:243
  614.6 18.9 %collective-permute-start.36 = (f32[64,2048]{1,0:T(8,128)}, f32[64,2048]{1,0:T(8,128)}, u32[]{:S(2)}, u32[]{:S(2)}) collective-permute-start(f32[64,2048]{1,0:T(8,128)} %get-tuple-element.188), channel_id=1, source_target_pairs={{0,1},{1,0},{2,3},{3,2},{4,5},{5,4},{6,7},{7,6},{8,9},{9,8},{10,11... | collective-permute-start | bytes 1572872 | tf_op jit(solution)/shard_map/ppermute | solution.py:243
  624.4 20.3 %collective-permute-start.28 = (f32[64,2048]{1,0:T(8,128)}, f32[64,2048]{1,0:T(8,128)}, u32[]{:S(2)}, u32[]{:S(2)}) collective-permute-start(f32[64,2048]{1,0:T(8,128)} %get-tuple-element.186), channel_id=1, source_target_pairs={{0,1},{1,0},{2,3},{3,2},{4,5},{5,4},{6,7},{7,6},{8,9},{9,8},{10,11... | collective-permute-start | bytes 1572872 | tf_op jit(solution)/shard_map/ppermute | solution.py:243
  626.2 21.7 %collective-permute-start.26 = (f32[64,2048]{1,0:T(8,128)}, f32[64,2048]{1,0:T(8,128)S(1)}, u32[]{:S(2)}, u32[]{:S(2)}) collective-permute-start(f32[64,2048]{1,0:T(8,128)} %get-tuple-element.185), channel_id=1, source_target_pairs={{0,2},{1,3},{2,0},{3,1},{4,6},{5,7},{6,4},{7,5},{8,10},{9,11},{10,... | collective-permute-start | bytes 1572872 | tf_op jit(solution)/shard_map/ppermute | solution.py:243
  635.1 32.9 %collective-permute-start.37 = (f32[128,2048]{1,0:T(8,128)S(1)}, f32[128,2048]{1,0:T(8,128)S(1)}, u32[]{:S(2)}, u32[]{:S(2)}) collective-permute-start(f32[128,2048]{1,0:T(8,128)S(1)} %maximum_select_fusion.23), channel_id=1, source_target_pairs={{0,2},{1,3},{2,0},{3,1},{4,6},{5,7},{6,4},{7,5},{8,10},{9,11},{10,... | collective-permute-start | bytes 3145736 | tf_op jit(solution)/shard_map/ppermute | solution.py:243
  638.3 30.0 %collective-permute-start.35 = (f32[128,2048]{1,0:T(8,128)S(1)}, f32[128,2048]{1,0:T(8,128)S(1)}, u32[]{:S(2)}, u32[]{:S(2)}) collective-permute-start(f32[128,2048]{1,0:T(8,128)S(1)} %maximum_select_fusion.22), channel_id=1, source_target_pairs={{0,1},{1,0},{2,3},{3,2},{4,5},{5,4},{6,7},{7,6},{8,9},{9,8},{10,11... | collective-permute-start | bytes 3145736 | tf_op jit(solution)/shard_map/ppermute | solution.py:243
  646.4 43.0 %collective-permute-start.29 = (f32[128,2048]{1,0:T(8,128)S(1)}, f32[128,2048]{1,0:T(8,128)S(1)}, u32[]{:S(2)}, u32[]{:S(2)}) collective-permute-start(f32[128,2048]{1,0:T(8,128)S(1)} %maximum_select_fusion.21), channel_id=1, source_target_pairs={{0,2},{1,3},{2,0},{3,1},{4,6},{5,7},{6,4},{7,5},{8,10},{9,11},{10,... | collective-permute-start | bytes 3145736 | tf_op jit(solution)/shard_map/ppermute | solution.py:243
  648.0 41.6 %collective-permute-start.27 = (f32[128,2048]{1,0:T(8,128)S(1)}, f32[128,2048]{1,0:T(8,128)S(1)}, u32[]{:S(2)}, u32[]{:S(2)}) collective-permute-start(f32[128,2048]{1,0:T(8,128)S(1)} %maximum_select_fusion.20), channel_id=1, source_target_pairs={{0,1},{1,0},{2,3},{3,2},{4,5},{5,4},{6,7},{7,6},{8,9},{9,8},{10,11... | collective-permute-start | bytes 3145736 | tf_op jit(solution)/shard_map/ppermute | solution.py:243
  699.8 50.8 %collective-permute-start.59 = (f32[128,2048]{1,0:T(8,128)S(1)}, f32[128,2048]{1,0:T(8,128)S(1)}, u32[]{:S(2)}, u32[]{:S(2)}) collective-permute-start(f32[128,2048]{1,0:T(8,128)S(1)} %get-tuple-element.117), channel_id=1, source_target_pairs={{0,1},{1,0},{2,3},{3,2},{4,5},{5,4},{6,7},{7,6},{8,9},{9,8},{10,11... | collective-permute-start | bytes 3145736 | tf_op jit(solution)/shard_map/ppermute | solution.py:243
  701.1 49.6 %collective-permute-start.61 = (f32[128,2048]{1,0:T(8,128)S(1)}, f32[128,2048]{1,0:T(8,128)S(1)}, u32[]{:S(2)}, u32[]{:S(2)}) collective-permute-start(f32[128,2048]{1,0:T(8,128)S(1)} %get-tuple-element.118), channel_id=1, source_target_pairs={{0,2},{1,3},{2,0},{3,1},{4,6},{5,7},{6,4},{7,5},{8,10},{9,11},{10,... | collective-permute-start | bytes 3145736 | tf_op jit(solution)/shard_map/ppermute | solution.py:243
  705.2 41.6 %collective-permute-start.47 = (f32[128,2048]{1,0:T(8,128)S(1)}, f32[128,2048]{1,0:T(8,128)S(1)}, u32[]{:S(2)}, u32[]{:S(2)}) collective-permute-start(f32[128,2048]{1,0:T(8,128)S(1)} %get-tuple-element.111), channel_id=1, source_target_pairs={{0,1},{1,0},{2,3},{3,2},{4,5},{5,4},{6,7},{7,6},{8,9},{9,8},{10,11... | collective-permute-start | bytes 3145736 | tf_op jit(solution)/shard_map/ppermute | solution.py:243
  706.1 41.6 %collective-permute-start.49 = (f32[128,2048]{1,0:T(8,128)S(1)}, f32[128,2048]{1,0:T(8,128)S(1)}, u32[]{:S(2)}, u32[]{:S(2)}) collective-permute-start(f32[128,2048]{1,0:T(8,128)S(1)} %get-tuple-element.112), channel_id=1, source_target_pairs={{0,2},{1,3},{2,0},{3,1},{4,6},{5,7},{6,4},{7,5},{8,10},{9,11},{10,... | collective-permute-start | bytes 3145736 | tf_op jit(solution)/shard_map/ppermute | solution.py:243
  748.0 14.9 %collective-permute-start.50 = (f32[64,2048]{1,0:T(8,128)S(1)}, f32[64,2048]{1,0:T(8,128)S(1)}, u32[]{:S(2)}, u32[]{:S(2)}) collective-permute-start(f32[64,2048]{1,0:T(8,128)S(1)} %constant_dynamic-slice_fusion.6), channel_id=1, source_target_pairs={{0,1},{1,0},{2,3},{3,2},{4,5},{5,4},{6,7},{7,6},{8,9},{9,8},{10,11... | collective-permute-start | bytes 1572872 | tf_op jit(solution)/shard_map/ppermute | solution.py:243
  749.0 14.9 %collective-permute-start.48 = (f32[64,2048]{1,0:T(8,128)S(1)}, f32[64,2048]{1,0:T(8,128)S(1)}, u32[]{:S(2)}, u32[]{:S(2)}) collective-permute-start(f32[64,2048]{1,0:T(8,128)S(1)} %constant_dynamic-slice_fusion.7), channel_id=1, source_target_pairs={{0,2},{1,3},{2,0},{3,1},{4,6},{5,7},{6,4},{7,5},{8,10},{9,11},{10,... | collective-permute-start | bytes 1572872 | tf_op jit(solution)/shard_map/ppermute | solution.py:243
  751.1 20.4 %collective-permute-start.62 = (f32[64,2048]{1,0:T(8,128)S(1)}, f32[64,2048]{1,0:T(8,128)S(1)}, u32[]{:S(2)}, u32[]{:S(2)}) collective-permute-start(f32[64,2048]{1,0:T(8,128)S(1)} %constant_dynamic-slice_fusion.2), channel_id=1, source_target_pairs={{0,1},{1,0},{2,3},{3,2},{4,5},{5,4},{6,7},{7,6},{8,9},{9,8},{10,11... | collective-permute-start | bytes 1572872 | tf_op jit(solution)/shard_map/ppermute | solution.py:243
  752.1 20.1 %collective-permute-start.60 = (f32[64,2048]{1,0:T(8,128)S(1)}, f32[64,2048]{1,0:T(8,128)S(1)}, u32[]{:S(2)}, u32[]{:S(2)}) collective-permute-start(f32[64,2048]{1,0:T(8,128)S(1)} %constant_dynamic-slice_fusion.3), channel_id=1, source_target_pairs={{0,2},{1,3},{2,0},{3,1},{4,6},{5,7},{6,4},{7,5},{8,10},{9,11},{10,... | collective-permute-start | bytes 1572872 | tf_op jit(solution)/shard_map/ppermute | solution.py:243
  774.4 17.0 %collective-permute-start.53 = (f32[64,2048]{1,0:T(8,128)S(1)}, f32[64,2048]{1,0:T(8,128)S(1)}, u32[]{:S(2)}, u32[]{:S(2)}) collective-permute-start(f32[64,2048]{1,0:T(8,128)S(1)} %get-tuple-element.178), channel_id=1, source_target_pairs={{0,1},{1,0},{2,3},{3,2},{4,5},{5,4},{6,7},{7,6},{8,9},{9,8},{10,11... | collective-permute-start | bytes 1572872 | tf_op jit(solution)/shard_map/ppermute | solution.py:243
  781.1 17.3 %collective-permute-start.65 = (f32[64,2048]{1,0:T(8,128)S(1)}, f32[64,2048]{1,0:T(8,128)S(1)}, u32[]{:S(2)}, u32[]{:S(2)}) collective-permute-start(f32[64,2048]{1,0:T(8,128)S(1)} %get-tuple-element.180), channel_id=1, source_target_pairs={{0,1},{1,0},{2,3},{3,2},{4,5},{5,4},{6,7},{7,6},{8,9},{9,8},{10,11... | collective-permute-start | bytes 1572872 | tf_op jit(solution)/shard_map/ppermute | solution.py:243
  788.0 20.2 %collective-permute-start.63 = (f32[64,2048]{1,0:T(8,128)S(1)}, f32[64,2048]{1,0:T(8,128)S(1)}, u32[]{:S(2)}, u32[]{:S(2)}) collective-permute-start(f32[64,2048]{1,0:T(8,128)S(1)} %get-tuple-element.179), channel_id=1, source_target_pairs={{0,2},{1,3},{2,0},{3,1},{4,6},{5,7},{6,4},{7,5},{8,10},{9,11},{10,... | collective-permute-start | bytes 1572872 | tf_op jit(solution)/shard_map/ppermute | solution.py:243
  791.5 39.3 %collective-permute-start.54 = (f32[128,2048]{1,0:T(8,128)S(1)}, f32[128,2048]{1,0:T(8,128)S(1)}, u32[]{:S(2)}, u32[]{:S(2)}) collective-permute-start(f32[128,2048]{1,0:T(8,128)S(1)} %maximum_select_fusion.27), channel_id=1, source_target_pairs={{0,2},{1,3},{2,0},{3,1},{4,6},{5,7},{6,4},{7,5},{8,10},{9,11},{10,... | collective-permute-start | bytes 3145736 | tf_op jit(solution)/shard_map/ppermute | solution.py:243
  797.4 33.6 %collective-permute-start.52 = (f32[128,2048]{1,0:T(8,128)S(1)}, f32[128,2048]{1,0:T(8,128)S(1)}, u32[]{:S(2)}, u32[]{:S(2)}) collective-permute-start(f32[128,2048]{1,0:T(8,128)S(1)} %maximum_select_fusion.26), channel_id=1, source_target_pairs={{0,1},{1,0},{2,3},{3,2},{4,5},{5,4},{6,7},{7,6},{8,9},{9,8},{10,11... | collective-permute-start | bytes 3145736 | tf_op jit(solution)/shard_map/ppermute | solution.py:243
  798.5 53.9 %collective-permute-start.66 = (f32[128,2048]{1,0:T(8,128)S(1)}, f32[128,2048]{1,0:T(8,128)S(1)}, u32[]{:S(2)}, u32[]{:S(2)}) collective-permute-start(f32[128,2048]{1,0:T(8,128)S(1)} %maximum_select_fusion.31), channel_id=1, source_target_pairs={{0,2},{1,3},{2,0},{3,1},{4,6},{5,7},{6,4},{7,5},{8,10},{9,11},{10,... | collective-permute-start | bytes 3145736 | tf_op jit(solution)/shard_map/ppermute | solution.py:243
  808.4 44.3 %collective-permute-start.64 = (f32[128,2048]{1,0:T(8,128)S(1)}, f32[128,2048]{1,0:T(8,128)S(1)}, u32[]{:S(2)}, u32[]{:S(2)}) collective-permute-start(f32[128,2048]{1,0:T(8,128)S(1)} %maximum_select_fusion.30), channel_id=1, source_target_pairs={{0,1},{1,0},{2,3},{3,2},{4,5},{5,4},{6,7},{7,6},{8,9},{9,8},{10,11... | collective-permute-start | bytes 3145736 | tf_op jit(solution)/shard_map/ppermute | solution.py:243
  (79 other events, 974.7 us)
Sparse Core Ops, SparseCore 0:
  538.8 145.3 reduce-scatter.4
  686.5 77.3 reduce-scatter.6
  766.2 77.9 reduce-scatter.8
  846.4 280.8 reduce-scatter.10

commit v4 on v3

--- a/solution.py
+++ b/solution.py
@@ -1,4 +1,5 @@
 import functools
+from types import SimpleNamespace
 
 import jax
 import jax.numpy as jnp
@@ -17,6 +18,8 @@
 ROPE_BASE = 130000.0
 MASKED = -1e30
 
+
+DP, TP = "dp", "tensor"
 
 F32 = jnp.float32
 BF16 = jnp.bfloat16
@@ -96,18 +99,19 @@
         attn_out[start:end, :] = jnp.concatenate(outs, axis=1).astype(BF16)
 
 
-def attend(x, gain, wq, wk, wv, cos, sin, mask):
-    rows, width = x.shape
+def attend(x, row_block, gain, wq, wk, wv, cos, sin, mask):
+    rows, width = mask.shape[0], x.shape[1]
     cols = wq.shape[1]
     step = min(256, cols)
     column = pl.BlockSpec((rows, step), lambda i: (0, i))
     whole = lambda shape: pl.BlockSpec(shape, lambda i: (0, 0))
+    chunk = lambda v: pl.BlockSpec((rows, v.shape[1]), lambda i: (row_block, 0))
     weight = pl.BlockSpec((width, step), lambda i: (0, i))
     return pl.pallas_call(
         attend_body,
         grid=(cols // step,),
-        in_specs=[whole((rows, width)), whole((1, width)), weight, weight, weight]
-        + [whole(cos.shape), whole(cos.shape), whole((rows, rows))],
+        in_specs=[chunk(x), whole((1, width)), weight, weight, weight]
+        + [chunk(cos), chunk(sin), whole((rows, rows))],
         out_specs=[whole((rows, width))] + [column] * 4,
         out_shape=[jax.ShapeDtypeStruct((rows, width), BF16)]
         + [jax.ShapeDtypeStruct((rows, cols), BF16)] * 4,
@@ -116,7 +120,6 @@
             bytes_accessed=4 * rows * width + 6 * width * cols + 8 * rows * cols,
             transcendentals=rows * rows * cols // HD,
         ),
-        name="attend",
     )(x, gain.reshape(1, width), wq, wk, wv, cos, sin, mask)
 
 
@@ -142,18 +145,19 @@
     out[2] = jnp.concatenate(v_list, axis=1).astype(BF16)
 
 
-def attend_back(hidden, wo, q, k, v, attn, cos, sin, mask, after):
+def attend_back(hidden, row_block, wo, q, k, v, attn, cos, sin, mask, after):
     rows, width = hidden.shape
     cols = wo.shape[0]
     step = min(256, cols)
     column = pl.BlockSpec((rows, step), lambda i: (0, i))
     whole = lambda shape: pl.BlockSpec(shape, lambda i: (0, 0))
+    chunk = lambda v: pl.BlockSpec((rows, v.shape[1]), lambda i: (row_block, 0))
     return pl.pallas_call(
         attend_back_body,
         grid=(cols // step,),
         in_specs=[whole((rows, width)), pl.BlockSpec((step, width), lambda i: (i, 0))]
         + [column] * 4
-        + [whole(cos.shape), whole(cos.shape), whole((rows, rows))]
+        + [chunk(cos), chunk(sin), whole((rows, rows))]
         + [pl.BlockSpec(memory_space=pl.ANY)] * len(after),
         out_specs=pl.BlockSpec((3, rows, step), lambda i: (0, 0, i)),
         out_shape=jax.ShapeDtypeStruct((3, rows, cols), BF16),
@@ -162,17 +166,47 @@
             bytes_accessed=2 * rows * width + 2 * width * cols + 14 * rows * cols,
             transcendentals=rows * rows * cols // HD,
         ),
-        name="attend_back",
     )(hidden, wo, q, k, v, attn, cos, sin, mask, *after)
 
 
-def outer_body(shape, has_add, which, *refs):
+def flip_body(value, keep, out):
+    kept = jnp.where(keep[...] > 0, value[...].astype(F32), 0.0)
+    out[...] = kept.astype(BF16).T
+
+
+def flip_rows(value, keep):
+    rows, width = value.shape
+    step = min(512, width)
+    return pl.pallas_call(
+        flip_body,
+        grid=(width // step,),
+        in_specs=[
+            pl.BlockSpec((rows, step), lambda i: (0, i)),
+            pl.BlockSpec((rows, 1), lambda i: (0, 0)),
+        ],
+        out_specs=pl.BlockSpec((step, rows), lambda i: (i, 0)),
+        out_shape=jax.ShapeDtypeStruct((width, rows), BF16),
+        cost_estimate=pl.CostEstimate(
+            flops=rows * width, bytes_accessed=4 * rows * width, transcendentals=0
+        ),
+    )(value, keep.reshape(rows, 1))
+
+
+def outer_body(shape, has_add, flipped, which, *refs):
     out, column, at = refs[-1], 0, 0
     adder = refs[-2] if has_add else None
     for count in shape:
-        lefts = [refs[at + c][...].T for c in range(count)]
-        rights = refs[at + count : at + 2 * count]
-        at += 2 * count
+        if flipped:
+            rights = refs[at + 1 : at + 1 + count]
+            lefts, start = [], 0
+            for right in rights:
+                lefts.append(refs[at][:, start : start + right.shape[0]])
+                start += right.shape[0]
+            at += 1 + count
+        else:
+            lefts = [refs[at + c][...].T for c in range(count)]
+            rights = refs[at + count : at + 2 * count]
+            at += 2 * count
         planes = rights[0].shape[0] if len(rights[0].shape) == 3 else 1
         width = rights[0].shape[-1]
         tile = min(512, width)
@@ -191,13 +225,16 @@
                 column += tile
 
 
-def outer(groups, which, pieces, add=None, part=(0, 1)):
-    piece = groups[0][0][0].shape[1] // pieces
+def outer(groups, which, pieces, add=None, part=(0, 1), flipped=False):
+    piece = groups[0][0][0].shape[0 if flipped else 1] // pieces
     index, parts = part
     specs, args, out_cols, work, moved = [], [], 0, 0, 0
     for lefts, rights in groups:
         for v in lefts:
-            specs.append(pl.BlockSpec((v.shape[0], piece), lambda j, w: (0, 2 * j + w[0])))
+            if flipped:
+                specs.append(pl.BlockSpec((piece, v.shape[1]), lambda j, w: (2 * j + w[0], 0)))
+            else:
+                specs.append(pl.BlockSpec((v.shape[0], piece), lambda j, w: (0, 2 * j + w[0])))
             moved += v.size
         for v in rights:
             if v.ndim == 3:
@@ -207,7 +244,7 @@
                 cols = v.shape[1] // parts
                 specs.append(pl.BlockSpec((v.shape[0], cols), lambda j, w: (0, index)))
             moved += v.size // parts * 2
-        work += sum(v.shape[0] for v in lefts) * cols
+        work += sum(v.shape[-2] for v in rights) * cols
         out_cols += cols
         args += list(lefts) + list(rights)
     out_rows = pieces // 2 * piece
@@ -216,7 +253,7 @@
         specs.append(out_spec)
         args.append(add)
     return pl.pallas_call(
-        functools.partial(outer_body, [len(g[0]) for g in groups], add is not None),
+        functools.partial(outer_body, [len(g[1]) for g in groups], add is not None, flipped),
         grid_spec=pltpu.PrefetchScalarGridSpec(
             num_scalar_prefetch=1,
             grid=(pieces // 2,),
@@ -229,6 +266,7 @@
             bytes_accessed=moved + 4 * out_rows * out_cols,
             transcendentals=0,
         ),
+        name="outer",
     )(which.reshape(1).astype(jnp.int32), *args)
 
 
@@ -303,8 +341,8 @@
         row_count, width = block_input.shape
         head_count = query_weight.shape[1] // HD
         head_cols = head_count * HD
-        tensor = Cube("tensor", tensor_size)
-        data = Cube("dp", dp_size)
+        tensor = Cube(TP, tensor_size)
+        data = Cube(DP, dp_size)
         core = data.bit_of(1)
         pair_lists = [[i for i in range(dp_size) if i % 2 == c] for c in range(2)]
 
@@ -366,17 +404,17 @@
                 [lax.dynamic_slice_in_dim(value, start, size, 0) for start in starts], axis=0
             )
 
-        def core_sum(groups, part=(0, 1)):
-            away = outer(groups, 1 - core, dp_size, part=part)
+        def core_sum(groups, part=(0, 1), flipped=False):
+            away = outer(groups, 1 - core, dp_size, part=part, flipped=flipped)
             got = data.swap(away, 1)
-            return outer(groups, core, dp_size, add=got, part=part)
+            return outer(groups, core, dp_size, add=got, part=part, flipped=flipped)
 
         def z_scatter(value):
             return lax.psum_scatter(
-                value, "dp", scatter_dimension=0, tiled=True, axis_index_groups=pair_lists
-            )
-
-        first_block = lax.axis_index("dp") * (row_count // BLK)
+                value, DP, scatter_dimension=0, tiled=True, axis_index_groups=pair_lists
+            )
+
+        first_block = lax.axis_index(DP) * (row_count // BLK)
         owners = jnp.broadcast_to(block_owner[:, None], (row_count // BLK, BLK)).reshape(-1)
         row_index = jnp.arange(row_count, dtype=jnp.int32)
         positions = (row_index // BLK + first_block - owners) * BLK + row_index % BLK
@@ -389,7 +427,10 @@
             rows = jnp.where(
                 token_mask[lo:hi, None] > 0, cotangent[lo:hi], jnp.zeros_like(cotangent[lo:hi])
             )
-            cos_g, sin_g = cosine[lo:hi], sine[lo:hi]
+            aligned = lo % size == 0
+            cut = (lambda v: v) if aligned else (lambda v, lo=lo, hi=hi: v[lo:hi])
+            row_block = lo // size if aligned else 0
+            cos_g, sin_g = cut(cosine), cut(sine)
             own_g, pos_g, mask_g = owners[lo:hi], positions[lo:hi], token_mask[lo:hi]
             allowed = (
                 (own_g[:, None] == own_g[None, :])
@@ -397,7 +438,7 @@
                 & ((mask_g[None, :] > 0) | (pos_g[None, :] == 0))
             ).astype(F32)
             act, q, k, v, flat = attend(
-                block_input[lo:hi], attention_gain, query_weight, key_weight, value_weight,
+                cut(block_input), row_block, attention_gain, query_weight, key_weight, value_weight,
                 cos_g, sin_g, allowed,
             )
             added = scatter_rows(
@@ -406,67 +447,68 @@
             x_own = own_rows(block_input[lo:hi]).astype(F32)
             hid = x_own + added
             inv_two = lax.rsqrt(jnp.mean(hid * hid, axis=-1, keepdims=True) + NORM_EPS)
-            after = saved[-1]["act_two"] if saved else None
+            after = saved[-1].act_two if saved else None
             unit = gather_rows(hid * inv_two, size, after)
             act_two = (unit * feedforward_gain).astype(BF16)
             saved.append(
-                dict(q=q, k=k, v=v, allowed=allowed, flat=flat, act=act, rows=rows, x_f=x_f,
-                     cos=cos_g, sin=sin_g, x_own=x_own, hid=hid, added=added, inv_two=inv_two,
+                SimpleNamespace(q=q, k=k, v=v, allowed=allowed, flat=flat, act=act, rows=rows, x_f=x_f,
+                     cos=cos_g, sin=sin_g, row_block=row_block, x_own=x_own, hid=hid, added=added, inv_two=inv_two,
                      act_two=act_two)
             )
 
-        def chunks(key):
-            return [s[key] for s in saved]
-
         for s in saved:
-            s["inner_grad"] = mm_nt(s["rows"], down_weight)
-            s["gate_pre"] = mm(s["act_two"], gate_weight)
-            s["up_pre"] = mm(s["act_two"], up_weight)
-            s["sig"] = jax.nn.sigmoid(s["gate_pre"])
-            s["inner"] = (s["gate_pre"] * s["sig"] * s["up_pre"]).astype(BF16)
-        down_parts = [core_sum([(chunks("rows"), chunks("inner"))], (i, 2)) for i in range(2)]
+            s.inner_grad = mm_nt(s.rows, down_weight)
+            s.gate_pre = mm(s.act_two, gate_weight)
+            s.up_pre = mm(s.act_two, up_weight)
+            s.sig = jax.nn.sigmoid(s.gate_pre)
+            s.inner = (s.gate_pre * s.sig * s.up_pre).astype(BF16)
+        flipped_rows = flip_rows(cotangent, token_mask)
+        down_parts = [
+            core_sum([([flipped_rows], [s.inner for s in saved])], (i, 2), True)
+            for i in range(2)
+        ]
         down_sums = [z_scatter(v) for v in down_parts]
 
         gain_parts = jnp.zeros((width,), F32)
         for index, ((lo, hi), s) in enumerate(zip(bounds, saved)):
             size = hi - lo
-            rows = s["rows"]
-            inner_grad = s["inner_grad"]
-            gate_pre, up_pre, sig = s["gate_pre"], s["up_pre"], s["sig"]
+            rows = s.rows
+            inner_grad = s.inner_grad
+            gate_pre, up_pre, sig = s.gate_pre, s.up_pre, s.sig
             if index:
                 gate_pre, up_pre, _ = lax.optimization_barrier((gate_pre, up_pre, down_parts))
             gate_back = (inner_grad * up_pre * sig * (1.0 + gate_pre * (1.0 - sig))).astype(BF16)
             up_back = (inner_grad * gate_pre * sig).astype(BF16)
-            s["gate_back"], s["up_back"] = gate_back, up_back
+            s.gate_back, s.up_back = gate_back, up_back
             part = scatter_rows(
                 lambda st, n, a=gate_back, b=up_back: mm_nt(rows_of(a, st, n), gate_weight)
                 + mm_nt(rows_of(b, st, n), up_weight),
                 size,
             )
-            s["part"] = part
-            unit = s["hid"] * s["inv_two"]
+            s.part = part
+            unit = s.hid * s.inv_two
             gain_parts = gain_parts + jnp.sum(part * unit, axis=0)
             scaled = part * feedforward_gain
-            back = s["inv_two"] * (
+            back = s.inv_two * (
                 scaled - unit * jnp.mean(scaled * unit, axis=-1, keepdims=True)
             )
-            s["hidden_grad"] = own_rows(rows).astype(F32) + back
-            after = saved[index - 1]["hidden_back"] if index else None
+            s.hidden_grad = own_rows(rows).astype(F32) + back
+            after = saved[index - 1].hidden_back if index else None
             full = gather_rows(back, size, after)
-            s["hidden_back"] = (rows.astype(F32) + full).astype(BF16)
+            s.hidden_back = (rows.astype(F32) + full).astype(BF16)
 
         both_part = core_sum(
-            [(chunks("act_two"), chunks("gate_back")), (chunks("act_two"), chunks("up_back"))],
+            [([s.act_two for s in saved], [s.gate_back for s in saved]), ([s.act_two for s in saved], [s.up_back for s in saved])],
         )
         both_sum = z_scatter(both_part)
 
         outs = []
         for s in saved:
-            size = s["rows"].shape[0]
-            late_inner, _ = lax.optimization_barrier((s["inner"], saved[-1]["part"]))
+            size = s.rows.shape[0]
+            late_inner, _ = lax.optimization_barrier((s.inner, saved[-1].part))
             mlp = scatter_rows(lambda st, n, a=late_inner: mm(rows_of(a, st, n), down_weight), size)
-            full = gather_rows(s["added"] + mlp, size)
-            outs.append((s["x_f"] + full).astype(BF16))
+            full = gather_rows(s.added + mlp, size)
+            outs.append((s.x_f + full).astype(BF16))
         block_output = jnp.concatenate(outs, axis=0)
 
         first_parts = jnp.zeros((width,), F32)
@@ -474,10 +516,10 @@
         for (lo, hi), s in zip(bounds, saved):
             size = hi - lo
             back3 = attend_back(
-                s["hidden_back"], output_weight, s["q"], s["k"], s["v"], s["flat"],
-                s["cos"], s["sin"], s["allowed"], (both_part,),
-            )
-            s["qkv_back"] = back3
+                s.hidden_back, s.row_block, output_weight, s.q, s.k, s.v, s.flat,
+                s.cos, s.sin, s.allowed, (both_part,),
+            )
+            s.qkv_back = back3
             q_back, k_back, v_back = back3[0], back3[1], back3[2]
             part = scatter_rows(
                 lambda st, n, a=q_back, b=k_back, c=v_back: mm_nt(rows_of(a, st, n), query_weight)
@@ -485,17 +527,17 @@
                 + mm_nt(rows_of(c, st, n), value_weight),
                 size,
             )
-            x_own = s["x_own"]
+            x_own = s.x_own
             inv_one = lax.rsqrt(jnp.mean(x_own * x_own, axis=-1, keepdims=True) + NORM_EPS)
             unit = x_own * inv_one
             first_parts = first_parts + jnp.sum(part * unit, axis=0)
             scaled = part * attention_gain
             back = inv_one * (scaled - unit * jnp.mean(scaled * unit, axis=-1, keepdims=True))
-            input_grads.append(gather_rows(s["hidden_grad"] + back, size))
+            input_grads.append(gather_rows(s.hidden_grad + back, size))
         input_gradient = jnp.concatenate(input_grads, axis=0)
 
         last_part = core_sum(
-            [(chunks("act"), chunks("qkv_back")), (chunks("hidden_back"), chunks("flat"))]
+            [([s.act for s in saved], [s.qkv_back for s in saved]), ([s.hidden_back for s in saved], [s.flat for s in saved])]
         )
         last_sum = z_scatter(last_part)
         down_sums, both_sum, _ = lax.optimization_barrier((down_sums, both_sum, last_part))
@@ -509,7 +551,7 @@
 
         gains = data.total(tensor.total(jnp.stack([first_parts, gain_parts])))
         gain_piece = width // dp_size
-        gains = lax.dynamic_slice_in_dim(gains, lax.axis_index("dp") * gain_piece, gain_piece, 1)
+        gains = lax.dynamic_slice_in_dim(gains, lax.axis_index(DP) * gain_piece, gain_piece, 1)
         return (
             block_output,
             input_gradient,
@@ -528,39 +570,39 @@
 
 
 def solution(mesh):
-    sizes = (mesh.shape["dp"], mesh.shape["tensor"])
+    sizes = (mesh.shape[DP], mesh.shape[TP])
     body = on_device(sizes)
 
     return jax.shard_map(
         body,
         mesh=mesh,
         in_specs=(
-            P("dp", None),
-            P("dp"),
-            P("dp"),
+            P(DP, None),
+            P(DP),
+            P(DP),
             P(),
-            P(None, "tensor"),
-            P(None, "tensor"),
-            P(None, "tensor"),
-            P("tensor", None),
+            P(None, TP),
+            P(None, TP),
+            P(None, TP),
+            P(TP, None),
             P(),
-            P(None, "tensor"),
-            P(None, "tensor"),
-            P("tensor", None),
-            P("dp", None),
+            P(None, TP),
+            P(None, TP),
+            P(TP, None),
+            P(DP, None),
         ),
         out_specs=(
-            P("dp", None),
-            P("dp", None),
-            P("dp"),
-            P("dp", "tensor"),
-            P("dp", "tensor"),
-            P("dp", "tensor"),
-            P("tensor", "dp"),
-            P("dp"),
-            P("dp", "tensor"),
-            P("dp", "tensor"),
-            P("tensor", "dp"),
+            P(DP, None),
+            P(DP, None),
+            P(DP),
+            P(DP, TP),
+            P(DP, TP),
+            P(DP, TP),
+            P(TP, DP),
+            P(DP),
+            P(DP, TP),
+            P(DP, TP),
+            P(TP, DP),
         ),
         check_vma=False,
     )

time: 1150 us -> 1150 us (level)
    pallas_call x10 -> x11, Pallas kernels: 118 us -> 123 us  [the longest x8 84.4 us: outer(): pl.pallas_call(functools.partial(outer_body, [len(g[1]) for g in groups],...]
  transfers between devices with their start and end apart: 77 -> 77, of which waited for: 48 -> 48; matrix products, arithmetic and copies ran while one was open for 13% -> 14% of each run, Pallas kernels for 3% -> 3%
where the time goes in v4:
time: 1150 us; the launch traced here: 1140 us
  waiting for transfers between devices  668 us (58%)
  Pallas kernels  157 us (14%)
  matrix products  117 us (10%)
  starting transfers between devices  74.5 us (6%)
  other arithmetic  57.9 us (5%)
  local copies, waits for them, and re-layouts  50.4 us (4%)
  between operations  16.2 us (1%)
    ppermute x73, waiting for transfers between devices, swap(): lax.ppermute(value, self.axis, [(i, i ^ bit) for i in range(self.size)])  398 us
    reduce_scatter x4, waiting for transfers between devices, z_scatter(): lax.psum_scatter(value, DP, scatter_dimension=0, tiled=True, axis_index_g...  268 us
    pallas_call x8, Pallas kernels, outer(): pl.pallas_call(functools.partial(outer_body, [len(g[1]) for g in groups],...  84.4 us
    ppermute x73, starting transfers between devices, swap(): lax.ppermute(value, self.axis, [(i, i ^ bit) for i in range(self.size)])  74.1 us
    dot_general x22, matrix products, mm_nt(): lax.dot_general(a, b, (((1,), (1,)), ((), ())), preferred_element_type=F32)  66.7 us
    dot_general x12, matrix products, mm(): return jnp.dot(a, b, preferred_element_type=F32)  49.8 us
    pallas_call x2, Pallas kernels, attend_back(): pl.pallas_call(attend_back_body, grid=(cols // step,), in_specs=[whole((r...  33.8 us
    pallas_call x2, Pallas kernels, attend(): pl.pallas_call(attend_body, grid=(cols // step,), in_specs=[chunk(x), who...  33 us
  transfers between devices with their start and end apart: 77, of which 48 were waited for; matrix products, arithmetic and copies ran while one was open for 14% of the time, Pallas kernels for 3%

profile of v4, /device:TPU:0, one launch (start us, length us, event | category | flops | bytes accessed | tf_op | source)
XLA Modules:
  0.0 1141.0 jit_solution(4872746310223618710)
XLA Ops:
  9.7 3.1 fusion.70
  14.4 16.3 %shard_map.213 = (bf16[512,2048]{1,0:T(8,128)(2,1)}, bf16[512,512]{1,0:T(8,128)(2,1)}, bf16[512,512]{1,0:T(8,128)(2,1)}, bf16[512,512]{1,0:T(8,128)(2,1)}, bf16[512,512]{1,0:T(8,128)(2,1)}) custom-call(bf16[1024,2048]{1,0:T(8,128)(2,1)} %x.3, f32[1,2048]{1,0:T(1,128)} %bitcast.115, bf16[2048,512]{1,0:T(8,128)(2,1)} %wq.3, bf16[2048,512]{1,0:T(8,128)(2,1)} %wk.3, ...), custom_call_target="tpu_custom_call" | custom-call | flops 5368709120 | bytes 12582912 | tf_op jit(solution)/shard_map/pallas_call | solution.py:110
  34.0 3.0 collective-permute-start.8
  38.5 16.7 %shard_map.212 = (bf16[512,2048]{1,0:T(8,128)(2,1)}, bf16[512,512]{1,0:T(8,128)(2,1)}, bf16[512,512]{1,0:T(8,128)(2,1)}, bf16[512,512]{1,0:T(8,128)(2,1)}, bf16[512,512]{1,0:T(8,128)(2,1)}) custom-call(bf16[1024,2048]{1,0:T(8,128)(2,1)} %x.3, f32[1,2048]{1,0:T(1,128)} %bitcast.116, bf16[2048,512]{1,0:T(8,128)(2,1)} %wq.3, bf16[2048,512]{1,0:T(8,128)(2,1)} %wk.3, ...), custom_call_target="tpu_custom_call" | custom-call | flops 5368709120 | bytes 12582912 | tf_op jit(solution)/shard_map/pallas_call | solution.py:110
  59.1 4.8 fusion.175
  72.5 10.7 collective-permute-done
  92.7 8.5 collective-permute-done.3
  102.7 7.9 collective-permute-done.11
  118.0 8.8 collective-permute-done.6
  130.9 6.3 fusion.200
  138.2 5.9 shard_map.214.refs_0_
  150.0 12.6 %collective-permute-done.7 = f32[128,2048]{1,0:T(8,128)} collective-permute-done((f32[128,2048]{1,0:T(8,128)S(1)}, f32[128,2048]{1,0:T(8,128)}, u32[]{:S(2)}, u32[]{:S(2)}) %collective-permute-start.7) | collective-permute-done | bytes 1048608 | tf_op jit(solution)/shard_map/ppermute | solution.py:281
  167.6 14.1 %collective-permute-done.15 = f32[128,2048]{1,0:T(8,128)S(1)} collective-permute-done((f32[128,2048]{1,0:T(8,128)S(1)}, f32[128,2048]{1,0:T(8,128)S(1)}, u32[]{:S(2)}, u32[]{:S(2)}) %collective-permute-start.15) | collective-permute-done | bytes 1048608 | tf_op jit(solution)/shard_map/ppermute | solution.py:281
  181.7 6.1 fusion.197
  188.9 4.6 fusion.199
  195.6 6.9 multiply_convert_fusion.4
  202.5 10.8 multiply_convert_fusion
  213.3 6.3 outer.8
  219.6 6.3 outer.10
  226.4 9.6 fusion.198
  239.2 7.1 fusion.61
  246.3 7.2 outer.9
  253.6 7.2 outer.11
  260.8 7.3 multiply_convert_fusion.2
  268.0 15.7 %outer.12 = f32[1024,4096]{1,0:T(8,128)} custom-call(s32[1]{0:T(128)} %bitcast.6.which, bf16[512,2048]{1,0:T(8,128)(2,1)} %copy-done.1, bf16[512,2048]{1,0:T(8,128)(2,1)} %copy-done.2, bf16[512,2048]{1,0:T(8,128)(2,1)} %get-tuple-element.104.refs_2_, bf16[512,2048]{1,0:T(8,128)(2,1)} %get-tuple-element.102.refs_3_, bf16[512,2048]{1,0:T(8,128)(2,1)} %copy-done.1, ...), custom_call_target="tpu_custom_call" | custom-call | flops 8589934592 | bytes 29360128 | tf_op jit(solution)/shard_map/outer/pallas_call | solution.py:255
  283.8 6.7 convolution_add_fusion.8
  292.8 5.7 fusion.54
  298.5 5.9 convolution_add_fusion.9
  304.5 11.9 %collective-permute-done.38 = f32[128,2048]{1,0:T(8,128)S(1)} collective-permute-done((f32[128,2048]{1,0:T(8,128)S(1)}, f32[128,2048]{1,0:T(8,128)S(1)}, u32[]{:S(2)}, u32[]{:S(2)}) %collective-permute-start.38) | collective-permute-done | bytes 1048608 | tf_op jit(solution)/shard_map/ppermute | solution.py:281
  319.3 11.1 collective-permute-done.41
  335.7 6.0 convolution_add_fusion.10
  346.4 5.8 convolution_add_fusion.11
  352.1 13.2 %collective-permute-done.18 = f32[128,2048]{1,0:T(8,128)S(1)} collective-permute-done((f32[128,2048]{1,0:T(8,128)S(1)}, f32[128,2048]{1,0:T(8,128)S(1)}, u32[]{:S(2)}, u32[]{:S(2)}) %collective-permute-start.18) | collective-permute-done | bytes 1048608 | tf_op jit(solution)/shard_map/ppermute | solution.py:281
  368.6 8.5 collective-permute-done.21
  381.6 8.9 collective-permute-done.44
  395.0 11.0 collective-permute-done.57
  407.8 20.1 %collective-permute-done.55 = f32[64,2048]{1,0:T(8,128)S(1)} collective-permute-done((f32[64,2048]{1,0:T(8,128)S(1)}, f32[64,2048]{1,0:T(8,128)S(1)}, u32[]{:S(2)}, u32[]{:S(2)}) %collective-permute-start.55) | collective-permute-done | bytes 524320 | tf_op jit(solution)/shard_map/ppermute | solution.py:281
  432.6 13.2 %collective-permute-done.58 = f32[128,2048]{1,0:T(8,128)S(1)} collective-permute-done((f32[128,2048]{1,0:T(8,128)S(1)}, f32[128,2048]{1,0:T(8,128)S(1)}, u32[]{:S(2)}, u32[]{:S(2)}) %collective-permute-start.58) | collective-permute-done | bytes 1048608 | tf_op jit(solution)/shard_map/ppermute | solution.py:281
  448.5 19.9 %outer.13.rest_0_ = f32[1024,4096]{1,0:T(8,128)} custom-call(s32[1]{0:T(128)} %bitcast.4.which, bf16[512,2048]{1,0:T(8,128)(2,1)} %copy-done.1, bf16[512,2048]{1,0:T(8,128)(2,1)} %copy-done.2, bf16[512,2048]{1,0:T(8,128)(2,1)} %get-tuple-element.104.refs_2_, bf16[512,2048]{1,0:T(8,128)(2,1)} %get-tuple-element.102.refs_3_, bf16[512,2048]{1,0:T(8,128)(2,1)} %copy-done.1, ...), custom_call_target="tpu_custom_call" | custom-call | flops 8589934592 | bytes 29360128 | tf_op jit(solution)/shard_map/outer/pallas_call | solution.py:255
  468.4 17.0 %shard_map.215.refs_2_ = bf16[3,512,512]{2,1,0:T(8,128)(2,1)} custom-call(bf16[512,2048]{1,0:T(8,128)(2,1)} %fusion.4.hidden.refs_4_, bf16[512,2048]{1,0:T(8,128)(2,1)} %wo.3, bf16[512,512]{1,0:T(8,128)(2,1)} %get-tuple-element.46.q_in, bf16[512,512]{1,0:T(8,128)(2,1)} %get-tuple-element.47.k_in, bf16[512,512]{1,0:T(8,128)(2,1)} %get-tuple-element.48.v_in, ...), custom_call_target="tpu_custom_call" | custom-call | flops 6442450944 | bytes 7864320 | tf_op jit(solution)/shard_map/pallas_call | solution.py:155
  485.4 16.8 %shard_map.216.refs_3_ = bf16[3,512,512]{2,1,0:T(8,128)(2,1)} custom-call(bf16[512,2048]{1,0:T(8,128)(2,1)} %fusion.5.hidden.refs_5_, bf16[512,2048]{1,0:T(8,128)(2,1)} %wo.3, bf16[512,512]{1,0:T(8,128)(2,1)} %get-tuple-element.53.q_in, bf16[512,512]{1,0:T(8,128)(2,1)} %get-tuple-element.54.k_in, bf16[512,512]{1,0:T(8,128)(2,1)} %get-tuple-element.55.v_in, ...), custom_call_target="tpu_custom_call" | custom-call | flops 6442450944 | bytes 7864320 | tf_op jit(solution)/shard_map/pallas_call | solution.py:155
  502.2 9.8 outer.14
  512.1 13.5 %collective-permute-done.72.refs_8_ = f32[1024,2048]{1,0:T(8,128)} collective-permute-done((f32[1024,2048]{1,0:T(8,128)}, f32[1024,2048]{1,0:T(8,128)}, u32[]{:S(2)}, u32[]{:S(2)}) %collective-permute-start.72) | collective-permute-done | bytes 8388640 | tf_op jit(solution)/shard_map/ppermute | solution.py:281
  525.6 11.9 %outer.15 = f32[1024,2048]{1,0:T(8,128)} custom-call(s32[1]{0:T(128)} %bitcast.4.which, bf16[512,2048]{1,0:T(8,128)(2,1)} %get-tuple-element.56.refs_0_, bf16[512,2048]{1,0:T(8,128)(2,1)} %get-tuple-element.57.refs_1_, bf16[3,512,512]{2,1,0:T(8,128)(2,1)} %shard_map.215.refs_2_, bf16[3,512,512]{2,1,0:T(8,128)(2,1)} %shard_map.216.refs_3_, ...), custom_call_target="tpu_custom_call" | custom-call | flops 4294967296 | bytes 16777216 | tf_op jit(solution)/shard_map/outer/pallas_call | solution.py:255
  541.8 6.5 fusion.50
  550.2 5.9 fusion.42
  564.0 10.7 collective-permute-done.30
  577.8 19.4 %collective-permute-done.22 = f32[128,2048]{1,0:T(8,128)S(1)} collective-permute-done((f32[128,2048]{1,0:T(8,128)S(1)}, f32[128,2048]{1,0:T(8,128)S(1)}, u32[]{:S(2)}, u32[]{:S(2)}) %collective-permute-start.22) | collective-permute-done | bytes 1048608 | tf_op jit(solution)/shard_map/ppermute | solution.py:281
  600.2 8.2 collective-permute-done.33
  611.3 8.3 collective-permute-done.25
  624.3 6.7 collective-permute-done.36
  634.9 7.3 collective-permute-done.28
  645.0 20.3 %collective-permute-done.37 = f32[128,2048]{1,0:T(8,128)S(1)} collective-permute-done((f32[128,2048]{1,0:T(8,128)S(1)}, f32[128,2048]{1,0:T(8,128)S(1)}, u32[]{:S(2)}, u32[]{:S(2)}) %collective-permute-start.37) | collective-permute-done | bytes 1048608 | tf_op jit(solution)/shard_map/ppermute | solution.py:281
  665.6 20.9 %collective-permute-done.29 = f32[128,2048]{1,0:T(8,128)S(1)} collective-permute-done((f32[128,2048]{1,0:T(8,128)S(1)}, f32[128,2048]{1,0:T(8,128)S(1)}, u32[]{:S(2)}, u32[]{:S(2)}) %collective-permute-start.29) | collective-permute-done | bytes 1048608 | tf_op jit(solution)/shard_map/ppermute | solution.py:281
  708.7 35.1 %collective-permute-done.47 = f32[128,2048]{1,0:T(8,128)S(1)} collective-permute-done((f32[128,2048]{1,0:T(8,128)S(1)}, f32[128,2048]{1,0:T(8,128)S(1)}, u32[]{:S(2)}, u32[]{:S(2)}) %collective-permute-start.47) | collective-permute-done | bytes 1048608 | tf_op jit(solution)/shard_map/ppermute | solution.py:281
  750.1 10.1 collective-permute-done.50
  761.4 6.9 collective-permute-done.62
  789.1 4.8 collective-permute-done.51
  796.1 9.0 collective-permute-done.63
  806.5 21.1 %collective-permute-done.54 = f32[128,2048]{1,0:T(8,128)S(1)} collective-permute-done((f32[128,2048]{1,0:T(8,128)S(1)}, f32[128,2048]{1,0:T(8,128)S(1)}, u32[]{:S(2)}, u32[]{:S(2)}) %collective-permute-start.54) | collective-permute-done | bytes 1048608 | tf_op jit(solution)/shard_map/ppermute | solution.py:281
  828.0 21.3 %collective-permute-done.66 = f32[128,2048]{1,0:T(8,128)S(1)} collective-permute-done((f32[128,2048]{1,0:T(8,128)S(1)}, f32[128,2048]{1,0:T(8,128)S(1)}, u32[]{:S(2)}, u32[]{:S(2)}) %collective-permute-start.66) | collective-permute-done | bytes 1048608 | tf_op jit(solution)/shard_map/ppermute | solution.py:281
  849.7 4.0 pad_maximum_fusion
  857.4 268.3 %reduce-scatter.11.cloned.1.call-done = f32[256,4096]{1,0:T(8,128)} async-done(((f32[1024,4096]{1,0:T(8,128)}), f32[256,4096]{1,0:T(8,128)}) %reduce-scatter.11.cloned.1.call-update) | async-done | bytes 4194320 | tf_op jit(solution)/shard_map/reduce_scatter | solution.py:413
  1129.3 4.7 fusion.174
  (442 shorter events, 194.5 us)
Async XLA Ops:
  7.2 846.6 %reduce-scatter.5.cloned.1.call-start = ((), (), s32[]{:S(2)}) async-start(), calls=%async_computation.4 | async-start | bytes 10485760 | tf_op jit(solution)/shard_map/reduce_scatter | solution.py:413
  34.0 54.5 %collective-permute-start.8 = (f32[128,2048]{1,0:T(8,128)}, f32[128,2048]{1,0:T(8,128)}, u32[]{:S(2)}, u32[]{:S(2)}) collective-permute-start(f32[128,2048]{1,0:T(8,128)} %get-tuple-element.180), channel_id=1, source_target_pairs={{0,1},{1,0},{2,3},{3,2},{4,5},{5,4},{6,7},{7,6},{8,9},{9,8},{10,11... | collective-permute-start | bytes 3145736 | tf_op jit(solution)/shard_map/ppermute | solution.py:281
  37.0 51.6 %collective-permute-start.10 = (f32[128,2048]{1,0:T(8,128)}, f32[128,2048]{1,0:T(8,128)}, u32[]{:S(2)}, u32[]{:S(2)}) collective-permute-start(f32[128,2048]{1,0:T(8,128)} %get-tuple-element.181), channel_id=1, source_target_pairs={{0,2},{1,3},{2,0},{3,1},{4,6},{5,7},{6,4},{7,5},{8,10},{9,11},{10,... | collective-permute-start | bytes 3145736 | tf_op jit(solution)/shard_map/ppermute | solution.py:281
  58.5 24.7 %collective-permute-start = (f32[128,2048]{1,0:T(8,128)}, f32[128,2048]{1,0:T(8,128)}, u32[]{:S(2)}, u32[]{:S(2)}) collective-permute-start(f32[128,2048]{1,0:T(8,128)} %get-tuple-element.174), channel_id=1, source_target_pairs={{0,1},{1,0},{2,3},{3,2},{4,5},{5,4},{6,7},{7,6},{8,9},{9,8},{10,11... | collective-permute-start | bytes 3145736 | tf_op jit(solution)/shard_map/ppermute | solution.py:281
  59.1 25.4 %collective-permute-start.2 = (f32[128,2048]{1,0:T(8,128)}, f32[128,2048]{1,0:T(8,128)}, u32[]{:S(2)}, u32[]{:S(2)}) collective-permute-start(f32[128,2048]{1,0:T(8,128)} %get-tuple-element.175), channel_id=1, source_target_pairs={{0,2},{1,3},{2,0},{3,1},{4,6},{5,7},{6,4},{7,5},{8,10},{9,11},{10,... | collective-permute-start | bytes 3145736 | tf_op jit(solution)/shard_map/ppermute | solution.py:281
  86.4 14.9 %collective-permute-start.3 = (f32[64,2048]{1,0:T(8,128)S(1)}, f32[64,2048]{1,0:T(8,128)S(1)}, u32[]{:S(2)}, u32[]{:S(2)}) collective-permute-start(f32[64,2048]{1,0:T(8,128)S(1)} %constant_dynamic-slice_fusion.52), channel_id=1, source_target_pairs={{0,1},{1,0},{2,3},{3,2},{4,5},{5,4},{6,7},{7,6},{8,9},{9,8},{10,11... | collective-permute-start | bytes 1572872 | tf_op jit(solution)/shard_map/ppermute | solution.py:281
  87.0 14.9 %collective-permute-start.1 = (f32[64,2048]{1,0:T(8,128)S(1)}, f32[64,2048]{1,0:T(8,128)S(1)}, u32[]{:S(2)}, u32[]{:S(2)}) collective-permute-start(f32[64,2048]{1,0:T(8,128)S(1)} %constant_dynamic-slice_fusion.53), channel_id=1, source_target_pairs={{0,2},{1,3},{2,0},{3,1},{4,6},{5,7},{6,4},{7,5},{8,10},{9,11},{10,... | collective-permute-start | bytes 1572872 | tf_op jit(solution)/shard_map/ppermute | solution.py:281
  90.6 20.0 %collective-permute-start.11 = (f32[64,2048]{1,0:T(8,128)S(1)}, f32[64,2048]{1,0:T(8,128)S(1)}, u32[]{:S(2)}, u32[]{:S(2)}) collective-permute-start(f32[64,2048]{1,0:T(8,128)S(1)} %constant_dynamic-slice_fusion.42), channel_id=1, source_target_pairs={{0,1},{1,0},{2,3},{3,2},{4,5},{5,4},{6,7},{7,6},{8,9},{9,8},{10,11... | collective-permute-start | bytes 1572872 | tf_op jit(solution)/shard_map/ppermute | solution.py:281
  92.2 18.6 %collective-permute-start.9 = (f32[64,2048]{1,0:T(8,128)S(1)}, f32[64,2048]{1,0:T(8,128)S(1)}, u32[]{:S(2)}, u32[]{:S(2)}) collective-permute-start(f32[64,2048]{1,0:T(8,128)S(1)} %constant_dynamic-slice_fusion.43), channel_id=1, source_target_pairs={{0,2},{1,3},{2,0},{3,1},{4,6},{5,7},{6,4},{7,5},{8,10},{9,11},{10,... | collective-permute-start | bytes 1572872 | tf_op jit(solution)/shard_map/ppermute | solution.py:281
  112.0 14.9 %collective-permute-start.6 = (f32[64,2048]{1,0:T(8,128)S(1)}, f32[64,2048]{1,0:T(8,128)S(1)}, u32[]{:S(2)}, u32[]{:S(2)}) collective-permute-start(f32[64,2048]{1,0:T(8,128)S(1)} %get-tuple-element.203), channel_id=1, source_target_pairs={{0,1},{1,0},{2,3},{3,2},{4,5},{5,4},{6,7},{7,6},{8,9},{9,8},{10,11... | collective-permute-start | bytes 1572872 | tf_op jit(solution)/shard_map/ppermute | solution.py:281
  113.9 14.9 %collective-permute-start.4 = (f32[64,2048]{1,0:T(8,128)S(1)}, f32[64,2048]{1,0:T(8,128)S(1)}, u32[]{:S(2)}, u32[]{:S(2)}) collective-permute-start(f32[64,2048]{1,0:T(8,128)S(1)} %get-tuple-element.202), channel_id=1, source_target_pairs={{0,2},{1,3},{2,0},{3,1},{4,6},{5,7},{6,4},{7,5},{8,10},{9,11},{10,... | collective-permute-start | bytes 1572872 | tf_op jit(solution)/shard_map/ppermute | solution.py:281
  116.2 30.9 %collective-permute-start.12 = (f32[64,2048]{1,0:T(8,128)}, f32[64,2048]{1,0:T(8,128)}, u32[]{:S(2)}, u32[]{:S(2)}) collective-permute-start(f32[64,2048]{1,0:T(8,128)} %get-tuple-element.200), channel_id=1, source_target_pairs={{0,2},{1,3},{2,0},{3,1},{4,6},{5,7},{6,4},{7,5},{8,10},{9,11},{10,... | collective-permute-start | bytes 1572872 | tf_op jit(solution)/shard_map/ppermute | solution.py:281
  117.1 27.1 %collective-permute-start.14 = (f32[64,2048]{1,0:T(8,128)}, f32[64,2048]{1,0:T(8,128)}, u32[]{:S(2)}, u32[]{:S(2)}) collective-permute-start(f32[64,2048]{1,0:T(8,128)} %get-tuple-element.201), channel_id=1, source_target_pairs={{0,1},{1,0},{2,3},{3,2},{4,5},{5,4},{6,7},{7,6},{8,9},{9,8},{10,11... | collective-permute-start | bytes 1572872 | tf_op jit(solution)/shard_map/ppermute | solution.py:281
  126.9 35.7 %collective-permute-start.7 = (f32[128,2048]{1,0:T(8,128)S(1)}, f32[128,2048]{1,0:T(8,128)}, u32[]{:S(2)}, u32[]{:S(2)}) collective-permute-start(f32[128,2048]{1,0:T(8,128)S(1)} %maximum_select_fusion.17), channel_id=1, source_target_pairs={{0,2},{1,3},{2,0},{3,1},{4,6},{5,7},{6,4},{7,5},{8,10},{9,11},{10,... | collective-permute-start | bytes 3145736 | tf_op jit(solution)/shard_map/ppermute | solution.py:281
  129.9 34.5 %collective-permute-start.5 = (f32[128,2048]{1,0:T(8,128)}, f32[128,2048]{1,0:T(8,128)}, u32[]{:S(2)}, u32[]{:S(2)}) collective-permute-start(f32[128,2048]{1,0:T(8,128)} %maximum_select_fusion.16), channel_id=1, source_target_pairs={{0,1},{1,0},{2,3},{3,2},{4,5},{5,4},{6,7},{7,6},{8,9},{9,8},{10,11... | collective-permute-start | bytes 3145736 | tf_op jit(solution)/shard_map/ppermute | solution.py:281
  145.9 35.8 %collective-permute-start.15 = (f32[128,2048]{1,0:T(8,128)S(1)}, f32[128,2048]{1,0:T(8,128)S(1)}, u32[]{:S(2)}, u32[]{:S(2)}) collective-permute-start(f32[128,2048]{1,0:T(8,128)S(1)} %maximum_select_fusion.19), channel_id=1, source_target_pairs={{0,2},{1,3},{2,0},{3,1},{4,6},{5,7},{6,4},{7,5},{8,10},{9,11},{10,... | collective-permute-start | bytes 3145736 | tf_op jit(solution)/shard_map/ppermute | solution.py:281
  148.8 32.9 %collective-permute-start.13 = (f32[128,2048]{1,0:T(8,128)S(1)}, f32[128,2048]{1,0:T(8,128)S(1)}, u32[]{:S(2)}, u32[]{:S(2)}) collective-permute-start(f32[128,2048]{1,0:T(8,128)S(1)} %maximum_select_fusion.18), channel_id=1, source_target_pairs={{0,1},{1,0},{2,3},{3,2},{4,5},{5,4},{6,7},{7,6},{8,9},{9,8},{10,11... | collective-permute-start | bytes 3145736 | tf_op jit(solution)/shard_map/ppermute | solution.py:281
  219.6 26.7 %collective-permute-start.16 = (f32[1024,1024]{1,0:T(8,128)}, f32[1024,1024]{1,0:T(8,128)}, u32[]{:S(2)}, u32[]{:S(2)}) collective-permute-start(f32[1024,1024]{1,0:T(8,128)} %outer.8), channel_id=1, source_target_pairs={{0,4},{4,0},{8,12},{12,8},{16,20},{20,16},{24,28},{28,24},{1,5},{5... | collective-permute-start | bytes 12582920 | tf_op jit(solution)/shard_map/ppermute | solution.py:281
  225.9 27.6 %collective-permute-start.17 = (f32[1024,1024]{1,0:T(8,128)}, f32[1024,1024]{1,0:T(8,128)}, u32[]{:S(2)}, u32[]{:S(2)}) collective-permute-start(f32[1024,1024]{1,0:T(8,128)} %outer.10), channel_id=1, source_target_pairs={{0,4},{4,0},{8,12},{12,8},{16,20},{20,16},{24,28},{28,24},{1,5},{5... | collective-permute-start | bytes 12582920 | tf_op jit(solution)/shard_map/ppermute | solution.py:281
  283.7 164.8 %collective-permute-start.46 = (f32[1024,4096]{1,0:T(8,128)}, f32[1024,4096]{1,0:T(8,128)}, u32[]{:S(2)}, u32[]{:S(2)}) collective-permute-start(f32[1024,4096]{1,0:T(8,128)} %outer.12), channel_id=1, source_target_pairs={{0,4},{4,0},{8,12},{12,8},{16,20},{20,16},{24,28},{28,24},{1,5},{5... | collective-permute-start | bytes 50331656 | tf_op jit(solution)/shard_map/ppermute | solution.py:281
  290.8 25.6 %collective-permute-start.38 = (f32[128,2048]{1,0:T(8,128)S(1)}, f32[128,2048]{1,0:T(8,128)S(1)}, u32[]{:S(2)}, u32[]{:S(2)}) collective-permute-start(f32[128,2048]{1,0:T(8,128)S(1)} %get-tuple-element.132), channel_id=1, source_target_pairs={{0,1},{1,0},{2,3},{3,2},{4,5},{5,4},{6,7},{7,6},{8,9},{9,8},{10,11... | collective-permute-start | bytes 3145736 | tf_op jit(solution)/shard_map/ppermute | solution.py:281
  291.6 25.3 %collective-permute-start.40 = (f32[128,2048]{1,0:T(8,128)S(1)}, f32[128,2048]{1,0:T(8,128)S(1)}, u32[]{:S(2)}, u32[]{:S(2)}) collective-permute-start(f32[128,2048]{1,0:T(8,128)S(1)} %get-tuple-element.133), channel_id=1, source_target_pairs={{0,2},{1,3},{2,0},{3,1},{4,6},{5,7},{6,4},{7,5},{8,10},{9,11},{10,... | collective-permute-start | bytes 3145736 | tf_op jit(solution)/shard_map/ppermute | solution.py:281
  342.0 23.3 %collective-permute-start.18 = (f32[128,2048]{1,0:T(8,128)S(1)}, f32[128,2048]{1,0:T(8,128)S(1)}, u32[]{:S(2)}, u32[]{:S(2)}) collective-permute-start(f32[128,2048]{1,0:T(8,128)S(1)} %get-tuple-element.160), channel_id=1, source_target_pairs={{0,1},{1,0},{2,3},{3,2},{4,5},{5,4},{6,7},{7,6},{8,9},{9,8},{10,11... | collective-permute-start | bytes 3145736 | tf_op jit(solution)/shard_map/ppermute | solution.py:281
  342.8 23.0 %collective-permute-start.20 = (f32[128,2048]{1,0:T(8,128)S(1)}, f32[128,2048]{1,0:T(8,128)S(1)}, u32[]{:S(2)}, u32[]{:S(2)}) collective-permute-start(f32[128,2048]{1,0:T(8,128)S(1)} %get-tuple-element.161), channel_id=1, source_target_pairs={{0,2},{1,3},{2,0},{3,1},{4,6},{5,7},{6,4},{7,5},{8,10},{9,11},{10,... | collective-permute-start | bytes 3145736 | tf_op jit(solution)/shard_map/ppermute | solution.py:281
  390.6 38.1 %collective-permute-start.45 = (f32[128,2048]{1,0:T(8,128)S(1)}, f32[128,2048]{1,0:T(8,128)S(1)}, u32[]{:S(2)}, u32[]{:S(2)}) collective-permute-start(f32[128,2048]{1,0:T(8,128)S(1)} %maximum_select_fusion.25), channel_id=1, source_target_pairs={{0,2},{1,3},{2,0},{3,1},{4,6},{5,7},{6,4},{7,5},{8,10},{9,11},{10,... | collective-permute-start | bytes 3145736 | tf_op jit(solution)/shard_map/ppermute | solution.py:281
  391.2 14.9 %collective-permute-start.57 = (f32[64,2048]{1,0:T(8,128)S(1)}, f32[64,2048]{1,0:T(8,128)S(1)}, u32[]{:S(2)}, u32[]{:S(2)}) collective-permute-start(f32[64,2048]{1,0:T(8,128)S(1)} %get-tuple-element.193), channel_id=1, source_target_pairs={{0,1},{1,0},{2,3},{3,2},{4,5},{5,4},{6,7},{7,6},{8,9},{9,8},{10,11... | collective-permute-start | bytes 1572872 | tf_op jit(solution)/shard_map/ppermute | solution.py:281
  392.6 35.3 %collective-permute-start.55 = (f32[64,2048]{1,0:T(8,128)S(1)}, f32[64,2048]{1,0:T(8,128)S(1)}, u32[]{:S(2)}, u32[]{:S(2)}) collective-permute-start(f32[64,2048]{1,0:T(8,128)S(1)} %get-tuple-element.192), channel_id=1, source_target_pairs={{0,2},{1,3},{2,0},{3,1},{4,6},{5,7},{6,4},{7,5},{8,10},{9,11},{10,... | collective-permute-start | bytes 1572872 | tf_op jit(solution)/shard_map/ppermute | solution.py:281
  393.5 35.4 %collective-permute-start.43 = (f32[128,2048]{1,0:T(8,128)S(1)}, f32[128,2048]{1,0:T(8,128)S(1)}, u32[]{:S(2)}, u32[]{:S(2)}) collective-permute-start(f32[128,2048]{1,0:T(8,128)S(1)} %maximum_select_fusion.24), channel_id=1, source_target_pairs={{0,1},{1,0},{2,3},{3,2},{4,5},{5,4},{6,7},{7,6},{8,9},{9,8},{10,11... | collective-permute-start | bytes 3145736 | tf_op jit(solution)/shard_map/ppermute | solution.py:281
  406.1 39.7 %collective-permute-start.58 = (f32[128,2048]{1,0:T(8,128)S(1)}, f32[128,2048]{1,0:T(8,128)S(1)}, u32[]{:S(2)}, u32[]{:S(2)}) collective-permute-start(f32[128,2048]{1,0:T(8,128)S(1)} %maximum_select_fusion.29), channel_id=1, source_target_pairs={{0,2},{1,3},{2,0},{3,1},{4,6},{5,7},{6,4},{7,5},{8,10},{9,11},{10,... | collective-permute-start | bytes 3145736 | tf_op jit(solution)/shard_map/ppermute | solution.py:281
  428.0 17.9 %collective-permute-start.56 = (f32[128,2048]{1,0:T(8,128)S(1)}, f32[128,2048]{1,0:T(8,128)S(1)}, u32[]{:S(2)}, u32[]{:S(2)}) collective-permute-start(f32[128,2048]{1,0:T(8,128)S(1)} %maximum_select_fusion.28), channel_id=1, source_target_pairs={{0,1},{1,0},{2,3},{3,2},{4,5},{5,4},{6,7},{7,6},{8,9},{9,8},{10,11... | collective-permute-start | bytes 3145736 | tf_op jit(solution)/shard_map/ppermute | solution.py:281
  537.5 319.9 %reduce-scatter.7.cloned.1.call-start = ((), (), s32[]{:S(2)}) async-start(), calls=%async_computation.5 | async-start | bytes 5242880 | tf_op jit(solution)/shard_map/reduce_scatter | solution.py:413
  538.3 319.1 %reduce-scatter.9.cloned.1.call-start = ((), (), s32[]{:S(2)}) async-start(), calls=%async_computation.6 | async-start | bytes 5242880 | tf_op jit(solution)/shard_map/reduce_scatter | solution.py:413
  539.0 586.8 %reduce-scatter.11.cloned.1.call-start = ((), (), s32[]{:S(2)}) async-start(), calls=%async_computation.7 | async-start | bytes 20971520 | tf_op jit(solution)/shard_map/reduce_scatter | solution.py:413
  548.6 26.1 %collective-permute-start.30 = (f32[128,2048]{1,0:T(8,128)S(1)}, f32[128,2048]{1,0:T(8,128)S(1)}, u32[]{:S(2)}, u32[]{:S(2)}) collective-permute-start(f32[128,2048]{1,0:T(8,128)S(1)} %get-tuple-element.152), channel_id=1, source_target_pairs={{0,1},{1,0},{2,3},{3,2},{4,5},{5,4},{6,7},{7,6},{8,9},{9,8},{10,11... | collective-permute-start | bytes 3145736 | tf_op jit(solution)/shard_map/ppermute | solution.py:281
  549.3 26.0 %collective-permute-start.32 = (f32[128,2048]{1,0:T(8,128)S(1)}, f32[128,2048]{1,0:T(8,128)S(1)}, u32[]{:S(2)}, u32[]{:S(2)}) collective-permute-start(f32[128,2048]{1,0:T(8,128)S(1)} %get-tuple-element.153), channel_id=1, source_target_pairs={{0,2},{1,3},{2,0},{3,1},{4,6},{5,7},{6,4},{7,5},{8,10},{9,11},{10,... | collective-permute-start | bytes 3145736 | tf_op jit(solution)/shard_map/ppermute | solution.py:281
  556.3 40.8 %collective-permute-start.22 = (f32[128,2048]{1,0:T(8,128)S(1)}, f32[128,2048]{1,0:T(8,128)S(1)}, u32[]{:S(2)}, u32[]{:S(2)}) collective-permute-start(f32[128,2048]{1,0:T(8,128)S(1)} %get-tuple-element.144), channel_id=1, source_target_pairs={{0,1},{1,0},{2,3},{3,2},{4,5},{5,4},{6,7},{7,6},{8,9},{9,8},{10,11... | collective-permute-start | bytes 3145736 | tf_op jit(solution)/shard_map/ppermute | solution.py:281
  557.6 40.2 %collective-permute-start.24 = (f32[128,2048]{1,0:T(8,128)S(1)}, f32[128,2048]{1,0:T(8,128)S(1)}, u32[]{:S(2)}, u32[]{:S(2)}) collective-permute-start(f32[128,2048]{1,0:T(8,128)S(1)} %get-tuple-element.145), channel_id=1, source_target_pairs={{0,2},{1,3},{2,0},{3,1},{4,6},{5,7},{6,4},{7,5},{8,10},{9,11},{10,... | collective-permute-start | bytes 3145736 | tf_op jit(solution)/shard_map/ppermute | solution.py:281
  575.7 32.7 %collective-permute-start.33 = (f32[64,2048]{1,0:T(8,128)S(1)}, f32[64,2048]{1,0:T(8,128)S(1)}, u32[]{:S(2)}, u32[]{:S(2)}) collective-permute-start(f32[64,2048]{1,0:T(8,128)S(1)} %constant_dynamic-slice_fusion.20), channel_id=1, source_target_pairs={{0,1},{1,0},{2,3},{3,2},{4,5},{5,4},{6,7},{7,6},{8,9},{9,8},{10,11... | collective-permute-start | bytes 1572872 | tf_op jit(solution)/shard_map/ppermute | solution.py:281
  577.2 31.8 %collective-permute-start.31 = (f32[64,2048]{1,0:T(8,128)S(1)}, f32[64,2048]{1,0:T(8,128)S(1)}, u32[]{:S(2)}, u32[]{:S(2)}) collective-permute-start(f32[64,2048]{1,0:T(8,128)S(1)} %constant_dynamic-slice_fusion.21), channel_id=1, source_target_pairs={{0,2},{1,3},{2,0},{3,1},{4,6},{5,7},{6,4},{7,5},{8,10},{9,11},{10,... | collective-permute-start | bytes 1572872 | tf_op jit(solution)/shard_map/ppermute | solution.py:281
  598.3 21.4 %collective-permute-start.25 = (f32[64,2048]{1,0:T(8,128)S(1)}, f32[64,2048]{1,0:T(8,128)S(1)}, u32[]{:S(2)}, u32[]{:S(2)}) collective-permute-start(f32[64,2048]{1,0:T(8,128)S(1)} %constant_dynamic-slice_fusion.26), channel_id=1, source_target_pairs={{0,1},{1,0},{2,3},{3,2},{4,5},{5,4},{6,7},{7,6},{8,9},{9,8},{10,11... | collective-permute-start | bytes 1572872 | tf_op jit(solution)/shard_map/ppermute | solution.py:281
  599.7 20.6 %collective-permute-start.23 = (f32[64,2048]{1,0:T(8,128)S(1)}, f32[64,2048]{1,0:T(8,128)S(1)}, u32[]{:S(2)}, u32[]{:S(2)}) collective-permute-start(f32[64,2048]{1,0:T(8,128)S(1)} %constant_dynamic-slice_fusion.27), channel_id=1, source_target_pairs={{0,2},{1,3},{2,0},{3,1},{4,6},{5,7},{6,4},{7,5},{8,10},{9,11},{10,... | collective-permute-start | bytes 1572872 | tf_op jit(solution)/shard_map/ppermute | solution.py:281
  609.4 23.4 %collective-permute-start.34 = (f32[64,2048]{1,0:T(8,128)S(1)}, f32[64,2048]{1,0:T(8,128)}, u32[]{:S(2)}, u32[]{:S(2)}) collective-permute-start(f32[64,2048]{1,0:T(8,128)S(1)} %get-tuple-element.198), channel_id=1, source_target_pairs={{0,2},{1,3},{2,0},{3,1},{4,6},{5,7},{6,4},{7,5},{8,10},{9,11},{10,... | collective-permute-start | bytes 1572872 | tf_op jit(solution)/shard_map/ppermute | solution.py:281
  610.0 21.0 %collective-permute-start.36 = (f32[64,2048]{1,0:T(8,128)S(1)}, f32[64,2048]{1,0:T(8,128)}, u32[]{:S(2)}, u32[]{:S(2)}) collective-permute-start(f32[64,2048]{1,0:T(8,128)S(1)} %get-tuple-element.199), channel_id=1, source_target_pairs={{0,1},{1,0},{2,3},{3,2},{4,5},{5,4},{6,7},{7,6},{8,9},{9,8},{10,11... | collective-permute-start | bytes 1572872 | tf_op jit(solution)/shard_map/ppermute | solution.py:281
  620.6 21.6 %collective-permute-start.28 = (f32[64,2048]{1,0:T(8,128)S(1)}, f32[64,2048]{1,0:T(8,128)}, u32[]{:S(2)}, u32[]{:S(2)}) collective-permute-start(f32[64,2048]{1,0:T(8,128)S(1)} %get-tuple-element.197), channel_id=1, source_target_pairs={{0,1},{1,0},{2,3},{3,2},{4,5},{5,4},{6,7},{7,6},{8,9},{9,8},{10,11... | collective-permute-start | bytes 1572872 | tf_op jit(solution)/shard_map/ppermute | solution.py:281
  623.8 20.3 %collective-permute-start.26 = (f32[64,2048]{1,0:T(8,128)S(1)}, f32[64,2048]{1,0:T(8,128)S(1)}, u32[]{:S(2)}, u32[]{:S(2)}) collective-permute-start(f32[64,2048]{1,0:T(8,128)S(1)} %get-tuple-element.196), channel_id=1, source_target_pairs={{0,2},{1,3},{2,0},{3,1},{4,6},{5,7},{6,4},{7,5},{8,10},{9,11},{10,... | collective-permute-start | bytes 1572872 | tf_op jit(solution)/shard_map/ppermute | solution.py:281
  632.3 32.9 %collective-permute-start.37 = (f32[128,2048]{1,0:T(8,128)S(1)}, f32[128,2048]{1,0:T(8,128)S(1)}, u32[]{:S(2)}, u32[]{:S(2)}) collective-permute-start(f32[128,2048]{1,0:T(8,128)S(1)} %maximum_select_fusion.23), channel_id=1, source_target_pairs={{0,2},{1,3},{2,0},{3,1},{4,6},{5,7},{6,4},{7,5},{8,10},{9,11},{10,... | collective-permute-start | bytes 3145736 | tf_op jit(solution)/shard_map/ppermute | solution.py:281
  634.1 31.3 %collective-permute-start.35 = (f32[128,2048]{1,0:T(8,128)S(1)}, f32[128,2048]{1,0:T(8,128)S(1)}, u32[]{:S(2)}, u32[]{:S(2)}) collective-permute-start(f32[128,2048]{1,0:T(8,128)S(1)} %maximum_select_fusion.22), channel_id=1, source_target_pairs={{0,1},{1,0},{2,3},{3,2},{4,5},{5,4},{6,7},{7,6},{8,9},{9,8},{10,11... | collective-permute-start | bytes 3145736 | tf_op jit(solution)/shard_map/ppermute | solution.py:281
  643.5 43.0 %collective-permute-start.29 = (f32[128,2048]{1,0:T(8,128)S(1)}, f32[128,2048]{1,0:T(8,128)S(1)}, u32[]{:S(2)}, u32[]{:S(2)}) collective-permute-start(f32[128,2048]{1,0:T(8,128)S(1)} %maximum_select_fusion.21), channel_id=1, source_target_pairs={{0,2},{1,3},{2,0},{3,1},{4,6},{5,7},{6,4},{7,5},{8,10},{9,11},{10,... | collective-permute-start | bytes 3145736 | tf_op jit(solution)/shard_map/ppermute | solution.py:281
  644.2 42.6 %collective-permute-start.27 = (f32[128,2048]{1,0:T(8,128)S(1)}, f32[128,2048]{1,0:T(8,128)S(1)}, u32[]{:S(2)}, u32[]{:S(2)}) collective-permute-start(f32[128,2048]{1,0:T(8,128)S(1)} %maximum_select_fusion.20), channel_id=1, source_target_pairs={{0,1},{1,0},{2,3},{3,2},{4,5},{5,4},{6,7},{7,6},{8,9},{9,8},{10,11... | collective-permute-start | bytes 3145736 | tf_op jit(solution)/shard_map/ppermute | solution.py:281
  697.2 49.5 %collective-permute-start.59 = (f32[128,2048]{1,0:T(8,128)S(1)}, f32[128,2048]{1,0:T(8,128)S(1)}, u32[]{:S(2)}, u32[]{:S(2)}) collective-permute-start(f32[128,2048]{1,0:T(8,128)S(1)} %get-tuple-element.128), channel_id=1, source_target_pairs={{0,1},{1,0},{2,3},{3,2},{4,5},{5,4},{6,7},{7,6},{8,9},{9,8},{10,11... | collective-permute-start | bytes 3145736 | tf_op jit(solution)/shard_map/ppermute | solution.py:281
  698.9 47.9 %collective-permute-start.61 = (f32[128,2048]{1,0:T(8,128)S(1)}, f32[128,2048]{1,0:T(8,128)S(1)}, u32[]{:S(2)}, u32[]{:S(2)}) collective-permute-start(f32[128,2048]{1,0:T(8,128)S(1)} %get-tuple-element.129), channel_id=1, source_target_pairs={{0,2},{1,3},{2,0},{3,1},{4,6},{5,7},{6,4},{7,5},{8,10},{9,11},{10,... | collective-permute-start | bytes 3145736 | tf_op jit(solution)/shard_map/ppermute | solution.py:281
  701.9 41.9 %collective-permute-start.47 = (f32[128,2048]{1,0:T(8,128)S(1)}, f32[128,2048]{1,0:T(8,128)S(1)}, u32[]{:S(2)}, u32[]{:S(2)}) collective-permute-start(f32[128,2048]{1,0:T(8,128)S(1)} %get-tuple-element.122), channel_id=1, source_target_pairs={{0,1},{1,0},{2,3},{3,2},{4,5},{5,4},{6,7},{7,6},{8,9},{9,8},{10,11... | collective-permute-start | bytes 3145736 | tf_op jit(solution)/shard_map/ppermute | solution.py:281
  702.8 42.1 %collective-permute-start.49 = (f32[128,2048]{1,0:T(8,128)S(1)}, f32[128,2048]{1,0:T(8,128)S(1)}, u32[]{:S(2)}, u32[]{:S(2)}) collective-permute-start(f32[128,2048]{1,0:T(8,128)S(1)} %get-tuple-element.123), channel_id=1, source_target_pairs={{0,2},{1,3},{2,0},{3,1},{4,6},{5,7},{6,4},{7,5},{8,10},{9,11},{10,... | collective-permute-start | bytes 3145736 | tf_op jit(solution)/shard_map/ppermute | solution.py:281
  745.3 14.9 %collective-permute-start.50 = (f32[64,2048]{1,0:T(8,128)S(1)}, f32[64,2048]{1,0:T(8,128)S(1)}, u32[]{:S(2)}, u32[]{:S(2)}) collective-permute-start(f32[64,2048]{1,0:T(8,128)S(1)} %constant_dynamic-slice_fusion.6), channel_id=1, source_target_pairs={{0,1},{1,0},{2,3},{3,2},{4,5},{5,4},{6,7},{7,6},{8,9},{9,8},{10,11... | collective-permute-start | bytes 1572872 | tf_op jit(solution)/shard_map/ppermute | solution.py:281
  746.0 14.9 %collective-permute-start.48 = (f32[64,2048]{1,0:T(8,128)S(1)}, f32[64,2048]{1,0:T(8,128)S(1)}, u32[]{:S(2)}, u32[]{:S(2)}) collective-permute-start(f32[64,2048]{1,0:T(8,128)S(1)} %constant_dynamic-slice_fusion.7), channel_id=1, source_target_pairs={{0,2},{1,3},{2,0},{3,1},{4,6},{5,7},{6,4},{7,5},{8,10},{9,11},{10,... | collective-permute-start | bytes 1572872 | tf_op jit(solution)/shard_map/ppermute | solution.py:281
  747.2 21.1 %collective-permute-start.62 = (f32[64,2048]{1,0:T(8,128)S(1)}, f32[64,2048]{1,0:T(8,128)S(1)}, u32[]{:S(2)}, u32[]{:S(2)}) collective-permute-start(f32[64,2048]{1,0:T(8,128)S(1)} %constant_dynamic-slice_fusion.2), channel_id=1, source_target_pairs={{0,1},{1,0},{2,3},{3,2},{4,5},{5,4},{6,7},{7,6},{8,9},{9,8},{10,11... | collective-permute-start | bytes 1572872 | tf_op jit(solution)/shard_map/ppermute | solution.py:281
  748.4 20.3 %collective-permute-start.60 = (f32[64,2048]{1,0:T(8,128)S(1)}, f32[64,2048]{1,0:T(8,128)S(1)}, u32[]{:S(2)}, u32[]{:S(2)}) collective-permute-start(f32[64,2048]{1,0:T(8,128)S(1)} %constant_dynamic-slice_fusion.3), channel_id=1, source_target_pairs={{0,2},{1,3},{2,0},{3,1},{4,6},{5,7},{6,4},{7,5},{8,10},{9,11},{10,... | collective-permute-start | bytes 1572872 | tf_op jit(solution)/shard_map/ppermute | solution.py:281
  771.2 16.5 %collective-permute-start.53 = (f32[64,2048]{1,0:T(8,128)S(1)}, f32[64,2048]{1,0:T(8,128)S(1)}, u32[]{:S(2)}, u32[]{:S(2)}) collective-permute-start(f32[64,2048]{1,0:T(8,128)S(1)} %get-tuple-element.189), channel_id=1, source_target_pairs={{0,1},{1,0},{2,3},{3,2},{4,5},{5,4},{6,7},{7,6},{8,9},{9,8},{10,11... | collective-permute-start | bytes 1572872 | tf_op jit(solution)/shard_map/ppermute | solution.py:281
  777.6 17.3 %collective-permute-start.65 = (f32[64,2048]{1,0:T(8,128)S(1)}, f32[64,2048]{1,0:T(8,128)S(1)}, u32[]{:S(2)}, u32[]{:S(2)}) collective-permute-start(f32[64,2048]{1,0:T(8,128)S(1)} %get-tuple-element.191), channel_id=1, source_target_pairs={{0,1},{1,0},{2,3},{3,2},{4,5},{5,4},{6,7},{7,6},{8,9},{9,8},{10,11... | collective-permute-start | bytes 1572872 | tf_op jit(solution)/shard_map/ppermute | solution.py:281
  784.1 21.0 %collective-permute-start.63 = (f32[64,2048]{1,0:T(8,128)S(1)}, f32[64,2048]{1,0:T(8,128)S(1)}, u32[]{:S(2)}, u32[]{:S(2)}) collective-permute-start(f32[64,2048]{1,0:T(8,128)S(1)} %get-tuple-element.190), channel_id=1, source_target_pairs={{0,2},{1,3},{2,0},{3,1},{4,6},{5,7},{6,4},{7,5},{8,10},{9,11},{10,... | collective-permute-start | bytes 1572872 | tf_op jit(solution)/shard_map/ppermute | solution.py:281
  787.8 39.8 %collective-permute-start.54 = (f32[128,2048]{1,0:T(8,128)S(1)}, f32[128,2048]{1,0:T(8,128)S(1)}, u32[]{:S(2)}, u32[]{:S(2)}) collective-permute-start(f32[128,2048]{1,0:T(8,128)S(1)} %maximum_select_fusion.27), channel_id=1, source_target_pairs={{0,2},{1,3},{2,0},{3,1},{4,6},{5,7},{6,4},{7,5},{8,10},{9,11},{10,... | collective-permute-start | bytes 3145736 | tf_op jit(solution)/shard_map/ppermute | solution.py:281
  794.3 33.5 %collective-permute-start.52 = (f32[128,2048]{1,0:T(8,128)S(1)}, f32[128,2048]{1,0:T(8,128)S(1)}, u32[]{:S(2)}, u32[]{:S(2)}) collective-permute-start(f32[128,2048]{1,0:T(8,128)S(1)} %maximum_select_fusion.26), channel_id=1, source_target_pairs={{0,1},{1,0},{2,3},{3,2},{4,5},{5,4},{6,7},{7,6},{8,9},{9,8},{10,11... | collective-permute-start | bytes 3145736 | tf_op jit(solution)/shard_map/ppermute | solution.py:281
  795.0 54.2 %collective-permute-start.66 = (f32[128,2048]{1,0:T(8,128)S(1)}, f32[128,2048]{1,0:T(8,128)S(1)}, u32[]{:S(2)}, u32[]{:S(2)}) collective-permute-start(f32[128,2048]{1,0:T(8,128)S(1)} %maximum_select_fusion.31), channel_id=1, source_target_pairs={{0,2},{1,3},{2,0},{3,1},{4,6},{5,7},{6,4},{7,5},{8,10},{9,11},{10,... | collective-permute-start | bytes 3145736 | tf_op jit(solution)/shard_map/ppermute | solution.py:281
  805.2 44.3 %collective-permute-start.64 = (f32[128,2048]{1,0:T(8,128)S(1)}, f32[128,2048]{1,0:T(8,128)S(1)}, u32[]{:S(2)}, u32[]{:S(2)}) collective-permute-start(f32[128,2048]{1,0:T(8,128)S(1)} %maximum_select_fusion.30), channel_id=1, source_target_pairs={{0,1},{1,0},{2,3},{3,2},{4,5},{5,4},{6,7},{7,6},{8,9},{9,8},{10,11... | collective-permute-start | bytes 3145736 | tf_op jit(solution)/shard_map/ppermute | solution.py:281
  (80 other events, 1208.0 us)
Sparse Core Ops, SparseCore 0:
  537.7 144.7 reduce-scatter.4
  684.8 77.3 reduce-scatter.6
  764.5 77.9 reduce-scatter.8
  844.8 280.9 reduce-scatter.10

commit v5 on v4

--- a/solution.py
+++ b/solution.py
@@ -111,7 +111,7 @@
         attend_body,
         grid=(cols // step,),
         in_specs=[chunk(x), whole((1, width)), weight, weight, weight]
-        + [chunk(cos), chunk(sin), whole((rows, rows))],
+        + [whole(cos.shape), whole(sin.shape), whole((rows, rows))],
         out_specs=[whole((rows, width))] + [column] * 4,
         out_shape=[jax.ShapeDtypeStruct((rows, width), BF16)]
         + [jax.ShapeDtypeStruct((rows, cols), BF16)] * 4,
@@ -145,19 +145,18 @@
     out[2] = jnp.concatenate(v_list, axis=1).astype(BF16)
 
 
-def attend_back(hidden, row_block, wo, q, k, v, attn, cos, sin, mask, after):
+def attend_back(hidden, wo, q, k, v, attn, cos, sin, mask, after):
     rows, width = hidden.shape
     cols = wo.shape[0]
     step = min(256, cols)
     column = pl.BlockSpec((rows, step), lambda i: (0, i))
     whole = lambda shape: pl.BlockSpec(shape, lambda i: (0, 0))
-    chunk = lambda v: pl.BlockSpec((rows, v.shape[1]), lambda i: (row_block, 0))
     return pl.pallas_call(
         attend_back_body,
         grid=(cols // step,),
         in_specs=[whole((rows, width)), pl.BlockSpec((step, width), lambda i: (i, 0))]
         + [column] * 4
-        + [chunk(cos), chunk(sin), whole((rows, rows))]
+        + [whole(cos.shape), whole(sin.shape), whole((rows, rows))]
         + [pl.BlockSpec(memory_space=pl.ANY)] * len(after),
         out_specs=pl.BlockSpec((3, rows, step), lambda i: (0, 0, i)),
         out_shape=jax.ShapeDtypeStruct((3, rows, cols), BF16),
@@ -352,12 +351,11 @@
         def halves(size):
             return [(0, size // 2, orders[0]), (size // 2, size // 2, orders[1])]
 
-        def own_rows(value):
-            size = value.shape[0]
+        def own_rows(value, low, size):
             return jnp.concatenate(
                 [
                     lax.dynamic_slice_in_dim(
-                        value, base + tensor.own_start(rows, bits), rows // tensor_size, 0
+                        value, low + base + tensor.own_start(rows, bits), rows // tensor_size, 0
                     )
                     for base, rows, bits in halves(size)
                 ],
@@ -418,8 +416,6 @@
         owners = jnp.broadcast_to(block_owner[:, None], (row_count // BLK, BLK)).reshape(-1)
         row_index = jnp.arange(row_count, dtype=jnp.int32)
         positions = (row_index // BLK + first_block - owners) * BLK + row_index % BLK
-        cosine, sine = rope_tables(positions, min(128, head_cols))
-
         saved = []
         for lo, hi in bounds:
             size = hi - lo
@@ -430,8 +426,12 @@
             aligned = lo % size == 0
             cut = (lambda v: v) if aligned else (lambda v, lo=lo, hi=hi: v[lo:hi])
             row_block = lo // size if aligned else 0
-            cos_g, sin_g = cut(cosine), cut(sine)
             own_g, pos_g, mask_g = owners[lo:hi], positions[lo:hi], token_mask[lo:hi]
+            if saved:
+                own_g, pos_g, mask_g, _ = lax.optimization_barrier(
+                    (own_g, pos_g, mask_g, saved[-1].flat)
+                )
+            cos_g, sin_g = rope_tables(pos_g, min(128, head_cols))
             allowed = (
                 (own_g[:, None] == own_g[None, :])
                 & (pos_g[None, :] <= pos_g[:, None])
@@ -444,7 +444,7 @@
             added = scatter_rows(
                 lambda s, n, flat=flat: mm(rows_of(flat, s, n), output_weight), size
             )
-            x_own = own_rows(block_input[lo:hi]).astype(F32)
+            x_own = own_rows(block_input, lo, size).astype(F32)
             hid = x_own + added
             inv_two = lax.rsqrt(jnp.mean(hid * hid, axis=-1, keepdims=True) + NORM_EPS)
             after = saved[-1].act_two if saved else None
@@ -452,7 +452,7 @@
             act_two = (unit * feedforward_gain).astype(BF16)
             saved.append(
                 SimpleNamespace(q=q, k=k, v=v, allowed=allowed, flat=flat, act=act, rows=rows, x_f=x_f,
-                     cos=cos_g, sin=sin_g, row_block=row_block, x_own=x_own, hid=hid, added=added, inv_two=inv_two,
+                     cos=cos_g, sin=sin_g, x_own=x_own, hid=hid, added=added, inv_two=inv_two,
                      act_two=act_two)
             )
 
@@ -492,7 +492,7 @@
             back = s.inv_two * (
                 scaled - unit * jnp.mean(scaled * unit, axis=-1, keepdims=True)
             )
-            s.hidden_grad = own_rows(rows).astype(F32) + back
+            s.hidden_grad = own_rows(rows, 0, size).astype(F32) + back
             after = saved[index - 1].hidden_back if index else None
             full = gather_rows(back, size, after)
             s.hidden_back = (rows.astype(F32) + full).astype(BF16)
@@ -516,7 +516,7 @@
         for (lo, hi), s in zip(bounds, saved):
             size = hi - lo
             back3 = attend_back(
-                s.hidden_back, s.row_block, output_weight, s.q, s.k, s.v, s.flat,
+                s.hidden_back, output_weight, s.q, s.k, s.v, s.flat,
                 s.cos, s.sin, s.allowed, (both_part,),
             )
             s.qkv_back = back3

time: 1150 us -> 1140 us (level)
  transfers between devices with their start and end apart: 77 -> 77, of which waited for: 48 -> 47; matrix products, arithmetic and copies ran while one was open for 14% -> 14% of each run, Pallas kernels for 3% -> 3%
where the time goes in v5:
time: 1140 us; the launch traced here: 1130 us
  waiting for transfers between devices  670 us (59%)
  Pallas kernels  157 us (14%)
  matrix products  116 us (10%)
  starting transfers between devices  68.4 us (6%)
  other arithmetic  59.9 us (5%)
  local copies, waits for them, and re-layouts  46.3 us (4%)
  between operations  16.2 us (1%)
    ppermute x73, waiting for transfers between devices, swap(): lax.ppermute(value, self.axis, [(i, i ^ bit) for i in range(self.size)])  400 us
    reduce_scatter x4, waiting for transfers between devices, z_scatter(): lax.psum_scatter(value, DP, scatter_dimension=0, tiled=True, axis_index_g...  268 us
    pallas_call x8, Pallas kernels, outer(): pl.pallas_call(functools.partial(outer_body, [len(g[1]) for g in groups],...  84.5 us
    ppermute x73, starting transfers between devices, swap(): lax.ppermute(value, self.axis, [(i, i ^ bit) for i in range(self.size)])  68 us
    dot_general x22, matrix products, mm_nt(): lax.dot_general(a, b, (((1,), (1,)), ((), ())), preferred_element_type=F32)  66.7 us
    dot_general x12, matrix products, mm(): return jnp.dot(a, b, preferred_element_type=F32)  49.8 us
    pallas_call x2, Pallas kernels, attend_back(): pl.pallas_call(attend_back_body, grid=(cols // step,), in_specs=[whole((r...  33.7 us
    pallas_call x2, Pallas kernels, attend(): pl.pallas_call(attend_body, grid=(cols // step,), in_specs=[chunk(x), who...  32.9 us
  transfers between devices with their start and end apart: 77, of which 47 were waited for; matrix products, arithmetic and copies ran while one was open for 14% of the time, Pallas kernels for 3%

profile of v5, /device:TPU:0, one launch (start us, length us, event | category | flops | bytes accessed | tf_op | source)
XLA Modules:
  0.0 1134.0 jit_solution(4722345041130229803)
XLA Ops:
  12.7 16.3 %shard_map.212 = (bf16[512,2048]{1,0:T(8,128)(2,1)}, bf16[512,512]{1,0:T(8,128)(2,1)}, bf16[512,512]{1,0:T(8,128)(2,1)}, bf16[512,512]{1,0:T(8,128)(2,1)}, bf16[512,512]{1,0:T(8,128)(2,1)}) custom-call(bf16[1024,2048]{1,0:T(8,128)(2,1)} %x.3, f32[1,2048]{1,0:T(1,128)} %bitcast.114, bf16[2048,512]{1,0:T(8,128)(2,1)} %wq.3, bf16[2048,512]{1,0:T(8,128)(2,1)} %wk.3, ...), custom_call_target="tpu_custom_call" | custom-call | flops 5368709120 | bytes 12582912 | tf_op jit(solution)/shard_map/pallas_call | solution.py:110
  32.4 3.0 collective-permute-start
  40.0 16.6 %shard_map.213 = (bf16[512,2048]{1,0:T(8,128)(2,1)}, bf16[512,512]{1,0:T(8,128)(2,1)}, bf16[512,512]{1,0:T(8,128)(2,1)}, bf16[512,512]{1,0:T(8,128)(2,1)}, bf16[512,512]{1,0:T(8,128)(2,1)}) custom-call(bf16[1024,2048]{1,0:T(8,128)(2,1)} %x.3, f32[1,2048]{1,0:T(1,128)} %bitcast.115, bf16[2048,512]{1,0:T(8,128)(2,1)} %wq.3, bf16[2048,512]{1,0:T(8,128)(2,1)} %wk.3, ...), custom_call_target="tpu_custom_call" | custom-call | flops 5368709120 | bytes 12582912 | tf_op jit(solution)/shard_map/pallas_call | solution.py:110
  74.6 11.7 %collective-permute-done.8 = f32[128,2048]{1,0:T(8,128)} collective-permute-done((f32[128,2048]{1,0:T(8,128)}, f32[128,2048]{1,0:T(8,128)}, u32[]{:S(2)}, u32[]{:S(2)}) %collective-permute-start.8) | collective-permute-done | bytes 1048608 | tf_op jit(solution)/shard_map/ppermute | solution.py:280
  90.9 6.5 collective-permute-done.3
  101.4 7.2 collective-permute-done.11
  114.3 5.6 collective-permute-done.6
  123.0 6.3 fusion.198
  130.4 5.9 shard_map.214.refs_0_
  142.2 12.0 %collective-permute-done.7 = f32[128,2048]{1,0:T(8,128)} collective-permute-done((f32[128,2048]{1,0:T(8,128)S(1)}, f32[128,2048]{1,0:T(8,128)}, u32[]{:S(2)}, u32[]{:S(2)}) %collective-permute-start.7) | collective-permute-done | bytes 1048608 | tf_op jit(solution)/shard_map/ppermute | solution.py:280
  159.2 15.4 %collective-permute-done.15 = f32[128,2048]{1,0:T(8,128)S(1)} collective-permute-done((f32[128,2048]{1,0:T(8,128)S(1)}, f32[128,2048]{1,0:T(8,128)S(1)}, u32[]{:S(2)}, u32[]{:S(2)}) %collective-permute-start.15) | collective-permute-done | bytes 1048608 | tf_op jit(solution)/shard_map/ppermute | solution.py:280
  174.6 6.1 fusion.195
  181.7 4.6 fusion.197
  188.4 6.9 multiply_convert_fusion.4
  195.2 10.8 multiply_convert_fusion
  206.1 6.3 outer.8
  212.3 6.3 outer.10
  219.1 9.6 fusion.196
  232.0 7.1 fusion.61
  239.0 7.3 outer.9
  246.3 7.2 outer.11
  253.6 7.3 multiply_convert_fusion.2
  260.8 15.7 %outer.12 = f32[1024,4096]{1,0:T(8,128)} custom-call(s32[1]{0:T(128)} %bitcast.6.which, bf16[512,2048]{1,0:T(8,128)(2,1)} %copy-done.1, bf16[512,2048]{1,0:T(8,128)(2,1)} %copy-done.2, bf16[512,2048]{1,0:T(8,128)(2,1)} %get-tuple-element.106.refs_2_, bf16[512,2048]{1,0:T(8,128)(2,1)} %get-tuple-element.104.refs_3_, bf16[512,2048]{1,0:T(8,128)(2,1)} %copy-done.1, ...), custom_call_target="tpu_custom_call" | custom-call | flops 8589934592 | bytes 29360128 | tf_op jit(solution)/shard_map/outer/pallas_call | solution.py:254
  276.6 6.7 convolution_add_fusion.8
  285.6 5.7 fusion.54
  291.4 5.9 convolution_add_fusion.9
  297.4 11.8 %collective-permute-done.38 = f32[128,2048]{1,0:T(8,128)S(1)} collective-permute-done((f32[128,2048]{1,0:T(8,128)S(1)}, f32[128,2048]{1,0:T(8,128)S(1)}, u32[]{:S(2)}, u32[]{:S(2)}) %collective-permute-start.38) | collective-permute-done | bytes 1048608 | tf_op jit(solution)/shard_map/ppermute | solution.py:280
  311.8 12.2 %collective-permute-done.41 = f32[64,2048]{1,0:T(8,128)S(1)} collective-permute-done((f32[64,2048]{1,0:T(8,128)S(1)}, f32[64,2048]{1,0:T(8,128)S(1)}, u32[]{:S(2)}, u32[]{:S(2)}) %collective-permute-start.41) | collective-permute-done | bytes 524320 | tf_op jit(solution)/shard_map/ppermute | solution.py:280
  328.8 6.0 convolution_add_fusion.10
  339.4 5.8 convolution_add_fusion.11
  345.2 13.2 %collective-permute-done.18 = f32[128,2048]{1,0:T(8,128)S(1)} collective-permute-done((f32[128,2048]{1,0:T(8,128)S(1)}, f32[128,2048]{1,0:T(8,128)S(1)}, u32[]{:S(2)}, u32[]{:S(2)}) %collective-permute-start.18) | collective-permute-done | bytes 1048608 | tf_op jit(solution)/shard_map/ppermute | solution.py:280
  361.6 9.2 collective-permute-done.21
  374.4 8.8 collective-permute-done.44
  387.8 11.5 %collective-permute-done.57 = f32[64,2048]{1,0:T(8,128)S(1)} collective-permute-done((f32[64,2048]{1,0:T(8,128)S(1)}, f32[64,2048]{1,0:T(8,128)S(1)}, u32[]{:S(2)}, u32[]{:S(2)}) %collective-permute-start.57) | collective-permute-done | bytes 524320 | tf_op jit(solution)/shard_map/ppermute | solution.py:280
  400.5 20.1 %collective-permute-done.55 = f32[64,2048]{1,0:T(8,128)S(1)} collective-permute-done((f32[64,2048]{1,0:T(8,128)S(1)}, f32[64,2048]{1,0:T(8,128)S(1)}, u32[]{:S(2)}, u32[]{:S(2)}) %collective-permute-start.55) | collective-permute-done | bytes 524320 | tf_op jit(solution)/shard_map/ppermute | solution.py:280
  426.7 12.7 %collective-permute-done.58 = f32[128,2048]{1,0:T(8,128)S(1)} collective-permute-done((f32[128,2048]{1,0:T(8,128)S(1)}, f32[128,2048]{1,0:T(8,128)S(1)}, u32[]{:S(2)}, u32[]{:S(2)}) %collective-permute-start.58) | collective-permute-done | bytes 1048608 | tf_op jit(solution)/shard_map/ppermute | solution.py:280
  442.1 19.9 %outer.13.rest_0_ = f32[1024,4096]{1,0:T(8,128)} custom-call(s32[1]{0:T(128)} %bitcast.4.which, bf16[512,2048]{1,0:T(8,128)(2,1)} %copy-done.1, bf16[512,2048]{1,0:T(8,128)(2,1)} %copy-done.2, bf16[512,2048]{1,0:T(8,128)(2,1)} %get-tuple-element.106.refs_2_, bf16[512,2048]{1,0:T(8,128)(2,1)} %get-tuple-element.104.refs_3_, bf16[512,2048]{1,0:T(8,128)(2,1)} %copy-done.1, ...), custom_call_target="tpu_custom_call" | custom-call | flops 8589934592 | bytes 29360128 | tf_op jit(solution)/shard_map/outer/pallas_call | solution.py:254
  461.9 17.0 %shard_map.215.refs_2_ = bf16[3,512,512]{2,1,0:T(8,128)(2,1)} custom-call(bf16[512,2048]{1,0:T(8,128)(2,1)} %fusion.4.hidden.refs_4_, bf16[512,2048]{1,0:T(8,128)(2,1)} %wo.3, bf16[512,512]{1,0:T(8,128)(2,1)} %get-tuple-element.52.q_in, bf16[512,512]{1,0:T(8,128)(2,1)} %get-tuple-element.53.k_in, bf16[512,512]{1,0:T(8,128)(2,1)} %get-tuple-element.54.v_in, ...), custom_call_target="tpu_custom_call" | custom-call | flops 6442450944 | bytes 7864320 | tf_op jit(solution)/shard_map/pallas_call | solution.py:154
  478.9 16.7 %shard_map.216.refs_3_ = bf16[3,512,512]{2,1,0:T(8,128)(2,1)} custom-call(bf16[512,2048]{1,0:T(8,128)(2,1)} %fusion.5.hidden.refs_5_, bf16[512,2048]{1,0:T(8,128)(2,1)} %wo.3, bf16[512,512]{1,0:T(8,128)(2,1)} %get-tuple-element.59.q_in, bf16[512,512]{1,0:T(8,128)(2,1)} %get-tuple-element.60.k_in, bf16[512,512]{1,0:T(8,128)(2,1)} %get-tuple-element.61.v_in, ...), custom_call_target="tpu_custom_call" | custom-call | flops 6442450944 | bytes 7864320 | tf_op jit(solution)/shard_map/pallas_call | solution.py:154
  495.7 9.8 outer.14
  505.5 13.5 %collective-permute-done.72.refs_8_ = f32[1024,2048]{1,0:T(8,128)} collective-permute-done((f32[1024,2048]{1,0:T(8,128)}, f32[1024,2048]{1,0:T(8,128)}, u32[]{:S(2)}, u32[]{:S(2)}) %collective-permute-start.72) | collective-permute-done | bytes 8388640 | tf_op jit(solution)/shard_map/ppermute | solution.py:280
  519.0 11.9 %outer.15 = f32[1024,2048]{1,0:T(8,128)} custom-call(s32[1]{0:T(128)} %bitcast.4.which, bf16[512,2048]{1,0:T(8,128)(2,1)} %get-tuple-element.62.refs_0_, bf16[512,2048]{1,0:T(8,128)(2,1)} %get-tuple-element.63.refs_1_, bf16[3,512,512]{2,1,0:T(8,128)(2,1)} %shard_map.215.refs_2_, bf16[3,512,512]{2,1,0:T(8,128)(2,1)} %shard_map.216.refs_3_, ...), custom_call_target="tpu_custom_call" | custom-call | flops 4294967296 | bytes 16777216 | tf_op jit(solution)/shard_map/outer/pallas_call | solution.py:254
  535.2 6.5 fusion.50
  543.6 6.0 fusion.42
  557.4 10.7 collective-permute-done.30
  570.7 19.9 %collective-permute-done.22 = f32[128,2048]{1,0:T(8,128)S(1)} collective-permute-done((f32[128,2048]{1,0:T(8,128)S(1)}, f32[128,2048]{1,0:T(8,128)S(1)}, u32[]{:S(2)}, u32[]{:S(2)}) %collective-permute-start.22) | collective-permute-done | bytes 1048608 | tf_op jit(solution)/shard_map/ppermute | solution.py:280
  593.1 8.7 collective-permute-done.33
  604.3 8.7 collective-permute-done.25
  617.2 7.2 collective-permute-done.36
  628.1 7.5 collective-permute-done.28
  638.2 20.8 %collective-permute-done.37 = f32[128,2048]{1,0:T(8,128)S(1)} collective-permute-done((f32[128,2048]{1,0:T(8,128)S(1)}, f32[128,2048]{1,0:T(8,128)S(1)}, u32[]{:S(2)}, u32[]{:S(2)}) %collective-permute-start.37) | collective-permute-done | bytes 1048608 | tf_op jit(solution)/shard_map/ppermute | solution.py:280
  659.3 21.0 %collective-permute-done.29 = f32[128,2048]{1,0:T(8,128)S(1)} collective-permute-done((f32[128,2048]{1,0:T(8,128)S(1)}, f32[128,2048]{1,0:T(8,128)S(1)}, u32[]{:S(2)}, u32[]{:S(2)}) %collective-permute-start.29) | collective-permute-done | bytes 1048608 | tf_op jit(solution)/shard_map/ppermute | solution.py:280
  702.0 35.8 %collective-permute-done.47 = f32[128,2048]{1,0:T(8,128)S(1)} collective-permute-done((f32[128,2048]{1,0:T(8,128)S(1)}, f32[128,2048]{1,0:T(8,128)S(1)}, u32[]{:S(2)}, u32[]{:S(2)}) %collective-permute-start.47) | collective-permute-done | bytes 1048608 | tf_op jit(solution)/shard_map/ppermute | solution.py:280
  743.4 10.1 collective-permute-done.50
  755.4 6.7 collective-permute-done.62
  769.1 3.0 collective-permute-done.68
  779.0 2.8 collective-permute-start.71
  782.4 5.3 collective-permute-done.51
  790.0 8.9 collective-permute-done.63
  801.1 20.3 %collective-permute-done.54 = f32[128,2048]{1,0:T(8,128)S(1)} collective-permute-done((f32[128,2048]{1,0:T(8,128)S(1)}, f32[128,2048]{1,0:T(8,128)S(1)}, u32[]{:S(2)}, u32[]{:S(2)}) %collective-permute-start.54) | collective-permute-done | bytes 1048608 | tf_op jit(solution)/shard_map/ppermute | solution.py:280
  821.8 21.3 %collective-permute-done.66 = f32[128,2048]{1,0:T(8,128)S(1)} collective-permute-done((f32[128,2048]{1,0:T(8,128)S(1)}, f32[128,2048]{1,0:T(8,128)S(1)}, u32[]{:S(2)}, u32[]{:S(2)}) %collective-permute-start.66) | collective-permute-done | bytes 1048608 | tf_op jit(solution)/shard_map/ppermute | solution.py:280
  843.5 4.0 pad_maximum_fusion
  851.2 267.6 %reduce-scatter.11.cloned.1.call-done = f32[256,4096]{1,0:T(8,128)} async-done(((f32[1024,4096]{1,0:T(8,128)}), f32[256,4096]{1,0:T(8,128)}) %reduce-scatter.11.cloned.1.call-update) | async-done | bytes 4194320 | tf_op jit(solution)/shard_map/reduce_scatter | solution.py:411
  1122.3 4.7 fusion.173
  (444 shorter events, 190.4 us)
Async XLA Ops:
  7.2 840.3 %reduce-scatter.5.cloned.1.call-start = ((), (), s32[]{:S(2)}) async-start(), calls=%async_computation.4 | async-start | bytes 10485760 | tf_op jit(solution)/shard_map/reduce_scatter | solution.py:411
  32.4 35.1 %collective-permute-start = (f32[128,2048]{1,0:T(8,128)}, f32[128,2048]{1,0:T(8,128)}, u32[]{:S(2)}, u32[]{:S(2)}) collective-permute-start(f32[128,2048]{1,0:T(8,128)} %get-tuple-element.176), channel_id=1, source_target_pairs={{0,1},{1,0},{2,3},{3,2},{4,5},{5,4},{6,7},{7,6},{8,9},{9,8},{10,11... | collective-permute-start | bytes 3145736 | tf_op jit(solution)/shard_map/ppermute | solution.py:280
  35.3 32.2 %collective-permute-start.2 = (f32[128,2048]{1,0:T(8,128)}, f32[128,2048]{1,0:T(8,128)}, u32[]{:S(2)}, u32[]{:S(2)}) collective-permute-start(f32[128,2048]{1,0:T(8,128)} %get-tuple-element.177), channel_id=1, source_target_pairs={{0,2},{1,3},{2,0},{3,1},{4,6},{5,7},{6,4},{7,5},{8,10},{9,11},{10,... | collective-permute-start | bytes 3145736 | tf_op jit(solution)/shard_map/ppermute | solution.py:280
  60.0 26.3 %collective-permute-start.8 = (f32[128,2048]{1,0:T(8,128)}, f32[128,2048]{1,0:T(8,128)}, u32[]{:S(2)}, u32[]{:S(2)}) collective-permute-start(f32[128,2048]{1,0:T(8,128)} %get-tuple-element.180), channel_id=1, source_target_pairs={{0,1},{1,0},{2,3},{3,2},{4,5},{5,4},{6,7},{7,6},{8,9},{9,8},{10,11... | collective-permute-start | bytes 3145736 | tf_op jit(solution)/shard_map/ppermute | solution.py:280
  60.5 26.3 %collective-permute-start.10 = (f32[128,2048]{1,0:T(8,128)}, f32[128,2048]{1,0:T(8,128)}, u32[]{:S(2)}, u32[]{:S(2)}) collective-permute-start(f32[128,2048]{1,0:T(8,128)} %get-tuple-element.181), channel_id=1, source_target_pairs={{0,2},{1,3},{2,0},{3,1},{4,6},{5,7},{6,4},{7,5},{8,10},{9,11},{10,... | collective-permute-start | bytes 3145736 | tf_op jit(solution)/shard_map/ppermute | solution.py:280
  70.9 26.5 %collective-permute-start.3 = (f32[64,2048]{1,0:T(8,128)S(1)}, f32[64,2048]{1,0:T(8,128)S(1)}, u32[]{:S(2)}, u32[]{:S(2)}) collective-permute-start(f32[64,2048]{1,0:T(8,128)S(1)} %constant_dynamic-slice_fusion.52), channel_id=1, source_target_pairs={{0,1},{1,0},{2,3},{3,2},{4,5},{5,4},{6,7},{7,6},{8,9},{9,8},{10,11... | collective-permute-start | bytes 1572872 | tf_op jit(solution)/shard_map/ppermute | solution.py:280
  73.0 25.0 %collective-permute-start.1 = (f32[64,2048]{1,0:T(8,128)S(1)}, f32[64,2048]{1,0:T(8,128)S(1)}, u32[]{:S(2)}, u32[]{:S(2)}) collective-permute-start(f32[64,2048]{1,0:T(8,128)S(1)} %constant_dynamic-slice_fusion.53), channel_id=1, source_target_pairs={{0,2},{1,3},{2,0},{3,1},{4,6},{5,7},{6,4},{7,5},{8,10},{9,11},{10,... | collective-permute-start | bytes 1572872 | tf_op jit(solution)/shard_map/ppermute | solution.py:280
  88.8 19.8 %collective-permute-start.11 = (f32[64,2048]{1,0:T(8,128)S(1)}, f32[64,2048]{1,0:T(8,128)S(1)}, u32[]{:S(2)}, u32[]{:S(2)}) collective-permute-start(f32[64,2048]{1,0:T(8,128)S(1)} %constant_dynamic-slice_fusion.42), channel_id=1, source_target_pairs={{0,1},{1,0},{2,3},{3,2},{4,5},{5,4},{6,7},{7,6},{8,9},{9,8},{10,11... | collective-permute-start | bytes 1572872 | tf_op jit(solution)/shard_map/ppermute | solution.py:280
  90.4 18.8 %collective-permute-start.9 = (f32[64,2048]{1,0:T(8,128)S(1)}, f32[64,2048]{1,0:T(8,128)S(1)}, u32[]{:S(2)}, u32[]{:S(2)}) collective-permute-start(f32[64,2048]{1,0:T(8,128)S(1)} %constant_dynamic-slice_fusion.43), channel_id=1, source_target_pairs={{0,2},{1,3},{2,0},{3,1},{4,6},{5,7},{6,4},{7,5},{8,10},{9,11},{10,... | collective-permute-start | bytes 1572872 | tf_op jit(solution)/shard_map/ppermute | solution.py:280
  99.4 21.1 %collective-permute-start.4 = (f32[64,2048]{1,0:T(8,128)S(1)}, f32[64,2048]{1,0:T(8,128)S(1)}, u32[]{:S(2)}, u32[]{:S(2)}) collective-permute-start(f32[64,2048]{1,0:T(8,128)S(1)} %get-tuple-element.202), channel_id=1, source_target_pairs={{0,2},{1,3},{2,0},{3,1},{4,6},{5,7},{6,4},{7,5},{8,10},{9,11},{10,... | collective-permute-start | bytes 1572872 | tf_op jit(solution)/shard_map/ppermute | solution.py:280
  99.5 20.4 %collective-permute-start.6 = (f32[64,2048]{1,0:T(8,128)S(1)}, f32[64,2048]{1,0:T(8,128)S(1)}, u32[]{:S(2)}, u32[]{:S(2)}) collective-permute-start(f32[64,2048]{1,0:T(8,128)S(1)} %get-tuple-element.203), channel_id=1, source_target_pairs={{0,1},{1,0},{2,3},{3,2},{4,5},{5,4},{6,7},{7,6},{8,9},{9,8},{10,11... | collective-permute-start | bytes 1572872 | tf_op jit(solution)/shard_map/ppermute | solution.py:280
  112.3 26.6 %collective-permute-start.12 = (f32[64,2048]{1,0:T(8,128)}, f32[64,2048]{1,0:T(8,128)}, u32[]{:S(2)}, u32[]{:S(2)}) collective-permute-start(f32[64,2048]{1,0:T(8,128)} %get-tuple-element.200), channel_id=1, source_target_pairs={{0,2},{1,3},{2,0},{3,1},{4,6},{5,7},{6,4},{7,5},{8,10},{9,11},{10,... | collective-permute-start | bytes 1572872 | tf_op jit(solution)/shard_map/ppermute | solution.py:280
  112.4 23.9 %collective-permute-start.14 = (f32[64,2048]{1,0:T(8,128)}, f32[64,2048]{1,0:T(8,128)}, u32[]{:S(2)}, u32[]{:S(2)}) collective-permute-start(f32[64,2048]{1,0:T(8,128)} %get-tuple-element.201), channel_id=1, source_target_pairs={{0,1},{1,0},{2,3},{3,2},{4,5},{5,4},{6,7},{7,6},{8,9},{9,8},{10,11... | collective-permute-start | bytes 1572872 | tf_op jit(solution)/shard_map/ppermute | solution.py:280
  120.0 34.3 %collective-permute-start.7 = (f32[128,2048]{1,0:T(8,128)S(1)}, f32[128,2048]{1,0:T(8,128)}, u32[]{:S(2)}, u32[]{:S(2)}) collective-permute-start(f32[128,2048]{1,0:T(8,128)S(1)} %maximum_select_fusion.17), channel_id=1, source_target_pairs={{0,2},{1,3},{2,0},{3,1},{4,6},{5,7},{6,4},{7,5},{8,10},{9,11},{10,... | collective-permute-start | bytes 3145736 | tf_op jit(solution)/shard_map/ppermute | solution.py:280
  121.7 34.4 %collective-permute-start.5 = (f32[128,2048]{1,0:T(8,128)}, f32[128,2048]{1,0:T(8,128)}, u32[]{:S(2)}, u32[]{:S(2)}) collective-permute-start(f32[128,2048]{1,0:T(8,128)} %maximum_select_fusion.16), channel_id=1, source_target_pairs={{0,1},{1,0},{2,3},{3,2},{4,5},{5,4},{6,7},{7,6},{8,9},{9,8},{10,11... | collective-permute-start | bytes 3145736 | tf_op jit(solution)/shard_map/ppermute | solution.py:280
  138.1 36.5 %collective-permute-start.15 = (f32[128,2048]{1,0:T(8,128)S(1)}, f32[128,2048]{1,0:T(8,128)S(1)}, u32[]{:S(2)}, u32[]{:S(2)}) collective-permute-start(f32[128,2048]{1,0:T(8,128)S(1)} %maximum_select_fusion.19), channel_id=1, source_target_pairs={{0,2},{1,3},{2,0},{3,1},{4,6},{5,7},{6,4},{7,5},{8,10},{9,11},{10,... | collective-permute-start | bytes 3145736 | tf_op jit(solution)/shard_map/ppermute | solution.py:280
  140.7 40.0 %collective-permute-start.13 = (f32[128,2048]{1,0:T(8,128)S(1)}, f32[128,2048]{1,0:T(8,128)S(1)}, u32[]{:S(2)}, u32[]{:S(2)}) collective-permute-start(f32[128,2048]{1,0:T(8,128)S(1)} %maximum_select_fusion.18), channel_id=1, source_target_pairs={{0,1},{1,0},{2,3},{3,2},{4,5},{5,4},{6,7},{7,6},{8,9},{9,8},{10,11... | collective-permute-start | bytes 3145736 | tf_op jit(solution)/shard_map/ppermute | solution.py:280
  212.3 26.7 %collective-permute-start.16 = (f32[1024,1024]{1,0:T(8,128)}, f32[1024,1024]{1,0:T(8,128)}, u32[]{:S(2)}, u32[]{:S(2)}) collective-permute-start(f32[1024,1024]{1,0:T(8,128)} %outer.8), channel_id=1, source_target_pairs={{0,4},{4,0},{8,12},{12,8},{16,20},{20,16},{24,28},{28,24},{1,5},{5... | collective-permute-start | bytes 12582920 | tf_op jit(solution)/shard_map/ppermute | solution.py:280
  218.7 27.7 %collective-permute-start.17 = (f32[1024,1024]{1,0:T(8,128)}, f32[1024,1024]{1,0:T(8,128)}, u32[]{:S(2)}, u32[]{:S(2)}) collective-permute-start(f32[1024,1024]{1,0:T(8,128)} %outer.10), channel_id=1, source_target_pairs={{0,4},{4,0},{8,12},{12,8},{16,20},{20,16},{24,28},{28,24},{1,5},{5... | collective-permute-start | bytes 12582920 | tf_op jit(solution)/shard_map/ppermute | solution.py:280
  276.6 165.5 %collective-permute-start.46 = (f32[1024,4096]{1,0:T(8,128)}, f32[1024,4096]{1,0:T(8,128)}, u32[]{:S(2)}, u32[]{:S(2)}) collective-permute-start(f32[1024,4096]{1,0:T(8,128)} %outer.12), channel_id=1, source_target_pairs={{0,4},{4,0},{8,12},{12,8},{16,20},{20,16},{24,28},{28,24},{1,5},{5... | collective-permute-start | bytes 50331656 | tf_op jit(solution)/shard_map/ppermute | solution.py:280
  283.6 25.6 %collective-permute-start.38 = (f32[128,2048]{1,0:T(8,128)S(1)}, f32[128,2048]{1,0:T(8,128)S(1)}, u32[]{:S(2)}, u32[]{:S(2)}) collective-permute-start(f32[128,2048]{1,0:T(8,128)S(1)} %get-tuple-element.136), channel_id=1, source_target_pairs={{0,1},{1,0},{2,3},{3,2},{4,5},{5,4},{6,7},{7,6},{8,9},{9,8},{10,11... | collective-permute-start | bytes 3145736 | tf_op jit(solution)/shard_map/ppermute | solution.py:280
  285.2 25.3 %collective-permute-start.40 = (f32[128,2048]{1,0:T(8,128)S(1)}, f32[128,2048]{1,0:T(8,128)S(1)}, u32[]{:S(2)}, u32[]{:S(2)}) collective-permute-start(f32[128,2048]{1,0:T(8,128)S(1)} %get-tuple-element.137), channel_id=1, source_target_pairs={{0,2},{1,3},{2,0},{3,1},{4,6},{5,7},{6,4},{7,5},{8,10},{9,11},{10,... | collective-permute-start | bytes 3145736 | tf_op jit(solution)/shard_map/ppermute | solution.py:280
  335.0 23.4 %collective-permute-start.18 = (f32[128,2048]{1,0:T(8,128)S(1)}, f32[128,2048]{1,0:T(8,128)S(1)}, u32[]{:S(2)}, u32[]{:S(2)}) collective-permute-start(f32[128,2048]{1,0:T(8,128)S(1)} %get-tuple-element.164), channel_id=1, source_target_pairs={{0,1},{1,0},{2,3},{3,2},{4,5},{5,4},{6,7},{7,6},{8,9},{9,8},{10,11... | collective-permute-start | bytes 3145736 | tf_op jit(solution)/shard_map/ppermute | solution.py:280
  336.5 23.0 %collective-permute-start.20 = (f32[128,2048]{1,0:T(8,128)S(1)}, f32[128,2048]{1,0:T(8,128)S(1)}, u32[]{:S(2)}, u32[]{:S(2)}) collective-permute-start(f32[128,2048]{1,0:T(8,128)S(1)} %get-tuple-element.165), channel_id=1, source_target_pairs={{0,2},{1,3},{2,0},{3,1},{4,6},{5,7},{6,4},{7,5},{8,10},{9,11},{10,... | collective-permute-start | bytes 3145736 | tf_op jit(solution)/shard_map/ppermute | solution.py:280
  383.3 39.5 %collective-permute-start.45 = (f32[128,2048]{1,0:T(8,128)S(1)}, f32[128,2048]{1,0:T(8,128)S(1)}, u32[]{:S(2)}, u32[]{:S(2)}) collective-permute-start(f32[128,2048]{1,0:T(8,128)S(1)} %maximum_select_fusion.25), channel_id=1, source_target_pairs={{0,2},{1,3},{2,0},{3,1},{4,6},{5,7},{6,4},{7,5},{8,10},{9,11},{10,... | collective-permute-start | bytes 3145736 | tf_op jit(solution)/shard_map/ppermute | solution.py:280
  384.5 14.9 %collective-permute-start.57 = (f32[64,2048]{1,0:T(8,128)S(1)}, f32[64,2048]{1,0:T(8,128)S(1)}, u32[]{:S(2)}, u32[]{:S(2)}) collective-permute-start(f32[64,2048]{1,0:T(8,128)S(1)} %get-tuple-element.193), channel_id=1, source_target_pairs={{0,1},{1,0},{2,3},{3,2},{4,5},{5,4},{6,7},{7,6},{8,9},{9,8},{10,11... | collective-permute-start | bytes 1572872 | tf_op jit(solution)/shard_map/ppermute | solution.py:280
  385.5 35.1 %collective-permute-start.55 = (f32[64,2048]{1,0:T(8,128)S(1)}, f32[64,2048]{1,0:T(8,128)S(1)}, u32[]{:S(2)}, u32[]{:S(2)}) collective-permute-start(f32[64,2048]{1,0:T(8,128)S(1)} %get-tuple-element.192), channel_id=1, source_target_pairs={{0,2},{1,3},{2,0},{3,1},{4,6},{5,7},{6,4},{7,5},{8,10},{9,11},{10,... | collective-permute-start | bytes 1572872 | tf_op jit(solution)/shard_map/ppermute | solution.py:280
  387.7 35.4 %collective-permute-start.43 = (f32[128,2048]{1,0:T(8,128)S(1)}, f32[128,2048]{1,0:T(8,128)S(1)}, u32[]{:S(2)}, u32[]{:S(2)}) collective-permute-start(f32[128,2048]{1,0:T(8,128)S(1)} %maximum_select_fusion.24), channel_id=1, source_target_pairs={{0,1},{1,0},{2,3},{3,2},{4,5},{5,4},{6,7},{7,6},{8,9},{9,8},{10,11... | collective-permute-start | bytes 3145736 | tf_op jit(solution)/shard_map/ppermute | solution.py:280
  399.5 39.9 %collective-permute-start.58 = (f32[128,2048]{1,0:T(8,128)S(1)}, f32[128,2048]{1,0:T(8,128)S(1)}, u32[]{:S(2)}, u32[]{:S(2)}) collective-permute-start(f32[128,2048]{1,0:T(8,128)S(1)} %maximum_select_fusion.29), channel_id=1, source_target_pairs={{0,2},{1,3},{2,0},{3,1},{4,6},{5,7},{6,4},{7,5},{8,10},{9,11},{10,... | collective-permute-start | bytes 3145736 | tf_op jit(solution)/shard_map/ppermute | solution.py:280
  420.7 18.7 %collective-permute-start.56 = (f32[128,2048]{1,0:T(8,128)S(1)}, f32[128,2048]{1,0:T(8,128)S(1)}, u32[]{:S(2)}, u32[]{:S(2)}) collective-permute-start(f32[128,2048]{1,0:T(8,128)S(1)} %maximum_select_fusion.28), channel_id=1, source_target_pairs={{0,1},{1,0},{2,3},{3,2},{4,5},{5,4},{6,7},{7,6},{8,9},{9,8},{10,11... | collective-permute-start | bytes 3145736 | tf_op jit(solution)/shard_map/ppermute | solution.py:280
  531.0 320.2 %reduce-scatter.7.cloned.1.call-start = ((), (), s32[]{:S(2)}) async-start(), calls=%async_computation.5 | async-start | bytes 5242880 | tf_op jit(solution)/shard_map/reduce_scatter | solution.py:411
  531.7 319.5 %reduce-scatter.9.cloned.1.call-start = ((), (), s32[]{:S(2)}) async-start(), calls=%async_computation.6 | async-start | bytes 5242880 | tf_op jit(solution)/shard_map/reduce_scatter | solution.py:411
  532.4 586.3 %reduce-scatter.11.cloned.1.call-start = ((), (), s32[]{:S(2)}) async-start(), calls=%async_computation.7 | async-start | bytes 20971520 | tf_op jit(solution)/shard_map/reduce_scatter | solution.py:411
  542.0 26.1 %collective-permute-start.30 = (f32[128,2048]{1,0:T(8,128)S(1)}, f32[128,2048]{1,0:T(8,128)S(1)}, u32[]{:S(2)}, u32[]{:S(2)}) collective-permute-start(f32[128,2048]{1,0:T(8,128)S(1)} %get-tuple-element.156), channel_id=1, source_target_pairs={{0,1},{1,0},{2,3},{3,2},{4,5},{5,4},{6,7},{7,6},{8,9},{9,8},{10,11... | collective-permute-start | bytes 3145736 | tf_op jit(solution)/shard_map/ppermute | solution.py:280
  543.0 26.0 %collective-permute-start.32 = (f32[128,2048]{1,0:T(8,128)S(1)}, f32[128,2048]{1,0:T(8,128)S(1)}, u32[]{:S(2)}, u32[]{:S(2)}) collective-permute-start(f32[128,2048]{1,0:T(8,128)S(1)} %get-tuple-element.157), channel_id=1, source_target_pairs={{0,2},{1,3},{2,0},{3,1},{4,6},{5,7},{6,4},{7,5},{8,10},{9,11},{10,... | collective-permute-start | bytes 3145736 | tf_op jit(solution)/shard_map/ppermute | solution.py:280
  549.8 40.8 %collective-permute-start.22 = (f32[128,2048]{1,0:T(8,128)S(1)}, f32[128,2048]{1,0:T(8,128)S(1)}, u32[]{:S(2)}, u32[]{:S(2)}) collective-permute-start(f32[128,2048]{1,0:T(8,128)S(1)} %get-tuple-element.148), channel_id=1, source_target_pairs={{0,1},{1,0},{2,3},{3,2},{4,5},{5,4},{6,7},{7,6},{8,9},{9,8},{10,11... | collective-permute-start | bytes 3145736 | tf_op jit(solution)/shard_map/ppermute | solution.py:280
  550.7 40.8 %collective-permute-start.24 = (f32[128,2048]{1,0:T(8,128)S(1)}, f32[128,2048]{1,0:T(8,128)S(1)}, u32[]{:S(2)}, u32[]{:S(2)}) collective-permute-start(f32[128,2048]{1,0:T(8,128)S(1)} %get-tuple-element.149), channel_id=1, source_target_pairs={{0,2},{1,3},{2,0},{3,1},{4,6},{5,7},{6,4},{7,5},{8,10},{9,11},{10,... | collective-permute-start | bytes 3145736 | tf_op jit(solution)/shard_map/ppermute | solution.py:280
  569.4 32.4 %collective-permute-start.33 = (f32[64,2048]{1,0:T(8,128)S(1)}, f32[64,2048]{1,0:T(8,128)S(1)}, u32[]{:S(2)}, u32[]{:S(2)}) collective-permute-start(f32[64,2048]{1,0:T(8,128)S(1)} %constant_dynamic-slice_fusion.20), channel_id=1, source_target_pairs={{0,1},{1,0},{2,3},{3,2},{4,5},{5,4},{6,7},{7,6},{8,9},{9,8},{10,11... | collective-permute-start | bytes 1572872 | tf_op jit(solution)/shard_map/ppermute | solution.py:280
  570.6 32.1 %collective-permute-start.31 = (f32[64,2048]{1,0:T(8,128)S(1)}, f32[64,2048]{1,0:T(8,128)S(1)}, u32[]{:S(2)}, u32[]{:S(2)}) collective-permute-start(f32[64,2048]{1,0:T(8,128)S(1)} %constant_dynamic-slice_fusion.21), channel_id=1, source_target_pairs={{0,2},{1,3},{2,0},{3,1},{4,6},{5,7},{6,4},{7,5},{8,10},{9,11},{10,... | collective-permute-start | bytes 1572872 | tf_op jit(solution)/shard_map/ppermute | solution.py:280
  592.0 21.1 %collective-permute-start.25 = (f32[64,2048]{1,0:T(8,128)S(1)}, f32[64,2048]{1,0:T(8,128)S(1)}, u32[]{:S(2)}, u32[]{:S(2)}) collective-permute-start(f32[64,2048]{1,0:T(8,128)S(1)} %constant_dynamic-slice_fusion.26), channel_id=1, source_target_pairs={{0,1},{1,0},{2,3},{3,2},{4,5},{5,4},{6,7},{7,6},{8,9},{9,8},{10,11... | collective-permute-start | bytes 1572872 | tf_op jit(solution)/shard_map/ppermute | solution.py:280
  593.1 20.9 %collective-permute-start.23 = (f32[64,2048]{1,0:T(8,128)S(1)}, f32[64,2048]{1,0:T(8,128)S(1)}, u32[]{:S(2)}, u32[]{:S(2)}) collective-permute-start(f32[64,2048]{1,0:T(8,128)S(1)} %constant_dynamic-slice_fusion.27), channel_id=1, source_target_pairs={{0,2},{1,3},{2,0},{3,1},{4,6},{5,7},{6,4},{7,5},{8,10},{9,11},{10,... | collective-permute-start | bytes 1572872 | tf_op jit(solution)/shard_map/ppermute | solution.py:280
  603.1 22.7 %collective-permute-start.34 = (f32[64,2048]{1,0:T(8,128)S(1)}, f32[64,2048]{1,0:T(8,128)}, u32[]{:S(2)}, u32[]{:S(2)}) collective-permute-start(f32[64,2048]{1,0:T(8,128)S(1)} %get-tuple-element.198), channel_id=1, source_target_pairs={{0,2},{1,3},{2,0},{3,1},{4,6},{5,7},{6,4},{7,5},{8,10},{9,11},{10,... | collective-permute-start | bytes 1572872 | tf_op jit(solution)/shard_map/ppermute | solution.py:280
  603.2 21.2 %collective-permute-start.36 = (f32[64,2048]{1,0:T(8,128)S(1)}, f32[64,2048]{1,0:T(8,128)}, u32[]{:S(2)}, u32[]{:S(2)}) collective-permute-start(f32[64,2048]{1,0:T(8,128)S(1)} %get-tuple-element.199), channel_id=1, source_target_pairs={{0,1},{1,0},{2,3},{3,2},{4,5},{5,4},{6,7},{7,6},{8,9},{9,8},{10,11... | collective-permute-start | bytes 1572872 | tf_op jit(solution)/shard_map/ppermute | solution.py:280
  614.3 21.3 %collective-permute-start.28 = (f32[64,2048]{1,0:T(8,128)S(1)}, f32[64,2048]{1,0:T(8,128)}, u32[]{:S(2)}, u32[]{:S(2)}) collective-permute-start(f32[64,2048]{1,0:T(8,128)S(1)} %get-tuple-element.197), channel_id=1, source_target_pairs={{0,1},{1,0},{2,3},{3,2},{4,5},{5,4},{6,7},{7,6},{8,9},{9,8},{10,11... | collective-permute-start | bytes 1572872 | tf_op jit(solution)/shard_map/ppermute | solution.py:280
  617.2 19.8 %collective-permute-start.26 = (f32[64,2048]{1,0:T(8,128)S(1)}, f32[64,2048]{1,0:T(8,128)S(1)}, u32[]{:S(2)}, u32[]{:S(2)}) collective-permute-start(f32[64,2048]{1,0:T(8,128)S(1)} %get-tuple-element.196), channel_id=1, source_target_pairs={{0,2},{1,3},{2,0},{3,1},{4,6},{5,7},{6,4},{7,5},{8,10},{9,11},{10,... | collective-permute-start | bytes 1572872 | tf_op jit(solution)/shard_map/ppermute | solution.py:280
  625.7 33.2 %collective-permute-start.37 = (f32[128,2048]{1,0:T(8,128)S(1)}, f32[128,2048]{1,0:T(8,128)S(1)}, u32[]{:S(2)}, u32[]{:S(2)}) collective-permute-start(f32[128,2048]{1,0:T(8,128)S(1)} %maximum_select_fusion.23), channel_id=1, source_target_pairs={{0,2},{1,3},{2,0},{3,1},{4,6},{5,7},{6,4},{7,5},{8,10},{9,11},{10,... | collective-permute-start | bytes 3145736 | tf_op jit(solution)/shard_map/ppermute | solution.py:280
  627.1 32.0 %collective-permute-start.35 = (f32[128,2048]{1,0:T(8,128)S(1)}, f32[128,2048]{1,0:T(8,128)S(1)}, u32[]{:S(2)}, u32[]{:S(2)}) collective-permute-start(f32[128,2048]{1,0:T(8,128)S(1)} %maximum_select_fusion.22), channel_id=1, source_target_pairs={{0,1},{1,0},{2,3},{3,2},{4,5},{5,4},{6,7},{7,6},{8,9},{9,8},{10,11... | collective-permute-start | bytes 3145736 | tf_op jit(solution)/shard_map/ppermute | solution.py:280
  636.9 43.4 %collective-permute-start.29 = (f32[128,2048]{1,0:T(8,128)S(1)}, f32[128,2048]{1,0:T(8,128)S(1)}, u32[]{:S(2)}, u32[]{:S(2)}) collective-permute-start(f32[128,2048]{1,0:T(8,128)S(1)} %maximum_select_fusion.21), channel_id=1, source_target_pairs={{0,2},{1,3},{2,0},{3,1},{4,6},{5,7},{6,4},{7,5},{8,10},{9,11},{10,... | collective-permute-start | bytes 3145736 | tf_op jit(solution)/shard_map/ppermute | solution.py:280
  637.1 43.4 %collective-permute-start.27 = (f32[128,2048]{1,0:T(8,128)S(1)}, f32[128,2048]{1,0:T(8,128)S(1)}, u32[]{:S(2)}, u32[]{:S(2)}) collective-permute-start(f32[128,2048]{1,0:T(8,128)S(1)} %maximum_select_fusion.20), channel_id=1, source_target_pairs={{0,1},{1,0},{2,3},{3,2},{4,5},{5,4},{6,7},{7,6},{8,9},{9,8},{10,11... | collective-permute-start | bytes 3145736 | tf_op jit(solution)/shard_map/ppermute | solution.py:280
  690.7 49.8 %collective-permute-start.59 = (f32[128,2048]{1,0:T(8,128)S(1)}, f32[128,2048]{1,0:T(8,128)S(1)}, u32[]{:S(2)}, u32[]{:S(2)}) collective-permute-start(f32[128,2048]{1,0:T(8,128)S(1)} %get-tuple-element.132), channel_id=1, source_target_pairs={{0,1},{1,0},{2,3},{3,2},{4,5},{5,4},{6,7},{7,6},{8,9},{9,8},{10,11... | collective-permute-start | bytes 3145736 | tf_op jit(solution)/shard_map/ppermute | solution.py:280
  692.2 48.3 %collective-permute-start.61 = (f32[128,2048]{1,0:T(8,128)S(1)}, f32[128,2048]{1,0:T(8,128)S(1)}, u32[]{:S(2)}, u32[]{:S(2)}) collective-permute-start(f32[128,2048]{1,0:T(8,128)S(1)} %get-tuple-element.133), channel_id=1, source_target_pairs={{0,2},{1,3},{2,0},{3,1},{4,6},{5,7},{6,4},{7,5},{8,10},{9,11},{10,... | collective-permute-start | bytes 3145736 | tf_op jit(solution)/shard_map/ppermute | solution.py:280
  695.1 42.8 %collective-permute-start.47 = (f32[128,2048]{1,0:T(8,128)S(1)}, f32[128,2048]{1,0:T(8,128)S(1)}, u32[]{:S(2)}, u32[]{:S(2)}) collective-permute-start(f32[128,2048]{1,0:T(8,128)S(1)} %get-tuple-element.126), channel_id=1, source_target_pairs={{0,1},{1,0},{2,3},{3,2},{4,5},{5,4},{6,7},{7,6},{8,9},{9,8},{10,11... | collective-permute-start | bytes 3145736 | tf_op jit(solution)/shard_map/ppermute | solution.py:280
  696.3 42.1 %collective-permute-start.49 = (f32[128,2048]{1,0:T(8,128)S(1)}, f32[128,2048]{1,0:T(8,128)S(1)}, u32[]{:S(2)}, u32[]{:S(2)}) collective-permute-start(f32[128,2048]{1,0:T(8,128)S(1)} %get-tuple-element.127), channel_id=1, source_target_pairs={{0,2},{1,3},{2,0},{3,1},{4,6},{5,7},{6,4},{7,5},{8,10},{9,11},{10,... | collective-permute-start | bytes 3145736 | tf_op jit(solution)/shard_map/ppermute | solution.py:280
  738.7 14.9 %collective-permute-start.50 = (f32[64,2048]{1,0:T(8,128)S(1)}, f32[64,2048]{1,0:T(8,128)S(1)}, u32[]{:S(2)}, u32[]{:S(2)}) collective-permute-start(f32[64,2048]{1,0:T(8,128)S(1)} %constant_dynamic-slice_fusion.6), channel_id=1, source_target_pairs={{0,1},{1,0},{2,3},{3,2},{4,5},{5,4},{6,7},{7,6},{8,9},{9,8},{10,11... | collective-permute-start | bytes 1572872 | tf_op jit(solution)/shard_map/ppermute | solution.py:280
  740.0 14.9 %collective-permute-start.48 = (f32[64,2048]{1,0:T(8,128)S(1)}, f32[64,2048]{1,0:T(8,128)S(1)}, u32[]{:S(2)}, u32[]{:S(2)}) collective-permute-start(f32[64,2048]{1,0:T(8,128)S(1)} %constant_dynamic-slice_fusion.7), channel_id=1, source_target_pairs={{0,2},{1,3},{2,0},{3,1},{4,6},{5,7},{6,4},{7,5},{8,10},{9,11},{10,... | collective-permute-start | bytes 1572872 | tf_op jit(solution)/shard_map/ppermute | solution.py:280
  740.9 21.2 %collective-permute-start.62 = (f32[64,2048]{1,0:T(8,128)S(1)}, f32[64,2048]{1,0:T(8,128)S(1)}, u32[]{:S(2)}, u32[]{:S(2)}) collective-permute-start(f32[64,2048]{1,0:T(8,128)S(1)} %constant_dynamic-slice_fusion.2), channel_id=1, source_target_pairs={{0,1},{1,0},{2,3},{3,2},{4,5},{5,4},{6,7},{7,6},{8,9},{9,8},{10,11... | collective-permute-start | bytes 1572872 | tf_op jit(solution)/shard_map/ppermute | solution.py:280
  742.2 21.1 %collective-permute-start.60 = (f32[64,2048]{1,0:T(8,128)S(1)}, f32[64,2048]{1,0:T(8,128)S(1)}, u32[]{:S(2)}, u32[]{:S(2)}) collective-permute-start(f32[64,2048]{1,0:T(8,128)S(1)} %constant_dynamic-slice_fusion.3), channel_id=1, source_target_pairs={{0,2},{1,3},{2,0},{3,1},{4,6},{5,7},{6,4},{7,5},{8,10},{9,11},{10,... | collective-permute-start | bytes 1572872 | tf_op jit(solution)/shard_map/ppermute | solution.py:280
  765.0 16.8 %collective-permute-start.53 = (f32[64,2048]{1,0:T(8,128)S(1)}, f32[64,2048]{1,0:T(8,128)S(1)}, u32[]{:S(2)}, u32[]{:S(2)}) collective-permute-start(f32[64,2048]{1,0:T(8,128)S(1)} %get-tuple-element.189), channel_id=1, source_target_pairs={{0,1},{1,0},{2,3},{3,2},{4,5},{5,4},{6,7},{7,6},{8,9},{9,8},{10,11... | collective-permute-start | bytes 1572872 | tf_op jit(solution)/shard_map/ppermute | solution.py:280
  772.2 17.3 %collective-permute-start.65 = (f32[64,2048]{1,0:T(8,128)S(1)}, f32[64,2048]{1,0:T(8,128)S(1)}, u32[]{:S(2)}, u32[]{:S(2)}) collective-permute-start(f32[64,2048]{1,0:T(8,128)S(1)} %get-tuple-element.191), channel_id=1, source_target_pairs={{0,1},{1,0},{2,3},{3,2},{4,5},{5,4},{6,7},{7,6},{8,9},{9,8},{10,11... | collective-permute-start | bytes 1572872 | tf_op jit(solution)/shard_map/ppermute | solution.py:280
  777.8 21.1 %collective-permute-start.63 = (f32[64,2048]{1,0:T(8,128)S(1)}, f32[64,2048]{1,0:T(8,128)S(1)}, u32[]{:S(2)}, u32[]{:S(2)}) collective-permute-start(f32[64,2048]{1,0:T(8,128)S(1)} %get-tuple-element.190), channel_id=1, source_target_pairs={{0,2},{1,3},{2,0},{3,1},{4,6},{5,7},{6,4},{7,5},{8,10},{9,11},{10,... | collective-permute-start | bytes 1572872 | tf_op jit(solution)/shard_map/ppermute | solution.py:280
  781.9 39.5 %collective-permute-start.54 = (f32[128,2048]{1,0:T(8,128)S(1)}, f32[128,2048]{1,0:T(8,128)S(1)}, u32[]{:S(2)}, u32[]{:S(2)}) collective-permute-start(f32[128,2048]{1,0:T(8,128)S(1)} %maximum_select_fusion.27), channel_id=1, source_target_pairs={{0,2},{1,3},{2,0},{3,1},{4,6},{5,7},{6,4},{7,5},{8,10},{9,11},{10,... | collective-permute-start | bytes 3145736 | tf_op jit(solution)/shard_map/ppermute | solution.py:280
  788.0 33.6 %collective-permute-start.52 = (f32[128,2048]{1,0:T(8,128)S(1)}, f32[128,2048]{1,0:T(8,128)S(1)}, u32[]{:S(2)}, u32[]{:S(2)}) collective-permute-start(f32[128,2048]{1,0:T(8,128)S(1)} %maximum_select_fusion.26), channel_id=1, source_target_pairs={{0,1},{1,0},{2,3},{3,2},{4,5},{5,4},{6,7},{7,6},{8,9},{9,8},{10,11... | collective-permute-start | bytes 3145736 | tf_op jit(solution)/shard_map/ppermute | solution.py:280
  789.7 53.4 %collective-permute-start.66 = (f32[128,2048]{1,0:T(8,128)S(1)}, f32[128,2048]{1,0:T(8,128)S(1)}, u32[]{:S(2)}, u32[]{:S(2)}) collective-permute-start(f32[128,2048]{1,0:T(8,128)S(1)} %maximum_select_fusion.31), channel_id=1, source_target_pairs={{0,2},{1,3},{2,0},{3,1},{4,6},{5,7},{6,4},{7,5},{8,10},{9,11},{10,... | collective-permute-start | bytes 3145736 | tf_op jit(solution)/shard_map/ppermute | solution.py:280
  799.0 44.3 %collective-permute-start.64 = (f32[128,2048]{1,0:T(8,128)S(1)}, f32[128,2048]{1,0:T(8,128)S(1)}, u32[]{:S(2)}, u32[]{:S(2)}) collective-permute-start(f32[128,2048]{1,0:T(8,128)S(1)} %maximum_select_fusion.30), channel_id=1, source_target_pairs={{0,1},{1,0},{2,3},{3,2},{4,5},{5,4},{6,7},{7,6},{8,9},{9,8},{10,11... | collective-permute-start | bytes 3145736 | tf_op jit(solution)/shard_map/ppermute | solution.py:280
  (80 other events, 1185.8 us)
Sparse Core Ops, SparseCore 0:
  531.1 144.3 reduce-scatter.4
  677.8 77.3 reduce-scatter.6
  757.5 77.9 reduce-scatter.8
  837.8 280.9 reduce-scatter.10

commit v6 on v5

--- a/solution.py
+++ b/solution.py
@@ -224,11 +224,11 @@
                 column += tile
 
 
-def outer(groups, which, pieces, add=None, part=(0, 1), flipped=False):
+def outer(groups, which, pieces, add=None, part=None, flipped=False):
     piece = groups[0][0][0].shape[0 if flipped else 1] // pieces
-    index, parts = part
+    indices, parts = part or ((0,) * len(groups), 1)
     specs, args, out_cols, work, moved = [], [], 0, 0, 0
-    for lefts, rights in groups:
+    for index, (lefts, rights) in zip(indices, groups):
         for v in lefts:
             if flipped:
                 specs.append(pl.BlockSpec((piece, v.shape[1]), lambda j, w: (2 * j + w[0], 0)))
@@ -241,7 +241,7 @@
                 specs.append(pl.BlockSpec(v.shape, lambda j, w: (0, 0, 0)))
             else:
                 cols = v.shape[1] // parts
-                specs.append(pl.BlockSpec((v.shape[0], cols), lambda j, w: (0, index)))
+                specs.append(pl.BlockSpec((v.shape[0], cols), lambda j, w, at=index: (0, at)))
             moved += v.size // parts * 2
         work += sum(v.shape[-2] for v in rights) * cols
         out_cols += cols
@@ -402,7 +402,7 @@
                 [lax.dynamic_slice_in_dim(value, start, size, 0) for start in starts], axis=0
             )
 
-        def core_sum(groups, part=(0, 1), flipped=False):
+        def core_sum(groups, part=None, flipped=False):
             away = outer(groups, 1 - core, dp_size, part=part, flipped=flipped)
             got = data.swap(away, 1)
             return outer(groups, core, dp_size, add=got, part=part, flipped=flipped)
@@ -464,8 +464,8 @@
             s.inner = (s.gate_pre * s.sig * s.up_pre).astype(BF16)
         flipped_rows = flip_rows(cotangent, token_mask)
         down_parts = [
-            core_sum([([flipped_rows], [s.inner for s in saved])], (i, 2), True)
-            for i in range(2)
+            core_sum([([flipped_rows], [s.inner for s in saved])] * len(at), (at, 4), True)
+            for at in ((0,), (1, 2, 3))
         ]
         down_sums = [z_scatter(v) for v in down_parts]
 

time: 1140 us -> 1140 us (level)
  transfers between devices with their start and end apart: 77 -> 77, of which waited for: 47 -> 49; matrix products, arithmetic and copies ran while one was open for 14% -> 14% of each run, Pallas kernels for 3% -> 3%
where the time goes in v6:
time: 1140 us
  waiting for transfers between devices  671 us (59%)
  Pallas kernels  159 us (14%)
  matrix products  116 us (10%)
  starting transfers between devices  66.8 us (6%)
  other arithmetic  60 us (5%)
  local copies, waits for them, and re-layouts  46 us (4%)
  between operations  16.2 us (1%)
    ppermute x73, waiting for transfers between devices, swap(): lax.ppermute(value, self.axis, [(i, i ^ bit) for i in range(self.size)])  402 us
    reduce_scatter x4, waiting for transfers between devices, z_scatter(): lax.psum_scatter(value, DP, scatter_dimension=0, tiled=True, axis_index_g...  267 us
    pallas_call x8, Pallas kernels, outer(): pl.pallas_call(functools.partial(outer_body, [len(g[1]) for g in groups],...  86.7 us
    dot_general x22, matrix products, mm_nt(): lax.dot_general(a, b, (((1,), (1,)), ((), ())), preferred_element_type=F32)  66.7 us
    ppermute x73, starting transfers between devices, swap(): lax.ppermute(value, self.axis, [(i, i ^ bit) for i in range(self.size)])  66.4 us
    dot_general x12, matrix products, mm(): return jnp.dot(a, b, preferred_element_type=F32)  49.8 us
    pallas_call x2, Pallas kernels, attend_back(): pl.pallas_call(attend_back_body, grid=(cols // step,), in_specs=[whole((r...  33.7 us
    pallas_call x2, Pallas kernels, attend(): pl.pallas_call(attend_body, grid=(cols // step,), in_specs=[chunk(x), who...  32.9 us
  transfers between devices with their start and end apart: 77, of which 49 were waited for; matrix products, arithmetic and copies ran while one was open for 14% of the time, Pallas kernels for 3%

profile of v6, /device:TPU:0, one launch (start us, length us, event | category | flops | bytes accessed | tf_op | source)
XLA Modules:
  0.0 1135.5 jit_solution(17969693147481397664)
XLA Ops:
  12.7 16.3 %shard_map.212 = (bf16[512,2048]{1,0:T(8,128)(2,1)}, bf16[512,512]{1,0:T(8,128)(2,1)}, bf16[512,512]{1,0:T(8,128)(2,1)}, bf16[512,512]{1,0:T(8,128)(2,1)}, bf16[512,512]{1,0:T(8,128)(2,1)}) custom-call(bf16[1024,2048]{1,0:T(8,128)(2,1)} %x.3, f32[1,2048]{1,0:T(1,128)} %bitcast.114, bf16[2048,512]{1,0:T(8,128)(2,1)} %wq.3, bf16[2048,512]{1,0:T(8,128)(2,1)} %wk.3, ...), custom_call_target="tpu_custom_call" | custom-call | flops 5368709120 | bytes 12582912 | tf_op jit(solution)/shard_map/pallas_call | solution.py:110
  32.4 3.0 collective-permute-start
  40.0 16.6 %shard_map.213 = (bf16[512,2048]{1,0:T(8,128)(2,1)}, bf16[512,512]{1,0:T(8,128)(2,1)}, bf16[512,512]{1,0:T(8,128)(2,1)}, bf16[512,512]{1,0:T(8,128)(2,1)}, bf16[512,512]{1,0:T(8,128)(2,1)}) custom-call(bf16[1024,2048]{1,0:T(8,128)(2,1)} %x.3, f32[1,2048]{1,0:T(1,128)} %bitcast.115, bf16[2048,512]{1,0:T(8,128)(2,1)} %wq.3, bf16[2048,512]{1,0:T(8,128)(2,1)} %wk.3, ...), custom_call_target="tpu_custom_call" | custom-call | flops 5368709120 | bytes 12582912 | tf_op jit(solution)/shard_map/pallas_call | solution.py:110
  74.6 11.7 %collective-permute-done.8 = f32[128,2048]{1,0:T(8,128)} collective-permute-done((f32[128,2048]{1,0:T(8,128)}, f32[128,2048]{1,0:T(8,128)}, u32[]{:S(2)}, u32[]{:S(2)}) %collective-permute-start.8) | collective-permute-done | bytes 1048608 | tf_op jit(solution)/shard_map/ppermute | solution.py:280
  90.9 6.5 collective-permute-done.3
  101.4 7.2 collective-permute-done.11
  114.3 5.6 collective-permute-done.6
  123.0 6.3 fusion.198
  130.3 5.9 shard_map.214.refs_0_.refs_3_.refs_6_
  142.2 12.1 %collective-permute-done.7 = f32[128,2048]{1,0:T(8,128)} collective-permute-done((f32[128,2048]{1,0:T(8,128)S(1)}, f32[128,2048]{1,0:T(8,128)}, u32[]{:S(2)}, u32[]{:S(2)}) %collective-permute-start.7) | collective-permute-done | bytes 1048608 | tf_op jit(solution)/shard_map/ppermute | solution.py:280
  159.2 15.4 %collective-permute-done.15 = f32[128,2048]{1,0:T(8,128)S(1)} collective-permute-done((f32[128,2048]{1,0:T(8,128)S(1)}, f32[128,2048]{1,0:T(8,128)S(1)}, u32[]{:S(2)}, u32[]{:S(2)}) %collective-permute-start.15) | collective-permute-done | bytes 1048608 | tf_op jit(solution)/shard_map/ppermute | solution.py:280
  174.6 6.1 fusion.195
  181.8 4.6 fusion.197
  188.4 6.9 multiply_convert_fusion.4
  195.2 10.8 multiply_convert_fusion
  206.1 8.7 outer.10
  214.8 4.9 outer.8
  220.2 9.6 fusion.196
  233.0 7.1 fusion.61
  240.1 5.3 outer.9
  245.4 10.4 outer.11
  255.8 7.3 multiply_convert_fusion.2
  263.1 15.7 %outer.12 = f32[1024,4096]{1,0:T(8,128)} custom-call(s32[1]{0:T(128)} %bitcast.6.which, bf16[512,2048]{1,0:T(8,128)(2,1)} %copy-done.3, bf16[512,2048]{1,0:T(8,128)(2,1)} %copy-done.4, bf16[512,2048]{1,0:T(8,128)(2,1)} %get-tuple-element.106.refs_2_, bf16[512,2048]{1,0:T(8,128)(2,1)} %get-tuple-element.104.refs_3_, bf16[512,2048]{1,0:T(8,128)(2,1)} %copy-done.3, ...), custom_call_target="tpu_custom_call" | custom-call | flops 8589934592 | bytes 29360128 | tf_op jit(solution)/shard_map/outer/pallas_call | solution.py:254
  278.8 6.7 convolution_add_fusion.8
  287.8 5.7 fusion.54
  293.6 5.9 convolution_add_fusion.9
  299.6 11.8 %collective-permute-done.38 = f32[128,2048]{1,0:T(8,128)S(1)} collective-permute-done((f32[128,2048]{1,0:T(8,128)S(1)}, f32[128,2048]{1,0:T(8,128)S(1)}, u32[]{:S(2)}, u32[]{:S(2)}) %collective-permute-start.38) | collective-permute-done | bytes 1048608 | tf_op jit(solution)/shard_map/ppermute | solution.py:280
  313.9 12.2 %collective-permute-done.41 = f32[64,2048]{1,0:T(8,128)S(1)} collective-permute-done((f32[64,2048]{1,0:T(8,128)S(1)}, f32[64,2048]{1,0:T(8,128)S(1)}, u32[]{:S(2)}, u32[]{:S(2)}) %collective-permute-start.41) | collective-permute-done | bytes 524320 | tf_op jit(solution)/shard_map/ppermute | solution.py:280
  330.8 6.0 convolution_add_fusion.10
  341.4 5.8 convolution_add_fusion.11
  347.2 13.2 %collective-permute-done.18 = f32[128,2048]{1,0:T(8,128)S(1)} collective-permute-done((f32[128,2048]{1,0:T(8,128)S(1)}, f32[128,2048]{1,0:T(8,128)S(1)}, u32[]{:S(2)}, u32[]{:S(2)}) %collective-permute-start.18) | collective-permute-done | bytes 1048608 | tf_op jit(solution)/shard_map/ppermute | solution.py:280
  363.6 9.2 collective-permute-done.21
  376.4 8.6 collective-permute-done.44
  389.8 11.7 %collective-permute-done.57 = f32[64,2048]{1,0:T(8,128)S(1)} collective-permute-done((f32[64,2048]{1,0:T(8,128)S(1)}, f32[64,2048]{1,0:T(8,128)S(1)}, u32[]{:S(2)}, u32[]{:S(2)}) %collective-permute-start.57) | collective-permute-done | bytes 524320 | tf_op jit(solution)/shard_map/ppermute | solution.py:280
  402.5 20.0 %collective-permute-done.55 = f32[64,2048]{1,0:T(8,128)S(1)} collective-permute-done((f32[64,2048]{1,0:T(8,128)S(1)}, f32[64,2048]{1,0:T(8,128)S(1)}, u32[]{:S(2)}, u32[]{:S(2)}) %collective-permute-start.55) | collective-permute-done | bytes 524320 | tf_op jit(solution)/shard_map/ppermute | solution.py:280
  428.7 12.7 %collective-permute-done.58 = f32[128,2048]{1,0:T(8,128)S(1)} collective-permute-done((f32[128,2048]{1,0:T(8,128)S(1)}, f32[128,2048]{1,0:T(8,128)S(1)}, u32[]{:S(2)}, u32[]{:S(2)}) %collective-permute-start.58) | collective-permute-done | bytes 1048608 | tf_op jit(solution)/shard_map/ppermute | solution.py:280
  444.1 19.9 %outer.13.rest_0_ = f32[1024,4096]{1,0:T(8,128)} custom-call(s32[1]{0:T(128)} %bitcast.4.which, bf16[512,2048]{1,0:T(8,128)(2,1)} %copy-done.3, bf16[512,2048]{1,0:T(8,128)(2,1)} %copy-done.4, bf16[512,2048]{1,0:T(8,128)(2,1)} %get-tuple-element.106.refs_2_, bf16[512,2048]{1,0:T(8,128)(2,1)} %get-tuple-element.104.refs_3_, bf16[512,2048]{1,0:T(8,128)(2,1)} %copy-done.3, ...), custom_call_target="tpu_custom_call" | custom-call | flops 8589934592 | bytes 29360128 | tf_op jit(solution)/shard_map/outer/pallas_call | solution.py:254
  464.0 17.0 %shard_map.215.refs_2_ = bf16[3,512,512]{2,1,0:T(8,128)(2,1)} custom-call(bf16[512,2048]{1,0:T(8,128)(2,1)} %fusion.4.hidden.refs_4_, bf16[512,2048]{1,0:T(8,128)(2,1)} %wo.3, bf16[512,512]{1,0:T(8,128)(2,1)} %get-tuple-element.52.q_in, bf16[512,512]{1,0:T(8,128)(2,1)} %get-tuple-element.53.k_in, bf16[512,512]{1,0:T(8,128)(2,1)} %get-tuple-element.54.v_in, ...), custom_call_target="tpu_custom_call" | custom-call | flops 6442450944 | bytes 7864320 | tf_op jit(solution)/shard_map/pallas_call | solution.py:154
  481.0 16.7 %shard_map.216.refs_3_ = bf16[3,512,512]{2,1,0:T(8,128)(2,1)} custom-call(bf16[512,2048]{1,0:T(8,128)(2,1)} %fusion.5.hidden.refs_5_, bf16[512,2048]{1,0:T(8,128)(2,1)} %wo.3, bf16[512,512]{1,0:T(8,128)(2,1)} %get-tuple-element.59.q_in, bf16[512,512]{1,0:T(8,128)(2,1)} %get-tuple-element.60.k_in, bf16[512,512]{1,0:T(8,128)(2,1)} %get-tuple-element.61.v_in, ...), custom_call_target="tpu_custom_call" | custom-call | flops 6442450944 | bytes 7864320 | tf_op jit(solution)/shard_map/pallas_call | solution.py:154
  497.7 9.8 outer.14
  507.5 13.5 %collective-permute-done.72.refs_8_ = f32[1024,2048]{1,0:T(8,128)} collective-permute-done((f32[1024,2048]{1,0:T(8,128)}, f32[1024,2048]{1,0:T(8,128)}, u32[]{:S(2)}, u32[]{:S(2)}) %collective-permute-start.72) | collective-permute-done | bytes 8388640 | tf_op jit(solution)/shard_map/ppermute | solution.py:280
  521.0 11.9 %outer.15 = f32[1024,2048]{1,0:T(8,128)} custom-call(s32[1]{0:T(128)} %bitcast.4.which, bf16[512,2048]{1,0:T(8,128)(2,1)} %get-tuple-element.62.refs_0_, bf16[512,2048]{1,0:T(8,128)(2,1)} %get-tuple-element.63.refs_1_, bf16[3,512,512]{2,1,0:T(8,128)(2,1)} %shard_map.215.refs_2_, bf16[3,512,512]{2,1,0:T(8,128)(2,1)} %shard_map.216.refs_3_, ...), custom_call_target="tpu_custom_call" | custom-call | flops 4294967296 | bytes 16777216 | tf_op jit(solution)/shard_map/outer/pallas_call | solution.py:254
  537.3 6.5 fusion.50
  545.6 6.0 fusion.42
  559.5 10.7 collective-permute-done.30
  572.8 19.9 %collective-permute-done.22 = f32[128,2048]{1,0:T(8,128)S(1)} collective-permute-done((f32[128,2048]{1,0:T(8,128)S(1)}, f32[128,2048]{1,0:T(8,128)S(1)}, u32[]{:S(2)}, u32[]{:S(2)}) %collective-permute-start.22) | collective-permute-done | bytes 1048608 | tf_op jit(solution)/shard_map/ppermute | solution.py:280
  595.2 8.7 collective-permute-done.33
  606.4 8.7 collective-permute-done.25
  619.3 7.2 collective-permute-done.36
  630.1 7.5 collective-permute-done.28
  640.2 20.7 %collective-permute-done.37 = f32[128,2048]{1,0:T(8,128)S(1)} collective-permute-done((f32[128,2048]{1,0:T(8,128)S(1)}, f32[128,2048]{1,0:T(8,128)S(1)}, u32[]{:S(2)}, u32[]{:S(2)}) %collective-permute-start.37) | collective-permute-done | bytes 1048608 | tf_op jit(solution)/shard_map/ppermute | solution.py:280
  661.4 21.0 %collective-permute-done.29 = f32[128,2048]{1,0:T(8,128)S(1)} collective-permute-done((f32[128,2048]{1,0:T(8,128)S(1)}, f32[128,2048]{1,0:T(8,128)S(1)}, u32[]{:S(2)}, u32[]{:S(2)}) %collective-permute-start.29) | collective-permute-done | bytes 1048608 | tf_op jit(solution)/shard_map/ppermute | solution.py:280
  704.0 35.5 %collective-permute-done.47 = f32[128,2048]{1,0:T(8,128)S(1)} collective-permute-done((f32[128,2048]{1,0:T(8,128)S(1)}, f32[128,2048]{1,0:T(8,128)S(1)}, u32[]{:S(2)}, u32[]{:S(2)}) %collective-permute-start.47) | collective-permute-done | bytes 1048608 | tf_op jit(solution)/shard_map/ppermute | solution.py:280
  745.3 10.1 collective-permute-done.50
  757.2 6.6 collective-permute-done.62
  770.6 3.0 collective-permute-done.68
  784.5 4.9 collective-permute-done.51
  791.9 8.7 collective-permute-done.63
  802.6 20.5 %collective-permute-done.54 = f32[128,2048]{1,0:T(8,128)S(1)} collective-permute-done((f32[128,2048]{1,0:T(8,128)S(1)}, f32[128,2048]{1,0:T(8,128)S(1)}, u32[]{:S(2)}, u32[]{:S(2)}) %collective-permute-start.54) | collective-permute-done | bytes 1048608 | tf_op jit(solution)/shard_map/ppermute | solution.py:280
  823.5 21.3 %collective-permute-done.66 = f32[128,2048]{1,0:T(8,128)S(1)} collective-permute-done((f32[128,2048]{1,0:T(8,128)S(1)}, f32[128,2048]{1,0:T(8,128)S(1)}, u32[]{:S(2)}, u32[]{:S(2)}) %collective-permute-start.66) | collective-permute-done | bytes 1048608 | tf_op jit(solution)/shard_map/ppermute | solution.py:280
  845.2 4.0 pad_maximum_fusion
  849.2 2.7 slice_bitcast_fusion
  852.9 267.4 %reduce-scatter.11.cloned.1.call-done = f32[256,4096]{1,0:T(8,128)} async-done(((f32[1024,4096]{1,0:T(8,128)}), f32[256,4096]{1,0:T(8,128)}) %reduce-scatter.11.cloned.1.call-update) | async-done | bytes 4194320 | tf_op jit(solution)/shard_map/reduce_scatter | solution.py:411
  1123.8 4.7 fusion.173
  (444 shorter events, 190.7 us)
Async XLA Ops:
  7.2 842.0 %reduce-scatter.5.cloned.1.call-start = ((), (), s32[]{:S(2)}) async-start(), calls=%async_computation.4 | async-start | bytes 10485760 | tf_op jit(solution)/shard_map/reduce_scatter | solution.py:411
  32.4 35.1 %collective-permute-start = (f32[128,2048]{1,0:T(8,128)}, f32[128,2048]{1,0:T(8,128)}, u32[]{:S(2)}, u32[]{:S(2)}) collective-permute-start(f32[128,2048]{1,0:T(8,128)} %get-tuple-element.176), channel_id=1, source_target_pairs={{0,1},{1,0},{2,3},{3,2},{4,5},{5,4},{6,7},{7,6},{8,9},{9,8},{10,11... | collective-permute-start | bytes 3145736 | tf_op jit(solution)/shard_map/ppermute | solution.py:280
  35.3 32.1 %collective-permute-start.2 = (f32[128,2048]{1,0:T(8,128)}, f32[128,2048]{1,0:T(8,128)}, u32[]{:S(2)}, u32[]{:S(2)}) collective-permute-start(f32[128,2048]{1,0:T(8,128)} %get-tuple-element.177), channel_id=1, source_target_pairs={{0,2},{1,3},{2,0},{3,1},{4,6},{5,7},{6,4},{7,5},{8,10},{9,11},{10,... | collective-permute-start | bytes 3145736 | tf_op jit(solution)/shard_map/ppermute | solution.py:280
  59.9 26.3 %collective-permute-start.8 = (f32[128,2048]{1,0:T(8,128)}, f32[128,2048]{1,0:T(8,128)}, u32[]{:S(2)}, u32[]{:S(2)}) collective-permute-start(f32[128,2048]{1,0:T(8,128)} %get-tuple-element.180), channel_id=1, source_target_pairs={{0,1},{1,0},{2,3},{3,2},{4,5},{5,4},{6,7},{7,6},{8,9},{9,8},{10,11... | collective-permute-start | bytes 3145736 | tf_op jit(solution)/shard_map/ppermute | solution.py:280
  60.5 26.3 %collective-permute-start.10 = (f32[128,2048]{1,0:T(8,128)}, f32[128,2048]{1,0:T(8,128)}, u32[]{:S(2)}, u32[]{:S(2)}) collective-permute-start(f32[128,2048]{1,0:T(8,128)} %get-tuple-element.181), channel_id=1, source_target_pairs={{0,2},{1,3},{2,0},{3,1},{4,6},{5,7},{6,4},{7,5},{8,10},{9,11},{10,... | collective-permute-start | bytes 3145736 | tf_op jit(solution)/shard_map/ppermute | solution.py:280
  70.9 26.5 %collective-permute-start.3 = (f32[64,2048]{1,0:T(8,128)S(1)}, f32[64,2048]{1,0:T(8,128)S(1)}, u32[]{:S(2)}, u32[]{:S(2)}) collective-permute-start(f32[64,2048]{1,0:T(8,128)S(1)} %constant_dynamic-slice_fusion.52), channel_id=1, source_target_pairs={{0,1},{1,0},{2,3},{3,2},{4,5},{5,4},{6,7},{7,6},{8,9},{9,8},{10,11... | collective-permute-start | bytes 1572872 | tf_op jit(solution)/shard_map/ppermute | solution.py:280
  73.0 25.0 %collective-permute-start.1 = (f32[64,2048]{1,0:T(8,128)S(1)}, f32[64,2048]{1,0:T(8,128)S(1)}, u32[]{:S(2)}, u32[]{:S(2)}) collective-permute-start(f32[64,2048]{1,0:T(8,128)S(1)} %constant_dynamic-slice_fusion.53), channel_id=1, source_target_pairs={{0,2},{1,3},{2,0},{3,1},{4,6},{5,7},{6,4},{7,5},{8,10},{9,11},{10,... | collective-permute-start | bytes 1572872 | tf_op jit(solution)/shard_map/ppermute | solution.py:280
  88.8 19.8 %collective-permute-start.11 = (f32[64,2048]{1,0:T(8,128)S(1)}, f32[64,2048]{1,0:T(8,128)S(1)}, u32[]{:S(2)}, u32[]{:S(2)}) collective-permute-start(f32[64,2048]{1,0:T(8,128)S(1)} %constant_dynamic-slice_fusion.42), channel_id=1, source_target_pairs={{0,1},{1,0},{2,3},{3,2},{4,5},{5,4},{6,7},{7,6},{8,9},{9,8},{10,11... | collective-permute-start | bytes 1572872 | tf_op jit(solution)/shard_map/ppermute | solution.py:280
  90.4 18.8 %collective-permute-start.9 = (f32[64,2048]{1,0:T(8,128)S(1)}, f32[64,2048]{1,0:T(8,128)S(1)}, u32[]{:S(2)}, u32[]{:S(2)}) collective-permute-start(f32[64,2048]{1,0:T(8,128)S(1)} %constant_dynamic-slice_fusion.43), channel_id=1, source_target_pairs={{0,2},{1,3},{2,0},{3,1},{4,6},{5,7},{6,4},{7,5},{8,10},{9,11},{10,... | collective-permute-start | bytes 1572872 | tf_op jit(solution)/shard_map/ppermute | solution.py:280
  99.4 21.1 %collective-permute-start.4 = (f32[64,2048]{1,0:T(8,128)S(1)}, f32[64,2048]{1,0:T(8,128)S(1)}, u32[]{:S(2)}, u32[]{:S(2)}) collective-permute-start(f32[64,2048]{1,0:T(8,128)S(1)} %get-tuple-element.202), channel_id=1, source_target_pairs={{0,2},{1,3},{2,0},{3,1},{4,6},{5,7},{6,4},{7,5},{8,10},{9,11},{10,... | collective-permute-start | bytes 1572872 | tf_op jit(solution)/shard_map/ppermute | solution.py:280
  99.5 20.4 %collective-permute-start.6 = (f32[64,2048]{1,0:T(8,128)S(1)}, f32[64,2048]{1,0:T(8,128)S(1)}, u32[]{:S(2)}, u32[]{:S(2)}) collective-permute-start(f32[64,2048]{1,0:T(8,128)S(1)} %get-tuple-element.203), channel_id=1, source_target_pairs={{0,1},{1,0},{2,3},{3,2},{4,5},{5,4},{6,7},{7,6},{8,9},{9,8},{10,11... | collective-permute-start | bytes 1572872 | tf_op jit(solution)/shard_map/ppermute | solution.py:280
  112.3 26.5 %collective-permute-start.12 = (f32[64,2048]{1,0:T(8,128)}, f32[64,2048]{1,0:T(8,128)}, u32[]{:S(2)}, u32[]{:S(2)}) collective-permute-start(f32[64,2048]{1,0:T(8,128)} %get-tuple-element.200), channel_id=1, source_target_pairs={{0,2},{1,3},{2,0},{3,1},{4,6},{5,7},{6,4},{7,5},{8,10},{9,11},{10,... | collective-permute-start | bytes 1572872 | tf_op jit(solution)/shard_map/ppermute | solution.py:280
  112.4 23.9 %collective-permute-start.14 = (f32[64,2048]{1,0:T(8,128)}, f32[64,2048]{1,0:T(8,128)}, u32[]{:S(2)}, u32[]{:S(2)}) collective-permute-start(f32[64,2048]{1,0:T(8,128)} %get-tuple-element.201), channel_id=1, source_target_pairs={{0,1},{1,0},{2,3},{3,2},{4,5},{5,4},{6,7},{7,6},{8,9},{9,8},{10,11... | collective-permute-start | bytes 1572872 | tf_op jit(solution)/shard_map/ppermute | solution.py:280
  120.0 34.3 %collective-permute-start.7 = (f32[128,2048]{1,0:T(8,128)S(1)}, f32[128,2048]{1,0:T(8,128)}, u32[]{:S(2)}, u32[]{:S(2)}) collective-permute-start(f32[128,2048]{1,0:T(8,128)S(1)} %maximum_select_fusion.17), channel_id=1, source_target_pairs={{0,2},{1,3},{2,0},{3,1},{4,6},{5,7},{6,4},{7,5},{8,10},{9,11},{10,... | collective-permute-start | bytes 3145736 | tf_op jit(solution)/shard_map/ppermute | solution.py:280
  121.6 34.4 %collective-permute-start.5 = (f32[128,2048]{1,0:T(8,128)}, f32[128,2048]{1,0:T(8,128)}, u32[]{:S(2)}, u32[]{:S(2)}) collective-permute-start(f32[128,2048]{1,0:T(8,128)} %maximum_select_fusion.16), channel_id=1, source_target_pairs={{0,1},{1,0},{2,3},{3,2},{4,5},{5,4},{6,7},{7,6},{8,9},{9,8},{10,11... | collective-permute-start | bytes 3145736 | tf_op jit(solution)/shard_map/ppermute | solution.py:280
  138.1 36.6 %collective-permute-start.15 = (f32[128,2048]{1,0:T(8,128)S(1)}, f32[128,2048]{1,0:T(8,128)S(1)}, u32[]{:S(2)}, u32[]{:S(2)}) collective-permute-start(f32[128,2048]{1,0:T(8,128)S(1)} %maximum_select_fusion.19), channel_id=1, source_target_pairs={{0,2},{1,3},{2,0},{3,1},{4,6},{5,7},{6,4},{7,5},{8,10},{9,11},{10,... | collective-permute-start | bytes 3145736 | tf_op jit(solution)/shard_map/ppermute | solution.py:280
  140.6 40.1 %collective-permute-start.13 = (f32[128,2048]{1,0:T(8,128)S(1)}, f32[128,2048]{1,0:T(8,128)S(1)}, u32[]{:S(2)}, u32[]{:S(2)}) collective-permute-start(f32[128,2048]{1,0:T(8,128)S(1)} %maximum_select_fusion.18), channel_id=1, source_target_pairs={{0,1},{1,0},{2,3},{3,2},{4,5},{5,4},{6,7},{7,6},{8,9},{9,8},{10,11... | collective-permute-start | bytes 3145736 | tf_op jit(solution)/shard_map/ppermute | solution.py:280
  214.8 30.6 %collective-permute-start.17 = (f32[1024,1536]{1,0:T(8,128)}, f32[1024,1536]{1,0:T(8,128)}, u32[]{:S(2)}, u32[]{:S(2)}) collective-permute-start(f32[1024,1536]{1,0:T(8,128)} %outer.10), channel_id=1, source_target_pairs={{0,4},{4,0},{8,12},{12,8},{16,20},{20,16},{24,28},{28,24},{1,5},{5... | collective-permute-start | bytes 18874376 | tf_op jit(solution)/shard_map/ppermute | solution.py:280
  219.7 20.4 %collective-permute-start.16 = (f32[1024,512]{1,0:T(8,128)}, f32[1024,512]{1,0:T(8,128)}, u32[]{:S(2)}, u32[]{:S(2)}) collective-permute-start(f32[1024,512]{1,0:T(8,128)} %outer.8), channel_id=1, source_target_pairs={{0,4},{4,0},{8,12},{12,8},{16,20},{20,16},{24,28},{28,24},{1,5},{5... | collective-permute-start | bytes 6291464 | tf_op jit(solution)/shard_map/ppermute | solution.py:280
  278.8 165.3 %collective-permute-start.46 = (f32[1024,4096]{1,0:T(8,128)}, f32[1024,4096]{1,0:T(8,128)}, u32[]{:S(2)}, u32[]{:S(2)}) collective-permute-start(f32[1024,4096]{1,0:T(8,128)} %outer.12), channel_id=1, source_target_pairs={{0,4},{4,0},{8,12},{12,8},{16,20},{20,16},{24,28},{28,24},{1,5},{5... | collective-permute-start | bytes 50331656 | tf_op jit(solution)/shard_map/ppermute | solution.py:280
  285.8 25.6 %collective-permute-start.38 = (f32[128,2048]{1,0:T(8,128)S(1)}, f32[128,2048]{1,0:T(8,128)S(1)}, u32[]{:S(2)}, u32[]{:S(2)}) collective-permute-start(f32[128,2048]{1,0:T(8,128)S(1)} %get-tuple-element.136), channel_id=1, source_target_pairs={{0,1},{1,0},{2,3},{3,2},{4,5},{5,4},{6,7},{7,6},{8,9},{9,8},{10,11... | collective-permute-start | bytes 3145736 | tf_op jit(solution)/shard_map/ppermute | solution.py:280
  287.3 25.3 %collective-permute-start.40 = (f32[128,2048]{1,0:T(8,128)S(1)}, f32[128,2048]{1,0:T(8,128)S(1)}, u32[]{:S(2)}, u32[]{:S(2)}) collective-permute-start(f32[128,2048]{1,0:T(8,128)S(1)} %get-tuple-element.137), channel_id=1, source_target_pairs={{0,2},{1,3},{2,0},{3,1},{4,6},{5,7},{6,4},{7,5},{8,10},{9,11},{10,... | collective-permute-start | bytes 3145736 | tf_op jit(solution)/shard_map/ppermute | solution.py:280
  337.0 23.4 %collective-permute-start.18 = (f32[128,2048]{1,0:T(8,128)S(1)}, f32[128,2048]{1,0:T(8,128)S(1)}, u32[]{:S(2)}, u32[]{:S(2)}) collective-permute-start(f32[128,2048]{1,0:T(8,128)S(1)} %get-tuple-element.164), channel_id=1, source_target_pairs={{0,1},{1,0},{2,3},{3,2},{4,5},{5,4},{6,7},{7,6},{8,9},{9,8},{10,11... | collective-permute-start | bytes 3145736 | tf_op jit(solution)/shard_map/ppermute | solution.py:280
  338.5 23.0 %collective-permute-start.20 = (f32[128,2048]{1,0:T(8,128)S(1)}, f32[128,2048]{1,0:T(8,128)S(1)}, u32[]{:S(2)}, u32[]{:S(2)}) collective-permute-start(f32[128,2048]{1,0:T(8,128)S(1)} %get-tuple-element.165), channel_id=1, source_target_pairs={{0,2},{1,3},{2,0},{3,1},{4,6},{5,7},{6,4},{7,5},{8,10},{9,11},{10,... | collective-permute-start | bytes 3145736 | tf_op jit(solution)/shard_map/ppermute | solution.py:280
  385.2 39.6 %collective-permute-start.45 = (f32[128,2048]{1,0:T(8,128)S(1)}, f32[128,2048]{1,0:T(8,128)S(1)}, u32[]{:S(2)}, u32[]{:S(2)}) collective-permute-start(f32[128,2048]{1,0:T(8,128)S(1)} %maximum_select_fusion.25), channel_id=1, source_target_pairs={{0,2},{1,3},{2,0},{3,1},{4,6},{5,7},{6,4},{7,5},{8,10},{9,11},{10,... | collective-permute-start | bytes 3145736 | tf_op jit(solution)/shard_map/ppermute | solution.py:280
  386.6 14.9 %collective-permute-start.57 = (f32[64,2048]{1,0:T(8,128)S(1)}, f32[64,2048]{1,0:T(8,128)S(1)}, u32[]{:S(2)}, u32[]{:S(2)}) collective-permute-start(f32[64,2048]{1,0:T(8,128)S(1)} %get-tuple-element.193), channel_id=1, source_target_pairs={{0,1},{1,0},{2,3},{3,2},{4,5},{5,4},{6,7},{7,6},{8,9},{9,8},{10,11... | collective-permute-start | bytes 1572872 | tf_op jit(solution)/shard_map/ppermute | solution.py:280
  387.5 35.0 %collective-permute-start.55 = (f32[64,2048]{1,0:T(8,128)S(1)}, f32[64,2048]{1,0:T(8,128)S(1)}, u32[]{:S(2)}, u32[]{:S(2)}) collective-permute-start(f32[64,2048]{1,0:T(8,128)S(1)} %get-tuple-element.192), channel_id=1, source_target_pairs={{0,2},{1,3},{2,0},{3,1},{4,6},{5,7},{6,4},{7,5},{8,10},{9,11},{10,... | collective-permute-start | bytes 1572872 | tf_op jit(solution)/shard_map/ppermute | solution.py:280
  389.6 35.4 %collective-permute-start.43 = (f32[128,2048]{1,0:T(8,128)S(1)}, f32[128,2048]{1,0:T(8,128)S(1)}, u32[]{:S(2)}, u32[]{:S(2)}) collective-permute-start(f32[128,2048]{1,0:T(8,128)S(1)} %maximum_select_fusion.24), channel_id=1, source_target_pairs={{0,1},{1,0},{2,3},{3,2},{4,5},{5,4},{6,7},{7,6},{8,9},{9,8},{10,11... | collective-permute-start | bytes 3145736 | tf_op jit(solution)/shard_map/ppermute | solution.py:280
  401.6 39.8 %collective-permute-start.58 = (f32[128,2048]{1,0:T(8,128)S(1)}, f32[128,2048]{1,0:T(8,128)S(1)}, u32[]{:S(2)}, u32[]{:S(2)}) collective-permute-start(f32[128,2048]{1,0:T(8,128)S(1)} %maximum_select_fusion.29), channel_id=1, source_target_pairs={{0,2},{1,3},{2,0},{3,1},{4,6},{5,7},{6,4},{7,5},{8,10},{9,11},{10,... | collective-permute-start | bytes 3145736 | tf_op jit(solution)/shard_map/ppermute | solution.py:280
  422.6 18.8 %collective-permute-start.56 = (f32[128,2048]{1,0:T(8,128)S(1)}, f32[128,2048]{1,0:T(8,128)S(1)}, u32[]{:S(2)}, u32[]{:S(2)}) collective-permute-start(f32[128,2048]{1,0:T(8,128)S(1)} %maximum_select_fusion.28), channel_id=1, source_target_pairs={{0,1},{1,0},{2,3},{3,2},{4,5},{5,4},{6,7},{7,6},{8,9},{9,8},{10,11... | collective-permute-start | bytes 3145736 | tf_op jit(solution)/shard_map/ppermute | solution.py:280
  533.0 319.9 %reduce-scatter.7.cloned.1.call-start = ((), (), s32[]{:S(2)}) async-start(), calls=%async_computation.5 | async-start | bytes 2621440 | tf_op jit(solution)/shard_map/reduce_scatter | solution.py:411
  533.8 319.1 %reduce-scatter.9.cloned.1.call-start = ((), (), s32[]{:S(2)}) async-start(), calls=%async_computation.6 | async-start | bytes 7864320 | tf_op jit(solution)/shard_map/reduce_scatter | solution.py:411
  534.5 585.8 %reduce-scatter.11.cloned.1.call-start = ((), (), s32[]{:S(2)}) async-start(), calls=%async_computation.7 | async-start | bytes 20971520 | tf_op jit(solution)/shard_map/reduce_scatter | solution.py:411
  544.1 26.1 %collective-permute-start.30 = (f32[128,2048]{1,0:T(8,128)S(1)}, f32[128,2048]{1,0:T(8,128)S(1)}, u32[]{:S(2)}, u32[]{:S(2)}) collective-permute-start(f32[128,2048]{1,0:T(8,128)S(1)} %get-tuple-element.156), channel_id=1, source_target_pairs={{0,1},{1,0},{2,3},{3,2},{4,5},{5,4},{6,7},{7,6},{8,9},{9,8},{10,11... | collective-permute-start | bytes 3145736 | tf_op jit(solution)/shard_map/ppermute | solution.py:280
  545.0 26.0 %collective-permute-start.32 = (f32[128,2048]{1,0:T(8,128)S(1)}, f32[128,2048]{1,0:T(8,128)S(1)}, u32[]{:S(2)}, u32[]{:S(2)}) collective-permute-start(f32[128,2048]{1,0:T(8,128)S(1)} %get-tuple-element.157), channel_id=1, source_target_pairs={{0,2},{1,3},{2,0},{3,1},{4,6},{5,7},{6,4},{7,5},{8,10},{9,11},{10,... | collective-permute-start | bytes 3145736 | tf_op jit(solution)/shard_map/ppermute | solution.py:280
  551.8 40.8 %collective-permute-start.22 = (f32[128,2048]{1,0:T(8,128)S(1)}, f32[128,2048]{1,0:T(8,128)S(1)}, u32[]{:S(2)}, u32[]{:S(2)}) collective-permute-start(f32[128,2048]{1,0:T(8,128)S(1)} %get-tuple-element.148), channel_id=1, source_target_pairs={{0,1},{1,0},{2,3},{3,2},{4,5},{5,4},{6,7},{7,6},{8,9},{9,8},{10,11... | collective-permute-start | bytes 3145736 | tf_op jit(solution)/shard_map/ppermute | solution.py:280
  552.8 40.8 %collective-permute-start.24 = (f32[128,2048]{1,0:T(8,128)S(1)}, f32[128,2048]{1,0:T(8,128)S(1)}, u32[]{:S(2)}, u32[]{:S(2)}) collective-permute-start(f32[128,2048]{1,0:T(8,128)S(1)} %get-tuple-element.149), channel_id=1, source_target_pairs={{0,2},{1,3},{2,0},{3,1},{4,6},{5,7},{6,4},{7,5},{8,10},{9,11},{10,... | collective-permute-start | bytes 3145736 | tf_op jit(solution)/shard_map/ppermute | solution.py:280
  571.5 32.4 %collective-permute-start.33 = (f32[64,2048]{1,0:T(8,128)S(1)}, f32[64,2048]{1,0:T(8,128)S(1)}, u32[]{:S(2)}, u32[]{:S(2)}) collective-permute-start(f32[64,2048]{1,0:T(8,128)S(1)} %constant_dynamic-slice_fusion.20), channel_id=1, source_target_pairs={{0,1},{1,0},{2,3},{3,2},{4,5},{5,4},{6,7},{7,6},{8,9},{9,8},{10,11... | collective-permute-start | bytes 1572872 | tf_op jit(solution)/shard_map/ppermute | solution.py:280
  572.7 32.1 %collective-permute-start.31 = (f32[64,2048]{1,0:T(8,128)S(1)}, f32[64,2048]{1,0:T(8,128)S(1)}, u32[]{:S(2)}, u32[]{:S(2)}) collective-permute-start(f32[64,2048]{1,0:T(8,128)S(1)} %constant_dynamic-slice_fusion.21), channel_id=1, source_target_pairs={{0,2},{1,3},{2,0},{3,1},{4,6},{5,7},{6,4},{7,5},{8,10},{9,11},{10,... | collective-permute-start | bytes 1572872 | tf_op jit(solution)/shard_map/ppermute | solution.py:280
  594.0 21.1 %collective-permute-start.25 = (f32[64,2048]{1,0:T(8,128)S(1)}, f32[64,2048]{1,0:T(8,128)S(1)}, u32[]{:S(2)}, u32[]{:S(2)}) collective-permute-start(f32[64,2048]{1,0:T(8,128)S(1)} %constant_dynamic-slice_fusion.26), channel_id=1, source_target_pairs={{0,1},{1,0},{2,3},{3,2},{4,5},{5,4},{6,7},{7,6},{8,9},{9,8},{10,11... | collective-permute-start | bytes 1572872 | tf_op jit(solution)/shard_map/ppermute | solution.py:280
  595.2 20.8 %collective-permute-start.23 = (f32[64,2048]{1,0:T(8,128)S(1)}, f32[64,2048]{1,0:T(8,128)S(1)}, u32[]{:S(2)}, u32[]{:S(2)}) collective-permute-start(f32[64,2048]{1,0:T(8,128)S(1)} %constant_dynamic-slice_fusion.27), channel_id=1, source_target_pairs={{0,2},{1,3},{2,0},{3,1},{4,6},{5,7},{6,4},{7,5},{8,10},{9,11},{10,... | collective-permute-start | bytes 1572872 | tf_op jit(solution)/shard_map/ppermute | solution.py:280
  605.1 22.7 %collective-permute-start.34 = (f32[64,2048]{1,0:T(8,128)S(1)}, f32[64,2048]{1,0:T(8,128)}, u32[]{:S(2)}, u32[]{:S(2)}) collective-permute-start(f32[64,2048]{1,0:T(8,128)S(1)} %get-tuple-element.198), channel_id=1, source_target_pairs={{0,2},{1,3},{2,0},{3,1},{4,6},{5,7},{6,4},{7,5},{8,10},{9,11},{10,... | collective-permute-start | bytes 1572872 | tf_op jit(solution)/shard_map/ppermute | solution.py:280
  605.2 21.2 %collective-permute-start.36 = (f32[64,2048]{1,0:T(8,128)S(1)}, f32[64,2048]{1,0:T(8,128)}, u32[]{:S(2)}, u32[]{:S(2)}) collective-permute-start(f32[64,2048]{1,0:T(8,128)S(1)} %get-tuple-element.199), channel_id=1, source_target_pairs={{0,1},{1,0},{2,3},{3,2},{4,5},{5,4},{6,7},{7,6},{8,9},{9,8},{10,11... | collective-permute-start | bytes 1572872 | tf_op jit(solution)/shard_map/ppermute | solution.py:280
  616.3 21.3 %collective-permute-start.28 = (f32[64,2048]{1,0:T(8,128)S(1)}, f32[64,2048]{1,0:T(8,128)}, u32[]{:S(2)}, u32[]{:S(2)}) collective-permute-start(f32[64,2048]{1,0:T(8,128)S(1)} %get-tuple-element.197), channel_id=1, source_target_pairs={{0,1},{1,0},{2,3},{3,2},{4,5},{5,4},{6,7},{7,6},{8,9},{9,8},{10,11... | collective-permute-start | bytes 1572872 | tf_op jit(solution)/shard_map/ppermute | solution.py:280
  619.3 19.8 %collective-permute-start.26 = (f32[64,2048]{1,0:T(8,128)S(1)}, f32[64,2048]{1,0:T(8,128)S(1)}, u32[]{:S(2)}, u32[]{:S(2)}) collective-permute-start(f32[64,2048]{1,0:T(8,128)S(1)} %get-tuple-element.196), channel_id=1, source_target_pairs={{0,2},{1,3},{2,0},{3,1},{4,6},{5,7},{6,4},{7,5},{8,10},{9,11},{10,... | collective-permute-start | bytes 1572872 | tf_op jit(solution)/shard_map/ppermute | solution.py:280
  627.8 33.2 %collective-permute-start.37 = (f32[128,2048]{1,0:T(8,128)S(1)}, f32[128,2048]{1,0:T(8,128)S(1)}, u32[]{:S(2)}, u32[]{:S(2)}) collective-permute-start(f32[128,2048]{1,0:T(8,128)S(1)} %maximum_select_fusion.23), channel_id=1, source_target_pairs={{0,2},{1,3},{2,0},{3,1},{4,6},{5,7},{6,4},{7,5},{8,10},{9,11},{10,... | collective-permute-start | bytes 3145736 | tf_op jit(solution)/shard_map/ppermute | solution.py:280
  629.2 32.0 %collective-permute-start.35 = (f32[128,2048]{1,0:T(8,128)S(1)}, f32[128,2048]{1,0:T(8,128)S(1)}, u32[]{:S(2)}, u32[]{:S(2)}) collective-permute-start(f32[128,2048]{1,0:T(8,128)S(1)} %maximum_select_fusion.22), channel_id=1, source_target_pairs={{0,1},{1,0},{2,3},{3,2},{4,5},{5,4},{6,7},{7,6},{8,9},{9,8},{10,11... | collective-permute-start | bytes 3145736 | tf_op jit(solution)/shard_map/ppermute | solution.py:280
  639.0 43.3 %collective-permute-start.29 = (f32[128,2048]{1,0:T(8,128)S(1)}, f32[128,2048]{1,0:T(8,128)S(1)}, u32[]{:S(2)}, u32[]{:S(2)}) collective-permute-start(f32[128,2048]{1,0:T(8,128)S(1)} %maximum_select_fusion.21), channel_id=1, source_target_pairs={{0,2},{1,3},{2,0},{3,1},{4,6},{5,7},{6,4},{7,5},{8,10},{9,11},{10,... | collective-permute-start | bytes 3145736 | tf_op jit(solution)/shard_map/ppermute | solution.py:280
  639.2 43.3 %collective-permute-start.27 = (f32[128,2048]{1,0:T(8,128)S(1)}, f32[128,2048]{1,0:T(8,128)S(1)}, u32[]{:S(2)}, u32[]{:S(2)}) collective-permute-start(f32[128,2048]{1,0:T(8,128)S(1)} %maximum_select_fusion.20), channel_id=1, source_target_pairs={{0,1},{1,0},{2,3},{3,2},{4,5},{5,4},{6,7},{7,6},{8,9},{9,8},{10,11... | collective-permute-start | bytes 3145736 | tf_op jit(solution)/shard_map/ppermute | solution.py:280
  692.7 49.5 %collective-permute-start.59 = (f32[128,2048]{1,0:T(8,128)S(1)}, f32[128,2048]{1,0:T(8,128)S(1)}, u32[]{:S(2)}, u32[]{:S(2)}) collective-permute-start(f32[128,2048]{1,0:T(8,128)S(1)} %get-tuple-element.132), channel_id=1, source_target_pairs={{0,1},{1,0},{2,3},{3,2},{4,5},{5,4},{6,7},{7,6},{8,9},{9,8},{10,11... | collective-permute-start | bytes 3145736 | tf_op jit(solution)/shard_map/ppermute | solution.py:280
  693.9 48.3 %collective-permute-start.61 = (f32[128,2048]{1,0:T(8,128)S(1)}, f32[128,2048]{1,0:T(8,128)S(1)}, u32[]{:S(2)}, u32[]{:S(2)}) collective-permute-start(f32[128,2048]{1,0:T(8,128)S(1)} %get-tuple-element.133), channel_id=1, source_target_pairs={{0,2},{1,3},{2,0},{3,1},{4,6},{5,7},{6,4},{7,5},{8,10},{9,11},{10,... | collective-permute-start | bytes 3145736 | tf_op jit(solution)/shard_map/ppermute | solution.py:280
  696.9 42.6 %collective-permute-start.47 = (f32[128,2048]{1,0:T(8,128)S(1)}, f32[128,2048]{1,0:T(8,128)S(1)}, u32[]{:S(2)}, u32[]{:S(2)}) collective-permute-start(f32[128,2048]{1,0:T(8,128)S(1)} %get-tuple-element.126), channel_id=1, source_target_pairs={{0,1},{1,0},{2,3},{3,2},{4,5},{5,4},{6,7},{7,6},{8,9},{9,8},{10,11... | collective-permute-start | bytes 3145736 | tf_op jit(solution)/shard_map/ppermute | solution.py:280
  698.1 42.1 %collective-permute-start.49 = (f32[128,2048]{1,0:T(8,128)S(1)}, f32[128,2048]{1,0:T(8,128)S(1)}, u32[]{:S(2)}, u32[]{:S(2)}) collective-permute-start(f32[128,2048]{1,0:T(8,128)S(1)} %get-tuple-element.127), channel_id=1, source_target_pairs={{0,2},{1,3},{2,0},{3,1},{4,6},{5,7},{6,4},{7,5},{8,10},{9,11},{10,... | collective-permute-start | bytes 3145736 | tf_op jit(solution)/shard_map/ppermute | solution.py:280
  740.6 14.9 %collective-permute-start.50 = (f32[64,2048]{1,0:T(8,128)S(1)}, f32[64,2048]{1,0:T(8,128)S(1)}, u32[]{:S(2)}, u32[]{:S(2)}) collective-permute-start(f32[64,2048]{1,0:T(8,128)S(1)} %constant_dynamic-slice_fusion.6), channel_id=1, source_target_pairs={{0,1},{1,0},{2,3},{3,2},{4,5},{5,4},{6,7},{7,6},{8,9},{9,8},{10,11... | collective-permute-start | bytes 1572872 | tf_op jit(solution)/shard_map/ppermute | solution.py:280
  741.8 14.9 %collective-permute-start.48 = (f32[64,2048]{1,0:T(8,128)S(1)}, f32[64,2048]{1,0:T(8,128)S(1)}, u32[]{:S(2)}, u32[]{:S(2)}) collective-permute-start(f32[64,2048]{1,0:T(8,128)S(1)} %constant_dynamic-slice_fusion.7), channel_id=1, source_target_pairs={{0,2},{1,3},{2,0},{3,1},{4,6},{5,7},{6,4},{7,5},{8,10},{9,11},{10,... | collective-permute-start | bytes 1572872 | tf_op jit(solution)/shard_map/ppermute | solution.py:280
  742.6 21.1 %collective-permute-start.62 = (f32[64,2048]{1,0:T(8,128)S(1)}, f32[64,2048]{1,0:T(8,128)S(1)}, u32[]{:S(2)}, u32[]{:S(2)}) collective-permute-start(f32[64,2048]{1,0:T(8,128)S(1)} %constant_dynamic-slice_fusion.2), channel_id=1, source_target_pairs={{0,1},{1,0},{2,3},{3,2},{4,5},{5,4},{6,7},{7,6},{8,9},{9,8},{10,11... | collective-permute-start | bytes 1572872 | tf_op jit(solution)/shard_map/ppermute | solution.py:280
  744.0 20.9 %collective-permute-start.60 = (f32[64,2048]{1,0:T(8,128)S(1)}, f32[64,2048]{1,0:T(8,128)S(1)}, u32[]{:S(2)}, u32[]{:S(2)}) collective-permute-start(f32[64,2048]{1,0:T(8,128)S(1)} %constant_dynamic-slice_fusion.3), channel_id=1, source_target_pairs={{0,2},{1,3},{2,0},{3,1},{4,6},{5,7},{6,4},{7,5},{8,10},{9,11},{10,... | collective-permute-start | bytes 1572872 | tf_op jit(solution)/shard_map/ppermute | solution.py:280
  766.7 17.2 %collective-permute-start.53 = (f32[64,2048]{1,0:T(8,128)S(1)}, f32[64,2048]{1,0:T(8,128)S(1)}, u32[]{:S(2)}, u32[]{:S(2)}) collective-permute-start(f32[64,2048]{1,0:T(8,128)S(1)} %get-tuple-element.189), channel_id=1, source_target_pairs={{0,1},{1,0},{2,3},{3,2},{4,5},{5,4},{6,7},{7,6},{8,9},{9,8},{10,11... | collective-permute-start | bytes 1572872 | tf_op jit(solution)/shard_map/ppermute | solution.py:280
  773.7 17.3 %collective-permute-start.65 = (f32[64,2048]{1,0:T(8,128)S(1)}, f32[64,2048]{1,0:T(8,128)S(1)}, u32[]{:S(2)}, u32[]{:S(2)}) collective-permute-start(f32[64,2048]{1,0:T(8,128)S(1)} %get-tuple-element.191), channel_id=1, source_target_pairs={{0,1},{1,0},{2,3},{3,2},{4,5},{5,4},{6,7},{7,6},{8,9},{9,8},{10,11... | collective-permute-start | bytes 1572872 | tf_op jit(solution)/shard_map/ppermute | solution.py:280
  779.4 21.2 %collective-permute-start.63 = (f32[64,2048]{1,0:T(8,128)S(1)}, f32[64,2048]{1,0:T(8,128)S(1)}, u32[]{:S(2)}, u32[]{:S(2)}) collective-permute-start(f32[64,2048]{1,0:T(8,128)S(1)} %get-tuple-element.190), channel_id=1, source_target_pairs={{0,2},{1,3},{2,0},{3,1},{4,6},{5,7},{6,4},{7,5},{8,10},{9,11},{10,... | collective-permute-start | bytes 1572872 | tf_op jit(solution)/shard_map/ppermute | solution.py:280
  784.0 39.1 %collective-permute-start.54 = (f32[128,2048]{1,0:T(8,128)S(1)}, f32[128,2048]{1,0:T(8,128)S(1)}, u32[]{:S(2)}, u32[]{:S(2)}) collective-permute-start(f32[128,2048]{1,0:T(8,128)S(1)} %maximum_select_fusion.27), channel_id=1, source_target_pairs={{0,2},{1,3},{2,0},{3,1},{4,6},{5,7},{6,4},{7,5},{8,10},{9,11},{10,... | collective-permute-start | bytes 3145736 | tf_op jit(solution)/shard_map/ppermute | solution.py:280
  789.7 33.6 %collective-permute-start.52 = (f32[128,2048]{1,0:T(8,128)S(1)}, f32[128,2048]{1,0:T(8,128)S(1)}, u32[]{:S(2)}, u32[]{:S(2)}) collective-permute-start(f32[128,2048]{1,0:T(8,128)S(1)} %maximum_select_fusion.26), channel_id=1, source_target_pairs={{0,1},{1,0},{2,3},{3,2},{4,5},{5,4},{6,7},{7,6},{8,9},{9,8},{10,11... | collective-permute-start | bytes 3145736 | tf_op jit(solution)/shard_map/ppermute | solution.py:280
  791.2 53.6 %collective-permute-start.66 = (f32[128,2048]{1,0:T(8,128)S(1)}, f32[128,2048]{1,0:T(8,128)S(1)}, u32[]{:S(2)}, u32[]{:S(2)}) collective-permute-start(f32[128,2048]{1,0:T(8,128)S(1)} %maximum_select_fusion.31), channel_id=1, source_target_pairs={{0,2},{1,3},{2,0},{3,1},{4,6},{5,7},{6,4},{7,5},{8,10},{9,11},{10,... | collective-permute-start | bytes 3145736 | tf_op jit(solution)/shard_map/ppermute | solution.py:280
  800.7 44.3 %collective-permute-start.64 = (f32[128,2048]{1,0:T(8,128)S(1)}, f32[128,2048]{1,0:T(8,128)S(1)}, u32[]{:S(2)}, u32[]{:S(2)}) collective-permute-start(f32[128,2048]{1,0:T(8,128)S(1)} %maximum_select_fusion.30), channel_id=1, source_target_pairs={{0,1},{1,0},{2,3},{3,2},{4,5},{5,4},{6,7},{7,6},{8,9},{9,8},{10,11... | collective-permute-start | bytes 3145736 | tf_op jit(solution)/shard_map/ppermute | solution.py:280
  (80 other events, 1186.7 us)
Sparse Core Ops, SparseCore 0:
  533.1 144.3 reduce-scatter.4
  679.8 44.2 reduce-scatter.6
  726.4 110.6 reduce-scatter.8
  839.3 280.9 reduce-scatter.10
